TPU v7x, 32 devices: a whole 2x2x4 slice. The times are simulated.
32 devices in a mesh: dp: 4 (over z), row: 2 (over x), col: 4 (over y, core).
Axes of the slice: x: 2, y: 2, z: 4, core: 2. Of those that a mesh axis runs over, the one named last changes fastest.
Arguments:
- tokens: bfloat16 [4096, 2048], P(('dp', 'row'), 'col'), may hold values from -6 to 6
- cotangent: bfloat16 [4096, 2048], P(('dp', 'row'), 'col'), may hold values from -6 to 6
- query_master: float32 [2048, 2048], P('col', ('row', 'dp')), may hold values from -0.1875 to 0.1875
- key_master: float32 [2048, 2048], P('col', ('row', 'dp')), may hold values from -0.125 to 0.125
- value_master: float32 [2048, 2048], P('col', ('row', 'dp')), may hold values from -0.125 to 0.125
- out_master: float32 [2048, 2048], P(('row', 'dp'), 'col'), may hold values from -2 to 2
- gate_master: float32 [2048, 8192], P('col', ('row', 'dp')), may hold values from -0.125 to 0.125
- up_master: float32 [2048, 8192], P('col', ('row', 'dp')), may hold values from -0.125 to 0.125
- down_master: float32 [8192, 2048], P(('row', 'dp'), 'col'), may hold values from -0.0625 to 0.0625
- attn_gain: float32 [2048], P('col'), may hold values from 0.1 to 1.9
- ffn_gain: float32 [2048], P('col'), may hold values from 0.1 to 1.9
- lengths: int32 [28], replicated, may hold values from 1 to 768, as said below
- permutation: int32 [4096], replicated, may hold values from 0 to 4095, as said below
Outputs:
- grad_tokens: float32 [4096, 2048], P(('dp', 'row'), 'col')
- grad_query: float32 [2048, 2048], P('col', ('row', 'dp'))
- grad_key: float32 [2048, 2048], P('col', ('row', 'dp'))
- grad_value: float32 [2048, 2048], P('col', ('row', 'dp'))
- grad_out: float32 [2048, 2048], P(('row', 'dp'), 'col')
- grad_gate: float32 [2048, 8192], P('col', ('row', 'dp'))
- grad_up: float32 [2048, 8192], P('col', ('row', 'dp'))
- grad_down: float32 [8192, 2048], P(('row', 'dp'), 'col')
- grad_attn_gain: float32 [2048], P('col')
- grad_ffn_gain: float32 [2048], P('col')
Inputs may be any that keep to these rules, and one draw needn't show every extreme that they name: 28 lengths; those of each group's 7 sequences sum to 1024, and the largest of every group is 768. A permutation of all token indices; the slots of group d hold exactly the tokens of 7 whole sequences; laid one after another, these sequences are cut into blocks of 32 tokens, and block b goes to the quarter b % 4 of the group's slots, in order.
All inputs are finite; a program needn't handle non-finite values.
Results may differ from a plain program's by a relative error of at most 0.015.
The roundings to bfloat16 on the way count: a program that leaves them out, or rounds other values in their place, can miss the bound.
Values may be sent and summed in bfloat16 or wider, within the bound.
A program may use at most 256 MiB of HBM per device.

v0:
```python
import jax
import jax.numpy as jnp
from jax import lax
from jax.sharding import PartitionSpec as P

D = 2048
HEAD_DIM = 128


EPSILON = 1e-06
NEG_FILL = -1e30


def make_picker(wanted, carried, pieces):
    amount = pieces[0].shape[0]
    inside = (wanted >= 0) & (wanted < amount)
    chosen = jnp.clip(wanted, 0, amount - 1)
    return tuple(
        (
            jnp.where(inside[:, None], jnp.take(shard_rows, chosen, axis=0), current)
            for shard_rows, current in zip(pieces, carried)
        )
    )


def sequence_marks(permutation, lengths, first_slot, amount):
    source = lax.dynamic_slice_in_dim(permutation, first_slot, amount)
    seq_ends = jnp.cumsum(lengths)
    passed = seq_ends[None, :] <= source[:, None]
    member = jnp.sum(passed.astype(jnp.int32), axis=1)
    begins = jnp.max(jnp.where(passed, seq_ends[None, :], 0), axis=1)
    return (member, source - begins)


def col_total(values):
    return lax.psum(jnp.sum(values, axis=1), "col")


def row_gather(values):
    return lax.all_gather(values, "row", axis=0, tiled=True)


def col_gather(values):
    return lax.all_gather(values, "col", axis=0, tiled=True)


def key_gather(keys_here, values_here):
    return (
        lax.all_gather(keys_here, "col", axis=0, tiled=True),
        lax.all_gather(values_here, "col", axis=0, tiled=True),
    )


def multiply(row_block, weight, transpose_right):
    if transpose_right:
        return lax.dot_general(
            row_block, weight, (((1,), (1,)), ((), ())), preferred_element_type=jnp.float32
        )
    return jnp.dot(row_block, weight, preferred_element_type=jnp.float32)


def outer_sum(left_rows, right_rows):
    return lax.dot_general(
        left_rows, right_rows, (((0,), (0,)), ((), ())), preferred_element_type=jnp.float32
    )


def col_reduce(spread, weight, transpose_right):
    return lax.psum_scatter(
        multiply(spread, weight, transpose_right), "col", scatter_dimension=0, tiled=True
    )


def row_reduce(spread, weight, transpose_right):
    return lax.psum_scatter(
        multiply(spread, weight, transpose_right), "row", scatter_dimension=0, tiled=True
    )


def visible(query_member, query_position, member, position):
    same = query_member[:, None] == member[None, :]
    behind = position[None, :] <= query_position[:, None]
    return same & behind


def attend_scores(query_block, key_all, allowed):
    scores = jnp.einsum(
        "qhd,khd->hqk", query_block, key_all, preferred_element_type=jnp.float32
    ) * HEAD_DIM ** (-0.5)
    return jnp.where(allowed[None, :, :], scores, NEG_FILL)


def norm_back(grad_normed, inputs_f, scale_rows, gain):
    gain_part = jnp.sum(grad_normed * inputs_f * scale_rows[:, None], axis=0)
    scaled = grad_normed * gain[None, :]
    inner = col_total(scaled * inputs_f)
    grad_inputs = scale_rows[:, None] * scaled - inputs_f * (scale_rows**3 * inner / D)[:, None]
    return (grad_inputs, gain_part)


def on_device(
    tokens,
    cotangent,
    query_master,
    key_master,
    value_master,
    out_master,
    gate_master,
    up_master,
    down_master,
    attn_gain,
    ffn_gain,
    lengths,
    permutation,
):
    own_rows = tokens.shape[0]
    group_rows = own_rows * lax.axis_size("row")
    quarter = group_rows // lax.axis_size("col")
    device_slot = lax.axis_index(("dp", "row"))
    group_slot = lax.axis_index("dp")
    col_slot = lax.axis_index("col")
    own_sources = lax.dynamic_slice_in_dim(permutation, device_slot * own_rows, own_rows)
    own_tokens, own_cotangent = make_picker(
        own_sources,
        (jnp.zeros_like(tokens), jnp.zeros_like(cotangent)),
        (
            lax.all_gather(tokens, ("dp", "row"), axis=0, tiled=True),
            lax.all_gather(cotangent, ("dp", "row"), axis=0, tiled=True),
        ),
    )
    masters = tuple(
        (
            matrix.astype(jnp.bfloat16)
            for matrix in (
                query_master,
                key_master,
                value_master,
                out_master,
                gate_master,
                up_master,
                down_master,
            )
        )
    )
    query_weight, key_weight, value_weight, out_weight, gate_weight, up_weight, down_weight = (
        lax.all_gather(masters[0], "dp", axis=1, tiled=True),
        lax.all_gather(masters[1], "dp", axis=1, tiled=True),
        lax.all_gather(masters[2], "dp", axis=1, tiled=True),
        lax.all_gather(masters[3], "dp", axis=0, tiled=True),
        lax.all_gather(masters[4], "dp", axis=1, tiled=True),
        lax.all_gather(masters[5], "dp", axis=1, tiled=True),
        lax.all_gather(masters[6], "dp", axis=0, tiled=True),
    )
    attention_in = jnp.concatenate([query_weight, key_weight, value_weight], axis=1)
    feedforward_in = jnp.concatenate([gate_weight, up_weight], axis=1)
    width_row = query_weight.shape[1]
    heads_row = width_row // HEAD_DIM
    hidden_row = gate_weight.shape[1]
    member, position = sequence_marks(permutation, lengths, group_slot * group_rows, group_rows)
    query_member = lax.dynamic_slice_in_dim(member, col_slot * quarter, quarter)
    query_position = lax.dynamic_slice_in_dim(position, col_slot * quarter, quarter)
    block_rows = min(512, quarter)
    block_count = quarter // block_rows
    residual_in = own_tokens.astype(jnp.float32)
    scale_one = lax.rsqrt(col_total(residual_in * residual_in) / D + EPSILON)
    normed_one = (residual_in * scale_one[:, None] * attn_gain[None, :]).astype(jnp.bfloat16)
    spread_one = row_gather(normed_one)
    projected = col_reduce(spread_one, attention_in, False).astype(jnp.bfloat16)
    queries = projected[:, :width_row].reshape(quarter, heads_row, HEAD_DIM)
    keys_here = projected[:, width_row : 2 * width_row]
    values_here = projected[:, 2 * width_row :]
    key_flat, value_flat = key_gather(keys_here, values_here)
    key_all = key_flat.reshape(group_rows, heads_row, HEAD_DIM)
    value_all = value_flat.reshape(group_rows, heads_row, HEAD_DIM)

    def block_mask(first_row):
        return visible(
            lax.dynamic_slice_in_dim(query_member, first_row, block_rows),
            lax.dynamic_slice_in_dim(query_position, first_row, block_rows),
            member,
            position,
        )

    def forward_block(block_id):
        first_row = block_id * block_rows
        query_block = lax.dynamic_slice_in_dim(queries, first_row, block_rows, 0)
        scores = attend_scores(query_block, key_all, block_mask(first_row))
        highest = jnp.max(scores, axis=2, keepdims=True)
        totals = jnp.sum(jnp.exp(scores - highest), axis=2, keepdims=True)
        log_total = highest + jnp.log(totals)
        probability = jnp.exp(scores - log_total)
        output = jnp.einsum(
            "hqk,khd->qhd",
            probability.astype(jnp.bfloat16),
            value_all,
            preferred_element_type=jnp.float32,
        )
        return (output.astype(jnp.bfloat16).reshape(block_rows, width_row), log_total[:, :, 0])

    blocks_out, log_totals = lax.map(forward_block, jnp.arange(block_count, dtype=jnp.int32))
    attended = blocks_out.reshape(quarter, width_row)
    spread_attn = col_gather(attended)
    midway = residual_in + row_reduce(spread_attn, out_weight, False)
    scale_two = lax.rsqrt(col_total(midway * midway) / D + EPSILON)
    normed_two = (midway * scale_two[:, None] * ffn_gain[None, :]).astype(jnp.bfloat16)
    spread_two = row_gather(normed_two)
    gate_and_up = col_reduce(spread_two, feedforward_in, False)
    gate_value = gate_and_up[:, :hidden_row]
    up_value = gate_and_up[:, hidden_row:]
    sigmoid_gate = jax.nn.sigmoid(gate_value)
    hidden = (gate_value * sigmoid_gate * up_value).astype(jnp.bfloat16)
    grad_output = own_cotangent.astype(jnp.float32)
    spread_down = row_gather(own_cotangent)
    grad_hidden = col_reduce(spread_down, down_weight, True)
    spread_hidden = col_gather(hidden)
    grad_down = outer_sum(spread_hidden, spread_down)
    grad_gate_value = (
        grad_hidden * up_value * sigmoid_gate * (1.0 + gate_value * (1.0 - sigmoid_gate))
    ).astype(jnp.bfloat16)
    grad_up_value = (grad_hidden * gate_value * sigmoid_gate).astype(jnp.bfloat16)
    spread_gate_up = col_gather(jnp.concatenate([grad_gate_value, grad_up_value], axis=1))
    grad_normed_two = row_reduce(spread_gate_up, feedforward_in, True)
    spread_two = row_gather(normed_two)
    grad_feedforward = outer_sum(spread_two, spread_gate_up)
    grad_mid_norm, gain_two_part = norm_back(grad_normed_two, midway, scale_two, ffn_gain)
    grad_midway = grad_output + grad_mid_norm
    rounded_midway = grad_midway.astype(jnp.bfloat16)
    spread_back = row_gather(rounded_midway)
    grad_attended = col_reduce(spread_back, out_weight, True).astype(jnp.bfloat16)
    spread_attn = col_gather(attended)
    key_flat, value_flat = key_gather(keys_here, values_here)
    key_all = key_flat.reshape(group_rows, heads_row, HEAD_DIM)
    value_all = value_flat.reshape(group_rows, heads_row, HEAD_DIM)
    grad_out_local = outer_sum(spread_attn, spread_back)

    def backward_block(carried, block_id):
        first_row = block_id * block_rows
        query_block = lax.dynamic_slice_in_dim(queries, first_row, block_rows, 0)
        scores = attend_scores(query_block, key_all, block_mask(first_row))
        probability = jnp.exp(
            scores - lax.dynamic_index_in_dim(log_totals, block_id, 0, keepdims=False)[:, :, None]
        )
        weights_low = probability.astype(jnp.bfloat16)
        grad_block = lax.dynamic_slice_in_dim(grad_attended, first_row, block_rows, 0).reshape(
            block_rows, heads_row, HEAD_DIM
        )
        grad_soft = jnp.einsum(
            "qhd,khd->hqk", grad_block, value_all, preferred_element_type=jnp.float32
        )
        row_inner = jnp.sum(probability * grad_soft, axis=2, keepdims=True)
        grad_scores = (probability * (grad_soft - row_inner)).astype(jnp.bfloat16)
        grad_query_block = jnp.einsum(
            "hqk,khd->qhd", grad_scores, key_all, preferred_element_type=jnp.float32
        ) * HEAD_DIM ** (-0.5)
        grad_key_all = carried[0] + jnp.einsum(
            "hqk,qhd->khd", grad_scores, query_block, preferred_element_type=jnp.float32
        ) * HEAD_DIM ** (-0.5)
        grad_value_all = carried[1] + jnp.einsum(
            "hqk,qhd->khd", weights_low, grad_block, preferred_element_type=jnp.float32
        )
        return (
            (grad_key_all, grad_value_all),
            grad_query_block.astype(jnp.bfloat16).reshape(block_rows, width_row),
        )

    start_grads = jnp.zeros((group_rows, heads_row, HEAD_DIM), jnp.float32)
    key_value_grads, grad_queries = lax.scan(
        backward_block, (start_grads, start_grads), jnp.arange(block_count, dtype=jnp.int32)
    )
    grad_queries = grad_queries.reshape(quarter, width_row)
    grad_key_part = key_value_grads[0].reshape(group_rows, width_row)
    grad_value_part = key_value_grads[1].reshape(group_rows, width_row)
    grad_key_mine, grad_value_mine = (
        lax.psum_scatter(grad_key_part, "col", scatter_dimension=0, tiled=True),
        lax.psum_scatter(grad_value_part, "col", scatter_dimension=0, tiled=True),
    )
    spread_projected = col_gather(
        jnp.concatenate(
            [
                grad_queries,
                grad_key_mine.astype(jnp.bfloat16),
                grad_value_mine.astype(jnp.bfloat16),
            ],
            axis=1,
        )
    )
    grad_normed_one = row_reduce(spread_projected, attention_in, True)
    spread_one = row_gather(normed_one)
    grad_attention = outer_sum(spread_one, spread_projected)
    grad_in_norm, gain_one_part = norm_back(grad_normed_one, residual_in, scale_one, attn_gain)
    grad_own_tokens = grad_midway + grad_in_norm
    grad_attn_gain, grad_ffn_gain = lax.psum((gain_one_part, gain_two_part), ("dp", "row"))
    grad_query, grad_key, grad_value, grad_out, grad_gate, grad_up, grad_down_mine = (
        lax.psum_scatter(
            grad_attention[:, :width_row].astype(jnp.bfloat16),
            "dp",
            scatter_dimension=1,
            tiled=True,
        ).astype(jnp.float32),
        lax.psum_scatter(
            grad_attention[:, width_row : 2 * width_row].astype(jnp.bfloat16),
            "dp",
            scatter_dimension=1,
            tiled=True,
        ).astype(jnp.float32),
        lax.psum_scatter(
            grad_attention[:, 2 * width_row :].astype(jnp.bfloat16),
            "dp",
            scatter_dimension=1,
            tiled=True,
        ).astype(jnp.float32),
        lax.psum_scatter(
            grad_out_local.astype(jnp.bfloat16), "dp", scatter_dimension=0, tiled=True
        ).astype(jnp.float32),
        lax.psum_scatter(
            grad_feedforward[:, :hidden_row].astype(jnp.bfloat16),
            "dp",
            scatter_dimension=1,
            tiled=True,
        ).astype(jnp.float32),
        lax.psum_scatter(
            grad_feedforward[:, hidden_row:].astype(jnp.bfloat16),
            "dp",
            scatter_dimension=1,
            tiled=True,
        ).astype(jnp.float32),
        lax.psum_scatter(
            grad_down.astype(jnp.bfloat16), "dp", scatter_dimension=0, tiled=True
        ).astype(jnp.float32),
    )
    total_tokens = permutation.shape[0]
    inverse = (
        jnp.zeros((total_tokens,), jnp.int32)
        .at[permutation]
        .set(jnp.arange(total_tokens, dtype=jnp.int32))
    )
    wanted_slots = lax.dynamic_slice_in_dim(inverse, device_slot * own_rows, own_rows)
    (grad_tokens,) = make_picker(
        wanted_slots,
        (jnp.zeros_like(grad_own_tokens),),
        (
            (
                lax.all_gather(
                    grad_own_tokens.astype(jnp.bfloat16), ("dp", "row"), axis=0, tiled=True
                ),
            )[0].astype(jnp.float32),
        ),
    )
    return (
        grad_tokens,
        grad_query,
        grad_key,
        grad_value,
        grad_out,
        grad_gate,
        grad_up,
        grad_down_mine,
        grad_attn_gain,
        grad_ffn_gain,
    )


def solution(mesh):
    placed = (
        P(("dp", "row"), "col"),
        P(("dp", "row"), "col"),
        P("col", ("row", "dp")),
        P("col", ("row", "dp")),
        P("col", ("row", "dp")),
        P(("row", "dp"), "col"),
        P("col", ("row", "dp")),
        P("col", ("row", "dp")),
        P(("row", "dp"), "col"),
        P("col"),
        P("col"),
        P(),
        P(),
    )
    return jax.shard_map(
        on_device,
        mesh=mesh,
        in_specs=placed,
        out_specs=(
            P(("dp", "row"), "col"),
            P("col", ("row", "dp")),
            P("col", ("row", "dp")),
            P("col", ("row", "dp")),
            P(("row", "dp"), "col"),
            P("col", ("row", "dp")),
            P("col", ("row", "dp")),
            P(("row", "dp"), "col"),
            P("col"),
            P("col"),
        ),
        check_vma=False,
    )
```

profile of v0, /device:TPU:0, one launch (start us, length us, event | category | flops | bytes accessed | tf_op | source)
XLA Modules:
  0.0 2124.0 jit_solution(9994761716558908774)
XLA Ops:
  14.3 72.0 %all-gather.23.cloned.1.call-done = bf16[4096,512]{1,0:T(8,128)(2,1)} async-done(((bf16[512,512]{1,0:T(8,128)(2,1)}), bf16[4096,512]{1,0:T(8,128)(2,1)}) %all-gather.23.cloned.1.call-update) | async-done | bytes 4194320 | tf_op jit(solution)/shard_map/all_gather | solution.py:127
  98.8 18.1 all-gather.27.cloned.1.call-done
  119.2 28.3 %all-gather.29.cloned.1.call-done = bf16[512,1024]{1,0:T(8,128)(2,1)} async-done(((bf16[512,256]{1,0:T(8,128)(2,1)}), bf16[512,1024]{1,0:T(8,128)(2,1)}) %all-gather.29.cloned.1.call-update) | async-done | bytes 1048592 | tf_op jit(solution)/shard_map/all_gather | solution.py:147
  149.9 28.2 %all-gather.31.cloned.1.call-done = bf16[512,1024]{1,0:T(8,128)(2,1)} async-done(((bf16[512,256]{1,0:T(8,128)(2,1)}), bf16[512,1024]{1,0:T(8,128)(2,1)}) %all-gather.31.cloned.1.call-update) | async-done | bytes 1048592 | tf_op jit(solution)/shard_map/all_gather | solution.py:148
  180.4 19.3 all-gather.25.cloned.1.call-done
  199.7 10.2 fusion.36
  210.0 99.1 %reduce-scatter.17.cloned.1.call-done = f32[256,3072]{1,0:T(8,128)} async-done(((f32[1024,3072]{1,0:T(8,128)}), f32[256,3072]{1,0:T(8,128)}) %reduce-scatter.17.cloned.1.call-update) | async-done | bytes 3145744 | tf_op jit(solution)/shard_map/reduce_scatter | solution.py:69
  315.3 19.8 all-gather.35.cloned.1.call-done
  343.1 16.8 all-gather.33.cloned.1.call-done
  359.8 7.2 fusion.9
  367.9 22.0 %all-gather.39.cloned.1.call-done = bf16[1024,512]{1,0:T(8,128)(2,1)} async-done(((bf16[256,512]{1,0:T(8,128)(2,1)}), bf16[1024,512]{1,0:T(8,128)(2,1)}) %all-gather.39.cloned.1.call-update) | async-done | bytes 1048592 | tf_op jit(solution)/shard_map/all_gather | solution.py:149
  390.0 24.3 %all-gather.37.cloned.1.call-done = bf16[1024,1024]{0,1:T(8,128)(2,1)} async-done(((bf16[256,1024]{0,1:T(8,128)(2,1)}), bf16[1024,1024]{0,1:T(8,128)(2,1)}) %all-gather.37.cloned.1.call-update) | async-done | bytes 2097168 | tf_op jit(solution)/shard_map/all_gather | solution.py:44
  420.0 69.8 %all-gather.21.cloned.1.call-done = bf16[4096,512]{1,0:T(8,128)(2,1)} async-done(((bf16[512,512]{1,0:T(8,128)(2,1)}), bf16[4096,512]{1,0:T(8,128)(2,1)}) %all-gather.21.cloned.1.call-update) | async-done | bytes 4194320 | tf_op jit(solution)/shard_map/all_gather | solution.py:128
  499.9 22.8 %reduce-scatter.19.cloned.1.call-done = f32[512,512]{1,0:T(8,128)} async-done(((f32[1024,512]{1,0:T(8,128)}), f32[512,512]{1,0:T(8,128)}) %reduce-scatter.19.cloned.1.call-update) | async-done | bytes 1048592 | tf_op jit(solution)/shard_map/reduce_scatter | solution.py:75
  534.0 71.6 %all-gather.43.cloned.1.call-done = bf16[4096,512]{1,0:T(8,128)(2,1)} async-done(((bf16[1024,512]{1,0:T(8,128)(2,1)}), bf16[4096,512]{1,0:T(8,128)(2,1)}) %all-gather.43.cloned.1.call-update) | async-done | bytes 4194320 | tf_op jit(solution)/shard_map/all_gather | solution.py:152
  605.7 21.9 %all-gather.41.cloned.1.call-done = bf16[1024,512]{1,0:T(8,128)(2,1)} async-done(((bf16[512,512]{1,0:T(8,128)(2,1)}), bf16[1024,512]{1,0:T(8,128)(2,1)}) %all-gather.41.cloned.1.call-update) | async-done | bytes 1048592 | tf_op jit(solution)/shard_map/all_gather | solution.py:40
  627.6 13.7 fusion.38
  641.3 69.1 %all-gather.47.cloned.1.call-done = bf16[512,4096]{1,0:T(8,128)(2,1)} async-done(((bf16[512,1024]{1,0:T(8,128)(2,1)}), bf16[512,4096]{1,0:T(8,128)(2,1)}) %all-gather.47.cloned.1.call-update) | async-done | bytes 4194320 | tf_op jit(solution)/shard_map/all_gather | solution.py:150
  715.1 76.1 %all-gather.49.cloned.1.call-done = bf16[512,4096]{1,0:T(8,128)(2,1)} async-done(((bf16[512,1024]{1,0:T(8,128)(2,1)}), bf16[512,4096]{1,0:T(8,128)(2,1)}) %all-gather.49.cloned.1.call-update) | async-done | bytes 4194320 | tf_op jit(solution)/shard_map/all_gather | solution.py:151
  795.9 17.3 all-gather.45.cloned.1.call-done
  813.2 25.4 %fusion.39 = f32[1024,8192]{1,0:T(8,128)} fusion(bf16[1024,512]{1,0:T(8,128)(2,1)} %all-gather.45.cloned.1.call-done, bf16[512,8192]{1,0:T(8,128)(2,1)} %constant_dynamic-update-slice_fusion.3), kind=kOutput, calls=%fused_computation.92 | convolution fusion | flops 8589934592 | bytes 42991616 | tf_op jit(solution)/shard_map/dot_general | solution.py:59
  838.7 103.3 %reduce-scatter.21.cloned.1.call-done = f32[256,4096]{1,0:T(8,128)} async-done(((f32[1024,4096]{1,0:T(8,128)}), f32[256,4096]{1,0:T(8,128)}) %reduce-scatter.21.cloned.1.call-update) | async-done | bytes 4194320 | tf_op jit(solution)/shard_map/reduce_scatter | solution.py:69
  942.0 237.5 %reduce-scatter.23.cloned.1.call-done = f32[256,8192]{1,0:T(8,128)} async-done(((f32[1024,8192]{1,0:T(8,128)}), f32[256,8192]{1,0:T(8,128)}) %reduce-scatter.23.cloned.1.call-update) | async-done | bytes 8388624 | tf_op jit(solution)/shard_map/reduce_scatter | solution.py:69
  1179.4 7.0 multiply_convert_fusion.3
  1189.1 105.8 %all-gather.51.cloned.1.call-done = bf16[1024,8192]{1,0:T(8,128)(2,1)} async-done(((bf16[256,8192]{1,0:T(8,128)(2,1)}), bf16[1024,8192]{1,0:T(8,128)(2,1)}) %all-gather.51.cloned.1.call-update) | async-done | bytes 16777232 | tf_op jit(solution)/shard_map/all_gather | solution.py:44
  1295.0 15.8 fusion.40
  1310.8 31.9 %reduce-scatter.25.cloned.1.call-done = f32[512,512]{1,0:T(8,128)} async-done(((f32[1024,512]{1,0:T(8,128)}), f32[512,512]{1,0:T(8,128)}) %reduce-scatter.25.cloned.1.call-update) | async-done | bytes 1048592 | tf_op jit(solution)/shard_map/reduce_scatter | solution.py:75
  1344.5 6.9 psum.44
  1354.0 20.5 all-gather.53.cloned.1.call-done
  1379.4 44.6 %reduce-scatter.27.cloned.1.call-done = f32[256,1024]{1,0:T(8,128)} async-done(((f32[1024,1024]{1,0:T(8,128)}), f32[256,1024]{1,0:T(8,128)}) %reduce-scatter.27.cloned.1.call-update) | async-done | bytes 1048592 | tf_op jit(solution)/shard_map/reduce_scatter | solution.py:69
  1438.0 7.7 fusion.29
  1451.7 30.7 %reduce-scatter.29.cloned.1.call-done = f32[256,1024]{0,1:T(8,128)} async-done(((f32[1024,1024]{0,1:T(8,128)}), f32[256,1024]{0,1:T(8,128)}) %reduce-scatter.29.cloned.1.call-update) | async-done | bytes 1048592 | tf_op jit(solution)/shard_map/reduce_scatter | solution.py:274
  1483.7 46.0 %reduce-scatter.31.cloned.1.call-done = f32[256,1024]{0,1:T(8,128)} async-done(((f32[1024,1024]{0,1:T(8,128)}), f32[256,1024]{0,1:T(8,128)}) %reduce-scatter.31.cloned.1.call-update) | async-done | bytes 1048592 | tf_op jit(solution)/shard_map/reduce_scatter | solution.py:275
  1533.9 46.7 %all-gather.55.cloned.1.call-done = bf16[1024,3072]{0,1:T(8,128)(2,1)} async-done(((bf16[256,3072]{0,1:T(8,128)(2,1)}), bf16[1024,3072]{0,1:T(8,128)(2,1)}) %all-gather.55.cloned.1.call-update) | async-done | bytes 6291472 | tf_op jit(solution)/shard_map/all_gather | solution.py:44
  1580.7 8.5 fusion.42
  1589.2 51.7 %all-gather.59.cloned.1.call-done = bf16[1024,4096]{1,0:T(8,128)(2,1)} async-done(((bf16[256,4096]{1,0:T(8,128)(2,1)}), bf16[1024,4096]{1,0:T(8,128)(2,1)}) %all-gather.59.cloned.1.call-update) | async-done | bytes 8388624 | tf_op jit(solution)/shard_map/all_gather | solution.py:44
  1641.0 9.8 convolution_convert_fusion.1
  1655.3 12.6 convolution_convert_fusion
  1693.8 15.5 scatter_custom_fusion
  1709.5 45.4 %reduce-scatter.47.cloned.1.call-done = bf16[1024,512]{1,0:T(8,128)(2,1)} async-done(((bf16[4096,512]{1,0:T(8,128)(2,1)}), bf16[1024,512]{1,0:T(8,128)(2,1)}) %reduce-scatter.47.cloned.1.call-update) | async-done | bytes 1048592 | tf_op jit(solution)/shard_map/reduce_scatter | solution.py:327
  1757.7 27.6 %reduce-scatter.41.cloned.1.call-done = bf16[256,512]{1,0:T(8,128)(2,1)} async-done(((bf16[1024,512]{1,0:T(8,128)(2,1)}), bf16[256,512]{1,0:T(8,128)(2,1)}) %reduce-scatter.41.cloned.1.call-update) | async-done | bytes 262160 | tf_op jit(solution)/shard_map/reduce_scatter | solution.py:312
  1787.1 76.0 %reduce-scatter.43.cloned.1.call-done = bf16[512,1024]{1,0:T(8,128)(2,1)} async-done(((bf16[512,4096]{1,0:T(8,128)(2,1)}), bf16[512,1024]{1,0:T(8,128)(2,1)}) %reduce-scatter.43.cloned.1.call-update) | async-done | bytes 1048592 | tf_op jit(solution)/shard_map/reduce_scatter | solution.py:315
  1865.9 76.8 %reduce-scatter.45.cloned.1.call-done = bf16[512,1024]{1,0:T(8,128)(2,1)} async-done(((bf16[512,4096]{1,0:T(8,128)(2,1)}), bf16[512,1024]{1,0:T(8,128)(2,1)}) %reduce-scatter.45.cloned.1.call-update) | async-done | bytes 1048592 | tf_op jit(solution)/shard_map/reduce_scatter | solution.py:321
  1945.5 27.1 %reduce-scatter.35.cloned.1.call-done = bf16[512,256]{1,0:T(8,128)(2,1)} async-done(((bf16[512,1024]{1,0:T(8,128)(2,1)}), bf16[512,256]{1,0:T(8,128)(2,1)}) %reduce-scatter.35.cloned.1.call-update) | async-done | bytes 262160 | tf_op jit(solution)/shard_map/reduce_scatter | solution.py:294
  1974.4 26.4 %reduce-scatter.37.cloned.1.call-done = bf16[512,256]{1,0:T(8,128)(2,1)} async-done(((bf16[512,1024]{1,0:T(8,128)(2,1)}), bf16[512,256]{1,0:T(8,128)(2,1)}) %reduce-scatter.37.cloned.1.call-update) | async-done | bytes 262160 | tf_op jit(solution)/shard_map/reduce_scatter | solution.py:300
  2002.5 27.0 %reduce-scatter.39.cloned.1.call-done = bf16[512,256]{1,0:T(8,128)(2,1)} async-done(((bf16[512,1024]{1,0:T(8,128)(2,1)}), bf16[512,256]{1,0:T(8,128)(2,1)}) %reduce-scatter.39.cloned.1.call-update) | async-done | bytes 262160 | tf_op jit(solution)/shard_map/reduce_scatter | solution.py:306
  2031.3 20.0 all-reduce
  2051.3 52.4 %all-gather.57.cloned.1.call-done = bf16[4096,512]{1,0:T(8,128)(2,1)} async-done(((bf16[512,512]{1,0:T(8,128)(2,1)}), bf16[4096,512]{1,0:T(8,128)(2,1)}) %all-gather.57.cloned.1.call-update) | async-done | bytes 4194320 | tf_op jit(solution)/shard_map/all_gather | solution.py:343
  (202 shorter events, 174.2 us)
Async XLA Ops:
  7.2 79.1 %all-gather.23.cloned.1.call-start = ((), (), s32[]{:S(2)}) async-start(), calls=%async_computation.17 | async-start | bytes 4718592 | tf_op jit(solution)/shard_map/all_gather | solution.py:127
  7.9 89.7 %copy-start.15 = (f32[512]{0:T(512)S(1)}, f32[512]{0:T(512)}, u32[]{:S(2)}) copy-start(f32[512]{0:T(512)} %param.24) | copy-start | bytes 6148
  7.9 109.0 %all-gather.27.cloned.1.call-start = ((), (), s32[]{:S(2)}) async-start(), calls=%async_computation.19 | async-start | bytes 1310720 | tf_op jit(solution)/shard_map/all_gather | solution.py:146
  9.8 137.8 %all-gather.29.cloned.1.call-start = ((), (), s32[]{:S(2)}) async-start(), calls=%async_computation.20 | async-start | bytes 1310720 | tf_op jit(solution)/shard_map/all_gather | solution.py:147
  11.6 166.5 %all-gather.31.cloned.1.call-start = ((), (), s32[]{:S(2)}) async-start(), calls=%async_computation.21 | async-start | bytes 1310720 | tf_op jit(solution)/shard_map/all_gather | solution.py:148
  13.5 186.3 %all-gather.25.cloned.1.call-start = ((), (), s32[]{:S(2)}) async-start(), calls=%async_computation.18 | async-start | bytes 1572864 | tf_op jit(solution)/shard_map/all_gather | solution.py:40
  97.0 112.9 %copy-start.17 = (f32[512]{0:T(512)}, f32[512]{0:T(512)S(1)}, u32[]{:S(2)}) copy-start(f32[512]{0:T(512)S(1)} %psum.42) | copy-start | bytes 6148
  98.7 210.4 %reduce-scatter.17.cloned.1.call-start = ((), (), s32[]{:S(2)}) async-start(), calls=%async_computation.22 | async-start | bytes 15728640 | tf_op jit(solution)/shard_map/reduce_scatter | solution.py:69
  209.9 103.2 %copy-start.9 = (f32[256,512]{1,0:T(8,128)S(1)}, f32[256,512]{1,0:T(8,128)}, u32[]{:S(2)}) copy-start(f32[256,512]{1,0:T(8,128)} %param.20) | copy-start | bytes 1572868
  209.9 104.2 %copy-start.10 = (s32[4096]{0:T(1024)S(1)}, s32[4096]{0:T(1024)}, u32[]{:S(2)}) copy-start(s32[4096]{0:T(1024)} %param.27) | copy-start | bytes 49156
  209.9 104.3 %copy-start.19 = (s32[28]{0:T(128)S(1)}, s32[28]{0:T(128)}, u32[]{:S(2)}) copy-start(s32[28]{0:T(128)} %param.26) | copy-start | bytes 340
  209.9 125.1 %all-gather.35.cloned.1.call-start = ((), (), s32[]{:S(2)}) async-start(), calls=%async_computation.24 | async-start | bytes 2621440 | tf_op jit(solution)/shard_map/all_gather | solution.py:49
  312.3 47.5 %all-gather.33.cloned.1.call-start = ((), (), s32[]{:S(2)}) async-start(), calls=%async_computation.23 | async-start | bytes 2621440 | tf_op jit(solution)/shard_map/all_gather | solution.py:50
  313.1 76.9 %all-gather.39.cloned.1.call-start = ((), (), s32[]{:S(2)}) async-start(), calls=%async_computation.26 | async-start | bytes 1310720 | tf_op jit(solution)/shard_map/all_gather | solution.py:149
  313.9 100.4 %all-gather.37.cloned.1.call-start = ((), (), s32[]{:S(2)}) async-start(), calls=%async_computation.25 | async-start | bytes 2621440 | tf_op jit(solution)/shard_map/all_gather | solution.py:44
  315.3 24.5 %copy-start.5 = (bf16[256,1024]{0,1:T(8,128)(2,1)}, bf16[256,1024]{0,1:T(8,128)(2,1)S(1)}, u32[]{:S(2)}) copy-start(bf16[256,1024]{0,1:T(8,128)(2,1)S(1)} %copy.50) | copy-start | bytes 1572868
  367.1 122.7 %all-gather.21.cloned.1.call-start = ((), (), s32[]{:S(2)}) async-start(), calls=%async_computation.16 | async-start | bytes 4718592 | tf_op jit(solution)/shard_map/all_gather | solution.py:128
  367.9 51.0 %copy-start.7 = (f32[1024,512]{1,0:T(8,128)S(1)}, f32[1024,512]{1,0:T(8,128)}, u32[]{:S(2)}) copy-start(f32[1024,512]{1,0:T(8,128)} %param.23) | copy-start | bytes 6291460
  367.9 154.8 %reduce-scatter.19.cloned.1.call-start = ((), (), s32[]{:S(2)}) async-start(), calls=%async_computation.27 | async-start | bytes 3145728 | tf_op jit(solution)/shard_map/reduce_scatter | solution.py:75
  418.8 186.9 %all-gather.43.cloned.1.call-start = ((), (), s32[]{:S(2)}) async-start(), calls=%async_computation.29 | async-start | bytes 5242880 | tf_op jit(solution)/shard_map/all_gather | solution.py:152
  419.9 75.7 %copy-start.8 = (f32[512,1024]{1,0:T(8,128)S(1)}, f32[512,1024]{1,0:T(8,128)}, u32[]{:S(2)}) copy-start(f32[512,1024]{1,0:T(8,128)} %param.21) | copy-start | bytes 6291460
  420.0 207.6 %all-gather.41.cloned.1.call-start = ((), (), s32[]{:S(2)}) async-start(), calls=%async_computation.28 | async-start | bytes 1572864 | tf_op jit(solution)/shard_map/all_gather | solution.py:40
  495.6 214.9 %all-gather.47.cloned.1.call-start = ((), (), s32[]{:S(2)}) async-start(), calls=%async_computation.32 | async-start | bytes 5242880 | tf_op jit(solution)/shard_map/all_gather | solution.py:150
  496.8 34.3 %copy-start.14 = (f32[512]{0:T(512)S(1)}, f32[512]{0:T(512)}, u32[]{:S(2)}) copy-start(f32[512]{0:T(512)} %param.25) | copy-start | bytes 6148
  496.8 294.5 %all-gather.49.cloned.1.call-start = ((), (), s32[]{:S(2)}) async-start(), calls=%async_computation.33 | async-start | bytes 5242880 | tf_op jit(solution)/shard_map/all_gather | solution.py:151
  499.8 313.4 %all-gather.45.cloned.1.call-start = ((), (), s32[]{:S(2)}) async-start(), calls=%async_computation.31 | async-start | bytes 1572864 | tf_op jit(solution)/shard_map/all_gather | solution.py:40
  533.6 408.4 %reduce-scatter.21.cloned.1.call-start = ((), (), s32[]{:S(2)}) async-start(), calls=%async_computation.30 | async-start | bytes 20971520 | tf_op jit(solution)/shard_map/reduce_scatter | solution.py:69
  641.3 538.2 %reduce-scatter.23.cloned.1.call-start = ((), (), s32[]{:S(2)}) async-start(), calls=%async_computation.34 | async-start | bytes 41943040 | tf_op jit(solution)/shard_map/reduce_scatter | solution.py:69
  838.6 456.3 %all-gather.51.cloned.1.call-start = ((), (), s32[]{:S(2)}) async-start(), calls=%async_computation.35 | async-start | bytes 20971520 | tf_op jit(solution)/shard_map/all_gather | solution.py:44
  1188.9 153.9 %copy-start.2 = (f32[512,512]{1,0:T(8,128)S(1)}, f32[512,512]{1,0:T(8,128)}, u32[]{:S(2)}) copy-start(f32[512,512]{1,0:T(8,128)} %reduce-scatter.19.cloned.1.call-done) | copy-start | bytes 3145732
  1188.9 153.8 %reduce-scatter.25.cloned.1.call-start = ((), (), s32[]{:S(2)}) async-start(), calls=%async_computation.36 | async-start | bytes 3145728 | tf_op jit(solution)/shard_map/reduce_scatter | solution.py:75
  1310.8 63.7 %all-gather.53.cloned.1.call-start = ((), (), s32[]{:S(2)}) async-start(), calls=%async_computation.37 | async-start | bytes 1572864 | tf_op jit(solution)/shard_map/all_gather | solution.py:40
  1354.0 70.0 %reduce-scatter.27.cloned.1.call-start = ((), (), s32[]{:S(2)}) async-start(), calls=%async_computation.38 | async-start | bytes 5242880 | tf_op jit(solution)/shard_map/reduce_scatter | solution.py:69
  1379.3 103.1 %reduce-scatter.29.cloned.1.call-start = ((), (), s32[]{:S(2)}) async-start(), calls=%async_computation.39 | async-start | bytes 5242880 | tf_op jit(solution)/shard_map/reduce_scatter | solution.py:274
  1437.8 91.9 %reduce-scatter.31.cloned.1.call-start = ((), (), s32[]{:S(2)}) async-start(), calls=%async_computation.40 | async-start | bytes 5242880 | tf_op jit(solution)/shard_map/reduce_scatter | solution.py:275
  1445.8 134.9 %all-gather.55.cloned.1.call-start = ((), (), s32[]{:S(2)}) async-start(), calls=%async_computation.41 | async-start | bytes 7864320 | tf_op jit(solution)/shard_map/all_gather | solution.py:44
  1533.3 107.7 %all-gather.59.cloned.1.call-start = ((), (), s32[]{:S(2)}) async-start(), calls=%async_computation.50 | async-start | bytes 10485760 | tf_op jit(solution)/shard_map/all_gather | solution.py:44
  1533.9 107.1 %copy-start.21 = (bf16[1024,512]{1,0:T(8,128)(2,1)S(1)}, bf16[1024,512]{1,0:T(8,128)(2,1)}, u32[]{:S(2)}) copy-start(bf16[1024,512]{1,0:T(8,128)(2,1)} %all-gather.41.cloned.1.call-done) | copy-start | bytes 3145732
  1533.9 148.9 %reduce-scatter.33.cloned.1.call-start = ((), (), s32[]{:S(2)}) async-start(), calls=%async_computation.42 | async-start | bytes 3145728 | tf_op jit(solution)/shard_map/reduce_scatter | solution.py:75
  1589.2 165.7 %reduce-scatter.47.cloned.1.call-start = ((), (), s32[]{:S(2)}) async-start(), calls=%async_computation.51 | async-start | bytes 5242880 | tf_op jit(solution)/shard_map/reduce_scatter | solution.py:327
  1650.8 134.5 %reduce-scatter.41.cloned.1.call-start = ((), (), s32[]{:S(2)}) async-start(), calls=%async_computation.47 | async-start | bytes 1310720 | tf_op jit(solution)/shard_map/reduce_scatter | solution.py:312
  1655.0 208.1 %reduce-scatter.43.cloned.1.call-start = ((), (), s32[]{:S(2)}) async-start(), calls=%async_computation.48 | async-start | bytes 5242880 | tf_op jit(solution)/shard_map/reduce_scatter | solution.py:315
  1671.6 271.1 %reduce-scatter.45.cloned.1.call-start = ((), (), s32[]{:S(2)}) async-start(), calls=%async_computation.49 | async-start | bytes 5242880 | tf_op jit(solution)/shard_map/reduce_scatter | solution.py:321
  1672.3 300.3 %reduce-scatter.35.cloned.1.call-start = ((), (), s32[]{:S(2)}) async-start(), calls=%async_computation.44 | async-start | bytes 1310720 | tf_op jit(solution)/shard_map/reduce_scatter | solution.py:294
  1681.2 319.5 %reduce-scatter.37.cloned.1.call-start = ((), (), s32[]{:S(2)}) async-start(), calls=%async_computation.45 | async-start | bytes 1310720 | tf_op jit(solution)/shard_map/reduce_scatter | solution.py:300
  1682.0 11.8 copy-start.11
  1682.0 347.6 %reduce-scatter.39.cloned.1.call-start = ((), (), s32[]{:S(2)}) async-start(), calls=%async_computation.46 | async-start | bytes 1310720 | tf_op jit(solution)/shard_map/reduce_scatter | solution.py:306
  1682.7 421.0 %all-gather.57.cloned.1.call-start = ((), (), s32[]{:S(2)}) async-start(), calls=%async_computation.43 | async-start | bytes 4718592 | tf_op jit(solution)/shard_map/all_gather | solution.py:343
  (13 other events, 60.4 us)
Sparse Core Ops, SparseCore 0:
  10.1 76.0 all-gather.22
  88.4 28.4 all-gather.26
  119.0 28.4 all-gather.28
  149.6 28.4 all-gather.30
  180.1 19.6 all-gather.24
  210.0 99.0 reduce-scatter.16
  312.4 22.5 all-gather.34
  337.2 22.5 all-gather.32
  362.0 27.9 all-gather.38
  391.9 22.3 all-gather.36
  416.4 73.3 all-gather.20
  492.5 30.0 reduce-scatter.18
  524.9 80.7 all-gather.42
  607.7 19.8 all-gather.40
  629.6 80.7 all-gather.46
  712.0 79.2 all-gather.48
  793.3 19.8 all-gather.44
  815.8 126.1 reduce-scatter.20
  944.5 234.8 reduce-scatter.22
  1189.0 105.9 all-gather.50
  1310.9 31.8 reduce-scatter.24
  1354.1 20.3 all-gather.52
  1379.5 44.5 reduce-scatter.26
  1437.9 44.5 reduce-scatter.28
  1485.1 44.5 reduce-scatter.30
  1533.4 47.1 all-gather.54
  1582.6 58.2 all-gather.58
  1643.8 31.8 reduce-scatter.32
  1678.0 76.7 reduce-scatter.46
  1757.6 27.6 reduce-scatter.40
  1787.7 75.4 reduce-scatter.42
  1865.4 77.2 reduce-scatter.44
  1944.9 27.6 reduce-scatter.34
  1974.9 25.7 reduce-scatter.36
  2003.7 25.7 reduce-scatter.38
  2031.5 72.1 all-gather.56
where the time goes:
time: 2130 us; the launch traced here: 2120 us
  waiting for transfers between devices  1780 us (84%)
  matrix products  148 us (7%)
  other arithmetic  73.5 us (3%)
  local copies, waits for them, and re-layouts  58.8 us (3%)
  blocking collectives  46 us (2%)
    reduce_scatter x4, waiting for transfers between devices, col_reduce(): lax.psum_scatter(multiply(spread, weight, transpose_right), 'col', scatte...  484 us
    all_gather x4, waiting for transfers between devices, col_gather(): return lax.all_gather(values, 'col', axis=0, tiled=True)  229 us
    all_gather x4, waiting for transfers between devices, row_gather(): return lax.all_gather(values, 'row', axis=0, tiled=True)  79 us
    reduce_scatter x1, waiting for transfers between devices, on_device(): lax.psum_scatter(grad_feedforward[:, hidden_row:].astype(jnp.bfloat16), '...  76.8 us
    all_gather x1, waiting for transfers between devices, on_device(): lax.all_gather(masters[5], 'dp', axis=1, tiled=True)  76.1 us
    reduce_scatter x1, waiting for transfers between devices, on_device(): lax.psum_scatter(grad_feedforward[:, :hidden_row].astype(jnp.bfloat16), '...  76 us
    all_gather x1, waiting for transfers between devices, on_device(): lax.all_gather(tokens, ('dp', 'row'), axis=0, tiled=True)  72 us
    all_gather x1, waiting for transfers between devices, on_device(): lax.all_gather(masters[6], 'dp', axis=0, tiled=True)  71.6 us
  transfers between devices with their start and end apart: 36, of which 35 were waited for; matrix products, arithmetic and copies ran while one was open for 9% of the time, Pallas kernels for 0%

commit v1 on v0

--- a/solution.py
+++ b/solution.py
@@ -1,6 +1,10 @@
+import functools
+
 import jax
 import jax.numpy as jnp
 from jax import lax
+from jax.experimental import pallas as pl
+from jax.experimental.pallas import tpu as pltpu
 from jax.sharding import PartitionSpec as P
 
 D = 2048
@@ -9,7 +13,17 @@
 
 EPSILON = 1e-06
 NEG_FILL = -1e30
-
+AXES = ("dp", "row", "col")
+DP, ROW, COL = 4, 2, 4
+REACH = 768
+BF = jnp.bfloat16
+F32 = jnp.float32
+
+
+def running_sum(lengths):
+    count = lengths.shape[0]
+    earlier = jnp.arange(count)[:, None] <= jnp.arange(count)[None, :]
+    return jnp.sum(jnp.where(earlier, lengths[:, None], 0), axis=0)
 
 def make_picker(wanted, carried, pieces):
     amount = pieces[0].shape[0]
@@ -25,7 +39,7 @@
 
 def sequence_marks(permutation, lengths, first_slot, amount):
     source = lax.dynamic_slice_in_dim(permutation, first_slot, amount)
-    seq_ends = jnp.cumsum(lengths)
+    seq_ends = running_sum(lengths)
     passed = seq_ends[None, :] <= source[:, None]
     member = jnp.sum(passed.astype(jnp.int32), axis=1)
     begins = jnp.max(jnp.where(passed, seq_ends[None, :], 0), axis=1)
@@ -98,7 +112,7 @@
     return (grad_inputs, gain_part)
 
 
-def on_device(
+def on_any_mesh(
     tokens,
     cotangent,
     query_master,
@@ -360,6 +374,388 @@
     )
 
 
+def move(array, to):
+    pairs = []
+    for d in range(DP):
+        for r in range(ROW):
+            for c in range(COL):
+                target = to(d, r, c)
+                if target is not None:
+                    e, s, b = target
+                    pairs.append(((d * ROW + r) * COL + c, (e * ROW + s) * COL + b))
+    return lax.ppermute(array, AXES, pairs)
+
+
+def by_col(array, step):
+    return move(array, lambda d, r, c: (d, r, c ^ step))
+
+
+def by_plane(array, step):
+    return move(array, lambda d, r, c: (d ^ step, r, c))
+
+
+def by_chip(array, over_x, over_y):
+    return move(array, lambda d, r, c: (d, r ^ over_x, c ^ (2 * over_y)))
+
+
+def col_sum(values):
+    return values + by_col(values, 2) + by_col(values, 1) + by_col(values, 3)
+
+
+def same_sum(values):
+    for step in (1, 2):
+        values = values + by_plane(values, step)
+    return values + by_chip(values, 1, 0)
+
+
+def plane_gather(block):
+    beside = by_chip(block, 1, 0)
+    across = by_chip(block, 0, 1)
+    corner = by_chip(block, 1, 1)
+    rail = jnp.concatenate(
+        [jnp.concatenate([block, across], 1), jnp.concatenate([beside, corner], 1)], 0
+    )
+    return jnp.concatenate([rail, by_col(rail, 1)], 1)
+
+
+def plane_scatter(left, weight, contract):
+    rows = left.shape[0] // 2
+    half = D // 2
+    numbers = (((1,), (contract,)), ((), ()))
+    kept, given = (weight[:, :half], weight[:, half:]) if contract == 0 else (weight[:half], weight[half:])
+    theirs = lax.dot_general(left, given, numbers, preferred_element_type=F32).astype(BF)
+    arrived = by_col(theirs, 1)
+    mine = lax.dot_general(left, kept, numbers, preferred_element_type=F32)
+    mine = mine + arrived.astype(F32)
+    low = mine.astype(BF)
+    part = half // 2
+    return (
+        mine[:rows, :part]
+        + by_chip(low[rows:, :part], 1, 0).astype(F32)
+        + by_chip(low[:rows, part:], 0, 1).astype(F32)
+        + by_chip(low[rows:, part:], 1, 1).astype(F32)
+    )
+
+
+def hidden_from(step):
+    def to(d, s, c):
+        b = c ^ step
+        return (d, s ^ (b & 1), b)
+
+    return to
+
+
+def hidden_back(step):
+    def to(d, r, c):
+        return (d, r ^ (c & 1), c ^ step)
+
+    return to
+
+
+def begins_of(lengths, first, amount):
+    ends = running_sum(lengths)
+    place = first + jnp.arange(amount, dtype=jnp.int32)
+    passed = ends[None, :] <= place[:, None]
+    return jnp.max(jnp.where(passed, ends[None, :], 0), axis=1)
+
+
+def seen(begin_ref, block, rows, span):
+    query = lax.broadcasted_iota(jnp.int32, (rows, span), 0)
+    key = lax.broadcasted_iota(jnp.int32, (rows, span), 1)
+    begin = begin_ref[:, 0:1] + (REACH - block * rows)
+    return (key <= query + REACH) & (key >= begin)
+
+
+def scores_of(query, key):
+    return lax.dot_general(
+        query, key, (((1,), (1,)), ((), ())), preferred_element_type=F32
+    ) * HEAD_DIM ** (-0.5)
+
+
+def attend_kernel(begin_ref, q_ref, k_ref, v_ref, o_ref, lse_ref):
+    block = pl.program_id(1)
+    rows = q_ref.shape[0]
+    span = rows + REACH
+    window = pl.ds(pl.multiple_of(block * rows, rows), span)
+    scores = scores_of(q_ref[...], k_ref[window, :])
+    scores = jnp.where(seen(begin_ref, block, rows, span), scores, NEG_FILL)
+    highest = jnp.max(scores, axis=1, keepdims=True)
+    expo = jnp.exp(scores - highest)
+    total = jnp.sum(expo, axis=1, keepdims=True)
+    probability = (expo * (1.0 / total)).astype(BF)
+    o_ref[...] = jnp.dot(probability, v_ref[window, :], preferred_element_type=F32).astype(BF)
+    lse_ref[...] = jnp.broadcast_to(highest + jnp.log(total), lse_ref.shape)
+
+
+def attend_back_kernel(
+    begin_ref, q_ref, k_ref, v_ref, do_ref, lse_ref, dq_ref, dk_ref, dv_ref
+):
+    block = pl.program_id(1)
+    rows = q_ref.shape[0]
+    span = rows + REACH
+    window = pl.ds(pl.multiple_of(block * rows, rows), span)
+
+    @pl.when(block == 0)
+    def _():
+        dk_ref[...] = jnp.zeros_like(dk_ref)
+        dv_ref[...] = jnp.zeros_like(dv_ref)
+
+    query, key = q_ref[...], k_ref[window, :]
+    grad = do_ref[...]
+    scores = scores_of(query, key)
+    allowed = seen(begin_ref, block, rows, span)
+    probability = jnp.where(allowed, jnp.exp(jnp.where(allowed, scores - lse_ref[:, 0:1], 0.0)), 0.0)
+    grad_soft = lax.dot_general(
+        grad, v_ref[window, :], (((1,), (1,)), ((), ())), preferred_element_type=F32
+    )
+    inner = jnp.sum(probability * grad_soft, axis=1, keepdims=True)
+    grad_scores = (probability * (grad_soft - inner)).astype(BF)
+    scale = HEAD_DIM ** (-0.5)
+    dq_ref[...] = (jnp.dot(grad_scores, key, preferred_element_type=F32) * scale).astype(BF)
+    over = (((0,), (0,)), ((), ()))
+    dk_ref[window, :] += lax.dot_general(grad_scores, query, over, preferred_element_type=F32) * scale
+    dv_ref[window, :] += lax.dot_general(
+        probability.astype(BF), grad, over, preferred_element_type=F32
+    )
+
+
+QROWS = 256
+
+
+def attention_specs(rows, width):
+    by_block = pl.BlockSpec((QROWS, HEAD_DIM), lambda h, i: (i, h))
+    whole = pl.BlockSpec((rows + REACH, HEAD_DIM), lambda h, i: (0, h))
+    begin = pl.BlockSpec((QROWS, 1), lambda h, i: (i, 0))
+    grid = (width // HEAD_DIM, rows // QROWS)
+    params = pltpu.CompilerParams(vmem_limit_bytes=40 << 20)
+    return grid, by_block, whole, begin, params
+
+
+def attend(begin, q, k, v):
+    rows, width = q.shape
+    grid, by_block, whole, begin_spec, params = attention_specs(rows, width)
+    area = grid[0] * rows * (QROWS + REACH)
+    return pl.pallas_call(
+        attend_kernel,
+        grid=grid,
+        in_specs=[begin_spec, by_block, whole, whole],
+        out_specs=[by_block, by_block],
+        out_shape=[
+            jax.ShapeDtypeStruct((rows, width), BF),
+            jax.ShapeDtypeStruct((rows, width), F32),
+        ],
+        compiler_params=params,
+        cost_estimate=pl.CostEstimate(
+            flops=4 * area * HEAD_DIM, bytes_accessed=8 * rows * width, transcendentals=area
+        ),
+    )(begin, q, k, v)
+
+
+def attend_back(begin, q, k, v, grad, lse):
+    rows, width = q.shape
+    grid, by_block, whole, begin_spec, params = attention_specs(rows, width)
+    area = grid[0] * rows * (QROWS + REACH)
+    return pl.pallas_call(
+        attend_back_kernel,
+        grid=grid,
+        in_specs=[begin_spec, by_block, whole, whole, by_block, by_block],
+        out_specs=[by_block, whole, whole],
+        out_shape=[
+            jax.ShapeDtypeStruct((rows, width), BF),
+            jax.ShapeDtypeStruct((rows + REACH, width), F32),
+            jax.ShapeDtypeStruct((rows + REACH, width), F32),
+        ],
+        compiler_params=params,
+        cost_estimate=pl.CostEstimate(
+            flops=10 * area * HEAD_DIM, bytes_accessed=24 * rows * width, transcendentals=area
+        ),
+    )(begin, q, k, v, grad, lse)
+
+
+def rounded_norm(values, scale, gain):
+    return (values * scale[:, None] * gain[None, :]).astype(BF)
+
+
+def norm_grads(grad_normed, inputs_f, scale_rows, gain):
+    gain_part = jnp.sum(grad_normed * inputs_f * scale_rows[:, None], axis=0)
+    scaled = grad_normed * gain[None, :]
+    inner = col_sum(jnp.sum(scaled * inputs_f, axis=1))
+    grad_inputs = scale_rows[:, None] * scaled - inputs_f * (scale_rows**3 * inner / D)[:, None]
+    return grad_inputs, gain_part
+
+
+def on_small_mesh(
+    tokens,
+    cotangent,
+    query_master,
+    key_master,
+    value_master,
+    out_master,
+    gate_master,
+    up_master,
+    down_master,
+    attn_gain,
+    ffn_gain,
+    lengths,
+    permutation,
+):
+    del permutation
+    d, r, c = (lax.axis_index(name) for name in AXES)
+    rows = tokens.shape[0]
+    group = rows * ROW
+    half_rows = rows // 2
+    width = query_master.shape[1]
+    y = c // 2
+
+    def pick(stack, index):
+        return lax.dynamic_index_in_dim(stack, index, 0, keepdims=False)
+
+    def flip(array):
+        swapped = jnp.concatenate([array[rows:], array[:rows]], 0)
+        return jnp.where(r == 0, array, swapped)
+
+    block_in = jnp.concatenate([query_master, key_master, value_master], 1).astype(BF)
+    block_out = out_master.astype(BF)
+    in_stack = jnp.stack([block_in] + [by_plane(block_in, j) for j in (1, 2, 3)])
+    out_stack = jnp.stack([block_out] + [by_plane(block_out, j) for j in (1, 2, 3)])
+
+    def spread_blocks(stack):
+        return [pick(stack, d ^ c)] + [
+            by_col(pick(stack, d ^ c ^ m), m) for m in (2, 1, 3)
+        ]
+
+    weight_in = jnp.concatenate(spread_blocks(in_stack), 0)
+    weight_out = jnp.concatenate(spread_blocks(out_stack), 1)
+
+    x = tokens.astype(F32)
+    scale_one = lax.rsqrt(col_sum(jnp.sum(x * x, axis=1)) / D + EPSILON)
+    normed_one = plane_gather(rounded_norm(x, scale_one, attn_gain))
+    projected = flip(jnp.dot(normed_one, weight_in, preferred_element_type=F32).astype(BF))
+    q = projected[:, :width]
+    halo = move(
+        projected[group - REACH :, width:],
+        lambda e, s, b: (e + 1, s, b) if e + 1 < DP else None,
+    )
+    key_value = jnp.concatenate([halo, projected[:, width:]], 0)
+    k, v = key_value[:, :width], key_value[:, width:]
+    begin = (begins_of(lengths, d * group, group) - d * group)[:, None]
+    attended, lse = attend(begin, q, k, v)
+    own_attended = flip(attended)
+    midway = x + plane_scatter(own_attended, weight_out, 0)
+
+    hidden_in = jnp.concatenate([gate_master, up_master], 1).astype(BF)
+    hidden_out = down_master.astype(BF)
+    order = (0, 2, 1, 3)
+    weight_hidden = jnp.concatenate([move(hidden_in, hidden_from(i)) for i in order], 0)
+    weight_down = jnp.concatenate([move(hidden_out, hidden_from(i)) for i in order], 1)
+
+    def spread_tokens(block):
+        kept = lax.dynamic_slice_in_dim(block, y * half_rows, half_rows, 0)
+        given = lax.dynamic_slice_in_dim(block, (1 - y) * half_rows, half_rows, 0)
+        mine = jnp.concatenate([kept, by_chip(given, 0, 1)], 1)
+        rail = jnp.concatenate([mine] + [by_plane(mine, j) for j in (1, 2, 3)], 0)
+        return jnp.concatenate([rail, by_col(rail, 1)], 1)
+
+    over = (((0,), (0,)), ((), ()))
+    across = (((1,), (1,)), ((), ()))
+    grad_all = spread_tokens(cotangent)
+    grad_hidden = lax.dot_general(grad_all, weight_down, across, preferred_element_type=F32)
+    scale_two = lax.rsqrt(col_sum(jnp.sum(midway * midway, axis=1)) / D + EPSILON)
+    normed_two = spread_tokens(rounded_norm(midway, scale_two, ffn_gain))
+    gate_and_up = jnp.dot(normed_two, weight_hidden, preferred_element_type=F32)
+    units = hidden_out.shape[0]
+    gate, up = gate_and_up[:, :units], gate_and_up[:, units:]
+    sigmoid = jax.nn.sigmoid(gate)
+    hidden = (gate * sigmoid * up).astype(BF)
+    grad_gate = (grad_hidden * up * sigmoid * (1.0 + gate * (1.0 - sigmoid))).astype(BF)
+    grad_up = (grad_hidden * gate * sigmoid).astype(BF)
+    grad_both = jnp.concatenate([grad_gate, grad_up], 1)
+
+    half = D // 2
+    theirs = lax.dot_general(
+        grad_both, weight_hidden[half:], across, preferred_element_type=F32
+    ).astype(BF)
+    arrived = by_col(theirs, 1)
+    mine = lax.dot_general(grad_both, weight_hidden[:half], across, preferred_element_type=F32)
+    mine = mine + arrived.astype(F32)
+    low = mine.astype(BF)
+    mine = mine[:half_rows]
+    for j in (1, 2, 3):
+        mine = mine + by_plane(low[j * half_rows : (j + 1) * half_rows], j).astype(F32)
+    part = half // 2
+    crossed = by_chip(mine[:, part:].astype(BF), 0, 1).astype(F32)
+    grad_normed_two = jnp.where(
+        y == 0,
+        jnp.concatenate([mine[:, :part], crossed], 0),
+        jnp.concatenate([crossed, mine[:, :part]], 0),
+    )
+
+    def plane_total(partial, axis):
+        size = D // COL
+        total = None
+        for place, i in enumerate(order):
+            piece = lax.slice_in_dim(partial, place * size, (place + 1) * size, axis=axis)
+            piece = move(piece, hidden_back(i)).astype(F32)
+            total = piece if total is None else total + piece
+        return total
+
+    down_part = lax.dot_general(hidden, grad_all, over, preferred_element_type=F32).astype(BF)
+    both_part = lax.dot_general(normed_two, grad_both, over, preferred_element_type=F32).astype(BF)
+    grad_down_own = plane_total(down_part, 1)
+    grad_both_own = plane_total(both_part, 0)
+
+    grad_mid_norm, gain_two_part = norm_grads(grad_normed_two, midway, scale_two, ffn_gain)
+    grad_midway = cotangent.astype(F32) + grad_mid_norm
+    back_all = plane_gather(grad_midway.astype(BF))
+    grad_attended = flip(
+        lax.dot_general(back_all, weight_out, across, preferred_element_type=F32).astype(BF)
+    )
+    dq, dk, dv = attend_back(begin, q, k, v, grad_attended, lse)
+    dkv = jnp.concatenate([dk, dv], 1)
+    spill = move(
+        dkv[:REACH].astype(BF), lambda e, s, b: (e - 1, s, b) if e > 0 else None
+    )
+    dkv = dkv[REACH:]
+    start = group - REACH
+    dkv = jnp.concatenate([dkv[:start], dkv[start:] + spill.astype(F32)], 0).astype(BF)
+    grad_projected = flip(jnp.concatenate([dq, dkv], 1))
+
+    in_part = lax.dot_general(normed_one, grad_projected, over, preferred_element_type=F32).astype(BF)
+    out_part = lax.dot_general(own_attended, back_all, over, preferred_element_type=F32).astype(BF)
+
+    def owners_total(partial, axis):
+        size = D // COL
+        parts = [
+            lax.slice_in_dim(partial, i * size, (i + 1) * size, axis=axis) for i in range(COL)
+        ]
+        by_step = {0: parts[0], 2: by_col(parts[1], 2), 1: by_col(parts[2], 1), 3: by_col(parts[3], 3)}
+        stack = jnp.stack([by_step[m] for m in range(COL)])
+        total = pick(stack, d ^ c).astype(F32)
+        for j in (1, 2, 3):
+            total = total + by_plane(pick(stack, d ^ c ^ j), j).astype(F32)
+        return total
+
+    grad_in = owners_total(in_part, 0)
+    grad_out = owners_total(out_part, 1)
+
+    grad_normed_one = plane_scatter(grad_projected, weight_in, 1)
+    grad_in_norm, gain_one_part = norm_grads(grad_normed_one, x, scale_one, attn_gain)
+    grad_tokens = grad_midway + grad_in_norm
+    gains = same_sum(jnp.stack([gain_one_part, gain_two_part]))
+    return (
+        grad_tokens,
+        grad_in[:, :width],
+        grad_in[:, width : 2 * width],
+        grad_in[:, 2 * width :],
+        grad_out,
+        grad_both_own[:, :units],
+        grad_both_own[:, units:],
+        grad_down_own,
+        gains[0],
+        gains[1],
+    )
+
+
 def solution(mesh):
     placed = (
         P(("dp", "row"), "col"),
@@ -376,8 +772,9 @@
         P(),
         P(),
     )
+    small = tuple(mesh.shape[name] for name in AXES) == (DP, ROW, COL)
     return jax.shard_map(
-        on_device,
+        on_small_mesh if small else on_any_mesh,
         mesh=mesh,
         in_specs=placed,
         out_specs=(

time: 2130 us -> 882 us (0.41)
  waiting for transfers between devices: 1780 us -> 491 us
  starting transfers between devices: 2.73 us -> 200 us
  matrix products: 148 us -> 93.8 us
  blocking collectives: 46 us -> 0 us
  other arithmetic: 73.5 us -> 39.4 us
  local copies, waits for them, and re-layouts: 58.8 us -> 29.2 us
    reduce_scatter x16 -> x0, waiting for transfers between devices: 922 us -> none  [the longest x4 484 us: col_reduce(): lax.psum_scatter(multiply(spread, weight, transpose_right), 'col', scatte...]
    all_gather x20 -> x0, waiting for transfers between devices: 852 us -> none  [the longest x4 229 us: col_gather(): return lax.all_gather(values, 'col', axis=0, tiled=True)]
    ppermute x0 -> x88, waiting for transfers between devices: none -> 491 us  [move(): return lax.ppermute(array, AXES, pairs)]
    ppermute x0 -> x88, starting transfers between devices: none -> 200 us  [move(): return lax.ppermute(array, AXES, pairs)]
    dot_general x17 -> x14, matrix products: 148 us -> 93.8 us  [the longest x1 16.9 us: on_small_mesh(): gate_and_up = jnp.dot(normed_two, weight_hidden, preferred_element_type=F32)]
    convert_element_type x25 -> x6, other arithmetic: 57.3 us -> 7.44 us  [the longest x2 2.35 us: rounded_norm(): return (values * scale[:, None] * gain[None, :]).astype(BF)]
    psum x5 -> x0, blocking collectives: 46 us -> none  [the longest x4 25.9 us: col_total(): return lax.psum(jnp.sum(values, axis=1), 'col')]
  transfers between devices with their start and end apart: 36 -> 88, of which waited for: 35 -> 41; matrix products, arithmetic and copies ran while one was open for 9% -> 13% of each run, Pallas kernels for 0% -> 2%
where the time goes in v1:
time: 882 us; the launch traced here: 875 us
  waiting for transfers between devices  491 us (56%)
  starting transfers between devices  200 us (23%)
  matrix products  93.8 us (11%)
  other arithmetic  39.4 us (4%)
  local copies, waits for them, and re-layouts  29.2 us (3%)
  Pallas kernels  18.9 us (2%)
    ppermute x88, waiting for transfers between devices, move(): return lax.ppermute(array, AXES, pairs)  491 us
    ppermute x88, starting transfers between devices, move(): return lax.ppermute(array, AXES, pairs)  200 us
  transfers between devices with their start and end apart: 88, of which 41 were waited for; matrix products, arithmetic and copies ran while one was open for 13% of the time, Pallas kernels for 2%

profile of v1, /device:TPU:0, one launch (start us, length us, event | category | flops | bytes accessed | tf_op | source)
XLA Modules:
  0.0 874.9 jit_solution(8109917859183224219)
XLA Ops:
  23.5 3.6 collective-permute-start.9
  27.1 8.8 %collective-permute-done.5 = bf16[512,512]{0,1:T(8,128)(2,1)} collective-permute-done((bf16[512,512]{0,1:T(8,128)(2,1)S(1)}, bf16[512,512]{0,1:T(8,128)(2,1)}, u32[]{:S(2)}, u32[]{:S(2)}) %collective-permute-start.5) | collective-permute-done | bytes 524320 | tf_op jit(solution)/shard_map/ppermute | solution.py:386
  39.0 12.2 %collective-permute-done.7 = bf16[512,768]{1,0:T(8,128)(2,1)} collective-permute-done((bf16[512,768]{1,0:T(8,128)(2,1)}, bf16[512,768]{1,0:T(8,128)(2,1)}, u32[]{:S(2)}, u32[]{:S(2)}) %collective-permute-start.7) | collective-permute-done | bytes 786464 | tf_op jit(solution)/shard_map/ppermute | solution.py:386
  51.2 21.5 %collective-permute-done.8 = bf16[512,768]{1,0:T(8,128)(2,1)} collective-permute-done((bf16[512,768]{1,0:T(8,128)(2,1)}, bf16[512,768]{1,0:T(8,128)(2,1)}, u32[]{:S(2)}, u32[]{:S(2)}) %collective-permute-start.8) | collective-permute-done | bytes 786464 | tf_op jit(solution)/shard_map/ppermute | solution.py:386
  78.6 15.7 %collective-permute-start.14 = (bf16[256,512]{1,0:T(8,128)(2,1)}, bf16[256,512]{1,0:T(8,128)(2,1)}, u32[]{:S(2)}, u32[]{:S(2)}) collective-permute-start(bf16[256,512]{1,0:T(8,128)(2,1)} %convert_element_type.178), channel_id=1, source_target_pairs={{0,8},{1,9},{2,10},{3,11},{4,12},{5,13},{6,14},{7,15},{8,0},{9,1},... | collective-permute-start | bytes 786440 | tf_op jit(solution)/shard_map/ppermute | solution.py:386
  96.5 16.7 %collective-permute-start.15 = (bf16[256,512]{1,0:T(8,128)(2,1)}, bf16[256,512]{1,0:T(8,128)(2,1)}, u32[]{:S(2)}, u32[]{:S(2)}) collective-permute-start(bf16[256,512]{1,0:T(8,128)(2,1)} %convert_element_type.178), channel_id=1, source_target_pairs={{0,16},{1,17},{2,18},{3,19},{4,20},{5,21},{6,22},{7,23},{8,24},{9,... | collective-permute-start | bytes 786440 | tf_op jit(solution)/shard_map/ppermute | solution.py:386
  114.7 6.2 fusion.38
  122.4 12.9 %collective-permute-start.13 = (bf16[768,512]{1,0:T(8,128)(2,1)}, bf16[768,512]{1,0:T(8,128)(2,1)}, u32[]{:S(2)}, u32[]{:S(2)}) collective-permute-start(bf16[768,512]{1,0:T(8,128)(2,1)} %slice.242), channel_id=1, source_target_pairs={{0,8},{1,9},{2,10},{3,11},{4,12},{5,13},{6,14},{7,15},{8,16},{9,17... | collective-permute-start | bytes 2359304 | tf_op jit(solution)/shard_map/ppermute | solution.py:386
  139.0 12.6 %collective-permute-done.13 = bf16[768,512]{1,0:T(8,128)(2,1)} collective-permute-done((bf16[768,512]{1,0:T(8,128)(2,1)}, bf16[768,512]{1,0:T(8,128)(2,1)}, u32[]{:S(2)}, u32[]{:S(2)}) %collective-permute-start.13) | collective-permute-done | bytes 786464 | tf_op jit(solution)/shard_map/ppermute | solution.py:386
  152.8 7.5 shard_map.195
  163.7 7.0 collective-permute-done.17
  175.2 11.4 %collective-permute-done.21 = bf16[512,512]{0,1:T(8,128)(2,1)S(1)} collective-permute-done((bf16[512,512]{0,1:T(8,128)(2,1)S(1)}, bf16[512,512]{0,1:T(8,128)(2,1)S(1)}, u32[]{:S(2)}, u32[]{:S(2)}) %collective-permute-start.21) | collective-permute-done | bytes 524320 | tf_op jit(solution)/shard_map/ppermute | solution.py:386
  186.6 10.3 %collective-permute-done.22 = bf16[512,512]{0,1:T(8,128)(2,1)S(1)} collective-permute-done((bf16[512,512]{0,1:T(8,128)(2,1)S(1)}, bf16[512,512]{0,1:T(8,128)(2,1)S(1)}, u32[]{:S(2)}, u32[]{:S(2)}) %collective-permute-start.22) | collective-permute-done | bytes 524320 | tf_op jit(solution)/shard_map/ppermute | solution.py:386
  206.0 8.1 collective-permute-done.36
  220.6 4.9 collective-permute-done.27
  228.7 10.5 %collective-permute-done.37 = bf16[256,1024]{0,1:T(8,128)(2,1)S(1)} collective-permute-done((bf16[256,1024]{0,1:T(8,128)(2,1)S(1)}, bf16[256,1024]{0,1:T(8,128)(2,1)S(1)}, u32[]{:S(2)}, u32[]{:S(2)}) %collective-permute-start.37) | collective-permute-done | bytes 524320 | tf_op jit(solution)/shard_map/ppermute | solution.py:386
  241.5 15.0 %collective-permute-done.38 = bf16[256,1024]{0,1:T(8,128)(2,1)S(1)} collective-permute-done((bf16[256,1024]{0,1:T(8,128)(2,1)S(1)}, bf16[256,1024]{0,1:T(8,128)(2,1)S(1)}, u32[]{:S(2)}, u32[]{:S(2)}) %collective-permute-start.38) | collective-permute-done | bytes 524320 | tf_op jit(solution)/shard_map/ppermute | solution.py:386
  262.9 38.5 %collective-permute-done.29 = bf16[256,1024]{1,0:T(8,128)(2,1)S(1)} collective-permute-done((bf16[256,1024]{1,0:T(8,128)(2,1)S(1)}, bf16[256,1024]{1,0:T(8,128)(2,1)S(1)}, u32[]{:S(2)}, u32[]{:S(2)}) %collective-permute-start.29) | collective-permute-done | bytes 524320 | tf_op jit(solution)/shard_map/ppermute | solution.py:386
  307.8 9.5 %collective-permute-start.32 = (bf16[1024,512]{1,0:T(8,128)(2,1)}, bf16[1024,512]{1,0:T(8,128)(2,1)}, u32[]{:S(2)}, u32[]{:S(2)}) collective-permute-start(bf16[1024,512]{1,0:T(8,128)(2,1)} %convert_element_type.185), channel_id=1, source_target_pairs={{0,0},{1,5},{2,2},{3,7},{4,4},{5,1},{6,6},{7,3},{8,8},{9,13},{10,1... | collective-permute-start | bytes 3145736 | tf_op jit(solution)/shard_map/ppermute | solution.py:386
  317.7 72.2 %collective-permute-done.44 = bf16[512,2048]{1,0:T(8,128)(2,1)S(1)} collective-permute-done((bf16[512,2048]{1,0:T(8,128)(2,1)S(1)}, bf16[512,2048]{1,0:T(8,128)(2,1)S(1)}, u32[]{:S(2)}, u32[]{:S(2)}) %collective-permute-start.44) | collective-permute-done | bytes 2097184 | tf_op jit(solution)/shard_map/ppermute | solution.py:386
  393.0 16.9 %fusion = f32[1024,2048]{0,1:T(8,128)} fusion(bf16[512,2048]{1,0:T(8,128)(2,1)} %copy-done.63, bf16[512,2048]{1,0:T(8,128)(2,1)} %copy-done.61, bf16[512,2048]{1,0:T(8,128)(2,1)} %copy-done.59, bf16[512,2048]{1,0:T(8,128)(2,1)} %copy-done.57, bf16[1024,1024]{0,1:T(8,128)(2,1)} %copy-done.55, bf16[256,1024]{0,1:T(8,128)(2,1)} %copy-done.32, ...), kind=kOutput, calls=%fused_computation | convolution fusion | flops 8648654848 | bytes 20971520 | tf_op jit(solution)/shard_map/dot_general | solution.py:665
  409.9 8.9 %collective-permute-done.35 = bf16[1024,512]{1,0:T(8,128)(2,1)} collective-permute-done((bf16[1024,512]{1,0:T(8,128)(2,1)}, bf16[1024,512]{1,0:T(8,128)(2,1)}, u32[]{:S(2)}, u32[]{:S(2)}) %collective-permute-start.35) | collective-permute-done | bytes 1048608 | tf_op jit(solution)/shard_map/ppermute | solution.py:386
  418.7 13.7 %multiply_convert_fusion.2 = (bf16[1024,1024]{0,1:T(8,128)(2,1)}, bf16[1024,1024]{0,1:T(8,128)(2,1)}) fusion(f32[1024,2048]{0,1:T(8,128)} %fusion, bf16[1024,512]{1,0:T(8,128)(2,1)} %collective-permute-done.35, bf16[1024,512]{1,0:T(8,128)(2,1)} %collective-permute-done.34, bf16[1024,512]{1,0:T(8,128)(2,1)} %collective-permute-done.33, ...), kind=kOutput, calls=%fused_computation.35 | convolution fusion | flops 4350541824 | bytes 20971520 | tf_op jit(solution)/shard_map/dot_general | solution.py:662
  432.4 7.5 fusion.35
  440.0 4.1 collective-permute-done.45
  444.2 4.5 fusion.112
  448.8 16.2 %collective-permute-start.46 = (bf16[256,1024]{0,1:T(8,128)(2,1)S(1)}, bf16[256,1024]{0,1:T(8,128)(2,1)S(1)}, u32[]{:S(2)}, u32[]{:S(2)}) collective-permute-start(bf16[256,1024]{0,1:T(8,128)(2,1)S(1)} %get-tuple-element.83), channel_id=1, source_target_pairs={{0,8},{1,9},{2,10},{3,11},{4,12},{5,13},{6,14},{7,15},{8,0},{9,1},... | collective-permute-start | bytes 1572872 | tf_op jit(solution)/shard_map/ppermute | solution.py:386
  468.8 19.6 %collective-permute-done.46 = bf16[256,1024]{0,1:T(8,128)(2,1)S(1)} collective-permute-done((bf16[256,1024]{0,1:T(8,128)(2,1)S(1)}, bf16[256,1024]{0,1:T(8,128)(2,1)S(1)}, u32[]{:S(2)}, u32[]{:S(2)}) %collective-permute-start.46) | collective-permute-done | bytes 524320 | tf_op jit(solution)/shard_map/ppermute | solution.py:386
  488.6 14.8 %collective-permute-done.48 = bf16[256,1024]{0,1:T(8,128)(2,1)S(1)} collective-permute-done((bf16[256,1024]{0,1:T(8,128)(2,1)S(1)}, bf16[256,1024]{0,1:T(8,128)(2,1)S(1)}, u32[]{:S(2)}, u32[]{:S(2)}) %collective-permute-start.48) | collective-permute-done | bytes 524320 | tf_op jit(solution)/shard_map/ppermute | solution.py:386
  508.2 4.8 collective-permute-done.49
  526.3 9.5 %convolution_convert_fusion.1 = bf16[1024,2048]{1,0:T(8,128)(2,1)S(1)} fusion(f32[1024,2048]{0,1:T(8,128)} %fusion, bf16[1024,1024]{1,0:T(8,128)(2,1)} %collective-permute-done.31, bf16[256,1024]{1,0:T(8,128)(2,1)} %copy-done.35, bf16[256,1024]{1,0:T(8,128)(2,1)} %copy-done.34, bf16[256,1024]{1,0:T(8,128)(2,1)} %copy-done.33, ...), kind=kOutput, calls=%fused_computation.38 | convolution fusion | flops 4328521728 | bytes 16777216 | tf_op jit(solution)/shard_map/dot_general | solution.py:702
  538.1 9.4 %collective-permute-start.81 = (bf16[1024,512]{1,0:T(8,128)(2,1)}, bf16[1024,512]{1,0:T(8,128)(2,1)}, u32[]{:S(2)}, u32[]{:S(2)}) collective-permute-start(bf16[1024,512]{1,0:T(8,128)(2,1)} %get-tuple-element.63), channel_id=1, source_target_pairs={{0,0},{1,5},{2,2},{3,7},{4,4},{5,1},{6,6},{7,3},{8,8},{9,13},{10,1... | collective-permute-start | bytes 3145736 | tf_op jit(solution)/shard_map/ppermute | solution.py:386
  552.0 15.8 %convolution_convert_fusion = bf16[2048,2048]{1,0:T(8,128)(2,1)} fusion(bf16[1024,1024]{0,1:T(8,128)(2,1)} %get-tuple-element.58, bf16[1024,1024]{0,1:T(8,128)(2,1)} %get-tuple-element.57, bf16[1024,1024]{0,1:T(8,128)(2,1)} %copy-done.55, bf16[256,1024]{0,1:T(8,128)(2,1)} %copy-done.32, bf16[256,1024]{0,1:T(8,128)(2,1)} %copy-done.31, ...), kind=kOutput, calls=%fused_computation.8 | convolution fusion | flops 8627683328 | bytes 16777216 | tf_op jit(solution)/shard_map/dot_general | solution.py:703
  567.8 5.0 fusion.99
  576.5 6.3 collective-permute-done.83
  582.8 12.2 %collective-permute-done.84 = bf16[1024,512]{1,0:T(8,128)(2,1)} collective-permute-done((bf16[1024,512]{1,0:T(8,128)(2,1)}, bf16[1024,512]{1,0:T(8,128)(2,1)}, u32[]{:S(2)}, u32[]{:S(2)}) %collective-permute-start.84) | collective-permute-done | bytes 1048608 | tf_op jit(solution)/shard_map/ppermute | solution.py:386
  597.1 4.0 convert_add_fusion.5
  604.4 11.4 %shard_map.196 = (bf16[1024,256]{1,0:T(8,128)(2,1)S(1)}, f32[1792,256]{1,0:T(8,128)S(1)}, f32[1792,256]{1,0:T(8,128)S(1)}) custom-call(s32[1024,1]{1,0:T(8,128)S(1)} %copy.46.begin_ref, bf16[1024,256]{1,0:T(8,128)(2,1)S(1)} %slice.241.q_ref, bf16[1792,256]{1,0:T(8,128)(2,1)S(1)} %get-tuple-element.90.k_ref, bf16[1792,256]{1,0:T(8,128)(2,1)S(1)} %get-tuple-element.89.v_ref, ...), custom_call_target="tpu_custom_call" | custom-call | flops 2684354560 | bytes 6291456 | tf_op jit(solution)/shard_map/pallas_call | solution.py:558
  621.0 25.9 %collective-permute-done.57 = bf16[768,512]{1,0:T(8,128)(2,1)S(1)} collective-permute-done((bf16[768,512]{1,0:T(8,128)(2,1)S(1)}, bf16[768,512]{1,0:T(8,128)(2,1)S(1)}, u32[]{:S(2)}, u32[]{:S(2)}) %collective-permute-start.57) | collective-permute-done | bytes 786464 | tf_op jit(solution)/shard_map/ppermute | solution.py:386
  651.1 5.4 convolution_convert_fusion.2
  661.5 26.2 %collective-permute-done.80 = bf16[512,2048]{1,0:T(8,128)(2,1)S(1)} collective-permute-done((bf16[512,2048]{1,0:T(8,128)(2,1)S(1)}, bf16[512,2048]{1,0:T(8,128)(2,1)S(1)}, u32[]{:S(2)}, u32[]{:S(2)}) %collective-permute-start.80) | collective-permute-done | bytes 2097184 | tf_op jit(solution)/shard_map/ppermute | solution.py:386
  694.4 36.4 %collective-permute-done.73 = bf16[256,512]{1,0:T(8,128)(2,1)S(1)} collective-permute-done((bf16[256,512]{1,0:T(8,128)(2,1)S(1)}, bf16[256,512]{1,0:T(8,128)(2,1)S(1)}, u32[]{:S(2)}, u32[]{:S(2)}) %collective-permute-start.73) | collective-permute-done | bytes 262176 | tf_op jit(solution)/shard_map/ppermute | solution.py:386
  731.8 11.2 %collective-permute-start.68 = (bf16[512,768]{1,0:T(8,128)(2,1)S(1)}, bf16[512,768]{1,0:T(8,128)(2,1)S(1)}, u32[]{:S(2)}, u32[]{:S(2)}) collective-permute-start(bf16[512,768]{1,0:T(8,128)(2,1)S(1)} %get-tuple-element.69), channel_id=1, source_target_pairs={{0,8},{1,9},{2,10},{3,11},{4,12},{5,13},{6,14},{7,15},{8,0},{9,1},... | collective-permute-start | bytes 2359304 | tf_op jit(solution)/shard_map/ppermute | solution.py:386
  750.5 3.7 fusion.113
  754.2 34.1 %collective-permute-done.74 = bf16[256,512]{1,0:T(8,128)(2,1)S(1)} collective-permute-done((bf16[256,512]{1,0:T(8,128)(2,1)S(1)}, bf16[256,512]{1,0:T(8,128)(2,1)S(1)}, u32[]{:S(2)}, u32[]{:S(2)}) %collective-permute-start.74) | collective-permute-done | bytes 262176 | tf_op jit(solution)/shard_map/ppermute | solution.py:386
  791.1 23.1 %collective-permute-done.76 = bf16[256,512]{1,0:T(8,128)(2,1)S(1)} collective-permute-done((bf16[256,512]{1,0:T(8,128)(2,1)S(1)}, bf16[256,512]{1,0:T(8,128)(2,1)S(1)}, u32[]{:S(2)}, u32[]{:S(2)}) %collective-permute-start.76) | collective-permute-done | bytes 262176 | tf_op jit(solution)/shard_map/ppermute | solution.py:386
  818.0 20.6 %collective-permute-done.60 = bf16[512,512]{0,1:T(8,128)(2,1)S(1)} collective-permute-done((bf16[512,512]{0,1:T(8,128)(2,1)S(1)}, bf16[512,512]{0,1:T(8,128)(2,1)S(1)}, u32[]{:S(2)}, u32[]{:S(2)}) %collective-permute-start.60) | collective-permute-done | bytes 524320 | tf_op jit(solution)/shard_map/ppermute | solution.py:386
  839.3 23.2 %collective-permute-start.85 = (f32[2,512]{1,0:T(2,128)S(1)}, f32[2,512]{1,0:T(2,128)S(1)}, u32[]{:S(2)}, u32[]{:S(2)}) collective-permute-start(f32[2,512]{1,0:T(2,128)S(1)} %pad_maximum_fusion.19), channel_id=1, source_target_pairs={{0,8},{1,9},{2,10},{3,11},{4,12},{5,13},{6,14},{7,15},{8,0},{9,1},... | collective-permute-start | bytes 12296 | tf_op jit(solution)/shard_map/ppermute | solution.py:386
  (368 shorter events, 173.1 us)
Async XLA Ops:
  15.8 35.4 %collective-permute-start.7 = (bf16[512,768]{1,0:T(8,128)(2,1)}, bf16[512,768]{1,0:T(8,128)(2,1)}, u32[]{:S(2)}, u32[]{:S(2)}) collective-permute-start(bf16[512,768]{1,0:T(8,128)(2,1)} %pad_maximum_fusion.16), channel_id=1, source_target_pairs={{0,8},{1,9},{2,10},{3,11},{4,12},{5,13},{6,14},{7,15},{8,0},{9,1},... | collective-permute-start | bytes 2359304 | tf_op jit(solution)/shard_map/ppermute | solution.py:386
  17.4 55.4 %collective-permute-start.8 = (bf16[512,768]{1,0:T(8,128)(2,1)}, bf16[512,768]{1,0:T(8,128)(2,1)}, u32[]{:S(2)}, u32[]{:S(2)}) collective-permute-start(bf16[512,768]{1,0:T(8,128)(2,1)} %pad_maximum_fusion.16), channel_id=1, source_target_pairs={{0,16},{1,17},{2,18},{3,19},{4,20},{5,21},{6,22},{7,23},{8,24},{9,... | collective-permute-start | bytes 2359304 | tf_op jit(solution)/shard_map/ppermute | solution.py:386
  23.5 49.2 %collective-permute-start.9 = (bf16[512,768]{1,0:T(8,128)(2,1)}, bf16[512,768]{1,0:T(8,128)(2,1)S(1)}, u32[]{:S(2)}, u32[]{:S(2)}) collective-permute-start(bf16[512,768]{1,0:T(8,128)(2,1)} %pad_maximum_fusion.16), channel_id=1, source_target_pairs={{0,24},{1,25},{2,26},{3,27},{4,28},{5,29},{6,30},{7,31},{8,16},{9,... | collective-permute-start | bytes 2359304 | tf_op jit(solution)/shard_map/ppermute | solution.py:386
  38.9 75.7 %collective-permute-start.6 = (bf16[1024,1024]{0,1:T(8,128)(2,1)}, bf16[1024,1024]{0,1:T(8,128)(2,1)}, u32[]{:S(2)}, u32[]{:S(2)}) collective-permute-start(bf16[1024,1024]{0,1:T(8,128)(2,1)} %maximum_maximum_fusion), channel_id=1, source_target_pairs={{0,1},{1,0},{2,3},{3,2},{4,5},{5,4},{6,7},{7,6},{8,9},{9,8},{10,11... | collective-permute-start | bytes 6291464 | tf_op jit(solution)/shard_map/ppermute | solution.py:386
  76.3 36.9 %collective-permute-start.11 = (bf16[512,768]{1,0:T(8,128)(2,1)}, bf16[512,768]{1,0:T(8,128)(2,1)}, u32[]{:S(2)}, u32[]{:S(2)}) collective-permute-start(bf16[512,768]{1,0:T(8,128)(2,1)} %get-tuple-element.78), channel_id=1, source_target_pairs={{0,1},{1,0},{2,3},{3,2},{4,5},{5,4},{6,7},{7,6},{8,9},{9,8},{10,11... | collective-permute-start | bytes 2359304 | tf_op jit(solution)/shard_map/ppermute | solution.py:386
  76.3 38.3 %collective-permute-start.12 = (bf16[512,768]{1,0:T(8,128)(2,1)}, bf16[512,768]{1,0:T(8,128)(2,1)}, u32[]{:S(2)}, u32[]{:S(2)}) collective-permute-start(bf16[512,768]{1,0:T(8,128)(2,1)} %get-tuple-element.77), channel_id=1, source_target_pairs={{0,3},{1,2},{2,1},{3,0},{4,7},{5,6},{6,5},{7,4},{8,11},{9,10},{10,... | collective-permute-start | bytes 2359304 | tf_op jit(solution)/shard_map/ppermute | solution.py:386
  78.6 57.1 %collective-permute-start.14 = (bf16[256,512]{1,0:T(8,128)(2,1)}, bf16[256,512]{1,0:T(8,128)(2,1)}, u32[]{:S(2)}, u32[]{:S(2)}) collective-permute-start(bf16[256,512]{1,0:T(8,128)(2,1)} %convert_element_type.178), channel_id=1, source_target_pairs={{0,8},{1,9},{2,10},{3,11},{4,12},{5,13},{6,14},{7,15},{8,0},{9,1},... | collective-permute-start | bytes 786440 | tf_op jit(solution)/shard_map/ppermute | solution.py:386
  96.5 39.1 %collective-permute-start.15 = (bf16[256,512]{1,0:T(8,128)(2,1)}, bf16[256,512]{1,0:T(8,128)(2,1)}, u32[]{:S(2)}, u32[]{:S(2)}) collective-permute-start(bf16[256,512]{1,0:T(8,128)(2,1)} %convert_element_type.178), channel_id=1, source_target_pairs={{0,16},{1,17},{2,18},{3,19},{4,20},{5,21},{6,22},{7,23},{8,24},{9,... | collective-permute-start | bytes 786440 | tf_op jit(solution)/shard_map/ppermute | solution.py:386
  122.4 29.2 %collective-permute-start.13 = (bf16[768,512]{1,0:T(8,128)(2,1)}, bf16[768,512]{1,0:T(8,128)(2,1)}, u32[]{:S(2)}, u32[]{:S(2)}) collective-permute-start(bf16[768,512]{1,0:T(8,128)(2,1)} %slice.242), channel_id=1, source_target_pairs={{0,8},{1,9},{2,10},{3,11},{4,12},{5,13},{6,14},{7,15},{8,16},{9,17... | collective-permute-start | bytes 2359304 | tf_op jit(solution)/shard_map/ppermute | solution.py:386
  218.2 38.3 %collective-permute-start.38 = (bf16[256,1024]{0,1:T(8,128)(2,1)S(1)}, bf16[256,1024]{0,1:T(8,128)(2,1)S(1)}, u32[]{:S(2)}, u32[]{:S(2)}) collective-permute-start(bf16[256,1024]{0,1:T(8,128)(2,1)S(1)} %pad_maximum_fusion.18), channel_id=1, source_target_pairs={{0,16},{1,17},{2,18},{3,19},{4,20},{5,21},{6,22},{7,23},{8,24},{9,... | collective-permute-start | bytes 1572872 | tf_op jit(solution)/shard_map/ppermute | solution.py:386
  219.3 37.9 %collective-permute-start.39 = (bf16[256,1024]{0,1:T(8,128)(2,1)S(1)}, bf16[256,1024]{0,1:T(8,128)(2,1)S(1)}, u32[]{:S(2)}, u32[]{:S(2)}) collective-permute-start(bf16[256,1024]{0,1:T(8,128)(2,1)S(1)} %pad_maximum_fusion.18), channel_id=1, source_target_pairs={{0,24},{1,25},{2,26},{3,27},{4,28},{5,29},{6,30},{7,31},{8,16},{9,... | collective-permute-start | bytes 1572872 | tf_op jit(solution)/shard_map/ppermute | solution.py:386
  225.6 37.3 %collective-permute-start.28 = (bf16[256,1024]{1,0:T(8,128)(2,1)S(1)}, bf16[256,1024]{1,0:T(8,128)(2,1)S(1)}, u32[]{:S(2)}, u32[]{:S(2)}) collective-permute-start(bf16[256,1024]{1,0:T(8,128)(2,1)S(1)} %pad_maximum_fusion.17), channel_id=1, source_target_pairs={{0,8},{1,9},{2,10},{3,11},{4,12},{5,13},{6,14},{7,15},{8,0},{9,1},... | collective-permute-start | bytes 1572872 | tf_op jit(solution)/shard_map/ppermute | solution.py:386
  226.0 75.4 %collective-permute-start.29 = (bf16[256,1024]{1,0:T(8,128)(2,1)S(1)}, bf16[256,1024]{1,0:T(8,128)(2,1)S(1)}, u32[]{:S(2)}, u32[]{:S(2)}) collective-permute-start(bf16[256,1024]{1,0:T(8,128)(2,1)S(1)} %pad_maximum_fusion.17), channel_id=1, source_target_pairs={{0,16},{1,17},{2,18},{3,19},{4,20},{5,21},{6,22},{7,23},{8,24},{9,... | collective-permute-start | bytes 1572872 | tf_op jit(solution)/shard_map/ppermute | solution.py:386
  239.2 62.2 %collective-permute-start.30 = (bf16[256,1024]{1,0:T(8,128)(2,1)S(1)}, bf16[256,1024]{1,0:T(8,128)(2,1)S(1)}, u32[]{:S(2)}, u32[]{:S(2)}) collective-permute-start(bf16[256,1024]{1,0:T(8,128)(2,1)S(1)} %pad_maximum_fusion.17), channel_id=1, source_target_pairs={{0,24},{1,25},{2,26},{3,27},{4,28},{5,29},{6,30},{7,31},{8,16},{9,... | collective-permute-start | bytes 1572872 | tf_op jit(solution)/shard_map/ppermute | solution.py:386
  256.5 49.8 %collective-permute-start.41 = (bf16[512,2048]{1,0:T(8,128)(2,1)S(1)}, bf16[512,2048]{1,0:T(8,128)(2,1)S(1)}, u32[]{:S(2)}, u32[]{:S(2)}) collective-permute-start(bf16[512,2048]{1,0:T(8,128)(2,1)S(1)} %pad_maximum_fusion.7), channel_id=1, source_target_pairs={{0,0},{1,5},{2,2},{3,7},{4,4},{5,1},{6,6},{7,3},{8,8},{9,13},{10,1... | collective-permute-start | bytes 6291464 | tf_op jit(solution)/shard_map/ppermute | solution.py:386
  257.3 50.6 %collective-permute-start.42 = (bf16[512,2048]{1,0:T(8,128)(2,1)S(1)}, bf16[512,2048]{1,0:T(8,128)(2,1)S(1)}, u32[]{:S(2)}, u32[]{:S(2)}) collective-permute-start(bf16[512,2048]{1,0:T(8,128)(2,1)S(1)} %pad_maximum_fusion.7), channel_id=1, source_target_pairs={{0,2},{1,7},{2,0},{3,5},{4,6},{5,3},{6,4},{7,1},{8,10},{9,15},{10,... | collective-permute-start | bytes 6291464 | tf_op jit(solution)/shard_map/ppermute | solution.py:386
  262.9 54.5 %collective-permute-start.43 = (bf16[512,2048]{1,0:T(8,128)(2,1)S(1)}, bf16[512,2048]{1,0:T(8,128)(2,1)S(1)}, u32[]{:S(2)}, u32[]{:S(2)}) collective-permute-start(bf16[512,2048]{1,0:T(8,128)(2,1)S(1)} %pad_maximum_fusion.7), channel_id=1, source_target_pairs={{0,5},{1,0},{2,7},{3,2},{4,1},{5,4},{6,3},{7,6},{8,13},{9,8},{10,1... | collective-permute-start | bytes 6291464 | tf_op jit(solution)/shard_map/ppermute | solution.py:386
  301.4 88.6 %collective-permute-start.44 = (bf16[512,2048]{1,0:T(8,128)(2,1)S(1)}, bf16[512,2048]{1,0:T(8,128)(2,1)S(1)}, u32[]{:S(2)}, u32[]{:S(2)}) collective-permute-start(bf16[512,2048]{1,0:T(8,128)(2,1)S(1)} %pad_maximum_fusion.7), channel_id=1, source_target_pairs={{0,7},{1,2},{2,5},{3,0},{4,3},{5,6},{6,1},{7,4},{8,15},{9,10},{10,... | collective-permute-start | bytes 6291464 | tf_op jit(solution)/shard_map/ppermute | solution.py:386
  301.4 88.5 %collective-permute-start.40 = (bf16[1024,1024]{0,1:T(8,128)(2,1)S(1)}, bf16[1024,1024]{0,1:T(8,128)(2,1)S(1)}, u32[]{:S(2)}, u32[]{:S(2)}) collective-permute-start(bf16[1024,1024]{0,1:T(8,128)(2,1)S(1)} %pad_maximum_fusion.9), channel_id=1, source_target_pairs={{0,1},{1,0},{2,3},{3,2},{4,5},{5,4},{6,7},{7,6},{8,9},{9,8},{10,11... | collective-permute-start | bytes 6291464 | tf_op jit(solution)/shard_map/ppermute | solution.py:386
  306.3 112.5 %collective-permute-start.31 = (bf16[1024,1024]{1,0:T(8,128)(2,1)}, bf16[1024,1024]{1,0:T(8,128)(2,1)}, u32[]{:S(2)}, u32[]{:S(2)}) collective-permute-start(bf16[1024,1024]{1,0:T(8,128)(2,1)} %pad_maximum_fusion.8), channel_id=1, source_target_pairs={{0,1},{1,0},{2,3},{3,2},{4,5},{5,4},{6,7},{7,6},{8,9},{9,8},{10,11... | collective-permute-start | bytes 6291464 | tf_op jit(solution)/shard_map/ppermute | solution.py:386
  307.8 102.0 %collective-permute-start.32 = (bf16[1024,512]{1,0:T(8,128)(2,1)}, bf16[1024,512]{1,0:T(8,128)(2,1)}, u32[]{:S(2)}, u32[]{:S(2)}) collective-permute-start(bf16[1024,512]{1,0:T(8,128)(2,1)} %convert_element_type.185), channel_id=1, source_target_pairs={{0,0},{1,5},{2,2},{3,7},{4,4},{5,1},{6,6},{7,3},{8,8},{9,13},{10,1... | collective-permute-start | bytes 3145736 | tf_op jit(solution)/shard_map/ppermute | solution.py:386
  317.3 92.5 %collective-permute-start.33 = (bf16[1024,512]{1,0:T(8,128)(2,1)}, bf16[1024,512]{1,0:T(8,128)(2,1)}, u32[]{:S(2)}, u32[]{:S(2)}) collective-permute-start(bf16[1024,512]{1,0:T(8,128)(2,1)} %convert_element_type.185), channel_id=1, source_target_pairs={{0,2},{1,7},{2,0},{3,5},{4,6},{5,3},{6,4},{7,1},{8,10},{9,15},{10,... | collective-permute-start | bytes 3145736 | tf_op jit(solution)/shard_map/ppermute | solution.py:386
  448.8 39.6 %collective-permute-start.46 = (bf16[256,1024]{0,1:T(8,128)(2,1)S(1)}, bf16[256,1024]{0,1:T(8,128)(2,1)S(1)}, u32[]{:S(2)}, u32[]{:S(2)}) collective-permute-start(bf16[256,1024]{0,1:T(8,128)(2,1)S(1)} %get-tuple-element.83), channel_id=1, source_target_pairs={{0,8},{1,9},{2,10},{3,11},{4,12},{5,13},{6,14},{7,15},{8,0},{9,1},... | collective-permute-start | bytes 1572872 | tf_op jit(solution)/shard_map/ppermute | solution.py:386
  467.4 35.9 %collective-permute-start.48 = (bf16[256,1024]{0,1:T(8,128)(2,1)S(1)}, bf16[256,1024]{0,1:T(8,128)(2,1)S(1)}, u32[]{:S(2)}, u32[]{:S(2)}) collective-permute-start(bf16[256,1024]{0,1:T(8,128)(2,1)S(1)} %get-tuple-element.84), channel_id=1, source_target_pairs={{0,24},{1,25},{2,26},{3,27},{4,28},{5,29},{6,30},{7,31},{8,16},{9,... | collective-permute-start | bytes 1572872 | tf_op jit(solution)/shard_map/ppermute | solution.py:386
  538.1 34.7 %collective-permute-start.81 = (bf16[1024,512]{1,0:T(8,128)(2,1)}, bf16[1024,512]{1,0:T(8,128)(2,1)}, u32[]{:S(2)}, u32[]{:S(2)}) collective-permute-start(bf16[1024,512]{1,0:T(8,128)(2,1)} %get-tuple-element.63), channel_id=1, source_target_pairs={{0,0},{1,5},{2,2},{3,7},{4,4},{5,1},{6,6},{7,3},{8,8},{9,13},{10,1... | collective-permute-start | bytes 3145736 | tf_op jit(solution)/shard_map/ppermute | solution.py:386
  547.5 27.8 %collective-permute-start.82 = (bf16[1024,512]{1,0:T(8,128)(2,1)}, bf16[1024,512]{1,0:T(8,128)(2,1)}, u32[]{:S(2)}, u32[]{:S(2)}) collective-permute-start(bf16[1024,512]{1,0:T(8,128)(2,1)} %get-tuple-element.66), channel_id=1, source_target_pairs={{0,2},{1,7},{2,0},{3,5},{4,6},{5,3},{6,4},{7,1},{8,10},{9,15},{10,... | collective-permute-start | bytes 3145736 | tf_op jit(solution)/shard_map/ppermute | solution.py:386
  548.7 34.1 %collective-permute-start.83 = (bf16[1024,512]{1,0:T(8,128)(2,1)}, bf16[1024,512]{1,0:T(8,128)(2,1)}, u32[]{:S(2)}, u32[]{:S(2)}) collective-permute-start(bf16[1024,512]{1,0:T(8,128)(2,1)} %get-tuple-element.65), channel_id=1, source_target_pairs={{0,1},{1,4},{2,3},{3,6},{4,5},{5,0},{6,7},{7,2},{8,9},{9,12},{10,1... | collective-permute-start | bytes 3145736 | tf_op jit(solution)/shard_map/ppermute | solution.py:386
  548.7 46.3 %collective-permute-start.84 = (bf16[1024,512]{1,0:T(8,128)(2,1)}, bf16[1024,512]{1,0:T(8,128)(2,1)}, u32[]{:S(2)}, u32[]{:S(2)}) collective-permute-start(bf16[1024,512]{1,0:T(8,128)(2,1)} %get-tuple-element.64), channel_id=1, source_target_pairs={{0,3},{1,6},{2,1},{3,4},{4,7},{5,2},{6,5},{7,0},{8,11},{9,14},{10,... | collective-permute-start | bytes 3145736 | tf_op jit(solution)/shard_map/ppermute | solution.py:386
  552.0 49.2 %collective-permute-start.56 = (bf16[1024,1024]{0,1:T(8,128)(2,1)}, bf16[1024,1024]{0,1:T(8,128)(2,1)}, u32[]{:S(2)}, u32[]{:S(2)}) collective-permute-start(bf16[1024,1024]{0,1:T(8,128)(2,1)} %maximum_maximum_fusion.1), channel_id=1, source_target_pairs={{0,1},{1,0},{2,3},{3,2},{4,5},{5,4},{6,7},{7,6},{8,9},{9,8},{10,11... | collective-permute-start | bytes 6291464 | tf_op jit(solution)/shard_map/ppermute | solution.py:386
  572.8 83.7 %collective-permute-start.77 = (bf16[512,2048]{1,0:T(8,128)(2,1)}, bf16[512,2048]{1,0:T(8,128)(2,1)S(1)}, u32[]{:S(2)}, u32[]{:S(2)}) collective-permute-start(bf16[512,2048]{1,0:T(8,128)(2,1)} %get-tuple-element.59), channel_id=1, source_target_pairs={{0,0},{1,5},{2,2},{3,7},{4,4},{5,1},{6,6},{7,3},{8,8},{9,13},{10,1... | collective-permute-start | bytes 6291464 | tf_op jit(solution)/shard_map/ppermute | solution.py:386
  575.3 82.0 %collective-permute-start.78 = (bf16[512,2048]{1,0:T(8,128)(2,1)S(1)}, bf16[512,2048]{1,0:T(8,128)(2,1)S(1)}, u32[]{:S(2)}, u32[]{:S(2)}) collective-permute-start(bf16[512,2048]{1,0:T(8,128)(2,1)S(1)} %get-tuple-element.62), channel_id=1, source_target_pairs={{0,2},{1,7},{2,0},{3,5},{4,6},{5,3},{6,4},{7,1},{8,10},{9,15},{10,... | collective-permute-start | bytes 6291464 | tf_op jit(solution)/shard_map/ppermute | solution.py:386
  582.8 78.6 %collective-permute-start.79 = (bf16[512,2048]{1,0:T(8,128)(2,1)S(1)}, bf16[512,2048]{1,0:T(8,128)(2,1)S(1)}, u32[]{:S(2)}, u32[]{:S(2)}) collective-permute-start(bf16[512,2048]{1,0:T(8,128)(2,1)S(1)} %get-tuple-element.61), channel_id=1, source_target_pairs={{0,1},{1,4},{2,3},{3,6},{4,5},{5,0},{6,7},{7,2},{8,9},{9,12},{10,1... | collective-permute-start | bytes 6291464 | tf_op jit(solution)/shard_map/ppermute | solution.py:386
  595.0 92.6 %collective-permute-start.80 = (bf16[512,2048]{1,0:T(8,128)(2,1)S(1)}, bf16[512,2048]{1,0:T(8,128)(2,1)S(1)}, u32[]{:S(2)}, u32[]{:S(2)}) collective-permute-start(bf16[512,2048]{1,0:T(8,128)(2,1)S(1)} %get-tuple-element.60), channel_id=1, source_target_pairs={{0,3},{1,6},{2,1},{3,4},{4,7},{5,2},{6,5},{7,0},{8,11},{9,14},{10,... | collective-permute-start | bytes 6291464 | tf_op jit(solution)/shard_map/ppermute | solution.py:386
  616.6 30.4 %collective-permute-start.57 = (bf16[768,512]{1,0:T(8,128)(2,1)S(1)}, bf16[768,512]{1,0:T(8,128)(2,1)S(1)}, u32[]{:S(2)}, u32[]{:S(2)}) collective-permute-start(bf16[768,512]{1,0:T(8,128)(2,1)S(1)} %slice.262), channel_id=1, source_target_pairs={{8,0},{9,1},{10,2},{11,3},{12,4},{13,5},{14,6},{15,7},{16,8},{17,9... | collective-permute-start | bytes 2359304 | tf_op jit(solution)/shard_map/ppermute | solution.py:386
  646.9 41.6 %collective-permute-start.71 = (bf16[256,512]{1,0:T(8,128)(2,1)S(1)}, bf16[256,512]{1,0:T(8,128)(2,1)S(1)}, u32[]{:S(2)}, u32[]{:S(2)}) collective-permute-start(bf16[256,512]{1,0:T(8,128)(2,1)S(1)} %get-tuple-element.104), channel_id=1, source_target_pairs={{0,1},{1,0},{2,3},{3,2},{4,5},{5,4},{6,7},{7,6},{8,9},{9,8},{10,11... | collective-permute-start | bytes 786440 | tf_op jit(solution)/shard_map/ppermute | solution.py:386
  656.5 90.2 %collective-permute-start.58 = (bf16[1024,1024]{0,1:T(8,128)(2,1)S(1)}, bf16[1024,1024]{0,1:T(8,128)(2,1)S(1)}, u32[]{:S(2)}, u32[]{:S(2)}) collective-permute-start(bf16[1024,1024]{0,1:T(8,128)(2,1)S(1)} %convolution_convert_fusion.5), channel_id=1, source_target_pairs={{0,1},{1,0},{2,3},{3,2},{4,5},{5,4},{6,7},{7,6},{8,9},{9,8},{10,11... | collective-permute-start | bytes 6291464 | tf_op jit(solution)/shard_map/ppermute | solution.py:386
  657.3 34.7 %collective-permute-start.72 = (bf16[256,512]{1,0:T(8,128)(2,1)S(1)}, bf16[256,512]{1,0:T(8,128)(2,1)S(1)}, u32[]{:S(2)}, u32[]{:S(2)}) collective-permute-start(bf16[256,512]{1,0:T(8,128)(2,1)S(1)} %get-tuple-element.103), channel_id=1, source_target_pairs={{0,2},{1,3},{2,0},{3,1},{4,6},{5,7},{6,4},{7,5},{8,10},{9,11},{10,... | collective-permute-start | bytes 786440 | tf_op jit(solution)/shard_map/ppermute | solution.py:386
  661.5 69.4 %collective-permute-start.65 = (bf16[512,768]{1,0:T(8,128)(2,1)S(1)}, bf16[512,768]{1,0:T(8,128)(2,1)S(1)}, u32[]{:S(2)}, u32[]{:S(2)}) collective-permute-start(bf16[512,768]{1,0:T(8,128)(2,1)S(1)} %get-tuple-element.75), channel_id=1, source_target_pairs={{0,1},{1,0},{2,3},{3,2},{4,5},{5,4},{6,7},{7,6},{8,9},{9,8},{10,11... | collective-permute-start | bytes 2359304 | tf_op jit(solution)/shard_map/ppermute | solution.py:386
  687.6 43.3 %collective-permute-start.66 = (bf16[512,768]{1,0:T(8,128)(2,1)S(1)}, bf16[512,768]{1,0:T(8,128)(2,1)S(1)}, u32[]{:S(2)}, u32[]{:S(2)}) collective-permute-start(bf16[512,768]{1,0:T(8,128)(2,1)S(1)} %get-tuple-element.74), channel_id=1, source_target_pairs={{0,2},{1,3},{2,0},{3,1},{4,6},{5,7},{6,4},{7,5},{8,10},{9,11},{10,... | collective-permute-start | bytes 2359304 | tf_op jit(solution)/shard_map/ppermute | solution.py:386
  688.5 42.4 %collective-permute-start.67 = (bf16[512,768]{1,0:T(8,128)(2,1)S(1)}, bf16[512,768]{1,0:T(8,128)(2,1)S(1)}, u32[]{:S(2)}, u32[]{:S(2)}) collective-permute-start(bf16[512,768]{1,0:T(8,128)(2,1)S(1)} %get-tuple-element.73), channel_id=1, source_target_pairs={{0,3},{1,2},{2,1},{3,0},{4,7},{5,6},{6,5},{7,4},{8,11},{9,10},{10,... | collective-permute-start | bytes 2359304 | tf_op jit(solution)/shard_map/ppermute | solution.py:386
  692.1 38.7 %collective-permute-start.73 = (bf16[256,512]{1,0:T(8,128)(2,1)S(1)}, bf16[256,512]{1,0:T(8,128)(2,1)S(1)}, u32[]{:S(2)}, u32[]{:S(2)}) collective-permute-start(bf16[256,512]{1,0:T(8,128)(2,1)S(1)} %get-tuple-element.102), channel_id=1, source_target_pairs={{0,3},{1,2},{2,1},{3,0},{4,7},{5,6},{6,5},{7,4},{8,11},{9,10},{10,... | collective-permute-start | bytes 786440 | tf_op jit(solution)/shard_map/ppermute | solution.py:386
  731.8 83.6 %collective-permute-start.68 = (bf16[512,768]{1,0:T(8,128)(2,1)S(1)}, bf16[512,768]{1,0:T(8,128)(2,1)S(1)}, u32[]{:S(2)}, u32[]{:S(2)}) collective-permute-start(bf16[512,768]{1,0:T(8,128)(2,1)S(1)} %get-tuple-element.69), channel_id=1, source_target_pairs={{0,8},{1,9},{2,10},{3,11},{4,12},{5,13},{6,14},{7,15},{8,0},{9,1},... | collective-permute-start | bytes 2359304 | tf_op jit(solution)/shard_map/ppermute | solution.py:386
  743.1 45.2 %collective-permute-start.74 = (bf16[256,512]{1,0:T(8,128)(2,1)S(1)}, bf16[256,512]{1,0:T(8,128)(2,1)S(1)}, u32[]{:S(2)}, u32[]{:S(2)}) collective-permute-start(bf16[256,512]{1,0:T(8,128)(2,1)S(1)} %get-tuple-element.98), channel_id=1, source_target_pairs={{0,8},{1,9},{2,10},{3,11},{4,12},{5,13},{6,14},{7,15},{8,0},{9,1},... | collective-permute-start | bytes 786440 | tf_op jit(solution)/shard_map/ppermute | solution.py:386
  743.1 47.0 %collective-permute-start.75 = (bf16[256,512]{1,0:T(8,128)(2,1)S(1)}, bf16[256,512]{1,0:T(8,128)(2,1)S(1)}, u32[]{:S(2)}, u32[]{:S(2)}) collective-permute-start(bf16[256,512]{1,0:T(8,128)(2,1)S(1)} %get-tuple-element.100), channel_id=1, source_target_pairs={{0,16},{1,17},{2,18},{3,19},{4,20},{5,21},{6,22},{7,23},{8,24},{9,... | collective-permute-start | bytes 786440 | tf_op jit(solution)/shard_map/ppermute | solution.py:386
  746.7 70.9 %collective-permute-start.69 = (bf16[512,768]{1,0:T(8,128)(2,1)S(1)}, bf16[512,768]{1,0:T(8,128)(2,1)S(1)}, u32[]{:S(2)}, u32[]{:S(2)}) collective-permute-start(bf16[512,768]{1,0:T(8,128)(2,1)S(1)} %get-tuple-element.71), channel_id=1, source_target_pairs={{0,16},{1,17},{2,18},{3,19},{4,20},{5,21},{6,22},{7,23},{8,24},{9,... | collective-permute-start | bytes 2359304 | tf_op jit(solution)/shard_map/ppermute | solution.py:386
  748.1 69.6 %collective-permute-start.70 = (bf16[512,768]{1,0:T(8,128)(2,1)S(1)}, bf16[512,768]{1,0:T(8,128)(2,1)S(1)}, u32[]{:S(2)}, u32[]{:S(2)}) collective-permute-start(bf16[512,768]{1,0:T(8,128)(2,1)S(1)} %get-tuple-element.70), channel_id=1, source_target_pairs={{0,24},{1,25},{2,26},{3,27},{4,28},{5,29},{6,30},{7,31},{8,16},{9,... | collective-permute-start | bytes 2359304 | tf_op jit(solution)/shard_map/ppermute | solution.py:386
  790.1 27.9 %collective-permute-start.59 = (bf16[512,512]{0,1:T(8,128)(2,1)S(1)}, bf16[512,512]{0,1:T(8,128)(2,1)S(1)}, u32[]{:S(2)}, u32[]{:S(2)}) collective-permute-start(bf16[512,512]{0,1:T(8,128)(2,1)S(1)} %get-tuple-element.80), channel_id=1, source_target_pairs={{0,4},{1,5},{2,6},{3,7},{4,0},{5,1},{6,2},{7,3},{8,12},{9,13},{10,... | collective-permute-start | bytes 1572872 | tf_op jit(solution)/shard_map/ppermute | solution.py:386
  839.3 26.5 %collective-permute-start.85 = (f32[2,512]{1,0:T(2,128)S(1)}, f32[2,512]{1,0:T(2,128)S(1)}, u32[]{:S(2)}, u32[]{:S(2)}) collective-permute-start(f32[2,512]{1,0:T(2,128)S(1)} %pad_maximum_fusion.19), channel_id=1, source_target_pairs={{0,8},{1,9},{2,10},{3,11},{4,12},{5,13},{6,14},{7,15},{8,0},{9,1},... | collective-permute-start | bytes 12296 | tf_op jit(solution)/shard_map/ppermute | solution.py:386
  (107 other events, 3087.1 us)

commit v2 on v1

--- a/solution.py
+++ b/solution.py
@@ -572,6 +572,486 @@
     )(begin, q, k, v, grad, lse)
 
 
+MESH = pl.DeviceIdType.MESH
+PLACE = {0: 0, 2: 1, 1: 2, 3: 3}
+TILE = 256
+
+
+class Post:
+    def __init__(self, send_sem, recv_sem):
+        self.send_sem, self.recv_sem, self.used = send_sem, recv_sem, 0
+
+    def ready(self, src, dst, target, slot=None):
+        if slot is None:
+            slot = self.used
+            self.used += 1
+        return pltpu.make_async_remote_copy(
+            src_ref=src,
+            dst_ref=dst,
+            send_sem=self.send_sem.at[slot],
+            recv_sem=self.recv_sem.at[slot],
+            device_id=target,
+            device_id_type=MESH,
+        )
+
+    def take(self, count):
+        first = self.used
+        self.used += count
+        return first
+
+    def send(self, src, dst, target):
+        copy = self.ready(src, dst, target)
+        copy.start()
+        return copy
+
+
+def greet(peers):
+    barrier = pltpu.get_barrier_semaphore()
+    for peer in peers:
+        pl.semaphore_signal(barrier, inc=1, device_id=peer, device_id_type=MESH)
+    pl.semaphore_wait(barrier, len(peers))
+
+
+def as_row(column):
+    return jnp.transpose(jnp.broadcast_to(column, (column.shape[0], 128)))[0:8]
+
+
+def as_column(row):
+    return jnp.transpose(row)[:, 0:1]
+
+
+def forward_kernel(
+    x_ref, gain_one_ref, gain_two_ref, begin_ref, own_in, own_out, own_hidden, own_down, own_grad,
+    normed_ref, weight_in, weight_out, q_ref, kv_ref, att_ref, lse_ref, mid_ref, scale_ref, n2_ref,
+    hidden_all, down_all, grad_all,
+    zin, zout, sums, wide, given, arrived, low, landed, x32,
+    send_sem, recv_sem, local_sem,
+):
+    d, r, c = (lax.axis_index(name) for name in AXES)
+    y, core = c // 2, lax.rem(c, 2)
+    rows = x_ref.shape[0]
+    fc = x_ref.shape[1]
+    group = 2 * rows
+    width = q_ref.shape[1]
+    half = 2 * fc
+    post = Post(send_sem, recv_sem)
+    in_plane = [(d, r ^ a, c ^ b) for a in (0, 1) for b in range(COL) if (a, b) != (0, 0)]
+    greet([(d ^ j, r, c) for j in (1, 2, 3)] + in_plane)
+
+    first = post.take(DP)
+
+    def line(p, target_plane):
+        return post.ready(zin.at[p], zin.at[p], (target_plane, r, c), first + p)
+
+    first_down = post.take(DP)
+
+    def line_down(p, target_plane):
+        return pltpu.make_async_remote_copy(
+            src_ref=zin.at[p], dst_ref=zin.at[p],
+            send_sem=send_sem.at[first_down + p], recv_sem=recv_sem.at[first + p],
+            device_id=(target_plane, r, c), device_id_type=MESH,
+        )
+
+    mine = pltpu.make_async_copy(own_in, zin.at[d], local_sem.at[0])
+    mine.start()
+    mine.wait()
+
+    @pl.when(d < DP - 1)
+    def _():
+        line(d, d + 1).start()
+
+    @pl.when(d > 0)
+    def _():
+        line_down(d, d - 1).start()
+
+    first_cols = post.take(DP)
+    first_keep = 1
+
+    def to_column(p):
+        return pltpu.make_async_remote_copy(
+            src_ref=zin.at[p],
+            dst_ref=weight_in.at[pl.ds(pl.multiple_of(place_of(p ^ c) * fc, fc), fc), :],
+            send_sem=send_sem.at[first_cols + p],
+            recv_sem=recv_sem.at[first_cols + (p ^ c)],
+            device_id=(d, r, p), device_id_type=MESH,
+        )
+
+    def place_of(m):
+        return lax.rem(m, 2) * 2 + m // 2
+
+    keep = pltpu.make_async_copy(zin.at[c], weight_in.at[pl.ds(0, fc), :], local_sem.at[first_keep])
+
+    def pass_on(p):
+        @pl.when(p == c)
+        def _():
+            keep.start()
+
+        @pl.when(p != c)
+        def _():
+            to_column(p).start()
+
+    pass_on(d)
+
+    def fill_x(t, total):
+        part = pl.ds(pl.multiple_of(t * 128, 128), 128)
+        value = x_ref[part, :].astype(F32)
+        x32[part, :] = value
+        sums[0, :, part] = as_row(jnp.sum(value * value, axis=1, keepdims=True))
+        return total
+
+    lax.fori_loop(0, rows // 128, fill_x, 0)
+    small = [post.send(sums.at[0], sums.at[m], (d, r, c ^ m)) for m in (1, 2, 3)]
+    half_rows = rows // 2
+    grad_cross = post.send(
+        own_grad.at[pl.ds(pl.multiple_of((1 - y) * half_rows, half_rows), half_rows), :],
+        grad_all.at[pl.ds(0, half_rows), pl.ds(fc, fc)],
+        (d, r, c ^ 2),
+    )
+    grad_keep = pltpu.make_async_copy(
+        own_grad.at[pl.ds(pl.multiple_of(y * half_rows, half_rows), half_rows), :],
+        grad_all.at[pl.ds(0, half_rows), pl.ds(0, fc)],
+        local_sem.at[2],
+    )
+    grad_keep.start()
+    for copy in small:
+        copy.wait_recv()
+
+    def norm_one(t, total):
+        part = pl.ds(pl.multiple_of(t * 128, 128), 128)
+        square = sums[0, :, part] + sums[2, :, part] + sums[1, :, part] + sums[3, :, part]
+        scale = lax.rsqrt(as_column(square) / D + EPSILON)
+        normed_ref[part, 0:fc] = (x32[part, :] * scale * gain_one_ref[...]).astype(BF)
+        return total
+
+    lax.fori_loop(0, rows // 128, norm_one, 0)
+    own_rows, other_rows = pl.ds(0, rows), pl.ds(rows, rows)
+
+    def columns(place):
+        return pl.ds(place * fc, fc)
+
+    own_block = normed_ref.at[own_rows, columns(0)]
+    beside = post.send(own_block, normed_ref.at[other_rows, columns(0)], (d, r ^ 1, c))
+    beyond = post.send(own_block, normed_ref.at[own_rows, columns(1)], (d, r, c ^ 2))
+    corner = post.send(own_block, normed_ref.at[other_rows, columns(1)], (d, r ^ 1, c ^ 2))
+    sibling = (d, r, c ^ 1)
+    shared = [post.send(own_block, normed_ref.at[own_rows, columns(2)], sibling)]
+
+    def line_step(s):
+        for p, valid, onward, forward in (
+            (d - s, d - s >= 0, d < DP - 1, lambda p: line(p, d + 1)),
+            (d + s, d + s < DP, d > 0, lambda p: line_down(p, d - 1)),
+        ):
+            @pl.when(valid)
+            def _(p=p, onward=onward, forward=forward):
+                line(p, d).wait_recv()
+
+                @pl.when(onward)
+                def _():
+                    forward(p).start()
+
+                pass_on(p)
+
+    line_step(1)
+    for copy, where, place in ((beside, other_rows, 0), (beyond, own_rows, 1), (corner, other_rows, 1)):
+        copy.wait_recv()
+        shared.append(
+            post.send(normed_ref.at[where, columns(place)], normed_ref.at[where, columns(place + 2)], sibling)
+        )
+
+    bulk = []
+    first_hidden = post.take(8)
+    for i in (0, 2, 1, 3):
+        b = c ^ i
+        target = (d, r ^ lax.rem(b, 2), b)
+        place = PLACE[i]
+        for kind, (src, dst) in enumerate((
+            (own_down, down_all.at[:, columns(place)]),
+            (own_hidden, hidden_all.at[pl.ds(place * fc, fc), :]),
+        )):
+            bulk.append((i, kind, post.ready(src, dst, target, first_hidden + 2 * place + kind),
+                         pltpu.make_async_copy(src, dst, local_sem.at[3 + kind])))
+    for i, kind, copy, local in bulk:
+        if i == 0:
+            @pl.when(core == 0)
+            def _(local=local):
+                local.start()
+
+            @pl.when(core == 1)
+            def _(copy=copy):
+                copy.start()
+        else:
+            copy.start()
+
+    line_step(2)
+    line_step(3)
+    outs = [
+        post.send(own_out, zout.at[j], (d ^ j, r, c)) for j in (1, 2, 3)
+    ]
+    mine = pltpu.make_async_copy(own_out, zout.at[0], local_sem.at[5])
+    mine.start()
+    mine.wait()
+
+    for copy in shared:
+        copy.wait_recv()
+    keep.wait()
+    for m in (1, 2, 3):
+        pltpu.make_async_remote_copy(
+            src_ref=zin.at[0], dst_ref=weight_in.at[pl.ds(0, fc), :],
+            send_sem=send_sem.at[first_cols], recv_sem=recv_sem.at[first_cols + m],
+            device_id=(d, r, c), device_id_type=MESH,
+        ).wait_recv()
+
+    def turned(t):
+        return lax.rem(t + 2 * r, group // TILE)
+
+    def project_kv(t, total):
+        part = pl.ds(pl.multiple_of(t * TILE, TILE), TILE)
+        to = pl.ds(pl.multiple_of(REACH + turned(t) * TILE, TILE), TILE)
+        kv_ref[to, :] = jnp.dot(
+            normed_ref[part, :], weight_in[:, width:], preferred_element_type=F32
+        ).astype(BF)
+        return total
+
+    lax.fori_loop(0, group // TILE, project_kv, 0)
+    halo = post.ready(kv_ref.at[pl.ds(group, REACH), :], kv_ref.at[pl.ds(0, REACH), :], (lax.rem(d + 1, DP), r, c))
+
+    @pl.when(d < DP - 1)
+    def _():
+        halo.start()
+
+    def project_q(t, total):
+        part = pl.ds(pl.multiple_of(t * TILE, TILE), TILE)
+        to = pl.ds(pl.multiple_of(turned(t) * TILE, TILE), TILE)
+        q_ref[to, :] = jnp.dot(
+            normed_ref[part, :], weight_in[:, :width], preferred_element_type=F32
+        ).astype(BF)
+        return total
+
+    lax.fori_loop(0, group // TILE, project_q, 0)
+
+    for copy in outs:
+        copy.wait_recv()
+    out_cols = [
+        post.send(zout.at[d ^ c ^ m], weight_out.at[:, columns(PLACE[m])], (d, r, c ^ m)) for m in (1, 2, 3)
+    ]
+    out_keep = pltpu.make_async_copy(zout.at[d ^ c], weight_out.at[:, columns(0)], local_sem.at[6])
+    out_keep.start()
+    grad_cross.wait_recv()
+    grad_keep.wait()
+    grads = [
+        post.send(
+            grad_all.at[pl.ds(0, half_rows), pl.ds(0, half)],
+            grad_all.at[pl.ds(j * half_rows, half_rows), pl.ds(0, half)],
+            (d ^ j, r, c),
+        )
+        for j in (1, 2, 3)
+    ]
+    grads_shared = [
+        post.send(
+            grad_all.at[pl.ds(0, half_rows), pl.ds(0, half)],
+            grad_all.at[pl.ds(0, half_rows), pl.ds(half, half)],
+            sibling,
+        )
+    ]
+
+    @pl.when(d == 0)
+    def _():
+        kv_ref[pl.ds(0, REACH), :] = jnp.zeros((REACH, 2 * width), BF)
+
+    @pl.when(d > 0)
+    def _():
+        halo.wait_recv()
+
+    span = TILE + REACH
+    for h in range(width // HEAD_DIM):
+        lanes = pl.ds(h * HEAD_DIM, HEAD_DIM)
+        value_lanes = pl.ds(width + h * HEAD_DIM, HEAD_DIM)
+
+        def one(t, total, lanes=lanes, value_lanes=value_lanes):
+            part = pl.ds(pl.multiple_of(t * TILE, TILE), TILE)
+            to = pl.ds(pl.multiple_of(turned(t) * TILE, TILE), TILE)
+            window = pl.ds(pl.multiple_of(t * TILE, TILE), span)
+            scores = scores_of(q_ref[part, lanes], kv_ref[window, lanes])
+            query = lax.broadcasted_iota(jnp.int32, (TILE, span), 0)
+            key = lax.broadcasted_iota(jnp.int32, (TILE, span), 1)
+            begin = begin_ref[part, 0:1] + (REACH - t * TILE)
+            allowed = (key <= query + REACH) & (key >= begin)
+            scores = jnp.where(allowed, scores, NEG_FILL)
+            highest = jnp.max(scores, axis=1, keepdims=True)
+            expo = jnp.exp(scores - highest)
+            total_e = jnp.sum(expo, axis=1, keepdims=True)
+            probability = (expo * (1.0 / total_e)).astype(BF)
+            att_ref[to, lanes] = jnp.dot(
+                probability, kv_ref[window, value_lanes], preferred_element_type=F32
+            ).astype(BF)
+            lse_ref[part, lanes] = jnp.broadcast_to(highest + jnp.log(total_e), (TILE, HEAD_DIM))
+            return total
+
+        lax.fori_loop(0, group // TILE, one, 0)
+
+    for copy in out_cols:
+        copy.wait_recv()
+    out_keep.wait()
+
+    def out_given(t, total):
+        part = pl.ds(pl.multiple_of(t * TILE, TILE), TILE)
+        given[part, :] = jnp.dot(
+            att_ref[part, :], weight_out[:, half:], preferred_element_type=F32
+        ).astype(BF)
+        return total
+
+    lax.fori_loop(0, group // TILE, out_given, 0)
+    to_sibling = post.send(given, arrived, sibling)
+
+    def out_kept(t, total):
+        part = pl.ds(pl.multiple_of(t * TILE, TILE), TILE)
+        wide[part, :] = jnp.dot(att_ref[part, :], weight_out[:, :half], preferred_element_type=F32)
+        return total
+
+    lax.fori_loop(0, group // TILE, out_kept, 0)
+    to_sibling.wait_recv()
+
+    def add_low(t, total):
+        part = pl.ds(pl.multiple_of(t * 128, 128), 128)
+        value = wide[part, :] + arrived[part, :].astype(F32)
+        wide[part, :] = value
+        low[part, :] = value.astype(BF)
+        return total
+
+    lax.fori_loop(0, group // 128, add_low, 0)
+    pieces = [
+        post.send(low.at[other_rows, columns(1)], landed.at[2], (d, r ^ 1, c ^ 2)),
+        post.send(low.at[other_rows, columns(0)], landed.at[0], (d, r ^ 1, c)),
+        post.send(low.at[own_rows, columns(1)], landed.at[1], (d, r, c ^ 2)),
+    ]
+    for copy in pieces:
+        copy.wait_recv()
+
+    def middle(t, total):
+        part = pl.ds(pl.multiple_of(t * 128, 128), 128)
+        value = (
+            x32[part, :] + wide[part, 0:fc] + landed[0, part, :].astype(F32)
+            + landed[1, part, :].astype(F32) + landed[2, part, :].astype(F32)
+        )
+        mid_ref[part, :] = value
+        sums[4, :, part] = as_row(jnp.sum(value * value, axis=1, keepdims=True))
+        return total
+
+    lax.fori_loop(0, rows // 128, middle, 0)
+    again = [post.send(sums.at[4], sums.at[4 + m], (d, r, c ^ m)) for m in (1, 2, 3)]
+    for copy in again:
+        copy.wait_recv()
+
+    def norm_two(t, total):
+        part = pl.ds(pl.multiple_of(t * 128, 128), 128)
+        square = sums[4, :, part] + sums[6, :, part] + sums[5, :, part] + sums[7, :, part]
+        scale = lax.rsqrt(as_column(square) / D + EPSILON)
+        scale_ref[part, :] = scale
+        n2_ref[part, :] = (mid_ref[part, :] * scale * gain_two_ref[...]).astype(BF)
+        return total
+
+    lax.fori_loop(0, rows // 128, norm_two, 0)
+
+    for j, copy in zip((1, 2, 3), grads):
+        copy.wait_recv()
+        there = pl.ds(j * half_rows, half_rows)
+        grads_shared.append(
+            post.send(grad_all.at[there, pl.ds(0, half)], grad_all.at[there, pl.ds(half, half)], sibling)
+        )
+    for copy in grads_shared:
+        copy.wait_recv()
+    for i, kind, copy, local in bulk:
+        if i == 0:
+            @pl.when(core == 0)
+            def _(local=local):
+                local.wait()
+
+            @pl.when(core == 1)
+            def _(copy=copy):
+                copy.wait()
+        else:
+            copy.wait()
+
+    for copy in (
+        small + [grad_cross, beside, beyond, corner] + shared + outs + out_cols + grads + grads_shared
+        + [to_sibling] + pieces + again
+    ):
+        copy.wait_send()
+
+    @pl.when(d < DP - 1)
+    def _():
+        halo.wait_send()
+
+    for p in range(DP):
+        @pl.when((d < DP - 1) & (p <= d))
+        def _(p=p):
+            line(p, d).wait_send()
+
+        @pl.when((d > 0) & (p >= d))
+        def _(p=p):
+            line_down(p, d).wait_send()
+
+        @pl.when(c != p)
+        def _(p=p):
+            to_column(p).wait_send()
+
+
+SENDS = 64
+
+
+def forward(x, gain_one, gain_two, begin, own_in, own_out, own_hidden, own_down, own_grad):
+    rows, fc = x.shape
+    group = 2 * rows
+    width = own_out.shape[0]
+    units = own_down.shape[0]
+    vmem = pl.BlockSpec(memory_space=pltpu.VMEM)
+    hbm = pl.BlockSpec(memory_space=pl.ANY)
+
+    def like(shape, dtype=BF):
+        return jax.ShapeDtypeStruct(shape, dtype)
+
+    return pl.pallas_call(
+        forward_kernel,
+        in_specs=[vmem] * 4 + [hbm] * 5,
+        out_specs=[vmem] * 10 + [hbm] * 3,
+        out_shape=[
+            like((group, D)),
+            like((D, 3 * width)),
+            like((width, D)),
+            like((group, width)),
+            like((REACH + group, 2 * width)),
+            like((group, width)),
+            like((group, width), F32),
+            like((rows, fc), F32),
+            like((rows, 1), F32),
+            like((rows, fc)),
+            like((D, 2 * units)),
+            like((units, D)),
+            like((group, D)),
+        ],
+        scratch_shapes=[
+            pltpu.VMEM((DP, fc, 3 * width), BF),
+            pltpu.VMEM((DP, width, fc), BF),
+            pltpu.VMEM((8, 8, rows), F32),
+            pltpu.VMEM((group, 2 * fc), F32),
+            pltpu.VMEM((group, 2 * fc), BF),
+            pltpu.VMEM((group, 2 * fc), BF),
+            pltpu.VMEM((group, 2 * fc), BF),
+            pltpu.VMEM((3, rows, fc), BF),
+            pltpu.VMEM((rows, fc), F32),
+            pltpu.SemaphoreType.DMA((SENDS,)),
+            pltpu.SemaphoreType.DMA((SENDS,)),
+            pltpu.SemaphoreType.DMA((8,)),
+        ],
+        compiler_params=pltpu.CompilerParams(
+            collective_id=1, has_side_effects=True, vmem_limit_bytes=56 << 20
+        ),
+        cost_estimate=pl.CostEstimate(
+            flops=6 * group * D * width, bytes_accessed=64 << 20, transcendentals=0
+        ),
+    )(x, gain_one, gain_two, begin, own_in, own_out, own_hidden, own_down, own_grad)
+
+
 def rounded_norm(values, scale, gain):
     return (values * scale[:, None] * gain[None, :]).astype(BF)
 
@@ -614,40 +1094,22 @@
         swapped = jnp.concatenate([array[rows:], array[:rows]], 0)
         return jnp.where(r == 0, array, swapped)
 
+    x = tokens.astype(F32)
+    begin = (begins_of(lengths, d * group, group) - d * group)[:, None]
     block_in = jnp.concatenate([query_master, key_master, value_master], 1).astype(BF)
-    block_out = out_master.astype(BF)
-    in_stack = jnp.stack([block_in] + [by_plane(block_in, j) for j in (1, 2, 3)])
-    out_stack = jnp.stack([block_out] + [by_plane(block_out, j) for j in (1, 2, 3)])
-
-    def spread_blocks(stack):
-        return [pick(stack, d ^ c)] + [
-            by_col(pick(stack, d ^ c ^ m), m) for m in (2, 1, 3)
-        ]
-
-    weight_in = jnp.concatenate(spread_blocks(in_stack), 0)
-    weight_out = jnp.concatenate(spread_blocks(out_stack), 1)
-
-    x = tokens.astype(F32)
-    scale_one = lax.rsqrt(col_sum(jnp.sum(x * x, axis=1)) / D + EPSILON)
-    normed_one = plane_gather(rounded_norm(x, scale_one, attn_gain))
-    projected = flip(jnp.dot(normed_one, weight_in, preferred_element_type=F32).astype(BF))
-    q = projected[:, :width]
-    halo = move(
-        projected[group - REACH :, width:],
-        lambda e, s, b: (e + 1, s, b) if e + 1 < DP else None,
-    )
-    key_value = jnp.concatenate([halo, projected[:, width:]], 0)
-    k, v = key_value[:, :width], key_value[:, width:]
-    begin = (begins_of(lengths, d * group, group) - d * group)[:, None]
-    attended, lse = attend(begin, q, k, v)
-    own_attended = flip(attended)
-    midway = x + plane_scatter(own_attended, weight_out, 0)
-
     hidden_in = jnp.concatenate([gate_master, up_master], 1).astype(BF)
     hidden_out = down_master.astype(BF)
+    (
+        normed_one, weight_in, weight_out, q, key_value, own_attended, lse, midway, scale_two,
+        n2, weight_hidden, weight_down, grad_all,
+    ) = forward(
+        tokens, attn_gain[None, :], ffn_gain[None, :], begin, block_in, out_master.astype(BF),
+        hidden_in, hidden_out, cotangent,
+    )
+    scale_two = scale_two[:, 0]
+    scale_one = lax.rsqrt(col_sum(jnp.sum(x * x, axis=1)) / D + EPSILON)
+    k, v = key_value[:, :width], key_value[:, width:]
     order = (0, 2, 1, 3)
-    weight_hidden = jnp.concatenate([move(hidden_in, hidden_from(i)) for i in order], 0)
-    weight_down = jnp.concatenate([move(hidden_out, hidden_from(i)) for i in order], 1)
 
     def spread_tokens(block):
         kept = lax.dynamic_slice_in_dim(block, y * half_rows, half_rows, 0)
@@ -658,10 +1120,8 @@
 
     over = (((0,), (0,)), ((), ()))
     across = (((1,), (1,)), ((), ()))
-    grad_all = spread_tokens(cotangent)
     grad_hidden = lax.dot_general(grad_all, weight_down, across, preferred_element_type=F32)
-    scale_two = lax.rsqrt(col_sum(jnp.sum(midway * midway, axis=1)) / D + EPSILON)
-    normed_two = spread_tokens(rounded_norm(midway, scale_two, ffn_gain))
+    normed_two = spread_tokens(n2)
     gate_and_up = jnp.dot(normed_two, weight_hidden, preferred_element_type=F32)
     units = hidden_out.shape[0]
     gate, up = gate_and_up[:, :units], gate_and_up[:, units:]

time: 882 us -> 828 us (0.939)
  Pallas kernels: 18.9 us -> 300 us
  waiting for transfers between devices: 491 us -> 305 us
  starting transfers between devices: 200 us -> 68.7 us
  local copies, waits for them, and re-layouts: 29.2 us -> 19.6 us
    pallas_call x1, Pallas kernels: 7.54 us -> 289 us  [forward(): pl.pallas_call(forward_kernel, in_specs=[vmem] * 4 + [hbm] * 5, out_specs...]
    ppermute x88 -> x51, waiting for transfers between devices: 491 us -> 305 us  [move(): return lax.ppermute(array, AXES, pairs)]
    ppermute x88 -> x51, starting transfers between devices: 200 us -> 68.7 us  [move(): return lax.ppermute(array, AXES, pairs)]
  transfers between devices with their start and end apart: 88 -> 51, of which waited for: 41 -> 27; matrix products, arithmetic and copies ran while one was open for 13% -> 9% of each run, Pallas kernels for 2% -> 1%
where the time goes in v2:
time: 828 us; the launch traced here: 822 us
  waiting for transfers between devices  305 us (37%)
  Pallas kernels  300 us (36%)
  matrix products  94.6 us (11%)
  starting transfers between devices  68.7 us (8%)
  other arithmetic  31.7 us (4%)
  local copies, waits for them, and re-layouts  19.6 us (2%)
    ppermute x51, waiting for transfers between devices, move(): return lax.ppermute(array, AXES, pairs)  305 us
    pallas_call x1, Pallas kernels, forward(): pl.pallas_call(forward_kernel, in_specs=[vmem] * 4 + [hbm] * 5, out_specs...  289 us
    ppermute x51, starting transfers between devices, move(): return lax.ppermute(array, AXES, pairs)  68.7 us
    dot_general x1, matrix products, on_small_mesh(): gate_and_up = jnp.dot(normed_two, weight_hidden, preferred_element_type=F32)  24.9 us
    dot_general x1, matrix products, on_small_mesh(): lax.dot_general(normed_two, grad_both, over, preferred_element_type=F32)  20.9 us
  transfers between devices with their start and end apart: 51, of which 27 were waited for; matrix products, arithmetic and copies ran while one was open for 9% of the time, Pallas kernels for 1%

profile of v2, /device:TPU:0, one launch (start us, length us, event | category | flops | bytes accessed | tf_op | source)
XLA Modules:
  0.0 821.7 jit_solution(13076695098816800908)
XLA Ops:
  9.9 2.7 convert_element_type.142.own_down
  15.1 288.7 %shard_map.195 = (bf16[1024,2048]{1,0:T(8,128)(2,1)}, bf16[2048,768]{1,0:T(8,128)(2,1)}, bf16[256,2048]{1,0:T(8,128)(2,1)}, bf16[1024,256]{1,0:T(8,128)(2,1)}, b...) custom-call(bf16[512,512]{1,0:T(8,128)(2,1)} %x_ref.1, ...), custom_call_target="tpu_custom_call" | custom-call | flops 3221225472 | bytes 67108864 | tf_op jit(solution)/shard_map/pallas_call | solution.py:1013
  306.3 7.2 collective-permute-done
  313.6 8.6 %collective-permute-start.3 = (bf16[256,1024]{1,0:T(8,128)(2,1)S(1)}, bf16[256,1024]{1,0:T(8,128)(2,1)S(1)}, u32[]{:S(2)}, u32[]{:S(2)}) collective-permute-start(bf16[256,1024]{1,0:T(8,128)(2,1)S(1)} %pad_maximum_fusion.11), channel_id=1, source_target_pairs={{0,24},{1,25},{2,26},{3,27},{4,28},{5,29},{6,30},{7,31},{8,16},{9,... | collective-permute-start | bytes 1572872 | tf_op jit(solution)/shard_map/ppermute | solution.py:386
  322.2 8.4 %collective-permute-start.2 = (bf16[256,1024]{1,0:T(8,128)(2,1)S(1)}, bf16[256,1024]{1,0:T(8,128)(2,1)S(1)}, u32[]{:S(2)}, u32[]{:S(2)}) collective-permute-start(bf16[256,1024]{1,0:T(8,128)(2,1)S(1)} %pad_maximum_fusion.11), channel_id=1, source_target_pairs={{0,16},{1,17},{2,18},{3,19},{4,20},{5,21},{6,22},{7,23},{8,24},{9,... | collective-permute-start | bytes 1572872 | tf_op jit(solution)/shard_map/ppermute | solution.py:386
  330.6 4.5 collective-permute-done.3
  335.0 32.6 %collective-permute-done.2 = bf16[256,1024]{1,0:T(8,128)(2,1)S(1)} collective-permute-done((bf16[256,1024]{1,0:T(8,128)(2,1)S(1)}, bf16[256,1024]{1,0:T(8,128)(2,1)S(1)}, u32[]{:S(2)}, u32[]{:S(2)}) %collective-permute-start.2) | collective-permute-done | bytes 524320 | tf_op jit(solution)/shard_map/ppermute | solution.py:386
  367.6 2.1 pad_maximum_fusion.5
  369.8 4.1 collective-permute-done.4
  373.9 24.9 %fusion.39 = f32[1024,2048]{0,1:T(8,128)} fusion(bf16[2048,2048]{1,0:T(8,128)(2,1)} %get-tuple-element.30, bf16[1024,1024]{1,0:T(8,128)(2,1)S(1)} %collective-permute-done.4, bf16[256,1024]{1,0:T(8,128)(2,1)S(1)} %collective-permute-done.3, bf16[256,1024]{1,0:T(8,128)(2,1)S(1)} %collective-permute-done.2, bf16[256,1024]{1,0:T(8,128)(2,1)S(1)} %collective-permute-done.1, ...), kind=kOutput, calls=%fused_computation.95 | convolution fusion | flops 8615100416 | bytes 20971520 | tf_op jit(solution)/shard_map/dot_general | solution.py:1125
  398.9 11.5 %multiply_convert_fusion.2 = (bf16[1024,1024]{0,1:T(8,128)(2,1)S(1)}, bf16[1024,1024]{0,1:T(8,128)(2,1)S(1)}) fusion(f32[1024,2048]{0,1:T(8,128)} %fusion.39, bf16[1024,2048]{1,0:T(8,128)(2,1)} %get-tuple-element.27, bf16[1024,2048]{1,0:T(8,128)(2,1)} %get-tuple-element.28), kind=kOutput, calls=%fused_computation.13 | convolution fusion | flops 4308598784 | bytes 20971520 | tf_op jit(solution)/shard_map/dot_general | solution.py:1123
  410.4 8.9 %fusion.7 = bf16[1024,1024]{1,0:T(8,128)(2,1)S(1)} fusion(bf16[2048,2048]{1,0:T(8,128)(2,1)} %get-tuple-element.30, bf16[1024,1024]{0,1:T(8,128)(2,1)S(1)} %get-tuple-element.50, bf16[1024,1024]{0,1:T(8,128)(2,1)S(1)} %get-tuple-element.49), kind=kOutput, calls=%fused_computation.24 | convolution fusion | flops 4304404480 | bytes 10485760 | tf_op jit(solution)/shard_map/dot_general | solution.py:1135
  419.5 4.0 collective-permute-done.5
  423.6 6.7 fusion.52
  431.1 3.0 collective-permute-start.8
  435.4 9.1 %collective-permute-done.6 = bf16[256,1024]{1,0:T(8,128)(2,1)S(1)} collective-permute-done((bf16[256,1024]{1,0:T(8,128)(2,1)S(1)}, bf16[256,1024]{1,0:T(8,128)(2,1)S(1)}, u32[]{:S(2)}, u32[]{:S(2)}) %collective-permute-start.6) | collective-permute-done | bytes 524320 | tf_op jit(solution)/shard_map/ppermute | solution.py:386
  444.9 13.2 %collective-permute-done.8 = bf16[256,1024]{1,0:T(8,128)(2,1)S(1)} collective-permute-done((bf16[256,1024]{1,0:T(8,128)(2,1)S(1)}, bf16[256,1024]{1,0:T(8,128)(2,1)S(1)}, u32[]{:S(2)}, u32[]{:S(2)}) %collective-permute-start.8) | collective-permute-done | bytes 524320 | tf_op jit(solution)/shard_map/ppermute | solution.py:386
  458.1 22.2 %collective-permute-done.7 = bf16[256,1024]{1,0:T(8,128)(2,1)S(1)} collective-permute-done((bf16[256,1024]{1,0:T(8,128)(2,1)S(1)}, bf16[256,1024]{1,0:T(8,128)(2,1)S(1)}, u32[]{:S(2)}, u32[]{:S(2)}) %collective-permute-start.7) | collective-permute-done | bytes 524320 | tf_op jit(solution)/shard_map/ppermute | solution.py:386
  484.3 4.9 collective-permute-done.9
  499.7 8.3 %convolution_convert_fusion.1 = bf16[1024,2048]{1,0:T(8,128)(2,1)S(1)} fusion(bf16[1024,2048]{1,0:T(8,128)(2,1)S(1)} %copy-done.32, f32[1024,2048]{0,1:T(8,128)} %fusion.39), kind=kOutput, calls=%fused_computation.15 | convolution fusion | flops 4303355904 | bytes 16777216 | tf_op jit(solution)/shard_map/dot_general | solution.py:1162
  508.0 2.1 fusion.43
  510.1 9.6 %collective-permute-start.44 = (bf16[1024,512]{1,0:T(8,128)(2,1)}, bf16[1024,512]{1,0:T(8,128)(2,1)}, u32[]{:S(2)}, u32[]{:S(2)}) collective-permute-start(bf16[1024,512]{1,0:T(8,128)(2,1)} %get-tuple-element.55), channel_id=1, source_target_pairs={{0,0},{1,5},{2,2},{3,7},{4,4},{5,1},{6,6},{7,3},{8,8},{9,13},{10,1... | collective-permute-start | bytes 3145736 | tf_op jit(solution)/shard_map/ppermute | solution.py:386
  521.2 2.2 collective-permute-done.17
  525.5 20.9 %convolution_convert_fusion = bf16[2048,2048]{1,0:T(8,128)(2,1)} fusion(bf16[1024,1024]{0,1:T(8,128)(2,1)} %copy-done.36, bf16[1024,1024]{0,1:T(8,128)(2,1)} %copy-done.35, bf16[1024,1024]{1,0:T(8,128)(2,1)} %copy-done.28, bf16[256,1024]{1,0:T(8,128)(2,1)S(1)} %copy-done.17, bf16[256,1024]{1,0:T(8,128)(2,1)} %copy-done.18, bf16[256,1024]{1,0:T(8,128)(2,1)} %copy-done.19, ...), kind=kOutput, calls=%fused_computation | convolution fusion | flops 8627683328 | bytes 16777216 | tf_op jit(solution)/shard_map/dot_general | solution.py:1163
  546.4 5.4 fusion.42
  551.9 2.5 collective-permute-start.40
  555.8 12.3 %collective-permute-done.45 = bf16[1024,512]{1,0:T(8,128)(2,1)} collective-permute-done((bf16[1024,512]{1,0:T(8,128)(2,1)}, bf16[1024,512]{1,0:T(8,128)(2,1)}, u32[]{:S(2)}, u32[]{:S(2)}) %collective-permute-start.45) | collective-permute-done | bytes 1048608 | tf_op jit(solution)/shard_map/ppermute | solution.py:386
  568.5 4.0 convert_add_fusion.3
  572.7 3.0 convolution_convert_fusion.5
  575.9 11.6 %shard_map.196 = (bf16[1024,256]{1,0:T(8,128)(2,1)S(1)}, f32[1792,256]{1,0:T(8,128)S(1)}, f32[1792,256]{1,0:T(8,128)S(1)}) custom-call(s32[1024,1]{1,0:T(8,128)S(1)} %copy-done, bf16[1024,256]{1,0:T(8,128)(2,1)S(1)} %copy-done.2, bf16[1792,256]{1,0:T(8,128)(2,1)S(1)} %get-tuple-element.75.k_ref, bf16[1792,256]{1,0:T(8,128)(2,1)S(1)} %get-tuple-element.74.v_ref, ...), custom_call_target="tpu_custom_call" | custom-call | flops 2684354560 | bytes 6291456 | tf_op jit(solution)/shard_map/pallas_call | solution.py:558
  589.7 2.9 convolution_convert_fusion.3
  592.7 15.7 %collective-permute-done.20 = bf16[768,512]{1,0:T(8,128)(2,1)S(1)} collective-permute-done((bf16[768,512]{1,0:T(8,128)(2,1)S(1)}, bf16[768,512]{1,0:T(8,128)(2,1)S(1)}, u32[]{:S(2)}, u32[]{:S(2)}) %collective-permute-start.20) | collective-permute-done | bytes 786464 | tf_op jit(solution)/shard_map/ppermute | solution.py:386
  612.8 3.8 convolution_convert_fusion.2
  619.1 14.6 %collective-permute-done.42 = bf16[512,2048]{1,0:T(8,128)(2,1)S(1)} collective-permute-done((bf16[512,2048]{1,0:T(8,128)(2,1)S(1)}, bf16[512,2048]{1,0:T(8,128)(2,1)S(1)}, u32[]{:S(2)}, u32[]{:S(2)}) %collective-permute-start.42) | collective-permute-done | bytes 2097184 | tf_op jit(solution)/shard_map/ppermute | solution.py:386
  633.7 37.0 %collective-permute-done.41 = bf16[512,2048]{1,0:T(8,128)(2,1)S(1)} collective-permute-done((bf16[512,2048]{1,0:T(8,128)(2,1)S(1)}, bf16[512,2048]{1,0:T(8,128)(2,1)S(1)}, u32[]{:S(2)}, u32[]{:S(2)}) %collective-permute-start.41) | collective-permute-done | bytes 2097184 | tf_op jit(solution)/shard_map/ppermute | solution.py:386
  670.7 2.5 collective-permute-done.36
  673.2 3.0 collective-permute-start.28
  677.9 4.1 collective-permute-done.35
  682.0 2.3 fusion.44
  684.6 7.8 collective-permute-done.30
  692.3 2.3 collective-permute-start.39
  694.7 8.2 collective-permute-done.29
  703.6 2.4 collective-permute-start.33
  711.3 73.4 %collective-permute-done.38 = bf16[256,512]{1,0:T(8,128)(2,1)S(1)} collective-permute-done((bf16[256,512]{1,0:T(8,128)(2,1)S(1)}, bf16[256,512]{1,0:T(8,128)(2,1)S(1)}, u32[]{:S(2)}, u32[]{:S(2)}) %collective-permute-start.38) | collective-permute-done | bytes 262176 | tf_op jit(solution)/shard_map/ppermute | solution.py:386
  788.6 8.5 %collective-permute-done.24 = bf16[512,512]{1,0:T(8,128)(2,1)S(1)} collective-permute-done((bf16[512,512]{1,0:T(8,128)(2,1)S(1)}, bf16[512,512]{1,0:T(8,128)(2,1)S(1)}, u32[]{:S(2)}, u32[]{:S(2)}) %collective-permute-start.24) | collective-permute-done | bytes 524320 | tf_op jit(solution)/shard_map/ppermute | solution.py:386
  797.1 11.1 %collective-permute-done.23 = bf16[512,512]{1,0:T(8,128)(2,1)S(1)} collective-permute-done((bf16[512,512]{1,0:T(8,128)(2,1)S(1)}, bf16[512,512]{1,0:T(8,128)(2,1)S(1)}, u32[]{:S(2)}, u32[]{:S(2)}) %collective-permute-start.23) | collective-permute-done | bytes 524320 | tf_op jit(solution)/shard_map/ppermute | solution.py:386
  813.8 2.2 collective-permute-done.25
  817.2 2.0 collective-permute-start.50
  (205 shorter events, 66.9 us)
Async XLA Ops:
  304.8 8.7 %collective-permute-start = (bf16[256,512]{1,0:T(8,128)(2,1)S(1)}, bf16[256,512]{1,0:T(8,128)(2,1)S(1)}, u32[]{:S(2)}, u32[]{:S(2)}) collective-permute-start(bf16[256,512]{1,0:T(8,128)(2,1)S(1)} %get-tuple-element.91), channel_id=1, source_target_pairs={{0,2},{1,3},{2,0},{3,1},{4,6},{5,7},{6,4},{7,5},{8,10},{9,11},{10,... | collective-permute-start | bytes 786440 | tf_op jit(solution)/shard_map/ppermute | solution.py:386
  313.6 21.4 %collective-permute-start.3 = (bf16[256,1024]{1,0:T(8,128)(2,1)S(1)}, bf16[256,1024]{1,0:T(8,128)(2,1)S(1)}, u32[]{:S(2)}, u32[]{:S(2)}) collective-permute-start(bf16[256,1024]{1,0:T(8,128)(2,1)S(1)} %pad_maximum_fusion.11), channel_id=1, source_target_pairs={{0,24},{1,25},{2,26},{3,27},{4,28},{5,29},{6,30},{7,31},{8,16},{9,... | collective-permute-start | bytes 1572872 | tf_op jit(solution)/shard_map/ppermute | solution.py:386
  322.2 45.4 %collective-permute-start.2 = (bf16[256,1024]{1,0:T(8,128)(2,1)S(1)}, bf16[256,1024]{1,0:T(8,128)(2,1)S(1)}, u32[]{:S(2)}, u32[]{:S(2)}) collective-permute-start(bf16[256,1024]{1,0:T(8,128)(2,1)S(1)} %pad_maximum_fusion.11), channel_id=1, source_target_pairs={{0,16},{1,17},{2,18},{3,19},{4,20},{5,21},{6,22},{7,23},{8,24},{9,... | collective-permute-start | bytes 1572872 | tf_op jit(solution)/shard_map/ppermute | solution.py:386
  330.6 37.0 %collective-permute-start.1 = (bf16[256,1024]{1,0:T(8,128)(2,1)S(1)}, bf16[256,1024]{1,0:T(8,128)(2,1)S(1)}, u32[]{:S(2)}, u32[]{:S(2)}) collective-permute-start(bf16[256,1024]{1,0:T(8,128)(2,1)S(1)} %pad_maximum_fusion.11), channel_id=1, source_target_pairs={{0,8},{1,9},{2,10},{3,11},{4,12},{5,13},{6,14},{7,15},{8,0},{9,1},... | collective-permute-start | bytes 1572872 | tf_op jit(solution)/shard_map/ppermute | solution.py:386
  369.7 4.2 collective-permute-start.4
  419.3 4.2 collective-permute-start.5
  430.4 14.0 %collective-permute-start.6 = (bf16[256,1024]{1,0:T(8,128)(2,1)S(1)}, bf16[256,1024]{1,0:T(8,128)(2,1)S(1)}, u32[]{:S(2)}, u32[]{:S(2)}) collective-permute-start(bf16[256,1024]{1,0:T(8,128)(2,1)S(1)} %get-tuple-element.71), channel_id=1, source_target_pairs={{0,8},{1,9},{2,10},{3,11},{4,12},{5,13},{6,14},{7,15},{8,0},{9,1},... | collective-permute-start | bytes 1572872 | tf_op jit(solution)/shard_map/ppermute | solution.py:386
  431.1 26.9 %collective-permute-start.8 = (bf16[256,1024]{1,0:T(8,128)(2,1)S(1)}, bf16[256,1024]{1,0:T(8,128)(2,1)S(1)}, u32[]{:S(2)}, u32[]{:S(2)}) collective-permute-start(bf16[256,1024]{1,0:T(8,128)(2,1)S(1)} %get-tuple-element.72), channel_id=1, source_target_pairs={{0,24},{1,25},{2,26},{3,27},{4,28},{5,29},{6,30},{7,31},{8,16},{9,... | collective-permute-start | bytes 1572872 | tf_op jit(solution)/shard_map/ppermute | solution.py:386
  434.1 46.1 %collective-permute-start.7 = (bf16[256,1024]{1,0:T(8,128)(2,1)S(1)}, bf16[256,1024]{1,0:T(8,128)(2,1)S(1)}, u32[]{:S(2)}, u32[]{:S(2)}) collective-permute-start(bf16[256,1024]{1,0:T(8,128)(2,1)S(1)} %get-tuple-element.73), channel_id=1, source_target_pairs={{0,16},{1,17},{2,18},{3,19},{4,20},{5,21},{6,22},{7,23},{8,24},{9,... | collective-permute-start | bytes 1572872 | tf_op jit(solution)/shard_map/ppermute | solution.py:386
  434.8 56.5 %collective-permute-start.15 = (f32[512]{0:T(512)S(1)}, f32[512]{0:T(512)S(1)}, u32[]{:S(2)}, u32[]{:S(2)}) collective-permute-start(f32[512]{0:T(512)S(1)} %fusion.18), channel_id=1, source_target_pairs={{0,3},{1,2},{2,1},{3,0},{4,7},{5,6},{6,5},{7,4},{8,11},{9,10},{10,... | collective-permute-start | bytes 6152 | tf_op jit(solution)/shard_map/ppermute | solution.py:386
  434.9 58.1 %collective-permute-start.14 = (f32[512]{0:T(512)S(1)}, f32[512]{0:T(512)S(1)}, u32[]{:S(2)}, u32[]{:S(2)}) collective-permute-start(f32[512]{0:T(512)S(1)} %fusion.18), channel_id=1, source_target_pairs={{0,1},{1,0},{2,3},{3,2},{4,5},{5,4},{6,7},{7,6},{8,9},{9,8},{10,11... | collective-permute-start | bytes 6152 | tf_op jit(solution)/shard_map/ppermute | solution.py:386
  444.5 48.5 %collective-permute-start.13 = (f32[512]{0:T(512)S(1)}, f32[512]{0:T(512)S(1)}, u32[]{:S(2)}, u32[]{:S(2)}) collective-permute-start(f32[512]{0:T(512)S(1)} %fusion.18), channel_id=1, source_target_pairs={{0,2},{1,3},{2,0},{3,1},{4,6},{5,7},{6,4},{7,5},{8,10},{9,11},{10,... | collective-permute-start | bytes 6152 | tf_op jit(solution)/shard_map/ppermute | solution.py:386
  481.4 7.8 collective-permute-start.9
  490.7 3.1 collective-permute-start.12
  491.3 3.6 collective-permute-start.10
  496.2 23.5 %collective-permute-start.18 = (bf16[512,512]{1,0:T(8,128)(2,1)S(1)}, bf16[512,512]{1,0:T(8,128)(2,1)S(1)}, u32[]{:S(2)}, u32[]{:S(2)}) collective-permute-start(bf16[512,512]{1,0:T(8,128)(2,1)S(1)} %get-tuple-element.47), channel_id=1, source_target_pairs={{0,6},{1,7},{2,4},{3,5},{4,2},{5,3},{6,0},{7,1},{8,14},{9,15},{10,... | collective-permute-start | bytes 1572872 | tf_op jit(solution)/shard_map/ppermute | solution.py:386
  497.5 25.9 %collective-permute-start.17 = (bf16[512,512]{1,0:T(8,128)(2,1)S(1)}, bf16[512,512]{1,0:T(8,128)(2,1)S(1)}, u32[]{:S(2)}, u32[]{:S(2)}) collective-permute-start(bf16[512,512]{1,0:T(8,128)(2,1)S(1)} %get-tuple-element.47), channel_id=1, source_target_pairs={{0,4},{1,5},{2,6},{3,7},{4,0},{5,1},{6,2},{7,3},{8,12},{9,13},{10,... | collective-permute-start | bytes 1572872 | tf_op jit(solution)/shard_map/ppermute | solution.py:386
  499.3 24.5 %collective-permute-start.16 = (bf16[512,512]{1,0:T(8,128)(2,1)S(1)}, bf16[512,512]{1,0:T(8,128)(2,1)S(1)}, u32[]{:S(2)}, u32[]{:S(2)}) collective-permute-start(bf16[512,512]{1,0:T(8,128)(2,1)S(1)} %get-tuple-element.47), channel_id=1, source_target_pairs={{0,2},{1,3},{2,0},{3,1},{4,6},{5,7},{6,4},{7,5},{8,10},{9,11},{10,... | collective-permute-start | bytes 1572872 | tf_op jit(solution)/shard_map/ppermute | solution.py:386
  510.1 41.7 %collective-permute-start.44 = (bf16[1024,512]{1,0:T(8,128)(2,1)}, bf16[1024,512]{1,0:T(8,128)(2,1)}, u32[]{:S(2)}, u32[]{:S(2)}) collective-permute-start(bf16[1024,512]{1,0:T(8,128)(2,1)} %get-tuple-element.55), channel_id=1, source_target_pairs={{0,0},{1,5},{2,2},{3,7},{4,4},{5,1},{6,6},{7,3},{8,8},{9,13},{10,1... | collective-permute-start | bytes 3145736 | tf_op jit(solution)/shard_map/ppermute | solution.py:386
  519.7 34.6 %collective-permute-start.47 = (bf16[1024,512]{1,0:T(8,128)(2,1)}, bf16[1024,512]{1,0:T(8,128)(2,1)}, u32[]{:S(2)}, u32[]{:S(2)}) collective-permute-start(bf16[1024,512]{1,0:T(8,128)(2,1)} %get-tuple-element.56), channel_id=1, source_target_pairs={{0,3},{1,6},{2,1},{3,4},{4,7},{5,2},{6,5},{7,0},{8,11},{9,14},{10,... | collective-permute-start | bytes 3145736 | tf_op jit(solution)/shard_map/ppermute | solution.py:386
  519.7 36.1 %collective-permute-start.46 = (bf16[1024,512]{1,0:T(8,128)(2,1)}, bf16[1024,512]{1,0:T(8,128)(2,1)}, u32[]{:S(2)}, u32[]{:S(2)}) collective-permute-start(bf16[1024,512]{1,0:T(8,128)(2,1)} %get-tuple-element.57), channel_id=1, source_target_pairs={{0,1},{1,4},{2,3},{3,6},{4,5},{5,0},{6,7},{7,2},{8,9},{9,12},{10,1... | collective-permute-start | bytes 3145736 | tf_op jit(solution)/shard_map/ppermute | solution.py:386
  523.4 44.8 %collective-permute-start.45 = (bf16[1024,512]{1,0:T(8,128)(2,1)}, bf16[1024,512]{1,0:T(8,128)(2,1)}, u32[]{:S(2)}, u32[]{:S(2)}) collective-permute-start(bf16[1024,512]{1,0:T(8,128)(2,1)} %get-tuple-element.58), channel_id=1, source_target_pairs={{0,2},{1,7},{2,0},{3,5},{4,6},{5,3},{6,4},{7,1},{8,10},{9,15},{10,... | collective-permute-start | bytes 3145736 | tf_op jit(solution)/shard_map/ppermute | solution.py:386
  525.4 47.2 %collective-permute-start.19 = (bf16[1024,1024]{1,0:T(8,128)(2,1)}, bf16[1024,1024]{1,0:T(8,128)(2,1)}, u32[]{:S(2)}, u32[]{:S(2)}) collective-permute-start(bf16[1024,1024]{1,0:T(8,128)(2,1)} %maximum_maximum_fusion), channel_id=1, source_target_pairs={{0,1},{1,0},{2,3},{3,2},{4,5},{5,4},{6,7},{7,6},{8,9},{9,8},{10,11... | collective-permute-start | bytes 6291464 | tf_op jit(solution)/shard_map/ppermute | solution.py:386
  551.9 64.8 %collective-permute-start.40 = (bf16[512,2048]{1,0:T(8,128)(2,1)}, bf16[512,2048]{1,0:T(8,128)(2,1)S(1)}, u32[]{:S(2)}, u32[]{:S(2)}) collective-permute-start(bf16[512,2048]{1,0:T(8,128)(2,1)} %get-tuple-element.51), channel_id=1, source_target_pairs={{0,0},{1,5},{2,2},{3,7},{4,4},{5,1},{6,6},{7,3},{8,8},{9,13},{10,1... | collective-permute-start | bytes 6291464 | tf_op jit(solution)/shard_map/ppermute | solution.py:386
  554.3 63.9 %collective-permute-start.43 = (bf16[512,2048]{1,0:T(8,128)(2,1)}, bf16[512,2048]{1,0:T(8,128)(2,1)S(1)}, u32[]{:S(2)}, u32[]{:S(2)}) collective-permute-start(bf16[512,2048]{1,0:T(8,128)(2,1)} %get-tuple-element.52), channel_id=1, source_target_pairs={{0,3},{1,6},{2,1},{3,4},{4,7},{5,2},{6,5},{7,0},{8,11},{9,14},{10,... | collective-permute-start | bytes 6291464 | tf_op jit(solution)/shard_map/ppermute | solution.py:386
  555.8 77.9 %collective-permute-start.42 = (bf16[512,2048]{1,0:T(8,128)(2,1)S(1)}, bf16[512,2048]{1,0:T(8,128)(2,1)S(1)}, u32[]{:S(2)}, u32[]{:S(2)}) collective-permute-start(bf16[512,2048]{1,0:T(8,128)(2,1)S(1)} %get-tuple-element.53), channel_id=1, source_target_pairs={{0,1},{1,4},{2,3},{3,6},{4,5},{5,0},{6,7},{7,2},{8,9},{9,12},{10,1... | collective-permute-start | bytes 6291464 | tf_op jit(solution)/shard_map/ppermute | solution.py:386
  568.1 102.6 %collective-permute-start.41 = (bf16[512,2048]{1,0:T(8,128)(2,1)S(1)}, bf16[512,2048]{1,0:T(8,128)(2,1)S(1)}, u32[]{:S(2)}, u32[]{:S(2)}) collective-permute-start(bf16[512,2048]{1,0:T(8,128)(2,1)S(1)} %get-tuple-element.54), channel_id=1, source_target_pairs={{0,2},{1,7},{2,0},{3,5},{4,6},{5,3},{6,4},{7,1},{8,10},{9,15},{10,... | collective-permute-start | bytes 6291464 | tf_op jit(solution)/shard_map/ppermute | solution.py:386
  588.4 20.0 %collective-permute-start.20 = (bf16[768,512]{1,0:T(8,128)(2,1)S(1)}, bf16[768,512]{1,0:T(8,128)(2,1)S(1)}, u32[]{:S(2)}, u32[]{:S(2)}) collective-permute-start(bf16[768,512]{1,0:T(8,128)(2,1)S(1)} %slice.211), channel_id=1, source_target_pairs={{8,0},{9,1},{10,2},{11,3},{12,4},{13,5},{14,6},{15,7},{16,8},{17,9... | collective-permute-start | bytes 2359304 | tf_op jit(solution)/shard_map/ppermute | solution.py:386
  608.3 64.9 %collective-permute-start.36 = (bf16[256,512]{1,0:T(8,128)(2,1)S(1)}, bf16[256,512]{1,0:T(8,128)(2,1)S(1)}, u32[]{:S(2)}, u32[]{:S(2)}) collective-permute-start(bf16[256,512]{1,0:T(8,128)(2,1)S(1)} %get-tuple-element.85), channel_id=1, source_target_pairs={{0,3},{1,2},{2,1},{3,0},{4,7},{5,6},{6,5},{7,4},{8,11},{9,10},{10,... | collective-permute-start | bytes 786440 | tf_op jit(solution)/shard_map/ppermute | solution.py:386
  616.6 89.3 %collective-permute-start.21 = (bf16[1024,1024]{1,0:T(8,128)(2,1)S(1)}, bf16[1024,1024]{1,0:T(8,128)(2,1)S(1)}, u32[]{:S(2)}, u32[]{:S(2)}) collective-permute-start(bf16[1024,1024]{1,0:T(8,128)(2,1)S(1)} %convolution_convert_fusion.4), channel_id=1, source_target_pairs={{0,1},{1,0},{2,3},{3,2},{4,5},{5,4},{6,7},{7,6},{8,9},{9,8},{10,11... | collective-permute-start | bytes 6291464 | tf_op jit(solution)/shard_map/ppermute | solution.py:386
  618.2 63.8 %collective-permute-start.35 = (bf16[256,512]{1,0:T(8,128)(2,1)S(1)}, bf16[256,512]{1,0:T(8,128)(2,1)S(1)}, u32[]{:S(2)}, u32[]{:S(2)}) collective-permute-start(bf16[256,512]{1,0:T(8,128)(2,1)S(1)} %get-tuple-element.86), channel_id=1, source_target_pairs={{0,2},{1,3},{2,0},{3,1},{4,6},{5,7},{6,4},{7,5},{8,10},{9,11},{10,... | collective-permute-start | bytes 786440 | tf_op jit(solution)/shard_map/ppermute | solution.py:386
  633.7 58.6 %collective-permute-start.30 = (bf16[512,768]{1,0:T(8,128)(2,1)S(1)}, bf16[512,768]{1,0:T(8,128)(2,1)S(1)}, u32[]{:S(2)}, u32[]{:S(2)}) collective-permute-start(bf16[512,768]{1,0:T(8,128)(2,1)S(1)} %get-tuple-element.65), channel_id=1, source_target_pairs={{0,3},{1,2},{2,1},{3,0},{4,7},{5,6},{6,5},{7,4},{8,11},{9,10},{10,... | collective-permute-start | bytes 2359304 | tf_op jit(solution)/shard_map/ppermute | solution.py:386
  670.7 32.1 %collective-permute-start.29 = (bf16[512,768]{1,0:T(8,128)(2,1)S(1)}, bf16[512,768]{1,0:T(8,128)(2,1)S(1)}, u32[]{:S(2)}, u32[]{:S(2)}) collective-permute-start(bf16[512,768]{1,0:T(8,128)(2,1)S(1)} %get-tuple-element.66), channel_id=1, source_target_pairs={{0,2},{1,3},{2,0},{3,1},{4,6},{5,7},{6,4},{7,5},{8,10},{9,11},{10,... | collective-permute-start | bytes 2359304 | tf_op jit(solution)/shard_map/ppermute | solution.py:386
  673.2 29.7 %collective-permute-start.28 = (bf16[512,768]{1,0:T(8,128)(2,1)S(1)}, bf16[512,768]{1,0:T(8,128)(2,1)S(1)}, u32[]{:S(2)}, u32[]{:S(2)}) collective-permute-start(bf16[512,768]{1,0:T(8,128)(2,1)S(1)} %get-tuple-element.67), channel_id=1, source_target_pairs={{0,1},{1,0},{2,3},{3,2},{4,5},{5,4},{6,7},{7,6},{8,9},{9,8},{10,11... | collective-permute-start | bytes 2359304 | tf_op jit(solution)/shard_map/ppermute | solution.py:386
  684.5 24.4 %collective-permute-start.37 = (bf16[256,512]{1,0:T(8,128)(2,1)S(1)}, bf16[256,512]{1,0:T(8,128)(2,1)S(1)}, u32[]{:S(2)}, u32[]{:S(2)}) collective-permute-start(bf16[256,512]{1,0:T(8,128)(2,1)S(1)} %get-tuple-element.81), channel_id=1, source_target_pairs={{0,8},{1,9},{2,10},{3,11},{4,12},{5,13},{6,14},{7,15},{8,0},{9,1},... | collective-permute-start | bytes 786440 | tf_op jit(solution)/shard_map/ppermute | solution.py:386
  692.3 18.6 %collective-permute-start.39 = (bf16[256,512]{1,0:T(8,128)(2,1)S(1)}, bf16[256,512]{1,0:T(8,128)(2,1)S(1)}, u32[]{:S(2)}, u32[]{:S(2)}) collective-permute-start(bf16[256,512]{1,0:T(8,128)(2,1)S(1)} %get-tuple-element.82), channel_id=1, source_target_pairs={{0,24},{1,25},{2,26},{3,27},{4,28},{5,29},{6,30},{7,31},{8,16},{9,... | collective-permute-start | bytes 786440 | tf_op jit(solution)/shard_map/ppermute | solution.py:386
  703.5 82.6 %collective-permute-start.31 = (bf16[512,768]{1,0:T(8,128)(2,1)S(1)}, bf16[512,768]{1,0:T(8,128)(2,1)S(1)}, u32[]{:S(2)}, u32[]{:S(2)}) collective-permute-start(bf16[512,768]{1,0:T(8,128)(2,1)S(1)} %get-tuple-element.61), channel_id=1, source_target_pairs={{0,8},{1,9},{2,10},{3,11},{4,12},{5,13},{6,14},{7,15},{8,0},{9,1},... | collective-permute-start | bytes 2359304 | tf_op jit(solution)/shard_map/ppermute | solution.py:386
  703.6 84.7 %collective-permute-start.33 = (bf16[512,768]{1,0:T(8,128)(2,1)S(1)}, bf16[512,768]{1,0:T(8,128)(2,1)S(1)}, u32[]{:S(2)}, u32[]{:S(2)}) collective-permute-start(bf16[512,768]{1,0:T(8,128)(2,1)S(1)} %get-tuple-element.62), channel_id=1, source_target_pairs={{0,24},{1,25},{2,26},{3,27},{4,28},{5,29},{6,30},{7,31},{8,16},{9,... | collective-permute-start | bytes 2359304 | tf_op jit(solution)/shard_map/ppermute | solution.py:386
  705.9 82.3 %collective-permute-start.32 = (bf16[512,768]{1,0:T(8,128)(2,1)S(1)}, bf16[512,768]{1,0:T(8,128)(2,1)S(1)}, u32[]{:S(2)}, u32[]{:S(2)}) collective-permute-start(bf16[512,768]{1,0:T(8,128)(2,1)S(1)} %get-tuple-element.63), channel_id=1, source_target_pairs={{0,16},{1,17},{2,18},{3,19},{4,20},{5,21},{6,22},{7,23},{8,24},{9,... | collective-permute-start | bytes 2359304 | tf_op jit(solution)/shard_map/ppermute | solution.py:386
  708.9 75.8 %collective-permute-start.38 = (bf16[256,512]{1,0:T(8,128)(2,1)S(1)}, bf16[256,512]{1,0:T(8,128)(2,1)S(1)}, u32[]{:S(2)}, u32[]{:S(2)}) collective-permute-start(bf16[256,512]{1,0:T(8,128)(2,1)S(1)} %get-tuple-element.83), channel_id=1, source_target_pairs={{0,16},{1,17},{2,18},{3,19},{4,20},{5,21},{6,22},{7,23},{8,24},{9,... | collective-permute-start | bytes 786440 | tf_op jit(solution)/shard_map/ppermute | solution.py:386
  711.0 77.6 %collective-permute-start.22 = (bf16[512,512]{1,0:T(8,128)(2,1)S(1)}, bf16[512,512]{1,0:T(8,128)(2,1)S(1)}, u32[]{:S(2)}, u32[]{:S(2)}) collective-permute-start(bf16[512,512]{1,0:T(8,128)(2,1)S(1)} %get-tuple-element.68), channel_id=1, source_target_pairs={{0,4},{1,5},{2,6},{3,7},{4,0},{5,1},{6,2},{7,3},{8,12},{9,13},{10,... | collective-permute-start | bytes 1572872 | tf_op jit(solution)/shard_map/ppermute | solution.py:386
  784.7 12.4 %collective-permute-start.24 = (bf16[512,512]{1,0:T(8,128)(2,1)S(1)}, bf16[512,512]{1,0:T(8,128)(2,1)S(1)}, u32[]{:S(2)}, u32[]{:S(2)}) collective-permute-start(bf16[512,512]{1,0:T(8,128)(2,1)S(1)} %get-tuple-element.69), channel_id=1, source_target_pairs={{0,6},{1,7},{2,4},{3,5},{4,2},{5,3},{6,0},{7,1},{8,14},{9,15},{10,... | collective-permute-start | bytes 1572872 | tf_op jit(solution)/shard_map/ppermute | solution.py:386
  786.1 22.2 %collective-permute-start.23 = (bf16[512,512]{1,0:T(8,128)(2,1)S(1)}, bf16[512,512]{1,0:T(8,128)(2,1)S(1)}, u32[]{:S(2)}, u32[]{:S(2)}) collective-permute-start(bf16[512,512]{1,0:T(8,128)(2,1)S(1)} %get-tuple-element.70), channel_id=1, source_target_pairs={{0,2},{1,3},{2,0},{3,1},{4,6},{5,7},{6,4},{7,5},{8,10},{9,11},{10,... | collective-permute-start | bytes 1572872 | tf_op jit(solution)/shard_map/ppermute | solution.py:386
  808.9 3.7 collective-permute-start.48
  810.1 3.7 collective-permute-start.27
  812.5 3.6 collective-permute-start.25
  812.6 4.6 collective-permute-start.49
  817.2 3.7 collective-permute-start.50
  (40 other events, 817.3 us)

commit v3 on v2

--- a/solution.py
+++ b/solution.py
@@ -621,10 +621,11 @@
 
 
 def forward_kernel(
-    x_ref, gain_one_ref, gain_two_ref, begin_ref, own_in, own_out, own_hidden, own_down, own_grad,
-    normed_ref, weight_in, weight_out, q_ref, kv_ref, att_ref, lse_ref, mid_ref, scale_ref, n2_ref,
-    hidden_all, down_all, grad_all,
-    zin, zout, sums, wide, given, arrived, low, landed, x32,
+    x_ref, gain_one_ref, gain_two_ref, lengths_ref, query_ref, key_ref, value_ref, out_ref, gate_ref, up_ref,
+    own_grad,
+    normed_ref, weight_in, weight_out, q_ref, kv_ref, att_ref, lse_ref, mid_ref, scale_ref, n2_ref, begin_ref, first_scale,
+    gate_all, up_all, grad_all,
+    zin, zout, sums, wide, given, arrived, low, landed, x32, hidden_own,
     send_sem, recv_sem, local_sem,
 ):
     d, r, c = (lax.axis_index(name) for name in AXES)
@@ -652,9 +653,19 @@
             device_id=(target_plane, r, c), device_id_type=MESH,
         )
 
-    mine = pltpu.make_async_copy(own_in, zin.at[d], local_sem.at[0])
-    mine.start()
-    mine.wait()
+    def cast_rows(src, dst, amount, step=64):
+        def one(t, total):
+            part = pl.ds(pl.multiple_of(t * step, step), step)
+            dst(part, src[part, :].astype(BF))
+            return total
+
+        lax.fori_loop(0, amount // step, one, 0)
+
+    for place, master in enumerate((query_ref, key_ref, value_ref)):
+        def put(part, value, place=place):
+            zin[d, part, place * width : (place + 1) * width] = value
+
+        cast_rows(master, put, fc)
 
     @pl.when(d < DP - 1)
     def _():
@@ -713,6 +724,11 @@
         local_sem.at[2],
     )
     grad_keep.start()
+    for kind, master in enumerate((gate_ref, up_ref)):
+        def put(part, value, kind=kind):
+            hidden_own[kind, part, :] = value
+
+        cast_rows(master, put, fc)
     for copy in small:
         copy.wait_recv()
 
@@ -720,6 +736,7 @@
         part = pl.ds(pl.multiple_of(t * 128, 128), 128)
         square = sums[0, :, part] + sums[2, :, part] + sums[1, :, part] + sums[3, :, part]
         scale = lax.rsqrt(as_column(square) / D + EPSILON)
+        first_scale[part, :] = scale
         normed_ref[part, 0:fc] = (x32[part, :] * scale * gain_one_ref[...]).astype(BF)
         return total
 
@@ -735,6 +752,76 @@
     corner = post.send(own_block, normed_ref.at[other_rows, columns(1)], (d, r ^ 1, c ^ 2))
     sibling = (d, r, c ^ 1)
     shared = [post.send(own_block, normed_ref.at[own_rows, columns(2)], sibling)]
+
+    hidden_all = (gate_all, up_all)
+    first_sent = post.take(10)
+    first_got = first_sent
+
+    def slab(kind, i):
+        return hidden_all[kind].at[pl.ds(pl.multiple_of(place_of(i) * fc, fc), fc), :]
+
+    def ship(kind, way, i, target, src=None):
+        return pltpu.make_async_remote_copy(
+            src_ref=hidden_own.at[kind] if src is None else src,
+            dst_ref=slab(kind, i),
+            send_sem=send_sem.at[first_sent + 5 * kind + way],
+            recv_sem=recv_sem.at[first_got + 4 * kind + i],
+            device_id=target, device_id_type=MESH,
+        )
+
+    def keep_hidden(kind):
+        return pltpu.make_async_copy(hidden_own.at[kind], slab(kind, 0), local_sem.at[3 + kind])
+
+    def to_core(kind):
+        return ship(kind, 0, 1, (d, r, c ^ 1))
+
+    def over_y(kind):
+        return ship(kind, 1, 2 + core, (d, r, 2 * (1 - y)))
+
+    def over_x(kind):
+        return ship(kind, 2, 1 - core, (d, r ^ 1, 2 * y + 1))
+
+    def relay(kind, i):
+        return ship(kind, i + 1, 5 - i, (d, r ^ 1, 2 * y + 1), slab(kind, i))
+
+    def start_home(kind):
+        over_x(kind).start()
+
+        @pl.when(core == 0)
+        def _():
+            keep_hidden(kind).start()
+
+        @pl.when(core == 1)
+        def _():
+            to_core(kind).start()
+
+    def start_relay(kind):
+        @pl.when(core == 0)
+        def _():
+            for i in (2, 3):
+                ship(kind, 0, i, (d, r, c)).wait_recv()
+                relay(kind, i).start()
+
+    over_y(0).start()
+    start_home(0)
+    start_home(1)
+    def put_out(part, value):
+        zout[0, part, :] = value
+
+    cast_rows(out_ref, put_out, width)
+
+    def find_begins(t, total):
+        part = pl.ds(pl.multiple_of(t * 128, 128), 128)
+        place = lax.broadcasted_iota(jnp.int32, (128, 1), 0) + (d * group + t * 128)
+        end = jnp.int32(0)
+        begin = jnp.zeros((128, 1), jnp.int32)
+        for n in range(lengths_ref.shape[0]):
+            end = end + lengths_ref[n]
+            begin = jnp.where(place >= end, end, begin)
+        begin_ref[part, :] = begin - d * group
+        return total
+
+    lax.fori_loop(0, group // 128, find_begins, 0)
 
     def line_step(s):
         for p, valid, onward, forward in (
@@ -758,38 +845,10 @@
             post.send(normed_ref.at[where, columns(place)], normed_ref.at[where, columns(place + 2)], sibling)
         )
 
-    bulk = []
-    first_hidden = post.take(8)
-    for i in (0, 2, 1, 3):
-        b = c ^ i
-        target = (d, r ^ lax.rem(b, 2), b)
-        place = PLACE[i]
-        for kind, (src, dst) in enumerate((
-            (own_down, down_all.at[:, columns(place)]),
-            (own_hidden, hidden_all.at[pl.ds(place * fc, fc), :]),
-        )):
-            bulk.append((i, kind, post.ready(src, dst, target, first_hidden + 2 * place + kind),
-                         pltpu.make_async_copy(src, dst, local_sem.at[3 + kind])))
-    for i, kind, copy, local in bulk:
-        if i == 0:
-            @pl.when(core == 0)
-            def _(local=local):
-                local.start()
-
-            @pl.when(core == 1)
-            def _(copy=copy):
-                copy.start()
-        else:
-            copy.start()
-
     line_step(2)
     line_step(3)
-    outs = [
-        post.send(own_out, zout.at[j], (d ^ j, r, c)) for j in (1, 2, 3)
-    ]
-    mine = pltpu.make_async_copy(own_out, zout.at[0], local_sem.at[5])
-    mine.start()
-    mine.wait()
+    outs = [post.send(zout.at[0], zout.at[j], (d ^ j, r, c)) for j in (1, 2, 3)]
+    start_relay(0)
 
     for copy in shared:
         copy.wait_recv()
@@ -800,6 +859,7 @@
             send_sem=send_sem.at[first_cols], recv_sem=recv_sem.at[first_cols + m],
             device_id=(d, r, c), device_id_type=MESH,
         ).wait_recv()
+    over_y(1).start()
 
     def turned(t):
         return lax.rem(t + 2 * r, group // TILE)
@@ -888,6 +948,7 @@
             return total
 
         lax.fori_loop(0, group // TILE, one, 0)
+    start_relay(1)
 
     for copy in out_cols:
         copy.wait_recv()
@@ -960,17 +1021,22 @@
         )
     for copy in grads_shared:
         copy.wait_recv()
-    for i, kind, copy, local in bulk:
-        if i == 0:
-            @pl.when(core == 0)
-            def _(local=local):
-                local.wait()
-
-            @pl.when(core == 1)
-            def _(copy=copy):
-                copy.wait()
-        else:
-            copy.wait()
+    for kind in (0, 1):
+        over_y(kind).wait_send()
+        over_x(kind).wait_send()
+
+        @pl.when(core == 0)
+        def _(kind=kind):
+            keep_hidden(kind).wait()
+            ship(kind, 0, 1, (d, r, c)).wait_recv()
+            for i in (2, 3):
+                relay(kind, i).wait_send()
+
+        @pl.when(core == 1)
+        def _(kind=kind):
+            to_core(kind).wait_send()
+            for i in range(COL):
+                ship(kind, 0, i, (d, r, c)).wait_recv()
 
     for copy in (
         small + [grad_cross, beside, beyond, corner] + shared + outs + out_cols + grads + grads_shared
@@ -999,12 +1065,13 @@
 SENDS = 64
 
 
-def forward(x, gain_one, gain_two, begin, own_in, own_out, own_hidden, own_down, own_grad):
+def forward(x, gain_one, gain_two, lengths, query, key, value, out, gate, up, own_grad):
     rows, fc = x.shape
     group = 2 * rows
-    width = own_out.shape[0]
-    units = own_down.shape[0]
+    width = out.shape[0]
+    units = gate.shape[1]
     vmem = pl.BlockSpec(memory_space=pltpu.VMEM)
+    smem = pl.BlockSpec(memory_space=pltpu.SMEM)
     hbm = pl.BlockSpec(memory_space=pl.ANY)
 
     def like(shape, dtype=BF):
@@ -1012,8 +1079,8 @@
 
     return pl.pallas_call(
         forward_kernel,
-        in_specs=[vmem] * 4 + [hbm] * 5,
-        out_specs=[vmem] * 10 + [hbm] * 3,
+        in_specs=[vmem] * 3 + [smem] + [vmem] * 6 + [hbm],
+        out_specs=[vmem] * 12 + [hbm] * 3,
         out_shape=[
             like((group, D)),
             like((D, 3 * width)),
@@ -1025,8 +1092,10 @@
             like((rows, fc), F32),
             like((rows, 1), F32),
             like((rows, fc)),
-            like((D, 2 * units)),
-            like((units, D)),
+            like((group, 1), jnp.int32),
+            like((rows, 1), F32),
+            like((D, units)),
+            like((D, units)),
             like((group, D)),
         ],
         scratch_shapes=[
@@ -1039,17 +1108,560 @@
             pltpu.VMEM((group, 2 * fc), BF),
             pltpu.VMEM((3, rows, fc), BF),
             pltpu.VMEM((rows, fc), F32),
+            pltpu.VMEM((2, fc, units), BF),
             pltpu.SemaphoreType.DMA((SENDS,)),
             pltpu.SemaphoreType.DMA((SENDS,)),
             pltpu.SemaphoreType.DMA((8,)),
         ],
         compiler_params=pltpu.CompilerParams(
-            collective_id=1, has_side_effects=True, vmem_limit_bytes=56 << 20
+            collective_id=1, has_side_effects=True, vmem_limit_bytes=60 << 20
         ),
         cost_estimate=pl.CostEstimate(
             flops=6 * group * D * width, bytes_accessed=64 << 20, transcendentals=0
         ),
-    )(x, gain_one, gain_two, begin, own_in, own_out, own_hidden, own_down, own_grad)
+    )(x, gain_one, gain_two, lengths, query, key, value, out, gate, up, own_grad)
+
+
+POSTS = 112
+
+
+def backward_kernel(
+    x_ref, gain_ref, scale_ref, mid_ref, gain_two_ref, weight_in, weight_out, q_ref, kv_ref, att_ref, lse_ref,
+    begin_ref, normed_hbm, n2_hbm, dgate_hbm, dup_hbm,
+    tokens_out, in_out, out_out, gains_out, got, comb,
+    n1, n2, dgu, dball, dotted, dproj, acc, spill, spilled, stage, own_f, arrived, landed,
+    zq, zo, zkv, rq, ro, rkv, sums, gsum,
+    send_sem, recv_sem, local_sem,
+):
+    d, r, c = (lax.axis_index(name) for name in AXES)
+    y, core = c // 2, lax.rem(c, 2)
+    rows, fc = x_ref.shape
+    group = 2 * rows
+    width = q_ref.shape[1]
+    units = dgate_hbm.shape[1]
+    half = 2 * fc
+    tiles = group // TILE
+    over = (((0,), (0,)), ((), ()))
+    across = (((1,), (1,)), ((), ()))
+    post = Post(send_sem, recv_sem)
+    others = [(a, b) for a in (0, 1) for b in range(COL) if (a, b) != (0, 0)]
+    greet(
+        [(d, r ^ a, c ^ b) for a, b in others]
+        + [(d ^ j, r ^ a, c) for j in (1, 2, 3) for a in (0, 1)]
+    )
+
+    def columns(place):
+        return pl.ds(place * fc, fc)
+
+    def at(t, size):
+        return pl.ds(pl.multiple_of(t * size, size), size)
+
+    def loop(count, body):
+        def one(t, total):
+            body(t)
+            return total
+
+        lax.fori_loop(0, count, one, 0)
+
+    def turned(t):
+        return lax.rem(t + 2 * r, tiles)
+
+    def raw(src, dst, sent, got_at, target):
+        return pltpu.make_async_remote_copy(
+            src_ref=src, dst_ref=dst, send_sem=send_sem.at[sent], recv_sem=recv_sem.at[got_at],
+            device_id=target, device_id_type=MESH,
+        )
+
+    me = (d, r, c)
+    sibling = (d, r, c ^ 1)
+    own_rows, other_rows = pl.ds(0, rows), pl.ds(rows, rows)
+    loads = [
+        pltpu.make_async_copy(src, dst, local_sem.at[n])
+        for n, (src, dst) in enumerate((
+            (n2_hbm, n2),
+            (dgate_hbm, dgu.at[pl.ds(0, group), :]),
+            (dup_hbm, dgu.at[pl.ds(group, group), :]),
+            (normed_hbm, n1),
+        ))
+    ]
+    for load in loads:
+        load.start()
+
+    def round_mid(t):
+        dball[at(t, 128), 0:fc] = mid_ref[at(t, 128), :].astype(BF)
+
+    loop(rows // 128, round_mid)
+    own_block = dball.at[own_rows, columns(0)]
+    beside = post.send(own_block, dball.at[other_rows, columns(0)], (d, r ^ 1, c))
+    beyond = post.send(own_block, dball.at[own_rows, columns(1)], (d, r, c ^ 2))
+    corner = post.send(own_block, dball.at[other_rows, columns(1)], (d, r ^ 1, c ^ 2))
+    shared = [post.send(own_block, dball.at[own_rows, columns(2)], sibling)]
+
+    for load in loads[:3]:
+        load.wait()
+    for i in (2, 3, 0, 1):
+        for kind in (0, 1):
+            def hidden_grad(t, i=i, kind=kind):
+                left = n2[:, pl.ds(pl.multiple_of(PLACE[i] * fc + t * TILE, TILE), TILE)]
+                stage[kind, i, at(t, TILE), :] = lax.dot_general(
+                    left, dgu[pl.ds(kind * group, group), :], over, preferred_element_type=F32
+                ).astype(BF)
+
+            loop(fc // TILE, hidden_grad)
+    loads[3].wait()
+
+    for copy, where, place in ((beside, other_rows, 0), (beyond, own_rows, 1), (corner, other_rows, 1)):
+        copy.wait_recv()
+        shared.append(post.send(dball.at[where, columns(place)], dball.at[where, columns(place + 2)], sibling))
+    bulk = post.take(20)
+
+    def from_one(kind, i):
+        if i < 2:
+            return raw(stage.at[kind, i], got.at[kind, 0], bulk + 4 * kind + i, bulk + 10 * kind + 0,
+                       (d, r ^ 1, 2 * y + 1 - i))
+        return raw(stage.at[kind, i], comb.at[kind, 3 - i], bulk + 4 * kind + i,
+                   bulk + 10 * kind + 3 + (3 - i), (d, r ^ 1, 2 * y))
+
+    def from_zero(kind, i):
+        if i == 1:
+            return raw(stage.at[kind, i], got.at[kind, 1], bulk + 4 * kind + i, bulk + 10 * kind + 1, sibling)
+        return raw(stage.at[kind, i], got.at[kind, 2], bulk + 4 * kind + i, bulk + 10 * kind + 2,
+                   (d, r, 2 * (1 - y) + i - 2))
+
+    def home(kind):
+        return pltpu.make_async_copy(stage.at[kind, 0], got.at[kind, 1], local_sem.at[4 + kind])
+
+    @pl.when(core == 1)
+    def _():
+        for i in (2, 3, 0, 1):
+            for kind in (0, 1):
+                from_one(kind, i).start()
+
+    @pl.when(core == 0)
+    def _():
+        for kind in (0, 1):
+            home(kind).start()
+            from_zero(kind, 1).start()
+
+    for copy in shared:
+        copy.wait_recv()
+
+    def head_grad(t):
+        dotted[at(turned(t), TILE), :] = lax.dot_general(
+            dball[at(t, TILE), :], weight_out[...], across, preferred_element_type=F32
+        ).astype(BF)
+
+    loop(tiles, head_grad)
+    span = TILE + REACH
+    scale = HEAD_DIM ** (-0.5)
+    spills = []
+    for h in range(width // HEAD_DIM):
+        lanes = pl.ds(h * HEAD_DIM, HEAD_DIM)
+        value_lanes = pl.ds(width + h * HEAD_DIM, HEAD_DIM)
+
+        def clear(t, lanes=lanes, value_lanes=value_lanes):
+            acc[at(t, TILE), lanes] = jnp.zeros((TILE, HEAD_DIM), F32)
+            acc[at(t, TILE), value_lanes] = jnp.zeros((TILE, HEAD_DIM), F32)
+
+        loop((group + REACH) // TILE, clear)
+
+        def one(t, lanes=lanes, value_lanes=value_lanes):
+            part = at(t, TILE)
+            window = pl.ds(pl.multiple_of(t * TILE, TILE), span)
+            query, key = q_ref[part, lanes], kv_ref[window, lanes]
+            grad = dotted[part, lanes]
+            scores = scores_of(query, key)
+            query_at = lax.broadcasted_iota(jnp.int32, (TILE, span), 0)
+            key_at = lax.broadcasted_iota(jnp.int32, (TILE, span), 1)
+            begin = begin_ref[part, 0:1] + (REACH - t * TILE)
+            allowed = (key_at <= query_at + REACH) & (key_at >= begin)
+            scores = jnp.where(allowed, scores - lse_ref[part, lanes][:, 0:1], NEG_FILL)
+            probability = jnp.exp(scores)
+            grad_soft = lax.dot_general(grad, kv_ref[window, value_lanes], across, preferred_element_type=F32)
+            inner = jnp.sum(probability * grad_soft, axis=1, keepdims=True)
+            grad_scores = (probability * (grad_soft - inner)).astype(BF)
+            dproj[at(turned(t), TILE), lanes] = (
+                jnp.dot(grad_scores, key, preferred_element_type=F32) * scale
+            ).astype(BF)
+            acc[window, lanes] += lax.dot_general(grad_scores, query, over, preferred_element_type=F32) * scale
+            acc[window, value_lanes] += lax.dot_general(
+                probability.astype(BF), grad, over, preferred_element_type=F32
+            )
+
+        loop(tiles, one)
+
+        def round_spill(t, h=h, lanes=lanes, value_lanes=value_lanes):
+            spill[h, at(t, TILE), 0:HEAD_DIM] = acc[at(t, TILE), lanes].astype(BF)
+            spill[h, at(t, TILE), HEAD_DIM:] = acc[at(t, TILE), value_lanes].astype(BF)
+
+        loop(REACH // TILE, round_spill)
+        copy = post.ready(spill.at[h], spilled.at[h], (lax.rem(d + DP - 1, DP), r, c))
+        spills.append(copy)
+
+        @pl.when(d > 0)
+        def _(copy=copy):
+            copy.start()
+
+    sent_out = [None] + [post.take(1) for _ in (1, 2, 3)]
+    outs = []
+    for place, m in enumerate((0, 2, 1, 3)):
+        value = lax.dot_general(
+            att_ref[...], dball[:, place * fc : (place + 1) * fc], over, preferred_element_type=F32
+        ).astype(BF)
+        if m == 0:
+            zo[c] = value
+        else:
+            n2[(m - 1) * width : m * width, half : half + fc] = value
+            staged = n2.at[pl.ds((m - 1) * width, width), pl.ds(half, fc)]
+            copy = raw(staged, zo.at[c], sent_out[m], sent_out[m], (d, r, c ^ m))
+            copy.start()
+            outs.append(copy)
+
+    def attention_grads(first_lane, lane_count, dest):
+        lanes = slice(first_lane, first_lane + lane_count)
+        slots = [None] + [post.take(1) for _ in (1, 2, 3)]
+        copies = []
+        for place, m in enumerate((0, 2, 1, 3)):
+            def tile(t, place=place, m=m):
+                left = n1[:, pl.ds(pl.multiple_of(place * fc + t * TILE, TILE), TILE)]
+                value = lax.dot_general(left, dproj[:, lanes], over, preferred_element_type=F32).astype(BF)
+                if m == 0:
+                    dest[c, at(t, TILE), :] = value
+                else:
+                    dgu[pl.ds(pl.multiple_of(place * fc + t * TILE, TILE), TILE), lanes] = value
+
+            loop(fc // TILE, tile)
+            if m:
+                copy = raw(
+                    dgu.at[pl.ds(place * fc, fc), pl.ds(first_lane, lane_count)], dest.at[c],
+                    slots[m], slots[m], (d, r, c ^ m),
+                )
+                copy.start()
+                copies.append(copy)
+        return copies
+
+    qs = attention_grads(0, width, zq)
+
+    @pl.when(d < DP - 1)
+    def _():
+        for copy in spills:
+            copy.wait_recv()
+
+    @pl.when(d == DP - 1)
+    def _():
+        spilled[...] = jnp.zeros_like(spilled)
+
+    for h in range(width // HEAD_DIM):
+        for which in (0, 1):
+            lanes = pl.ds(which * width + h * HEAD_DIM, HEAD_DIM)
+            out_lanes = pl.ds((1 + which) * width + h * HEAD_DIM, HEAD_DIM)
+
+            def whole(t, h=h, which=which, lanes=lanes, out_lanes=out_lanes):
+                total = acc[pl.ds(pl.multiple_of(REACH + t * TILE, TILE), TILE), lanes]
+                extra = spilled[
+                    h, at(jnp.maximum(t - 1, 0), TILE), which * HEAD_DIM : (which + 1) * HEAD_DIM
+                ].astype(F32)
+                total = total + jnp.where(t > 0, extra, 0.0)
+                dproj[at(turned(t), TILE), out_lanes] = total.astype(BF)
+
+            loop(tiles, whole)
+
+    kvs = attention_grads(width, 2 * width, zkv)
+
+    def given_part(t):
+        n2[at(t, TILE), 0:half] = lax.dot_general(
+            dproj[at(t, TILE), :], weight_in[half:, :], across, preferred_element_type=F32
+        ).astype(BF)
+
+    loop(tiles, given_part)
+    to_sibling = post.send(n2.at[:, pl.ds(0, half)], arrived, sibling)
+
+    @pl.when(core == 0)
+    def _():
+        fetches = {}
+        for i in (2, 3):
+            for kind in (0, 1):
+                raw(stage.at[kind, i], comb.at[kind, i - 2], bulk, bulk + 10 * kind + 3 + (i - 2), me).wait_recv()
+                room = n1.at[pl.ds((i - 2) * fc, fc), pl.ds(kind * units, units)]
+                fetches[i, kind] = pltpu.make_async_copy(
+                    comb.at[kind, i - 2], room, local_sem.at[2 * kind + i - 2]
+                )
+                fetches[i, kind].start()
+        for i in (2, 3):
+            for kind in (0, 1):
+                fetches[i, kind].wait()
+
+                def add(t, kind=kind, i=i):
+                    there = pl.ds(pl.multiple_of((i - 2) * fc + t * 64, 64), 64)
+                    stage[kind, i, at(t, 64), :] = (
+                        stage[kind, i, at(t, 64), :].astype(F32)
+                        + n1[there, kind * units : (kind + 1) * units].astype(F32)
+                    ).astype(BF)
+
+                loop(fc // 64, add)
+                from_zero(kind, i).start()
+
+    to_sibling.wait_recv()
+    for copy in outs:
+        copy.wait_send()
+
+    def kept_part(t):
+        part = at(t, TILE)
+        value = lax.dot_general(
+            dproj[part, :], weight_in[:half, :], across, preferred_element_type=F32
+        ) + arrived[part, :].astype(F32)
+        n2[part, half:] = value.astype(BF)
+
+        @pl.when(t < rows // TILE)
+        def _():
+            own_f[part, :] = value[:, 0:fc]
+
+    loop(tiles, kept_part)
+
+    def low(where, place):
+        return n2.at[where, pl.ds(half + place * fc, fc)]
+
+    pieces = [
+        post.send(low(other_rows, 1), landed.at[2], (d, r ^ 1, c ^ 2)),
+        post.send(low(other_rows, 0), landed.at[0], (d, r ^ 1, c)),
+        post.send(low(own_rows, 1), landed.at[1], (d, r, c ^ 2)),
+    ]
+
+    def line_sum(arrays, base):
+        def sem(n, p, down):
+            return base + 8 * n + 4 * down + p
+
+        def add(p):
+            for z, got_z in arrays:
+                def one(t, z=z, got_z=got_z):
+                    z[p, at(t, 64), :] = (
+                        z[p, at(t, 64), :].astype(F32) + got_z[p, at(t, 64), :].astype(F32)
+                    ).astype(BF)
+
+                loop(z.shape[1] // 64, one)
+
+        def up(p):
+            @pl.when((d > 0) & (d <= p))
+            def _():
+                for n, (z, got_z) in enumerate(arrays):
+                    raw(z.at[p], got_z.at[p], sem(n, p, 0), sem(n, p, 0), me).wait_recv()
+
+                @pl.when(d < p)
+                def _():
+                    add(p)
+
+            @pl.when(d < p)
+            def _():
+                for n, (z, got_z) in enumerate(arrays):
+                    raw(z.at[p], got_z.at[p], sem(n, p, 0), sem(n, p, 0), (d + 1, r, c)).start()
+
+        def down(p):
+            @pl.when((d < DP - 1) & (d >= p))
+            def _():
+                for n, (z, got_z) in enumerate(arrays):
+                    raw(z.at[p], got_z.at[p], sem(n, p, 1), sem(n, p, 1), me).wait_recv()
+
+                @pl.when(d > p)
+                def _():
+                    add(p)
+
+            @pl.when(d > p)
+            def _():
+                slot = jnp.where(p < d - 1, p, DP)
+                for n, (z, got_z) in enumerate(arrays):
+                    raw(z.at[p], got_z.at[slot], sem(n, p, 1), sem(n, p, 1), (d - 1, r, c)).start()
+
+        @pl.when(d < DP // 2)
+        def _():
+            for s in range(DP - 1):
+                up(DP - 1 - s)
+                down(s)
+
+        @pl.when(d >= DP // 2)
+        def _():
+            for s in range(DP - 1):
+                down(s)
+                up(DP - 1 - s)
+
+        def settle():
+            for p in range(DP):
+                for n, (z, got_z) in enumerate(arrays):
+                    @pl.when(d < p)
+                    def _(p=p, n=n, z=z, got_z=got_z):
+                        raw(z.at[p], got_z.at[p], sem(n, p, 0), sem(n, p, 0), me).wait_send()
+
+                    @pl.when(d > p)
+                    def _(p=p, n=n, z=z, got_z=got_z):
+                        raw(z.at[p], got_z.at[p], sem(n, p, 1), sem(n, p, 1), me).wait_send()
+
+        return settle
+
+    def finish(z, got_z, dest, lanes):
+        def one(t):
+            part = at(t, 64)
+            value = z[d, part, :].astype(F32)
+            value = value + jnp.where(d > 0, got_z[d, part, :].astype(F32), 0.0)
+            value = value + jnp.where(d < DP - 1, got_z[DP, part, :].astype(F32), 0.0)
+            dest[part, lanes] = value
+
+        loop(z.shape[1] // 64, one)
+
+    for copy in outs + qs:
+        copy.wait_recv()
+    first_line = post.take(24)
+    settle_a = line_sum(((zq, rq), (zo, ro)), first_line)
+
+    for copy in pieces:
+        copy.wait_recv()
+
+    def inner_sum(t):
+        part = at(t, 128)
+        value = own_f[part, :]
+        for n in range(3):
+            value = value + landed[n, part, :].astype(F32)
+        own_f[part, :] = value
+        inner = value * gain_ref[...] * x_ref[part, :].astype(F32)
+        sums[0, :, part] = as_row(jnp.sum(inner, axis=1, keepdims=True))
+
+    loop(rows // 128, inner_sum)
+    small = [post.send(sums.at[0], sums.at[m], (d, r, c ^ m)) for m in (1, 2, 3)]
+    seat = ROW * d + r
+    gain_part = jnp.zeros((1, fc), F32)
+
+    def gain_sum(t, total):
+        part = at(t, 128)
+        value = own_f[part, :] * x_ref[part, :].astype(F32) * scale_ref[part, :]
+        return total + jnp.sum(value, axis=0, keepdims=True)
+
+    gain_part = lax.fori_loop(0, rows // 128, gain_sum, gain_part)
+    gsum[seat, 0:1, :] = gain_part
+    gsum[seat, 1:2, :] = gain_two_ref[...]
+    gsum[seat, 2:8, :] = jnp.zeros((6, fc), F32)
+    gain_sent = post.take(8)
+    gain_got = gain_sent
+
+    def gain_copy(n, j, a):
+        return raw(gsum.at[seat], gsum.at[seat], gain_sent + n, gain_got + seat, (d ^ j, r ^ a, c))
+
+    far = [(j, a) for j in range(DP) for a in (0, 1) if (j, a) != (0, 0)]
+    for n, (j, a) in enumerate(far):
+        gain_copy(n, j, a).start()
+    for copy in small:
+        copy.wait_recv()
+
+    def finish_tokens(t):
+        part = at(t, 128)
+        inner = as_column(sums[0, :, part] + sums[2, :, part] + sums[1, :, part] + sums[3, :, part])
+        scale_rows = scale_ref[part, :]
+        value = x_ref[part, :].astype(F32)
+        tokens_out[part, :] = (
+            mid_ref[part, :] + scale_rows * (own_f[part, :] * gain_ref[...])
+            - value * (scale_rows * scale_rows * scale_rows * inner / D)
+        )
+
+    loop(rows // 128, finish_tokens)
+
+    for copy in kvs:
+        copy.wait_recv()
+    settle_b = line_sum(((zkv, rkv),), first_line + 16)
+    finish(zq, rq, in_out, slice(0, width))
+    finish(zo, ro, out_out, slice(0, fc))
+    finish(zkv, rkv, in_out, slice(width, 3 * width))
+    for e in range(2 * DP):
+        @pl.when(e != seat)
+        def _(e=e):
+            raw(gsum.at[e], gsum.at[e], gain_sent, gain_got + e, me).wait_recv()
+
+    gains = gsum[0]
+    for e in range(1, 2 * DP):
+        gains = gains + gsum[e]
+    gains_out[...] = gains
+
+    for kind in (0, 1):
+        for n in (0, 2):
+            raw(stage.at[kind, 0], got.at[kind, n], bulk, bulk + 10 * kind + n, me).wait_recv()
+
+        @pl.when(core == 1)
+        def _(kind=kind):
+            raw(stage.at[kind, 0], got.at[kind, 1], bulk, bulk + 10 * kind + 1, me).wait_recv()
+            for i in range(COL):
+                from_one(kind, i).wait_send()
+
+        @pl.when(core == 0)
+        def _(kind=kind):
+            home(kind).wait()
+            for i in (1, 2, 3):
+                from_zero(kind, i).wait_send()
+
+    settle_a()
+    settle_b()
+    for copy in [beside, beyond, corner] + shared + qs + kvs + [to_sibling] + pieces + small:
+        copy.wait_send()
+    for n, (j, a) in enumerate(far):
+        gain_copy(n, j, a).wait_send()
+
+    @pl.when(d > 0)
+    def _():
+        for copy in spills:
+            copy.wait_send()
+
+
+def backward(x, gain, scale, mid, gain_two, weight_in, weight_out, q, kv, att, lse, begin, normed, n2, dgate, dup):
+    rows, fc = x.shape
+    group = 2 * rows
+    width = q.shape[1]
+    units = dgate.shape[1]
+    vmem = pl.BlockSpec(memory_space=pltpu.VMEM)
+    hbm = pl.BlockSpec(memory_space=pl.ANY)
+
+    def like(shape, dtype=BF):
+        return jax.ShapeDtypeStruct(shape, dtype)
+
+    return pl.pallas_call(
+        backward_kernel,
+        in_specs=[vmem] * 12 + [hbm] * 4,
+        out_specs=[vmem] * 4 + [hbm] * 2,
+        out_shape=[
+            like((rows, fc), F32),
+            like((fc, 3 * width), F32),
+            like((width, fc), F32),
+            like((8, fc), F32),
+            like((2, 3, fc, units)),
+            like((2, 2, fc, units)),
+        ],
+        scratch_shapes=[
+            pltpu.VMEM((group, D), BF),
+            pltpu.VMEM((group, D), BF),
+            pltpu.VMEM((2 * group, units), BF),
+            pltpu.VMEM((group, D), BF),
+            pltpu.VMEM((group, width), BF),
+            pltpu.VMEM((group, 3 * width), BF),
+            pltpu.VMEM((group + REACH, 2 * width), F32),
+            pltpu.VMEM((width // HEAD_DIM, REACH, 2 * HEAD_DIM), BF),
+            pltpu.VMEM((width // HEAD_DIM, REACH, 2 * HEAD_DIM), BF),
+            pltpu.VMEM((2, COL, fc, units), BF),
+            pltpu.VMEM((rows, fc), F32),
+            pltpu.VMEM((group, 2 * fc), BF),
+            pltpu.VMEM((3, rows, fc), BF),
+            pltpu.VMEM((DP, fc, width), BF),
+            pltpu.VMEM((DP, width, fc), BF),
+            pltpu.VMEM((DP, fc, 2 * width), BF),
+            pltpu.VMEM((DP + 1, fc, width), BF),
+            pltpu.VMEM((DP + 1, width, fc), BF),
+            pltpu.VMEM((DP + 1, fc, 2 * width), BF),
+            pltpu.VMEM((4, 8, rows), F32),
+            pltpu.VMEM((2 * DP, 8, fc), F32),
+            pltpu.SemaphoreType.DMA((POSTS,)),
+            pltpu.SemaphoreType.DMA((POSTS,)),
+            pltpu.SemaphoreType.DMA((8,)),
+        ],
+        compiler_params=pltpu.CompilerParams(
+            collective_id=2, has_side_effects=True, vmem_limit_bytes=62 << 20
+        ),
+        cost_estimate=pl.CostEstimate(
+            flops=12 * group * D * width + 4 * group * D * units, bytes_accessed=64 << 20, transcendentals=0
+        ),
+    )(x, gain, scale, mid, gain_two, weight_in, weight_out, q, kv, att, lse, begin, normed, n2, dgate, dup)
 
 
 def rounded_norm(values, scale, gain):
@@ -1094,22 +1706,18 @@
         swapped = jnp.concatenate([array[rows:], array[:rows]], 0)
         return jnp.where(r == 0, array, swapped)
 
-    x = tokens.astype(F32)
-    begin = (begins_of(lengths, d * group, group) - d * group)[:, None]
-    block_in = jnp.concatenate([query_master, key_master, value_master], 1).astype(BF)
-    hidden_in = jnp.concatenate([gate_master, up_master], 1).astype(BF)
-    hidden_out = down_master.astype(BF)
     (
         normed_one, weight_in, weight_out, q, key_value, own_attended, lse, midway, scale_two,
-        n2, weight_hidden, weight_down, grad_all,
+        n2, begin, scale_one, weight_gate, weight_up, grad_all,
     ) = forward(
-        tokens, attn_gain[None, :], ffn_gain[None, :], begin, block_in, out_master.astype(BF),
-        hidden_in, hidden_out, cotangent,
-    )
+        tokens, attn_gain[None, :], ffn_gain[None, :], lengths, query_master, key_master,
+        value_master, out_master, gate_master, up_master, cotangent,
+    )
+    hidden_out = down_master.astype(BF)
     scale_two = scale_two[:, 0]
-    scale_one = lax.rsqrt(col_sum(jnp.sum(x * x, axis=1)) / D + EPSILON)
-    k, v = key_value[:, :width], key_value[:, width:]
     order = (0, 2, 1, 3)
+    weight_hidden = jnp.concatenate([weight_gate, weight_up], 1)
+    weight_down = jnp.concatenate([move(hidden_out, hidden_from(i)) for i in order], 1)
 
     def spread_tokens(block):
         kept = lax.dynamic_slice_in_dim(block, y * half_rows, half_rows, 0)
@@ -1160,56 +1768,24 @@
         return total
 
     down_part = lax.dot_general(hidden, grad_all, over, preferred_element_type=F32).astype(BF)
-    both_part = lax.dot_general(normed_two, grad_both, over, preferred_element_type=F32).astype(BF)
     grad_down_own = plane_total(down_part, 1)
-    grad_both_own = plane_total(both_part, 0)
 
     grad_mid_norm, gain_two_part = norm_grads(grad_normed_two, midway, scale_two, ffn_gain)
     grad_midway = cotangent.astype(F32) + grad_mid_norm
-    back_all = plane_gather(grad_midway.astype(BF))
-    grad_attended = flip(
-        lax.dot_general(back_all, weight_out, across, preferred_element_type=F32).astype(BF)
-    )
-    dq, dk, dv = attend_back(begin, q, k, v, grad_attended, lse)
-    dkv = jnp.concatenate([dk, dv], 1)
-    spill = move(
-        dkv[:REACH].astype(BF), lambda e, s, b: (e - 1, s, b) if e > 0 else None
-    )
-    dkv = dkv[REACH:]
-    start = group - REACH
-    dkv = jnp.concatenate([dkv[:start], dkv[start:] + spill.astype(F32)], 0).astype(BF)
-    grad_projected = flip(jnp.concatenate([dq, dkv], 1))
-
-    in_part = lax.dot_general(normed_one, grad_projected, over, preferred_element_type=F32).astype(BF)
-    out_part = lax.dot_general(own_attended, back_all, over, preferred_element_type=F32).astype(BF)
-
-    def owners_total(partial, axis):
-        size = D // COL
-        parts = [
-            lax.slice_in_dim(partial, i * size, (i + 1) * size, axis=axis) for i in range(COL)
-        ]
-        by_step = {0: parts[0], 2: by_col(parts[1], 2), 1: by_col(parts[2], 1), 3: by_col(parts[3], 3)}
-        stack = jnp.stack([by_step[m] for m in range(COL)])
-        total = pick(stack, d ^ c).astype(F32)
-        for j in (1, 2, 3):
-            total = total + by_plane(pick(stack, d ^ c ^ j), j).astype(F32)
-        return total
-
-    grad_in = owners_total(in_part, 0)
-    grad_out = owners_total(out_part, 1)
-
-    grad_normed_one = plane_scatter(grad_projected, weight_in, 1)
-    grad_in_norm, gain_one_part = norm_grads(grad_normed_one, x, scale_one, attn_gain)
-    grad_tokens = grad_midway + grad_in_norm
-    gains = same_sum(jnp.stack([gain_one_part, gain_two_part]))
+    grad_tokens, grad_in, grad_out, gains, got, _ = backward(
+        tokens, attn_gain[None, :], scale_one, grad_midway, gain_two_part[None, :], weight_in, weight_out, q,
+        key_value, own_attended, lse, begin, normed_one, normed_two, grad_gate, grad_up,
+    )
+    got = got.astype(F32)
+    grad_hidden_own = got[:, 0] + got[:, 1] + got[:, 2]
     return (
         grad_tokens,
         grad_in[:, :width],
         grad_in[:, width : 2 * width],
         grad_in[:, 2 * width :],
         grad_out,
-        grad_both_own[:, :units],
-        grad_both_own[:, units:],
+        grad_hidden_own[0],
+        grad_hidden_own[1],
         grad_down_own,
         gains[0],
         gains[1],

time: 828 us -> 671 us (0.81)
  waiting for transfers between devices: 305 us -> 104 us
  Pallas kernels: 300 us -> 434 us
  matrix products: 94.6 us -> 54.9 us
  starting transfers between devices: 68.7 us -> 30.1 us
  local copies, waits for them, and re-layouts: 19.6 us -> 11.2 us
    ppermute x51 -> x21, waiting for transfers between devices: 305 us -> 104 us  [move(): return lax.ppermute(array, AXES, pairs)]
    pallas_call x2, Pallas kernels: 300 us -> 434 us  [the longest x1 227 us: backward(): pl.pallas_call(backward_kernel, in_specs=[vmem] * 12 + [hbm] * 4, out_spe...]
    ppermute x51 -> x21, starting transfers between devices: 68.7 us -> 30.1 us  [move(): return lax.ppermute(array, AXES, pairs)]
    dot_general x6 -> x0, matrix products: 34.3 us -> none  [the longest x1 20.9 us: on_small_mesh(): lax.dot_general(normed_two, grad_both, over, preferred_element_type=F32)]
    concatenate x4 -> x1, other arithmetic: 4.12 us -> 15.1 us  [spread_tokens(): return jnp.concatenate([rail, by_col(rail, 1)], 1)]
  transfers between devices with their start and end apart: 51 -> 21, of which waited for: 27 -> 9; matrix products, arithmetic and copies ran while one was open for 9% -> 8% of each run, Pallas kernels for 1% -> 0%
where the time goes in v3:
time: 671 us; the launch traced here: 664 us
  Pallas kernels  434 us (65%)
  waiting for transfers between devices  104 us (15%)
  matrix products  54.9 us (8%)
  starting transfers between devices  30.1 us (4%)
  other arithmetic  28.3 us (4%)
  local copies, waits for them, and re-layouts  11.2 us (2%)
    pallas_call x1, Pallas kernels, backward(): pl.pallas_call(backward_kernel, in_specs=[vmem] * 12 + [hbm] * 4, out_spe...  227 us
    pallas_call x1, Pallas kernels, forward(): pl.pallas_call(forward_kernel, in_specs=[vmem] * 3 + [smem] + [vmem] * 6...  207 us
    ppermute x21, waiting for transfers between devices, move(): return lax.ppermute(array, AXES, pairs)  104 us
    ppermute x21, starting transfers between devices, move(): return lax.ppermute(array, AXES, pairs)  30.1 us
    dot_general x1, matrix products, on_small_mesh(): gate_and_up = jnp.dot(normed_two, weight_hidden, preferred_element_type=F32)  22.7 us
    concatenate x1, other arithmetic, spread_tokens(): return jnp.concatenate([rail, by_col(rail, 1)], 1)  15.1 us
  transfers between devices with their start and end apart: 21, of which 9 were waited for; matrix products, arithmetic and copies ran while one was open for 8% of the time, Pallas kernels for 0%

profile of v3, /device:TPU:0, one launch (start us, length us, event | category | flops | bytes accessed | tf_op | source)
XLA Modules:
  0.0 663.5 jit_solution(5203248373776977038)
XLA Ops:
  0.7 206.7 %shard_map.195 = (bf16[1024,2048]{1,0:T(8,128)(2,1)}, bf16[2048,768]{1,0:T(8,128)(2,1)}, bf16[256,2048]{1,0:T(8,128)(2,1)}, bf16[1024,256]{1,0:T(8,128)(2,1)}, b...) custom-call(bf16[512,512]{1,0:T(8,128)(2,1)} %x_ref.3, ...), custom_call_target="tpu_custom_call" | custom-call | flops 3221225472 | bytes 67108864 | tf_op jit(solution)/shard_map/pallas_call | solution.py:1080
  207.4 1.2 constant_dynamic-slice_fusion.1
  208.7 8.6 %collective-permute-done.4 = bf16[256,512]{1,0:T(8,128)(2,1)S(1)} collective-permute-done((bf16[256,512]{1,0:T(8,128)(2,1)S(1)}, bf16[256,512]{1,0:T(8,128)(2,1)S(1)}, u32[]{:S(2)}, u32[]{:S(2)}) %collective-permute-start.4) | collective-permute-done | bytes 262176 | tf_op jit(solution)/shard_map/ppermute | solution.py:386
  217.4 0.7 collective-permute-start.5
  218.1 2.7 collective-permute-start.6
  220.8 1.0 collective-permute-start.7
  221.9 19.5 %collective-permute-done.5 = bf16[256,1024]{1,0:T(8,128)(2,1)S(1)} collective-permute-done((bf16[256,1024]{1,0:T(8,128)(2,1)S(1)}, bf16[256,1024]{1,0:T(8,128)(2,1)S(1)}, u32[]{:S(2)}, u32[]{:S(2)}) %collective-permute-start.5) | collective-permute-done | bytes 524320 | tf_op jit(solution)/shard_map/ppermute | solution.py:386
  241.4 14.9 %collective-permute-done.6 = bf16[256,1024]{1,0:T(8,128)(2,1)S(1)} collective-permute-done((bf16[256,1024]{1,0:T(8,128)(2,1)S(1)}, bf16[256,1024]{1,0:T(8,128)(2,1)S(1)}, u32[]{:S(2)}, u32[]{:S(2)}) %collective-permute-start.6) | collective-permute-done | bytes 524320 | tf_op jit(solution)/shard_map/ppermute | solution.py:386
  256.3 2.1 pad_maximum_fusion.4
  258.7 0.7 collective-permute-start
  259.4 1.7 collective-permute-start.1
  261.1 3.2 collective-permute-start.2
  264.2 0.5 collective-permute-start.3
  264.8 0.5 constant_dynamic-update-slice_fusion.1
  265.3 1.7 copy-done
  266.9 0.5 constant_dynamic-update-slice_fusion
  267.5 22.7 %fusion.26 = f32[1024,2048]{1,0:T(8,128)} fusion(bf16[2048,2048]{1,0:T(8,128)(2,1)S(1)} %constant_dynamic-update-slice_fusion, bf16[1024,1024]{1,0:T(8,128)(2,1)S(1)} %collective-permute-done.8, bf16[256,1024]{1,0:T(8,128)(2,1)S(1)} %collective-permute-done.7, bf16[256,1024]{1,0:T(8,128)(2,1)S(1)} %collective-permute-done.6, ...), kind=kOutput, calls=%fused_computation.48 | convolution fusion | flops 8615100416 | bytes 20971520 | tf_op jit(solution)/shard_map/dot_general | solution.py:1733
  290.2 16.7 %collective-permute-done.3 = bf16[1024,512]{1,0:T(8,128)(2,1)S(1)} collective-permute-done((bf16[1024,512]{1,0:T(8,128)(2,1)S(1)}, bf16[1024,512]{1,0:T(8,128)(2,1)S(1)}, u32[]{:S(2)}, u32[]{:S(2)}) %collective-permute-start.3) | collective-permute-done | bytes 1048608 | tf_op jit(solution)/shard_map/ppermute | solution.py:386
  306.9 9.0 %multiply_convert_fusion.2 = (bf16[1024,1024]{1,0:T(8,128)(2,1)S(1)}, bf16[1024,1024]{1,0:T(8,128)(2,1)S(1)}) fusion(f32[1024,2048]{1,0:T(8,128)} %fusion.26, bf16[1024,2048]{1,0:T(8,128)(2,1)} %get-tuple-element.32, bf16[1024,512]{1,0:T(8,128)(2,1)S(1)} %collective-permute-done.3, bf16[1024,512]{1,0:T(8,128)(2,1)S(1)} %collective-permute-done.2, ...), kind=kOutput, calls=%fused_computation.19 | convolution fusion | flops 4325376000 | bytes 20971520 | tf_op jit(solution)/shard_map/dot_general | solution.py:1731
  315.9 5.9 fusion.15
  321.8 2.5 collective-permute-start.9
  324.5 4.0 collective-permute-done.9
  328.5 8.6 %fusion.31 = (bf16[1024,1024]{1,0:T(8,128)(2,1)S(1)}, f32[1024,1024]{1,0:T(8,128)S(1)}) fusion(bf16[1024,1024]{1,0:T(8,128)(2,1)} %collective-permute-done.9, bf16[2048,2048]{1,0:T(8,128)(2,1)} %copy-done.4, bf16[1024,1024]{1,0:T(8,128)(2,1)} %copy-done.17, bf16[1024,1024]{1,0:T(8,128)(2,1)} %copy-done.16), kind=kOutput, calls=%fused_computation.53 | convolution fusion | flops 4306501632 | bytes 16777216 | tf_op jit(solution)/shard_map/dot_general | solution.py:1747
  337.2 10.4 %collective-permute-start.10 = (bf16[256,1024]{1,0:T(8,128)(2,1)S(1)}, bf16[256,1024]{1,0:T(8,128)(2,1)S(1)}, u32[]{:S(2)}, u32[]{:S(2)}) collective-permute-start(bf16[256,1024]{1,0:T(8,128)(2,1)S(1)} %get-tuple-element.60), channel_id=1, source_target_pairs={{0,8},{1,9},{2,10},{3,11},{4,12},{5,13},{6,14},{7,15},{8,0},{9,1},... | collective-permute-start | bytes 1572872 | tf_op jit(solution)/shard_map/ppermute | solution.py:386
  347.7 1.0 collective-permute-start.11
  348.7 1.4 collective-permute-start.12
  350.1 8.7 %convolution_convert_fusion = bf16[1024,2048]{1,0:T(8,128)(2,1)S(1)} fusion(bf16[1024,2048]{1,0:T(8,128)(2,1)S(1)} %copy-done.15, f32[1024,2048]{1,0:T(8,128)} %fusion.26), kind=kOutput, calls=%fused_computation.21 | convolution fusion | flops 4303355904 | bytes 16777216 | tf_op jit(solution)/shard_map/dot_general | solution.py:1770
  359.3 0.9 collective-permute-start.17
  360.1 0.5 collective-permute-start.18
  360.6 10.2 %collective-permute-done.10 = bf16[256,1024]{1,0:T(8,128)(2,1)S(1)} collective-permute-done((bf16[256,1024]{1,0:T(8,128)(2,1)S(1)}, bf16[256,1024]{1,0:T(8,128)(2,1)S(1)}, u32[]{:S(2)}, u32[]{:S(2)}) %collective-permute-start.10) | collective-permute-done | bytes 524320 | tf_op jit(solution)/shard_map/ppermute | solution.py:386
  370.8 15.0 %collective-permute-done.11 = bf16[256,1024]{1,0:T(8,128)(2,1)S(1)} collective-permute-done((bf16[256,1024]{1,0:T(8,128)(2,1)S(1)}, bf16[256,1024]{1,0:T(8,128)(2,1)S(1)}, u32[]{:S(2)}, u32[]{:S(2)}) %collective-permute-start.11) | collective-permute-done | bytes 524320 | tf_op jit(solution)/shard_map/ppermute | solution.py:386
  386.2 0.5 collective-permute-start.13
  386.8 15.1 %pad_maximum_fusion.n2_hbm = bf16[1024,2048]{1,0:T(8,128)(2,1)} fusion(bf16[1024,1024]{1,0:T(8,128)(2,1)S(1)} %collective-permute-done.8, bf16[256,1024]{1,0:T(8,128)(2,1)S(1)} %copy-done.8, bf16[256,1024]{1,0:T(8,128)(2,1)S(1)} %copy-done.6, bf16[256,1024]{1,0:T(8,128)(2,1)S(1)} %collective-permute-done.5, bf16[256,512]{1,0:T(8,128)(2,1)S(1)} %collective-permute-done.4, ...), kind=kLoop, calls=%fused_computation.14 | loop fusion | flops 25165824 | bytes 8388608 | tf_op jit(solution)/shard_map/concatenate | solution.py:1727
  401.9 14.1 %collective-permute-done.13 = bf16[256,512]{1,0:T(8,128)(2,1)S(1)} collective-permute-done((bf16[256,512]{1,0:T(8,128)(2,1)S(1)}, bf16[256,512]{1,0:T(8,128)(2,1)S(1)}, u32[]{:S(2)}, u32[]{:S(2)}) %collective-permute-start.13) | collective-permute-done | bytes 262176 | tf_op jit(solution)/shard_map/ppermute | solution.py:386
  416.1 0.9 multiply_reduce_fusion
  417.0 1.6 collective-permute-start.14
  418.6 0.6 collective-permute-start.16
  419.2 1.9 convert_add_fusion.1
  421.0 0.6 collective-permute-done.16
  421.7 1.3 subtract_add_fusion.mid_ref
  423.0 227.1 %shard_map.196 = (f32[512,512]{1,0:T(8,128)}, f32[512,768]{1,0:T(8,128)}, f32[256,512]{1,0:T(8,128)}, f32[8,512]{1,0:T(8,128)}, bf16[2,3,512,1024]{3,2,1,0:T(8,128)(2,1)}, /*index=5*/bf16[2,2,512,1024]{3,2,1,0:T(8,128)(2,1)}) custom-call(bf16[512,512]{1,0:T(8,128)(2,1)} %x_ref.3, f32[1,512]{1,0:T(1,128)} %bitcast.17, f32[512,1]{1,0:T(8,128)} %get-tuple-element.30.scale_ref, ...), custom_call_target="tpu_custom_call" | custom-call | flops 15032385536 | bytes 67108864 | tf_op jit(solution)/shard_map/pallas_call | solution.py:1620
  650.1 4.3 convert_element_type.66
  654.4 1.9 slice_add_fusion
  656.4 2.3 slice_bitcast_fusion
  658.7 1.2 fusion.29
  659.9 1.4 fusion.30
  661.3 1.0 copy.30
  662.2 0.8 copy.31
  (62 shorter events, 1.5 us)
Async XLA Ops:
  207.4 51.1 %copy-start.3 = (f32[1024,512]{1,0:T(8,128)S(1)}, f32[1024,512]{1,0:T(8,128)}, u32[]{:S(2)}) copy-start(f32[1024,512]{1,0:T(8,128)} %param.21) | copy-start | bytes 6291460
  208.6 8.7 %collective-permute-start.4 = (bf16[256,512]{1,0:T(8,128)(2,1)S(1)}, bf16[256,512]{1,0:T(8,128)(2,1)S(1)}, u32[]{:S(2)}, u32[]{:S(2)}) collective-permute-start(bf16[256,512]{1,0:T(8,128)(2,1)S(1)} %get-tuple-element.67), channel_id=1, source_target_pairs={{0,2},{1,3},{2,0},{3,1},{4,6},{5,7},{6,4},{7,5},{8,10},{9,11},{10,... | collective-permute-start | bytes 786440 | tf_op jit(solution)/shard_map/ppermute | solution.py:386
  217.3 47.4 %copy-start.1 = (bf16[2048,1024]{1,0:T(8,128)(2,1)S(1)}, bf16[2048,1024]{1,0:T(8,128)(2,1)}, u32[]{:S(2)}) copy-start(bf16[2048,1024]{1,0:T(8,128)(2,1)} %get-tuple-element.34) | copy-start | bytes 12582916
  217.4 24.0 %collective-permute-start.5 = (bf16[256,1024]{1,0:T(8,128)(2,1)S(1)}, bf16[256,1024]{1,0:T(8,128)(2,1)S(1)}, u32[]{:S(2)}, u32[]{:S(2)}) collective-permute-start(bf16[256,1024]{1,0:T(8,128)(2,1)S(1)} %pad_maximum_fusion.9), channel_id=1, source_target_pairs={{0,8},{1,9},{2,10},{3,11},{4,12},{5,13},{6,14},{7,15},{8,0},{9,1},... | collective-permute-start | bytes 1572872 | tf_op jit(solution)/shard_map/ppermute | solution.py:386
  218.1 38.2 %collective-permute-start.6 = (bf16[256,1024]{1,0:T(8,128)(2,1)S(1)}, bf16[256,1024]{1,0:T(8,128)(2,1)S(1)}, u32[]{:S(2)}, u32[]{:S(2)}) collective-permute-start(bf16[256,1024]{1,0:T(8,128)(2,1)S(1)} %pad_maximum_fusion.9), channel_id=1, source_target_pairs={{0,16},{1,17},{2,18},{3,19},{4,20},{5,21},{6,22},{7,23},{8,24},{9,... | collective-permute-start | bytes 1572872 | tf_op jit(solution)/shard_map/ppermute | solution.py:386
  220.8 35.5 %collective-permute-start.7 = (bf16[256,1024]{1,0:T(8,128)(2,1)S(1)}, bf16[256,1024]{1,0:T(8,128)(2,1)S(1)}, u32[]{:S(2)}, u32[]{:S(2)}) collective-permute-start(bf16[256,1024]{1,0:T(8,128)(2,1)S(1)} %pad_maximum_fusion.9), channel_id=1, source_target_pairs={{0,24},{1,25},{2,26},{3,27},{4,28},{5,29},{6,30},{7,31},{8,16},{9,... | collective-permute-start | bytes 1572872 | tf_op jit(solution)/shard_map/ppermute | solution.py:386
  256.3 11.2 %copy-start.5 = (bf16[256,1024]{1,0:T(8,128)(2,1)}, bf16[256,1024]{1,0:T(8,128)(2,1)S(1)}, u32[]{:S(2)}) copy-start(bf16[256,1024]{1,0:T(8,128)(2,1)S(1)} %collective-permute-done.6) | copy-start | bytes 1572868
  256.3 11.2 %copy-start.7 = (bf16[256,1024]{1,0:T(8,128)(2,1)}, bf16[256,1024]{1,0:T(8,128)(2,1)S(1)}, u32[]{:S(2)}) copy-start(bf16[256,1024]{1,0:T(8,128)(2,1)S(1)} %collective-permute-done.7) | copy-start | bytes 1572868
  258.4 9.0 %collective-permute-start.8 = (bf16[1024,1024]{1,0:T(8,128)(2,1)S(1)}, bf16[1024,1024]{1,0:T(8,128)(2,1)S(1)}, u32[]{:S(2)}, u32[]{:S(2)}) collective-permute-start(bf16[1024,1024]{1,0:T(8,128)(2,1)S(1)} %pad_maximum_fusion.4), channel_id=1, source_target_pairs={{0,1},{1,0},{2,3},{3,2},{4,5},{5,4},{6,7},{7,6},{8,9},{9,8},{10,11... | collective-permute-start | bytes 6291464 | tf_op jit(solution)/shard_map/ppermute | solution.py:386
  258.7 31.5 %collective-permute-start = (bf16[1024,512]{1,0:T(8,128)(2,1)S(1)}, bf16[1024,512]{1,0:T(8,128)(2,1)S(1)}, u32[]{:S(2)}, u32[]{:S(2)}) collective-permute-start(bf16[1024,512]{1,0:T(8,128)(2,1)S(1)} %convert_element_type.56), channel_id=1, source_target_pairs={{0,0},{1,5},{2,2},{3,7},{4,4},{5,1},{6,6},{7,3},{8,8},{9,13},{10,1... | collective-permute-start | bytes 3145736 | tf_op jit(solution)/shard_map/ppermute | solution.py:386
  259.4 30.8 %collective-permute-start.1 = (bf16[1024,512]{1,0:T(8,128)(2,1)S(1)}, bf16[1024,512]{1,0:T(8,128)(2,1)S(1)}, u32[]{:S(2)}, u32[]{:S(2)}) collective-permute-start(bf16[1024,512]{1,0:T(8,128)(2,1)S(1)} %convert_element_type.56), channel_id=1, source_target_pairs={{0,2},{1,7},{2,0},{3,5},{4,6},{5,3},{6,4},{7,1},{8,10},{9,15},{10,... | collective-permute-start | bytes 3145736 | tf_op jit(solution)/shard_map/ppermute | solution.py:386
  261.1 29.1 %collective-permute-start.2 = (bf16[1024,512]{1,0:T(8,128)(2,1)S(1)}, bf16[1024,512]{1,0:T(8,128)(2,1)S(1)}, u32[]{:S(2)}, u32[]{:S(2)}) collective-permute-start(bf16[1024,512]{1,0:T(8,128)(2,1)S(1)} %convert_element_type.56), channel_id=1, source_target_pairs={{0,5},{1,0},{2,7},{3,2},{4,1},{5,4},{6,3},{7,6},{8,13},{9,8},{10,1... | collective-permute-start | bytes 3145736 | tf_op jit(solution)/shard_map/ppermute | solution.py:386
  264.2 42.7 %collective-permute-start.3 = (bf16[1024,512]{1,0:T(8,128)(2,1)S(1)}, bf16[1024,512]{1,0:T(8,128)(2,1)S(1)}, u32[]{:S(2)}, u32[]{:S(2)}) collective-permute-start(bf16[1024,512]{1,0:T(8,128)(2,1)S(1)} %convert_element_type.56), channel_id=1, source_target_pairs={{0,7},{1,2},{2,5},{3,0},{4,3},{5,6},{6,1},{7,4},{8,15},{9,10},{10,... | collective-permute-start | bytes 3145736 | tf_op jit(solution)/shard_map/ppermute | solution.py:386
  264.8 2.2 copy-start
  267.4 48.5 %copy-start.4 = (bf16[2048,2048]{1,0:T(8,128)(2,1)}, bf16[2048,2048]{1,0:T(8,128)(2,1)S(1)}, u32[]{:S(2)}) copy-start(bf16[2048,2048]{1,0:T(8,128)(2,1)S(1)} %constant_dynamic-update-slice_fusion) | copy-start | bytes 25165828
  315.9 5.9 copy-start.16
  315.9 5.9 copy-start.17
  315.9 8.5 %copy-start.13 = (f32[512,1]{1,0:T(8,128)S(1)}, f32[512,1]{1,0:T(8,128)}, u32[]{:S(2)}) copy-start(f32[512,1]{1,0:T(8,128)} %get-tuple-element.31) | copy-start | bytes 6148
  321.8 6.7 %collective-permute-start.9 = (bf16[1024,1024]{1,0:T(8,128)(2,1)}, bf16[1024,1024]{1,0:T(8,128)(2,1)}, u32[]{:S(2)}, u32[]{:S(2)}) collective-permute-start(bf16[1024,1024]{1,0:T(8,128)(2,1)} %fusion.15), channel_id=1, source_target_pairs={{0,1},{1,0},{2,3},{3,2},{4,5},{5,4},{6,7},{7,6},{8,9},{9,8},{10,11... | collective-permute-start | bytes 6291464 | tf_op jit(solution)/shard_map/ppermute | solution.py:386
  324.5 25.6 %copy-start.15 = (bf16[1024,2048]{1,0:T(8,128)(2,1)S(1)}, bf16[1024,2048]{1,0:T(8,128)(2,1)}, u32[]{:S(2)}) copy-start(bf16[1024,2048]{1,0:T(8,128)(2,1)} %get-tuple-element.32) | copy-start | bytes 12582916
  337.2 33.6 %collective-permute-start.10 = (bf16[256,1024]{1,0:T(8,128)(2,1)S(1)}, bf16[256,1024]{1,0:T(8,128)(2,1)S(1)}, u32[]{:S(2)}, u32[]{:S(2)}) collective-permute-start(bf16[256,1024]{1,0:T(8,128)(2,1)S(1)} %get-tuple-element.60), channel_id=1, source_target_pairs={{0,8},{1,9},{2,10},{3,11},{4,12},{5,13},{6,14},{7,15},{8,0},{9,1},... | collective-permute-start | bytes 1572872 | tf_op jit(solution)/shard_map/ppermute | solution.py:386
  347.7 38.2 %collective-permute-start.11 = (bf16[256,1024]{1,0:T(8,128)(2,1)S(1)}, bf16[256,1024]{1,0:T(8,128)(2,1)S(1)}, u32[]{:S(2)}, u32[]{:S(2)}) collective-permute-start(bf16[256,1024]{1,0:T(8,128)(2,1)S(1)} %get-tuple-element.62), channel_id=1, source_target_pairs={{0,16},{1,17},{2,18},{3,19},{4,20},{5,21},{6,22},{7,23},{8,24},{9,... | collective-permute-start | bytes 1572872 | tf_op jit(solution)/shard_map/ppermute | solution.py:386
  348.7 37.2 %collective-permute-start.12 = (bf16[256,1024]{1,0:T(8,128)(2,1)S(1)}, bf16[256,1024]{1,0:T(8,128)(2,1)S(1)}, u32[]{:S(2)}, u32[]{:S(2)}) collective-permute-start(bf16[256,1024]{1,0:T(8,128)(2,1)S(1)} %get-tuple-element.61), channel_id=1, source_target_pairs={{0,24},{1,25},{2,26},{3,27},{4,28},{5,29},{6,30},{7,31},{8,16},{9,... | collective-permute-start | bytes 1572872 | tf_op jit(solution)/shard_map/ppermute | solution.py:386
  359.2 27.5 %copy-start.6 = (bf16[256,1024]{1,0:T(8,128)(2,1)S(1)}, bf16[256,1024]{1,0:T(8,128)(2,1)}, u32[]{:S(2)}) copy-start(bf16[256,1024]{1,0:T(8,128)(2,1)} %copy-done.5) | copy-start | bytes 1572868
  359.2 27.5 %copy-start.8 = (bf16[256,1024]{1,0:T(8,128)(2,1)S(1)}, bf16[256,1024]{1,0:T(8,128)(2,1)}, u32[]{:S(2)}) copy-start(bf16[256,1024]{1,0:T(8,128)(2,1)} %copy-done.7) | copy-start | bytes 1572868
  359.3 59.3 %collective-permute-start.17 = (bf16[1024,512]{1,0:T(8,128)(2,1)S(1)}, bf16[1024,512]{1,0:T(8,128)(2,1)S(1)}, u32[]{:S(2)}, u32[]{:S(2)}) collective-permute-start(bf16[1024,512]{1,0:T(8,128)(2,1)S(1)} %get-tuple-element.54), channel_id=1, source_target_pairs={{0,0},{1,5},{2,2},{3,7},{4,4},{5,1},{6,6},{7,3},{8,8},{9,13},{10,1... | collective-permute-start | bytes 3145736 | tf_op jit(solution)/shard_map/ppermute | solution.py:386
  360.1 58.5 %collective-permute-start.18 = (bf16[1024,512]{1,0:T(8,128)(2,1)S(1)}, bf16[1024,512]{1,0:T(8,128)(2,1)S(1)}, u32[]{:S(2)}, u32[]{:S(2)}) collective-permute-start(bf16[1024,512]{1,0:T(8,128)(2,1)S(1)} %get-tuple-element.57), channel_id=1, source_target_pairs={{0,2},{1,7},{2,0},{3,5},{4,6},{5,3},{6,4},{7,1},{8,10},{9,15},{10,... | collective-permute-start | bytes 3145736 | tf_op jit(solution)/shard_map/ppermute | solution.py:386
  370.8 48.3 %collective-permute-start.19 = (bf16[1024,512]{1,0:T(8,128)(2,1)S(1)}, bf16[1024,512]{1,0:T(8,128)(2,1)S(1)}, u32[]{:S(2)}, u32[]{:S(2)}) collective-permute-start(bf16[1024,512]{1,0:T(8,128)(2,1)S(1)} %get-tuple-element.56), channel_id=1, source_target_pairs={{0,1},{1,4},{2,3},{3,6},{4,5},{5,0},{6,7},{7,2},{8,9},{9,12},{10,1... | collective-permute-start | bytes 3145736 | tf_op jit(solution)/shard_map/ppermute | solution.py:386
  385.9 33.3 %collective-permute-start.20 = (bf16[1024,512]{1,0:T(8,128)(2,1)S(1)}, bf16[1024,512]{1,0:T(8,128)(2,1)S(1)}, u32[]{:S(2)}, u32[]{:S(2)}) collective-permute-start(bf16[1024,512]{1,0:T(8,128)(2,1)S(1)} %get-tuple-element.55), channel_id=1, source_target_pairs={{0,3},{1,6},{2,1},{3,4},{4,7},{5,2},{6,5},{7,0},{8,11},{9,14},{10,... | collective-permute-start | bytes 3145736 | tf_op jit(solution)/shard_map/ppermute | solution.py:386
  386.2 29.8 %copy-start.2 = (f32[512,512]{1,0:T(8,128)S(1)}, f32[512,512]{1,0:T(8,128)}, u32[]{:S(2)}) copy-start(f32[512,512]{1,0:T(8,128)} %get-tuple-element.36) | copy-start | bytes 3145732
  386.2 29.8 %copy-start.14 = (f32[512]{0:T(512)S(1)}, f32[512]{0:T(512)}, u32[]{:S(2)}) copy-start(f32[512]{0:T(512)} %param.23) | copy-start | bytes 6148
  386.2 29.7 %collective-permute-start.13 = (bf16[256,512]{1,0:T(8,128)(2,1)S(1)}, bf16[256,512]{1,0:T(8,128)(2,1)S(1)}, u32[]{:S(2)}, u32[]{:S(2)}) collective-permute-start(bf16[256,512]{1,0:T(8,128)(2,1)S(1)} %slice.147), channel_id=1, source_target_pairs={{0,2},{1,3},{2,0},{3,1},{4,6},{5,7},{6,4},{7,5},{8,10},{9,11},{10,... | collective-permute-start | bytes 786440 | tf_op jit(solution)/shard_map/ppermute | solution.py:386
  416.0 5.6 copy-start.12
  417.0 4.0 collective-permute-start.14
  418.6 2.4 collective-permute-start.15
  418.6 3.1 collective-permute-start.16
  656.4 2.3 copy-start.9
  656.4 4.9 copy-start.10
  658.7 3.5 copy-start.11

commit v4 on v3

--- a/solution.py
+++ b/solution.py
@@ -374,202 +374,10 @@
     )
 
 
-def move(array, to):
-    pairs = []
-    for d in range(DP):
-        for r in range(ROW):
-            for c in range(COL):
-                target = to(d, r, c)
-                if target is not None:
-                    e, s, b = target
-                    pairs.append(((d * ROW + r) * COL + c, (e * ROW + s) * COL + b))
-    return lax.ppermute(array, AXES, pairs)
-
-
-def by_col(array, step):
-    return move(array, lambda d, r, c: (d, r, c ^ step))
-
-
-def by_plane(array, step):
-    return move(array, lambda d, r, c: (d ^ step, r, c))
-
-
-def by_chip(array, over_x, over_y):
-    return move(array, lambda d, r, c: (d, r ^ over_x, c ^ (2 * over_y)))
-
-
-def col_sum(values):
-    return values + by_col(values, 2) + by_col(values, 1) + by_col(values, 3)
-
-
-def same_sum(values):
-    for step in (1, 2):
-        values = values + by_plane(values, step)
-    return values + by_chip(values, 1, 0)
-
-
-def plane_gather(block):
-    beside = by_chip(block, 1, 0)
-    across = by_chip(block, 0, 1)
-    corner = by_chip(block, 1, 1)
-    rail = jnp.concatenate(
-        [jnp.concatenate([block, across], 1), jnp.concatenate([beside, corner], 1)], 0
-    )
-    return jnp.concatenate([rail, by_col(rail, 1)], 1)
-
-
-def plane_scatter(left, weight, contract):
-    rows = left.shape[0] // 2
-    half = D // 2
-    numbers = (((1,), (contract,)), ((), ()))
-    kept, given = (weight[:, :half], weight[:, half:]) if contract == 0 else (weight[:half], weight[half:])
-    theirs = lax.dot_general(left, given, numbers, preferred_element_type=F32).astype(BF)
-    arrived = by_col(theirs, 1)
-    mine = lax.dot_general(left, kept, numbers, preferred_element_type=F32)
-    mine = mine + arrived.astype(F32)
-    low = mine.astype(BF)
-    part = half // 2
-    return (
-        mine[:rows, :part]
-        + by_chip(low[rows:, :part], 1, 0).astype(F32)
-        + by_chip(low[:rows, part:], 0, 1).astype(F32)
-        + by_chip(low[rows:, part:], 1, 1).astype(F32)
-    )
-
-
-def hidden_from(step):
-    def to(d, s, c):
-        b = c ^ step
-        return (d, s ^ (b & 1), b)
-
-    return to
-
-
-def hidden_back(step):
-    def to(d, r, c):
-        return (d, r ^ (c & 1), c ^ step)
-
-    return to
-
-
-def begins_of(lengths, first, amount):
-    ends = running_sum(lengths)
-    place = first + jnp.arange(amount, dtype=jnp.int32)
-    passed = ends[None, :] <= place[:, None]
-    return jnp.max(jnp.where(passed, ends[None, :], 0), axis=1)
-
-
-def seen(begin_ref, block, rows, span):
-    query = lax.broadcasted_iota(jnp.int32, (rows, span), 0)
-    key = lax.broadcasted_iota(jnp.int32, (rows, span), 1)
-    begin = begin_ref[:, 0:1] + (REACH - block * rows)
-    return (key <= query + REACH) & (key >= begin)
-
-
 def scores_of(query, key):
     return lax.dot_general(
         query, key, (((1,), (1,)), ((), ())), preferred_element_type=F32
     ) * HEAD_DIM ** (-0.5)
-
-
-def attend_kernel(begin_ref, q_ref, k_ref, v_ref, o_ref, lse_ref):
-    block = pl.program_id(1)
-    rows = q_ref.shape[0]
-    span = rows + REACH
-    window = pl.ds(pl.multiple_of(block * rows, rows), span)
-    scores = scores_of(q_ref[...], k_ref[window, :])
-    scores = jnp.where(seen(begin_ref, block, rows, span), scores, NEG_FILL)
-    highest = jnp.max(scores, axis=1, keepdims=True)
-    expo = jnp.exp(scores - highest)
-    total = jnp.sum(expo, axis=1, keepdims=True)
-    probability = (expo * (1.0 / total)).astype(BF)
-    o_ref[...] = jnp.dot(probability, v_ref[window, :], preferred_element_type=F32).astype(BF)
-    lse_ref[...] = jnp.broadcast_to(highest + jnp.log(total), lse_ref.shape)
-
-
-def attend_back_kernel(
-    begin_ref, q_ref, k_ref, v_ref, do_ref, lse_ref, dq_ref, dk_ref, dv_ref
-):
-    block = pl.program_id(1)
-    rows = q_ref.shape[0]
-    span = rows + REACH
-    window = pl.ds(pl.multiple_of(block * rows, rows), span)
-
-    @pl.when(block == 0)
-    def _():
-        dk_ref[...] = jnp.zeros_like(dk_ref)
-        dv_ref[...] = jnp.zeros_like(dv_ref)
-
-    query, key = q_ref[...], k_ref[window, :]
-    grad = do_ref[...]
-    scores = scores_of(query, key)
-    allowed = seen(begin_ref, block, rows, span)
-    probability = jnp.where(allowed, jnp.exp(jnp.where(allowed, scores - lse_ref[:, 0:1], 0.0)), 0.0)
-    grad_soft = lax.dot_general(
-        grad, v_ref[window, :], (((1,), (1,)), ((), ())), preferred_element_type=F32
-    )
-    inner = jnp.sum(probability * grad_soft, axis=1, keepdims=True)
-    grad_scores = (probability * (grad_soft - inner)).astype(BF)
-    scale = HEAD_DIM ** (-0.5)
-    dq_ref[...] = (jnp.dot(grad_scores, key, preferred_element_type=F32) * scale).astype(BF)
-    over = (((0,), (0,)), ((), ()))
-    dk_ref[window, :] += lax.dot_general(grad_scores, query, over, preferred_element_type=F32) * scale
-    dv_ref[window, :] += lax.dot_general(
-        probability.astype(BF), grad, over, preferred_element_type=F32
-    )
-
-
-QROWS = 256
-
-
-def attention_specs(rows, width):
-    by_block = pl.BlockSpec((QROWS, HEAD_DIM), lambda h, i: (i, h))
-    whole = pl.BlockSpec((rows + REACH, HEAD_DIM), lambda h, i: (0, h))
-    begin = pl.BlockSpec((QROWS, 1), lambda h, i: (i, 0))
-    grid = (width // HEAD_DIM, rows // QROWS)
-    params = pltpu.CompilerParams(vmem_limit_bytes=40 << 20)
-    return grid, by_block, whole, begin, params
-
-
-def attend(begin, q, k, v):
-    rows, width = q.shape
-    grid, by_block, whole, begin_spec, params = attention_specs(rows, width)
-    area = grid[0] * rows * (QROWS + REACH)
-    return pl.pallas_call(
-        attend_kernel,
-        grid=grid,
-        in_specs=[begin_spec, by_block, whole, whole],
-        out_specs=[by_block, by_block],
-        out_shape=[
-            jax.ShapeDtypeStruct((rows, width), BF),
-            jax.ShapeDtypeStruct((rows, width), F32),
-        ],
-        compiler_params=params,
-        cost_estimate=pl.CostEstimate(
-            flops=4 * area * HEAD_DIM, bytes_accessed=8 * rows * width, transcendentals=area
-        ),
-    )(begin, q, k, v)
-
-
-def attend_back(begin, q, k, v, grad, lse):
-    rows, width = q.shape
-    grid, by_block, whole, begin_spec, params = attention_specs(rows, width)
-    area = grid[0] * rows * (QROWS + REACH)
-    return pl.pallas_call(
-        attend_back_kernel,
-        grid=grid,
-        in_specs=[begin_spec, by_block, whole, whole, by_block, by_block],
-        out_specs=[by_block, whole, whole],
-        out_shape=[
-            jax.ShapeDtypeStruct((rows, width), BF),
-            jax.ShapeDtypeStruct((rows + REACH, width), F32),
-            jax.ShapeDtypeStruct((rows + REACH, width), F32),
-        ],
-        compiler_params=params,
-        cost_estimate=pl.CostEstimate(
-            flops=10 * area * HEAD_DIM, bytes_accessed=24 * rows * width, transcendentals=area
-        ),
-    )(begin, q, k, v, grad, lse)
 
 
 MESH = pl.DeviceIdType.MESH
@@ -639,70 +447,6 @@
     in_plane = [(d, r ^ a, c ^ b) for a in (0, 1) for b in range(COL) if (a, b) != (0, 0)]
     greet([(d ^ j, r, c) for j in (1, 2, 3)] + in_plane)
 
-    first = post.take(DP)
-
-    def line(p, target_plane):
-        return post.ready(zin.at[p], zin.at[p], (target_plane, r, c), first + p)
-
-    first_down = post.take(DP)
-
-    def line_down(p, target_plane):
-        return pltpu.make_async_remote_copy(
-            src_ref=zin.at[p], dst_ref=zin.at[p],
-            send_sem=send_sem.at[first_down + p], recv_sem=recv_sem.at[first + p],
-            device_id=(target_plane, r, c), device_id_type=MESH,
-        )
-
-    def cast_rows(src, dst, amount, step=64):
-        def one(t, total):
-            part = pl.ds(pl.multiple_of(t * step, step), step)
-            dst(part, src[part, :].astype(BF))
-            return total
-
-        lax.fori_loop(0, amount // step, one, 0)
-
-    for place, master in enumerate((query_ref, key_ref, value_ref)):
-        def put(part, value, place=place):
-            zin[d, part, place * width : (place + 1) * width] = value
-
-        cast_rows(master, put, fc)
-
-    @pl.when(d < DP - 1)
-    def _():
-        line(d, d + 1).start()
-
-    @pl.when(d > 0)
-    def _():
-        line_down(d, d - 1).start()
-
-    first_cols = post.take(DP)
-    first_keep = 1
-
-    def to_column(p):
-        return pltpu.make_async_remote_copy(
-            src_ref=zin.at[p],
-            dst_ref=weight_in.at[pl.ds(pl.multiple_of(place_of(p ^ c) * fc, fc), fc), :],
-            send_sem=send_sem.at[first_cols + p],
-            recv_sem=recv_sem.at[first_cols + (p ^ c)],
-            device_id=(d, r, p), device_id_type=MESH,
-        )
-
-    def place_of(m):
-        return lax.rem(m, 2) * 2 + m // 2
-
-    keep = pltpu.make_async_copy(zin.at[c], weight_in.at[pl.ds(0, fc), :], local_sem.at[first_keep])
-
-    def pass_on(p):
-        @pl.when(p == c)
-        def _():
-            keep.start()
-
-        @pl.when(p != c)
-        def _():
-            to_column(p).start()
-
-    pass_on(d)
-
     def fill_x(t, total):
         part = pl.ds(pl.multiple_of(t * 128, 128), 128)
         value = x_ref[part, :].astype(F32)
@@ -712,23 +456,129 @@
 
     lax.fori_loop(0, rows // 128, fill_x, 0)
     small = [post.send(sums.at[0], sums.at[m], (d, r, c ^ m)) for m in (1, 2, 3)]
-    half_rows = rows // 2
-    grad_cross = post.send(
-        own_grad.at[pl.ds(pl.multiple_of((1 - y) * half_rows, half_rows), half_rows), :],
-        grad_all.at[pl.ds(0, half_rows), pl.ds(fc, fc)],
-        (d, r, c ^ 2),
-    )
-    grad_keep = pltpu.make_async_copy(
-        own_grad.at[pl.ds(pl.multiple_of(y * half_rows, half_rows), half_rows), :],
-        grad_all.at[pl.ds(0, half_rows), pl.ds(0, fc)],
-        local_sem.at[2],
-    )
-    grad_keep.start()
-    for kind, master in enumerate((gate_ref, up_ref)):
-        def put(part, value, kind=kind):
+
+    parts = (pl.ds(width, 2 * width), pl.ds(0, width))
+    first, first_down = post.take(2 * DP), post.take(2 * DP)
+
+    def line(n, p, target_plane):
+        block = zin.at[p, :, parts[n]]
+        return post.ready(block, block, (target_plane, r, c), first + DP * n + p)
+
+    def line_down(n, p, target_plane):
+        block = zin.at[p, :, parts[n]]
+        return pltpu.make_async_remote_copy(
+            src_ref=block, dst_ref=block,
+            send_sem=send_sem.at[first_down + DP * n + p], recv_sem=recv_sem.at[first + DP * n + p],
+            device_id=(target_plane, r, c), device_id_type=MESH,
+        )
+
+    def cast_rows(src, dst, amount, step=64):
+        def one(t, total):
+            part = pl.ds(pl.multiple_of(t * step, step), step)
+            dst(part, src[part, :].astype(BF))
+            return total
+
+        lax.fori_loop(0, amount // step, one, 0)
+
+    for place, master in enumerate((query_ref, key_ref, value_ref)):
+        def put(part, value, place=place):
+            zin[d, part, place * width : (place + 1) * width] = value
+
+        cast_rows(master, put, fc)
+    for n in (0, 1):
+        @pl.when(d < DP - 1)
+        def _(n=n):
+            line(n, d, d + 1).start()
+
+        @pl.when(d > 0)
+        def _(n=n):
+            line_down(n, d, d - 1).start()
+
+    first_cols = post.take(2 * DP)
+
+    def place_of(m):
+        return lax.rem(m, 2) * 2 + m // 2
+
+    def to_column(n, p):
+        there = pl.ds(pl.multiple_of(place_of(p ^ c) * fc, fc), fc)
+        return pltpu.make_async_remote_copy(
+            src_ref=zin.at[p, :, parts[n]],
+            dst_ref=weight_in.at[there, parts[n]],
+            send_sem=send_sem.at[first_cols + DP * n + p],
+            recv_sem=recv_sem.at[first_cols + DP * n + (p ^ c)],
+            device_id=(d, r, p), device_id_type=MESH,
+        )
+
+    def keep(n):
+        return pltpu.make_async_copy(
+            zin.at[c, :, parts[n]], weight_in.at[pl.ds(0, fc), parts[n]], local_sem.at[n]
+        )
+
+    def pass_on(n, p):
+        @pl.when(p == c)
+        def _():
+            keep(n).start()
+
+        @pl.when(p != c)
+        def _():
+            to_column(n, p).start()
+
+    hidden_all = (gate_all, up_all)
+    first_sent = post.take(10)
+    first_got = first_sent
+
+    def slab(kind, i):
+        return hidden_all[kind].at[pl.ds(pl.multiple_of(place_of(i) * fc, fc), fc), :]
+
+    def ship(kind, way, i, target, src=None):
+        return pltpu.make_async_remote_copy(
+            src_ref=hidden_own.at[kind] if src is None else src,
+            dst_ref=slab(kind, i),
+            send_sem=send_sem.at[first_sent + 5 * kind + way],
+            recv_sem=recv_sem.at[first_got + 4 * kind + i],
+            device_id=target, device_id_type=MESH,
+        )
+
+    def keep_hidden(kind):
+        return pltpu.make_async_copy(hidden_own.at[kind], slab(kind, 0), local_sem.at[3 + kind])
+
+    def to_core(kind):
+        return ship(kind, 0, 1, (d, r, c ^ 1))
+
+    def over_y(kind):
+        return ship(kind, 1, 2 + core, (d, r, 2 * (1 - y)))
+
+    def over_x(kind):
+        return ship(kind, 2, 1 - core, (d, r ^ 1, 2 * y + 1))
+
+    def relay(kind, i):
+        return ship(kind, i + 1, 5 - i, (d, r ^ 1, 2 * y + 1), slab(kind, i))
+
+    def start_home(kind):
+        @pl.when(core == 0)
+        def _():
+            keep_hidden(kind).start()
+
+        @pl.when(core == 1)
+        def _():
+            to_core(kind).start()
+
+    def start_relay(kind):
+        @pl.when(core == 0)
+        def _():
+            for i in (2, 3):
+                ship(kind, 0, i, (d, r, c)).wait_recv()
+                relay(kind, i).start()
+
+    def cast_hidden(kind):
+        def put(part, value):
             hidden_own[kind, part, :] = value
 
-        cast_rows(master, put, fc)
+        cast_rows((gate_ref, up_ref)[kind], put, fc)
+
+    cast_hidden(0)
+    over_x(0).start()
+    over_y(0).start()
     for copy in small:
         copy.wait_recv()
 
@@ -752,59 +602,25 @@
     corner = post.send(own_block, normed_ref.at[other_rows, columns(1)], (d, r ^ 1, c ^ 2))
     sibling = (d, r, c ^ 1)
     shared = [post.send(own_block, normed_ref.at[own_rows, columns(2)], sibling)]
-
-    hidden_all = (gate_all, up_all)
-    first_sent = post.take(10)
-    first_got = first_sent
-
-    def slab(kind, i):
-        return hidden_all[kind].at[pl.ds(pl.multiple_of(place_of(i) * fc, fc), fc), :]
-
-    def ship(kind, way, i, target, src=None):
-        return pltpu.make_async_remote_copy(
-            src_ref=hidden_own.at[kind] if src is None else src,
-            dst_ref=slab(kind, i),
-            send_sem=send_sem.at[first_sent + 5 * kind + way],
-            recv_sem=recv_sem.at[first_got + 4 * kind + i],
-            device_id=target, device_id_type=MESH,
-        )
-
-    def keep_hidden(kind):
-        return pltpu.make_async_copy(hidden_own.at[kind], slab(kind, 0), local_sem.at[3 + kind])
-
-    def to_core(kind):
-        return ship(kind, 0, 1, (d, r, c ^ 1))
-
-    def over_y(kind):
-        return ship(kind, 1, 2 + core, (d, r, 2 * (1 - y)))
-
-    def over_x(kind):
-        return ship(kind, 2, 1 - core, (d, r ^ 1, 2 * y + 1))
-
-    def relay(kind, i):
-        return ship(kind, i + 1, 5 - i, (d, r ^ 1, 2 * y + 1), slab(kind, i))
-
-    def start_home(kind):
-        over_x(kind).start()
-
-        @pl.when(core == 0)
-        def _():
-            keep_hidden(kind).start()
-
-        @pl.when(core == 1)
-        def _():
-            to_core(kind).start()
-
-    def start_relay(kind):
-        @pl.when(core == 0)
-        def _():
-            for i in (2, 3):
-                ship(kind, 0, i, (d, r, c)).wait_recv()
-                relay(kind, i).start()
-
-    over_y(0).start()
+    pass_on(0, d)
+    pass_on(1, d)
+    cast_hidden(1)
     start_home(0)
     start_home(1)
+    over_x(1).start()
+    half_rows = rows // 2
+    grad_cross = post.send(
+        own_grad.at[pl.ds(pl.multiple_of((1 - y) * half_rows, half_rows), half_rows), :],
+        grad_all.at[pl.ds(0, half_rows), pl.ds(fc, fc)],
+        (d, r, c ^ 2),
+    )
+    grad_keep = pltpu.make_async_copy(
+        own_grad.at[pl.ds(pl.multiple_of(y * half_rows, half_rows), half_rows), :],
+        grad_all.at[pl.ds(0, half_rows), pl.ds(0, fc)],
+        local_sem.at[2],
+    )
+    grad_keep.start()
+
     def put_out(part, value):
         zout[0, part, :] = value
 
@@ -824,42 +640,45 @@
     lax.fori_loop(0, group // 128, find_begins, 0)
 
     def line_step(s):
-        for p, valid, onward, forward in (
-            (d - s, d - s >= 0, d < DP - 1, lambda p: line(p, d + 1)),
-            (d + s, d + s < DP, d > 0, lambda p: line_down(p, d - 1)),
-        ):
-            @pl.when(valid)
-            def _(p=p, onward=onward, forward=forward):
-                line(p, d).wait_recv()
-
-                @pl.when(onward)
-                def _():
-                    forward(p).start()
-
-                pass_on(p)
+        for n in (0, 1):
+            for p, valid, onward, forward in (
+                (d - s, d - s >= 0, d < DP - 1, lambda n, p: line(n, p, d + 1)),
+                (d + s, d + s < DP, d > 0, lambda n, p: line_down(n, p, d - 1)),
+            ):
+                @pl.when(valid)
+                def _(n=n, p=p, onward=onward, forward=forward):
+                    line(n, p, d).wait_recv()
+
+                    @pl.when(onward)
+                    def _():
+                        forward(n, p).start()
+
+                    pass_on(n, p)
 
     line_step(1)
+    line_step(2)
+    outs = [post.send(zout.at[0], zout.at[j], (d ^ j, r, c)) for j in (1, 2, 3)]
+    over_y(1).start()
     for copy, where, place in ((beside, other_rows, 0), (beyond, own_rows, 1), (corner, other_rows, 1)):
         copy.wait_recv()
         shared.append(
             post.send(normed_ref.at[where, columns(place)], normed_ref.at[where, columns(place + 2)], sibling)
         )
-
-    line_step(2)
     line_step(3)
-    outs = [post.send(zout.at[0], zout.at[j], (d ^ j, r, c)) for j in (1, 2, 3)]
     start_relay(0)
+
+    def arrived_blocks(n):
+        keep(n).wait()
+        for m in (1, 2, 3):
+            pltpu.make_async_remote_copy(
+                src_ref=zin.at[0, :, parts[n]], dst_ref=weight_in.at[pl.ds(0, fc), parts[n]],
+                send_sem=send_sem.at[first_cols], recv_sem=recv_sem.at[first_cols + DP * n + m],
+                device_id=(d, r, c), device_id_type=MESH,
+            ).wait_recv()
 
     for copy in shared:
         copy.wait_recv()
-    keep.wait()
-    for m in (1, 2, 3):
-        pltpu.make_async_remote_copy(
-            src_ref=zin.at[0], dst_ref=weight_in.at[pl.ds(0, fc), :],
-            send_sem=send_sem.at[first_cols], recv_sem=recv_sem.at[first_cols + m],
-            device_id=(d, r, c), device_id_type=MESH,
-        ).wait_recv()
-    over_y(1).start()
+    arrived_blocks(0)
 
     def turned(t):
         return lax.rem(t + 2 * r, group // TILE)
@@ -878,6 +697,8 @@
     @pl.when(d < DP - 1)
     def _():
         halo.start()
+
+    arrived_blocks(1)
 
     def project_q(t, total):
         part = pl.ds(pl.multiple_of(t * TILE, TILE), TILE)
@@ -948,7 +769,6 @@
             return total
 
         lax.fori_loop(0, group // TILE, one, 0)
-    start_relay(1)
 
     for copy in out_cols:
         copy.wait_recv()
@@ -985,6 +805,7 @@
         post.send(low.at[other_rows, columns(0)], landed.at[0], (d, r ^ 1, c)),
         post.send(low.at[own_rows, columns(1)], landed.at[1], (d, r, c ^ 2)),
     ]
+    start_relay(1)
     for copy in pieces:
         copy.wait_recv()
 
@@ -1048,21 +869,22 @@
     def _():
         halo.wait_send()
 
-    for p in range(DP):
-        @pl.when((d < DP - 1) & (p <= d))
-        def _(p=p):
-            line(p, d).wait_send()
-
-        @pl.when((d > 0) & (p >= d))
-        def _(p=p):
-            line_down(p, d).wait_send()
-
-        @pl.when(c != p)
-        def _(p=p):
-            to_column(p).wait_send()
-
-
-SENDS = 64
+    for n in (0, 1):
+        for p in range(DP):
+            @pl.when((d < DP - 1) & (p <= d))
+            def _(n=n, p=p):
+                line(n, p, d).wait_send()
+
+            @pl.when((d > 0) & (p >= d))
+            def _(n=n, p=p):
+                line_down(n, p, d).wait_send()
+
+            @pl.when(c != p)
+            def _(n=n, p=p):
+                to_column(n, p).wait_send()
+
+
+SENDS = 80
 
 
 def forward(x, gain_one, gain_two, lengths, query, key, value, out, gate, up, own_grad):
@@ -1122,6 +944,564 @@
     )(x, gain_one, gain_two, lengths, query, key, value, out, gate, up, own_grad)
 
 
+def at(t, size):
+    return pl.ds(pl.multiple_of(t * size, size), size)
+
+
+def loop(count, body):
+    def one(t, total):
+        body(t)
+        return total
+
+    lax.fori_loop(0, count, one, 0)
+
+
+def maker(send_sem, recv_sem):
+    def raw(src, dst, sent, got_at, target):
+        return pltpu.make_async_remote_copy(
+            src_ref=src, dst_ref=dst, send_sem=send_sem.at[sent], recv_sem=recv_sem.at[got_at],
+            device_id=target, device_id_type=MESH,
+        )
+
+    return raw
+
+
+class LineSum:
+    def __init__(self, raw, arrays, base, me):
+        self.raw, self.arrays, self.base, self.me = raw, arrays, base, me
+
+    def sem(self, n, p, down):
+        return self.base + 8 * n + 4 * down + p
+
+    def take(self, p, down, done):
+        d = self.me[0]
+        for n, (z, got_z) in enumerate(self.arrays):
+            self.raw(z.at[p], got_z.at[p], self.sem(n, p, down), self.sem(n, p, down), self.me).wait_recv()
+
+        @pl.when(jnp.logical_not(done))
+        def _():
+            for z, got_z in self.arrays:
+                def one(t, z=z, got_z=got_z):
+                    z[p, at(t, 64), :] = (
+                        z[p, at(t, 64), :].astype(F32) + got_z[p, at(t, 64), :].astype(F32)
+                    ).astype(BF)
+
+                loop(z.shape[1] // 64, one)
+
+    def up(self, p):
+        d, r, c = self.me
+
+        @pl.when((d > 0) & (d <= p))
+        def _():
+            self.take(p, 0, d == p)
+
+        @pl.when(d < p)
+        def _():
+            for n, (z, got_z) in enumerate(self.arrays):
+                self.raw(z.at[p], got_z.at[p], self.sem(n, p, 0), self.sem(n, p, 0), (d + 1, r, c)).start()
+
+    def down(self, p):
+        d, r, c = self.me
+
+        @pl.when((d < DP - 1) & (d >= p))
+        def _():
+            self.take(p, 1, d == p)
+
+        @pl.when(d > p)
+        def _():
+            slot = jnp.where(p < d - 1, p, DP)
+            for n, (z, got_z) in enumerate(self.arrays):
+                self.raw(z.at[p], got_z.at[slot], self.sem(n, p, 1), self.sem(n, p, 1), (d - 1, r, c)).start()
+
+    def step(self, s):
+        d = self.me[0]
+
+        @pl.when(d < DP // 2)
+        def _():
+            self.up(DP - 1 - s)
+            self.down(s)
+
+        @pl.when(d >= DP // 2)
+        def _():
+            self.down(s)
+            self.up(DP - 1 - s)
+
+    def settle(self):
+        d = self.me[0]
+        for p in range(DP):
+            for n, (z, got_z) in enumerate(self.arrays):
+                for down, sent in ((0, d < p), (1, d > p)):
+                    @pl.when(sent)
+                    def _(p=p, n=n, z=z, got_z=got_z, down=down):
+                        self.raw(
+                            z.at[p], got_z.at[p], self.sem(n, p, down), self.sem(n, p, down), self.me
+                        ).wait_send()
+
+    def total(self, z, got_z, part):
+        d = self.me[0]
+        value = z[d, part, :].astype(F32)
+        value = value + jnp.where(d > 0, got_z[d, part, :].astype(F32), 0.0)
+        return value + jnp.where(d < DP - 1, got_z[DP, part, :].astype(F32), 0.0)
+
+
+class PlaneSum:
+    def __init__(self, raw, stage, got, comb, base, local_sem, local_base, me):
+        self.raw, self.stage, self.got, self.comb, self.base = raw, stage, got, comb, base
+        self.local_sem, self.local_base, self.me = local_sem, local_base, me
+        self.kinds = range(stage.shape[0])
+
+    def from_one(self, kind, i):
+        d, r, c = self.me
+        y = c // 2
+        sent, base = self.base + 10 * kind + i, self.base + 10 * kind
+        if i < 2:
+            return self.raw(self.stage.at[kind, i], self.got.at[kind, 0], sent, base, (d, r ^ 1, 2 * y + 1 - i))
+        return self.raw(
+            self.stage.at[kind, i], self.comb.at[kind, 3 - i], sent, base + 3 + (3 - i), (d, r ^ 1, 2 * y)
+        )
+
+    def from_zero(self, kind, i):
+        d, r, c = self.me
+        sent, base = self.base + 10 * kind + i, self.base + 10 * kind
+        if i == 1:
+            return self.raw(self.stage.at[kind, i], self.got.at[kind, 1], sent, base + 1, (d, r, c ^ 1))
+        return self.raw(
+            self.stage.at[kind, i], self.got.at[kind, 2], sent, base + 2, (d, r, 2 * (1 - c // 2) + i - 2)
+        )
+
+    def home(self, kind):
+        return pltpu.make_async_copy(
+            self.stage.at[kind, 0], self.got.at[kind, 1], self.local_sem.at[self.local_base + kind]
+        )
+
+    def start_far(self):
+        @pl.when(lax.rem(self.me[2], 2) == 1)
+        def _():
+            for i in (2, 3):
+                for kind in self.kinds:
+                    self.from_one(kind, i).start()
+
+    def start_near(self):
+        core = lax.rem(self.me[2], 2)
+
+        @pl.when(core == 1)
+        def _():
+            for i in (0, 1):
+                for kind in self.kinds:
+                    self.from_one(kind, i).start()
+
+        @pl.when(core == 0)
+        def _():
+            for kind in self.kinds:
+                self.home(kind).start()
+                self.from_zero(kind, 1).start()
+
+    def combine(self, room, local_base):
+        core = lax.rem(self.me[2], 2)
+
+        @pl.when(core == 0)
+        def _():
+            fetches = {}
+            for i in (2, 3):
+                for kind in self.kinds:
+                    self.raw(
+                        self.stage.at[kind, i], self.comb.at[kind, i - 2], self.base,
+                        self.base + 10 * kind + 3 + (i - 2), self.me,
+                    ).wait_recv()
+                    fetches[i, kind] = pltpu.make_async_copy(
+                        self.comb.at[kind, i - 2], room(kind, i - 2),
+                        self.local_sem.at[local_base + 2 * kind + i - 2],
+                    )
+                    fetches[i, kind].start()
+            for i in (2, 3):
+                for kind in self.kinds:
+                    fetches[i, kind].wait()
+
+                    def add(t, kind=kind, i=i):
+                        self.stage[kind, i, at(t, 64), :] = (
+                            self.stage[kind, i, at(t, 64), :].astype(F32)
+                            + room(kind, i - 2)[at(t, 64), :].astype(F32)
+                        ).astype(BF)
+
+                    loop(self.stage.shape[2] // 64, add)
+                    self.from_zero(kind, i).start()
+
+    def settle(self):
+        core = lax.rem(self.me[2], 2)
+        for kind in self.kinds:
+            base = self.base + 10 * kind
+            for n in (0, 2):
+                self.raw(self.stage.at[kind, 0], self.got.at[kind, n], self.base, base + n, self.me).wait_recv()
+
+            @pl.when(core == 1)
+            def _(kind=kind, base=base):
+                self.raw(self.stage.at[kind, 0], self.got.at[kind, 1], self.base, base + 1, self.me).wait_recv()
+                for i in range(COL):
+                    self.from_one(kind, i).wait_send()
+
+            @pl.when(core == 0)
+            def _(kind=kind):
+                self.home(kind).wait()
+                for i in (1, 2, 3):
+                    self.from_zero(kind, i).wait_send()
+
+
+def middle_kernel(
+    n2_ref, mid_ref, scale_ref, gain_ref, own_grad, down_ref, gate_hbm, up_hbm, grad_hbm,
+    n2, dgate, dup, grad_out, gain_out, got, comb,
+    wg, wu, wd, gb, own_down, gate, up, du, hidden, given, arrived, z, got_z, crossing, crossed, gn, sums, stage,
+    send_sem, recv_sem, local_sem,
+):
+    d, r, c = (lax.axis_index(name) for name in AXES)
+    me = (d, r, c)
+    y, core = c // 2, lax.rem(c, 2)
+    rows, fc = n2_ref.shape
+    block = rows // 2
+    units = own_down.shape[0]
+    half = 2 * fc
+    over = (((0,), (0,)), ((), ()))
+    across = (((1,), (1,)), ((), ()))
+    post = Post(send_sem, recv_sem)
+    raw = maker(send_sem, recv_sem)
+    sibling = (d, r, c ^ 1)
+    others = [(a, b) for a in (0, 1) for b in range(COL) if (a, b) != (0, 0)]
+    greet([(d, r ^ a, c ^ b) for a, b in others] + [(d ^ j, r, c) for j in (1, 2, 3)])
+
+    cross = post.send(
+        n2_ref.at[pl.ds(pl.multiple_of((1 - y) * block, block), block), :],
+        n2.at[pl.ds(0, block), pl.ds(fc, fc)],
+        (d, r, c ^ 2),
+    )
+    loads = [
+        pltpu.make_async_copy(src, dst, local_sem.at[n])
+        for n, (src, dst) in enumerate(((gate_hbm, wg), (up_hbm, wu), (grad_hbm, gb)))
+    ]
+    for load in loads:
+        load.start()
+
+    def cast_down(t):
+        own_down[at(t, 64), :] = down_ref[at(t, 64), :].astype(BF)
+
+    loop(units // 64, cast_down)
+    first_sent = post.take(5)
+
+    def place_of(i):
+        return lax.rem(i, 2) * 2 + i // 2
+
+    def ship(way, i, target, src=None):
+        return raw(
+            own_down if src is None else src, wd.at[place_of(i)], first_sent + way, first_sent + i, target
+        )
+
+    keep_down = pltpu.make_async_copy(own_down, wd.at[0], local_sem.at[3])
+    to_core = ship(0, 1, sibling)
+    over_y = ship(1, 2 + core, (d, r, 2 * (1 - y)))
+    over_x = ship(2, 1 - core, (d, r ^ 1, 2 * y + 1))
+
+    def relay(i):
+        return ship(i + 1, 5 - i, (d, r ^ 1, 2 * y + 1), wd.at[PLACE[i]])
+
+    over_y.start()
+    over_x.start()
+
+    @pl.when(core == 0)
+    def _():
+        keep_down.start()
+
+    @pl.when(core == 1)
+    def _():
+        to_core.start()
+
+    n2[0:block, 0:fc] = n2_ref[pl.ds(pl.multiple_of(y * block, block), block), :]
+    cross.wait_recv()
+
+    first_up, first_down = post.take(DP), post.take(DP)
+    first_shared = post.take(DP)
+
+    def rail(p, e):
+        return n2.at[at(p ^ e, block), pl.ds(0, half)]
+
+    def go_up(p):
+        return raw(rail(p, d), rail(p, d + 1), first_up + p, first_up + p, (d + 1, r, c))
+
+    def go_down(p):
+        return raw(rail(p, d), rail(p, d - 1), first_down + p, first_up + p, (d - 1, r, c))
+
+    def share(p):
+        return raw(
+            rail(p, d), n2.at[at(p ^ d, block), pl.ds(half, half)], first_shared + p, first_shared + p, sibling
+        )
+
+    def onward(p):
+        @pl.when((p <= d) & (d < DP - 1))
+        def _():
+            go_up(p).start()
+
+        @pl.when((p >= d) & (d > 0))
+        def _():
+            go_down(p).start()
+
+        share(p).start()
+
+    def project(p):
+        share(p).wait_recv()
+        part = at(p ^ d, block)
+        gate[part, :] = jnp.dot(n2[part, :], wg[...], preferred_element_type=F32)
+        up[part, :] = jnp.dot(n2[part, :], wu[...], preferred_element_type=F32)
+
+    def hidden_grads(first, fresh):
+        def one(t):
+            part = at(t, block)
+            value = jnp.zeros((block, units), F32) if fresh else du[part, :]
+            for i in (first, first + 1):
+                place = PLACE[i]
+                value = value + lax.dot_general(
+                    gb[part, place * fc : (place + 1) * fc], wd[place], across, preferred_element_type=F32
+                )
+            du[part, :] = value
+
+        loop(DP, one)
+
+    onward(d)
+    turns = [
+        d,
+        jnp.where(d == 0, 1, d - 1),
+        jnp.where(d < 2, 2, jnp.where(d == 2, 3, 1)),
+        jnp.where(d < 2, 3, 0),
+    ]
+    inner = (d == 1) | (d == 2)
+
+    def arrival(n):
+        raw(rail(turns[n], d), rail(turns[n], d), first_up, first_up + turns[n], me).wait_recv()
+        onward(turns[n])
+
+    for load in loads:
+        load.wait()
+    arrival(1)
+
+    @pl.when(inner)
+    def _():
+        arrival(2)
+
+    project(turns[0])
+
+    @pl.when(core == 0)
+    def _():
+        keep_down.wait()
+        ship(0, 1, me).wait_recv()
+        for i in (2, 3):
+            ship(0, i, me).wait_recv()
+            relay(i).start()
+
+    project(turns[1])
+
+    @pl.when(jnp.logical_not(inner))
+    def _():
+        arrival(2)
+
+    @pl.when(inner)
+    def _():
+        arrival(3)
+
+    @pl.when(core == 1)
+    def _():
+        for i in (0, 1):
+            ship(0, i, me).wait_recv()
+
+    hidden_grads(0, True)
+    project(turns[2])
+
+    @pl.when(jnp.logical_not(inner))
+    def _():
+        arrival(3)
+
+    project(turns[3])
+
+    @pl.when(core == 1)
+    def _():
+        for i in (2, 3):
+            ship(0, i, me).wait_recv()
+
+    hidden_grads(2, False)
+
+    def units_of(t):
+        part = at(t, 64)
+        g, u, grad = gate[part, :], up[part, :], du[part, :]
+        sigmoid = 1.0 / (1.0 + jnp.exp(-g))
+        silu = g * sigmoid
+        hidden[part, :] = (silu * u).astype(BF)
+        dgate[part, :] = (grad * u * sigmoid * (1.0 + g * (1.0 - sigmoid))).astype(BF)
+        dup[part, :] = (grad * silu).astype(BF)
+
+    loop(2 * rows // 64, units_of)
+
+    def back(part, cols):
+        return lax.dot_general(
+            dgate[part, :], wg[cols, :], across, preferred_element_type=F32
+        ) + lax.dot_general(dup[part, :], wu[cols, :], across, preferred_element_type=F32)
+
+    def down_part(i):
+        def down_grad(t):
+            place = PLACE[i]
+            stage[0, i, at(t, TILE), :] = lax.dot_general(
+                hidden[:, at(t, TILE)], gb[:, place * fc : (place + 1) * fc], over, preferred_element_type=F32
+            ).astype(BF)
+
+        loop(units // TILE, down_grad)
+
+    owners = PlaneSum(raw, stage, got, comb, post.take(10), local_sem, 4, me)
+    down_part(2)
+    down_part(3)
+    owners.start_far()
+
+    def given_part(t):
+        given[at(t, block), :] = back(at(t, block), slice(half, None)).astype(BF)
+
+    loop(DP, given_part)
+    to_sibling = post.send(given, arrived, sibling)
+    down_part(0)
+    down_part(1)
+    owners.start_near()
+    to_sibling.wait_recv()
+
+    def kept_part(t):
+        part = at(t, block)
+        z[t ^ d] = (back(part, slice(0, half)) + arrived[part, :].astype(F32)).astype(BF)
+
+    loop(DP, kept_part)
+    line = LineSum(raw, ((z, got_z),), post.take(8), me)
+    line.step(0)
+    line.step(1)
+    owners.combine(lambda kind, j: wg.at[pl.ds(0, units), pl.ds(j * fc, fc)], 5)
+    line.step(2)
+
+    def settle_rows(t):
+        part = at(t, 64)
+        total = line.total(z, got_z, part)
+        gn[pl.ds(pl.multiple_of(y * block + t * 64, 64), 64), :] = total[:, 0:fc]
+        crossing[part, :] = total[:, fc:].astype(BF)
+
+    loop(block // 64, settle_rows)
+    other = post.send(crossing, crossed, (d, r, c ^ 2))
+    other.wait_recv()
+
+    def other_rows(t):
+        gn[pl.ds(pl.multiple_of((1 - y) * block + t * 64, 64), 64), :] = crossed[at(t, 64), :].astype(F32)
+
+    loop(block // 64, other_rows)
+
+    def inner_sum(t):
+        part = at(t, 128)
+        inner = gn[part, :] * gain_ref[...] * mid_ref[part, :]
+        sums[0, :, part] = as_row(jnp.sum(inner, axis=1, keepdims=True))
+
+    loop(rows // 128, inner_sum)
+    small = [post.send(sums.at[0], sums.at[m], (d, r, c ^ m)) for m in (1, 2, 3)]
+
+    def gain_sum(t, total):
+        part = at(t, 128)
+        value = gn[part, :] * mid_ref[part, :] * scale_ref[part, :]
+        return total + jnp.sum(value, axis=0, keepdims=True)
+
+    gain_out[...] = lax.fori_loop(0, rows // 128, gain_sum, jnp.zeros((1, fc), F32))
+    for copy in small:
+        copy.wait_recv()
+
+    def finish(t):
+        part = at(t, 128)
+        inner = as_column(sums[0, :, part] + sums[2, :, part] + sums[1, :, part] + sums[3, :, part])
+        scale = scale_ref[part, :]
+        grad_out[part, :] = (
+            own_grad[part, :].astype(F32) + scale * (gn[part, :] * gain_ref[...])
+            - mid_ref[part, :] * (scale * scale * scale * inner / D)
+        )
+
+    loop(rows // 128, finish)
+
+    owners.settle()
+    line.settle()
+    for copy in [cross, to_sibling, other] + small:
+        copy.wait_send()
+    over_y.wait_send()
+    over_x.wait_send()
+
+    @pl.when(core == 0)
+    def _():
+        for i in (2, 3):
+            relay(i).wait_send()
+
+    @pl.when(core == 1)
+    def _():
+        to_core.wait_send()
+
+    for p in range(DP):
+        share(p).wait_send()
+
+        @pl.when((p <= d) & (d < DP - 1))
+        def _(p=p):
+            go_up(p).wait_send()
+
+        @pl.when((p >= d) & (d > 0))
+        def _(p=p):
+            go_down(p).wait_send()
+
+
+def middle(n2, mid, scale, gain, own_grad, down, gate, up, grad_all):
+    rows, fc = n2.shape
+    group = 2 * rows
+    block = rows // 2
+    units = down.shape[0]
+    vmem = pl.BlockSpec(memory_space=pltpu.VMEM)
+    hbm = pl.BlockSpec(memory_space=pl.ANY)
+
+    def like(shape, dtype=BF):
+        return jax.ShapeDtypeStruct(shape, dtype)
+
+    return pl.pallas_call(
+        middle_kernel,
+        in_specs=[vmem] * 6 + [hbm] * 3,
+        out_specs=[vmem] * 5 + [hbm] * 2,
+        out_shape=[
+            like((group, D)),
+            like((group, units)),
+            like((group, units)),
+            like((rows, fc), F32),
+            like((1, fc), F32),
+            like((1, 3, units, fc)),
+            like((1, 2, units, fc)),
+        ],
+        scratch_shapes=[
+            pltpu.VMEM((D, units), BF),
+            pltpu.VMEM((D, units), BF),
+            pltpu.VMEM((COL, units, fc), BF),
+            pltpu.VMEM((group, D), BF),
+            pltpu.VMEM((units, fc), BF),
+            pltpu.VMEM((group, units), F32),
+            pltpu.VMEM((group, units), F32),
+            pltpu.VMEM((group, units), F32),
+            pltpu.VMEM((group, units), BF),
+            pltpu.VMEM((group, 2 * fc), BF),
+            pltpu.VMEM((group, 2 * fc), BF),
+            pltpu.VMEM((DP, block, 2 * fc), BF),
+            pltpu.VMEM((DP + 1, block, 2 * fc), BF),
+            pltpu.VMEM((block, fc), BF),
+            pltpu.VMEM((block, fc), BF),
+            pltpu.VMEM((rows, fc), F32),
+            pltpu.VMEM((4, 8, rows), F32),
+            pltpu.VMEM((1, COL, units, fc), BF),
+            pltpu.SemaphoreType.DMA((SENDS,)),
+            pltpu.SemaphoreType.DMA((SENDS,)),
+            pltpu.SemaphoreType.DMA((8,)),
+        ],
+        compiler_params=pltpu.CompilerParams(
+            collective_id=3, has_side_effects=True, vmem_limit_bytes=62 << 20
+        ),
+        cost_estimate=pl.CostEstimate(
+            flops=14 * group * D * units, bytes_accessed=48 << 20, transcendentals=group * units
+        ),
+    )(n2, mid, scale, gain, own_grad, down, gate, up, grad_all)
+
+
 POSTS = 112
 
 
@@ -1144,37 +1524,6 @@
     over = (((0,), (0,)), ((), ()))
     across = (((1,), (1,)), ((), ()))
     post = Post(send_sem, recv_sem)
-    others = [(a, b) for a in (0, 1) for b in range(COL) if (a, b) != (0, 0)]
-    greet(
-        [(d, r ^ a, c ^ b) for a, b in others]
-        + [(d ^ j, r ^ a, c) for j in (1, 2, 3) for a in (0, 1)]
-    )
-
-    def columns(place):
-        return pl.ds(place * fc, fc)
-
-    def at(t, size):
-        return pl.ds(pl.multiple_of(t * size, size), size)
-
-    def loop(count, body):
-        def one(t, total):
-            body(t)
-            return total
-
-        lax.fori_loop(0, count, one, 0)
-
-    def turned(t):
-        return lax.rem(t + 2 * r, tiles)
-
-    def raw(src, dst, sent, got_at, target):
-        return pltpu.make_async_remote_copy(
-            src_ref=src, dst_ref=dst, send_sem=send_sem.at[sent], recv_sem=recv_sem.at[got_at],
-            device_id=target, device_id_type=MESH,
-        )
-
-    me = (d, r, c)
-    sibling = (d, r, c ^ 1)
-    own_rows, other_rows = pl.ds(0, rows), pl.ds(rows, rows)
     loads = [
         pltpu.make_async_copy(src, dst, local_sem.at[n])
         for n, (src, dst) in enumerate((
@@ -1187,6 +1536,22 @@
     for load in loads:
         load.start()
 
+    others = [(a, b) for a in (0, 1) for b in range(COL) if (a, b) != (0, 0)]
+    greet(
+        [(d, r ^ a, c ^ b) for a, b in others]
+        + [(d ^ j, r ^ a, c) for j in (1, 2, 3) for a in (0, 1)]
+    )
+
+    def columns(place):
+        return pl.ds(place * fc, fc)
+
+    def turned(t):
+        return lax.rem(t + 2 * r, tiles)
+
+    raw = maker(send_sem, recv_sem)
+    me = (d, r, c)
+    sibling = (d, r, c ^ 1)
+    own_rows, other_rows = pl.ds(0, rows), pl.ds(rows, rows)
     def round_mid(t):
         dball[at(t, 128), 0:fc] = mid_ref[at(t, 128), :].astype(BF)
 
@@ -1199,50 +1564,28 @@
 
     for load in loads[:3]:
         load.wait()
-    for i in (2, 3, 0, 1):
+    owners = PlaneSum(raw, stage, got, comb, post.take(20), local_sem, 4, me)
+
+    def hidden_part(i):
         for kind in (0, 1):
-            def hidden_grad(t, i=i, kind=kind):
+            def hidden_grad(t, kind=kind):
                 left = n2[:, pl.ds(pl.multiple_of(PLACE[i] * fc + t * TILE, TILE), TILE)]
                 stage[kind, i, at(t, TILE), :] = lax.dot_general(
                     left, dgu[pl.ds(kind * group, group), :], over, preferred_element_type=F32
                 ).astype(BF)
 
             loop(fc // TILE, hidden_grad)
+
+    hidden_part(2)
+    hidden_part(3)
+    owners.start_far()
+    hidden_part(0)
+    hidden_part(1)
     loads[3].wait()
 
     for copy, where, place in ((beside, other_rows, 0), (beyond, own_rows, 1), (corner, other_rows, 1)):
         copy.wait_recv()
         shared.append(post.send(dball.at[where, columns(place)], dball.at[where, columns(place + 2)], sibling))
-    bulk = post.take(20)
-
-    def from_one(kind, i):
-        if i < 2:
-            return raw(stage.at[kind, i], got.at[kind, 0], bulk + 4 * kind + i, bulk + 10 * kind + 0,
-                       (d, r ^ 1, 2 * y + 1 - i))
-        return raw(stage.at[kind, i], comb.at[kind, 3 - i], bulk + 4 * kind + i,
-                   bulk + 10 * kind + 3 + (3 - i), (d, r ^ 1, 2 * y))
-
-    def from_zero(kind, i):
-        if i == 1:
-            return raw(stage.at[kind, i], got.at[kind, 1], bulk + 4 * kind + i, bulk + 10 * kind + 1, sibling)
-        return raw(stage.at[kind, i], got.at[kind, 2], bulk + 4 * kind + i, bulk + 10 * kind + 2,
-                   (d, r, 2 * (1 - y) + i - 2))
-
-    def home(kind):
-        return pltpu.make_async_copy(stage.at[kind, 0], got.at[kind, 1], local_sem.at[4 + kind])
-
-    @pl.when(core == 1)
-    def _():
-        for i in (2, 3, 0, 1):
-            for kind in (0, 1):
-                from_one(kind, i).start()
-
-    @pl.when(core == 0)
-    def _():
-        for kind in (0, 1):
-            home(kind).start()
-            from_zero(kind, 1).start()
-
     for copy in shared:
         copy.wait_recv()
 
@@ -1376,31 +1719,6 @@
     loop(tiles, given_part)
     to_sibling = post.send(n2.at[:, pl.ds(0, half)], arrived, sibling)
 
-    @pl.when(core == 0)
-    def _():
-        fetches = {}
-        for i in (2, 3):
-            for kind in (0, 1):
-                raw(stage.at[kind, i], comb.at[kind, i - 2], bulk, bulk + 10 * kind + 3 + (i - 2), me).wait_recv()
-                room = n1.at[pl.ds((i - 2) * fc, fc), pl.ds(kind * units, units)]
-                fetches[i, kind] = pltpu.make_async_copy(
-                    comb.at[kind, i - 2], room, local_sem.at[2 * kind + i - 2]
-                )
-                fetches[i, kind].start()
-        for i in (2, 3):
-            for kind in (0, 1):
-                fetches[i, kind].wait()
-
-                def add(t, kind=kind, i=i):
-                    there = pl.ds(pl.multiple_of((i - 2) * fc + t * 64, 64), 64)
-                    stage[kind, i, at(t, 64), :] = (
-                        stage[kind, i, at(t, 64), :].astype(F32)
-                        + n1[there, kind * units : (kind + 1) * units].astype(F32)
-                    ).astype(BF)
-
-                loop(fc // 64, add)
-                from_zero(kind, i).start()
-
     to_sibling.wait_recv()
     for copy in outs:
         copy.wait_send()
@@ -1427,90 +1745,27 @@
         post.send(low(own_rows, 1), landed.at[1], (d, r, c ^ 2)),
     ]
 
-    def line_sum(arrays, base):
-        def sem(n, p, down):
-            return base + 8 * n + 4 * down + p
-
-        def add(p):
-            for z, got_z in arrays:
-                def one(t, z=z, got_z=got_z):
-                    z[p, at(t, 64), :] = (
-                        z[p, at(t, 64), :].astype(F32) + got_z[p, at(t, 64), :].astype(F32)
-                    ).astype(BF)
-
-                loop(z.shape[1] // 64, one)
-
-        def up(p):
-            @pl.when((d > 0) & (d <= p))
-            def _():
-                for n, (z, got_z) in enumerate(arrays):
-                    raw(z.at[p], got_z.at[p], sem(n, p, 0), sem(n, p, 0), me).wait_recv()
-
-                @pl.when(d < p)
-                def _():
-                    add(p)
-
-            @pl.when(d < p)
-            def _():
-                for n, (z, got_z) in enumerate(arrays):
-                    raw(z.at[p], got_z.at[p], sem(n, p, 0), sem(n, p, 0), (d + 1, r, c)).start()
-
-        def down(p):
-            @pl.when((d < DP - 1) & (d >= p))
-            def _():
-                for n, (z, got_z) in enumerate(arrays):
-                    raw(z.at[p], got_z.at[p], sem(n, p, 1), sem(n, p, 1), me).wait_recv()
-
-                @pl.when(d > p)
-                def _():
-                    add(p)
-
-            @pl.when(d > p)
-            def _():
-                slot = jnp.where(p < d - 1, p, DP)
-                for n, (z, got_z) in enumerate(arrays):
-                    raw(z.at[p], got_z.at[slot], sem(n, p, 1), sem(n, p, 1), (d - 1, r, c)).start()
-
-        @pl.when(d < DP // 2)
-        def _():
-            for s in range(DP - 1):
-                up(DP - 1 - s)
-                down(s)
-
-        @pl.when(d >= DP // 2)
-        def _():
-            for s in range(DP - 1):
-                down(s)
-                up(DP - 1 - s)
-
-        def settle():
-            for p in range(DP):
-                for n, (z, got_z) in enumerate(arrays):
-                    @pl.when(d < p)
-                    def _(p=p, n=n, z=z, got_z=got_z):
-                        raw(z.at[p], got_z.at[p], sem(n, p, 0), sem(n, p, 0), me).wait_send()
-
-                    @pl.when(d > p)
-                    def _(p=p, n=n, z=z, got_z=got_z):
-                        raw(z.at[p], got_z.at[p], sem(n, p, 1), sem(n, p, 1), me).wait_send()
-
-        return settle
-
-    def finish(z, got_z, dest, lanes):
+    owners.start_near()
+    owners.combine(lambda kind, j: n1.at[pl.ds(j * fc, fc), pl.ds(kind * units, units)], 0)
+
+    def finish(line, z, got_z, dest, lanes):
         def one(t):
-            part = at(t, 64)
-            value = z[d, part, :].astype(F32)
-            value = value + jnp.where(d > 0, got_z[d, part, :].astype(F32), 0.0)
-            value = value + jnp.where(d < DP - 1, got_z[DP, part, :].astype(F32), 0.0)
-            dest[part, lanes] = value
+            dest[at(t, 64), lanes] = line.total(z, got_z, at(t, 64))
 
         loop(z.shape[1] // 64, one)
 
     for copy in outs + qs:
         copy.wait_recv()
     first_line = post.take(24)
-    settle_a = line_sum(((zq, rq), (zo, ro)), first_line)
-
+    line_a = LineSum(raw, ((zq, rq), (zo, ro)), first_line, me)
+    for s in range(DP - 1):
+        line_a.step(s)
+
+    for copy in kvs:
+        copy.wait_recv()
+    line_b = LineSum(raw, ((zkv, rkv),), first_line + 16, me)
+    for s in range(DP - 1):
+        line_b.step(s)
     for copy in pieces:
         copy.wait_recv()
 
@@ -1546,6 +1801,9 @@
     far = [(j, a) for j in range(DP) for a in (0, 1) if (j, a) != (0, 0)]
     for n, (j, a) in enumerate(far):
         gain_copy(n, j, a).start()
+    finish(line_a, zq, rq, in_out, slice(0, width))
+    finish(line_a, zo, ro, out_out, slice(0, fc))
+    finish(line_b, zkv, rkv, in_out, slice(width, 3 * width))
     for copy in small:
         copy.wait_recv()
 
@@ -1561,12 +1819,6 @@
 
     loop(rows // 128, finish_tokens)
 
-    for copy in kvs:
-        copy.wait_recv()
-    settle_b = line_sum(((zkv, rkv),), first_line + 16)
-    finish(zq, rq, in_out, slice(0, width))
-    finish(zo, ro, out_out, slice(0, fc))
-    finish(zkv, rkv, in_out, slice(width, 3 * width))
     for e in range(2 * DP):
         @pl.when(e != seat)
         def _(e=e):
@@ -1577,24 +1829,9 @@
         gains = gains + gsum[e]
     gains_out[...] = gains
 
-    for kind in (0, 1):
-        for n in (0, 2):
-            raw(stage.at[kind, 0], got.at[kind, n], bulk, bulk + 10 * kind + n, me).wait_recv()
-
-        @pl.when(core == 1)
-        def _(kind=kind):
-            raw(stage.at[kind, 0], got.at[kind, 1], bulk, bulk + 10 * kind + 1, me).wait_recv()
-            for i in range(COL):
-                from_one(kind, i).wait_send()
-
-        @pl.when(core == 0)
-        def _(kind=kind):
-            home(kind).wait()
-            for i in (1, 2, 3):
-                from_zero(kind, i).wait_send()
-
-    settle_a()
-    settle_b()
+    owners.settle()
+    line_a.settle()
+    line_b.settle()
     for copy in [beside, beyond, corner] + shared + qs + kvs + [to_sibling] + pieces + small:
         copy.wait_send()
     for n, (j, a) in enumerate(far):
@@ -1664,18 +1901,6 @@
     )(x, gain, scale, mid, gain_two, weight_in, weight_out, q, kv, att, lse, begin, normed, n2, dgate, dup)
 
 
-def rounded_norm(values, scale, gain):
-    return (values * scale[:, None] * gain[None, :]).astype(BF)
-
-
-def norm_grads(grad_normed, inputs_f, scale_rows, gain):
-    gain_part = jnp.sum(grad_normed * inputs_f * scale_rows[:, None], axis=0)
-    scaled = grad_normed * gain[None, :]
-    inner = col_sum(jnp.sum(scaled * inputs_f, axis=1))
-    grad_inputs = scale_rows[:, None] * scaled - inputs_f * (scale_rows**3 * inner / D)[:, None]
-    return grad_inputs, gain_part
-
-
 def on_small_mesh(
     tokens,
     cotangent,
@@ -1692,92 +1917,25 @@
     permutation,
 ):
     del permutation
-    d, r, c = (lax.axis_index(name) for name in AXES)
-    rows = tokens.shape[0]
-    group = rows * ROW
-    half_rows = rows // 2
+    units = gate_master.shape[1]
     width = query_master.shape[1]
-    y = c // 2
-
-    def pick(stack, index):
-        return lax.dynamic_index_in_dim(stack, index, 0, keepdims=False)
-
-    def flip(array):
-        swapped = jnp.concatenate([array[rows:], array[:rows]], 0)
-        return jnp.where(r == 0, array, swapped)
-
     (
-        normed_one, weight_in, weight_out, q, key_value, own_attended, lse, midway, scale_two,
+        normed_one, weight_in, weight_out, q, key_value, own_attended, lse, mid, scale_two,
         n2, begin, scale_one, weight_gate, weight_up, grad_all,
     ) = forward(
         tokens, attn_gain[None, :], ffn_gain[None, :], lengths, query_master, key_master,
         value_master, out_master, gate_master, up_master, cotangent,
     )
-    hidden_out = down_master.astype(BF)
-    scale_two = scale_two[:, 0]
-    order = (0, 2, 1, 3)
-    weight_hidden = jnp.concatenate([weight_gate, weight_up], 1)
-    weight_down = jnp.concatenate([move(hidden_out, hidden_from(i)) for i in order], 1)
-
-    def spread_tokens(block):
-        kept = lax.dynamic_slice_in_dim(block, y * half_rows, half_rows, 0)
-        given = lax.dynamic_slice_in_dim(block, (1 - y) * half_rows, half_rows, 0)
-        mine = jnp.concatenate([kept, by_chip(given, 0, 1)], 1)
-        rail = jnp.concatenate([mine] + [by_plane(mine, j) for j in (1, 2, 3)], 0)
-        return jnp.concatenate([rail, by_col(rail, 1)], 1)
-
-    over = (((0,), (0,)), ((), ()))
-    across = (((1,), (1,)), ((), ()))
-    grad_hidden = lax.dot_general(grad_all, weight_down, across, preferred_element_type=F32)
-    normed_two = spread_tokens(n2)
-    gate_and_up = jnp.dot(normed_two, weight_hidden, preferred_element_type=F32)
-    units = hidden_out.shape[0]
-    gate, up = gate_and_up[:, :units], gate_and_up[:, units:]
-    sigmoid = jax.nn.sigmoid(gate)
-    hidden = (gate * sigmoid * up).astype(BF)
-    grad_gate = (grad_hidden * up * sigmoid * (1.0 + gate * (1.0 - sigmoid))).astype(BF)
-    grad_up = (grad_hidden * gate * sigmoid).astype(BF)
-    grad_both = jnp.concatenate([grad_gate, grad_up], 1)
-
-    half = D // 2
-    theirs = lax.dot_general(
-        grad_both, weight_hidden[half:], across, preferred_element_type=F32
-    ).astype(BF)
-    arrived = by_col(theirs, 1)
-    mine = lax.dot_general(grad_both, weight_hidden[:half], across, preferred_element_type=F32)
-    mine = mine + arrived.astype(F32)
-    low = mine.astype(BF)
-    mine = mine[:half_rows]
-    for j in (1, 2, 3):
-        mine = mine + by_plane(low[j * half_rows : (j + 1) * half_rows], j).astype(F32)
-    part = half // 2
-    crossed = by_chip(mine[:, part:].astype(BF), 0, 1).astype(F32)
-    grad_normed_two = jnp.where(
-        y == 0,
-        jnp.concatenate([mine[:, :part], crossed], 0),
-        jnp.concatenate([crossed, mine[:, :part]], 0),
-    )
-
-    def plane_total(partial, axis):
-        size = D // COL
-        total = None
-        for place, i in enumerate(order):
-            piece = lax.slice_in_dim(partial, place * size, (place + 1) * size, axis=axis)
-            piece = move(piece, hidden_back(i)).astype(F32)
-            total = piece if total is None else total + piece
-        return total
-
-    down_part = lax.dot_general(hidden, grad_all, over, preferred_element_type=F32).astype(BF)
-    grad_down_own = plane_total(down_part, 1)
-
-    grad_mid_norm, gain_two_part = norm_grads(grad_normed_two, midway, scale_two, ffn_gain)
-    grad_midway = cotangent.astype(F32) + grad_mid_norm
+    normed_two, grad_gate, grad_up, grad_mid, gain_two_part, got_down, _ = middle(
+        n2, mid, scale_two, ffn_gain[None, :], cotangent, down_master, weight_gate, weight_up, grad_all
+    )
     grad_tokens, grad_in, grad_out, gains, got, _ = backward(
-        tokens, attn_gain[None, :], scale_one, grad_midway, gain_two_part[None, :], weight_in, weight_out, q,
+        tokens, attn_gain[None, :], scale_one, grad_mid, gain_two_part, weight_in, weight_out, q,
         key_value, own_attended, lse, begin, normed_one, normed_two, grad_gate, grad_up,
     )
     got = got.astype(F32)
     grad_hidden_own = got[:, 0] + got[:, 1] + got[:, 2]
+    got_down = got_down[0].astype(F32)
     return (
         grad_tokens,
         grad_in[:, :width],
@@ -1786,7 +1944,7 @@
         grad_out,
         grad_hidden_own[0],
         grad_hidden_own[1],
-        grad_down_own,
+        got_down[0] + got_down[1] + got_down[2],
         gains[0],
         gains[1],
     )

time: 671 us -> 565 us (0.84); the launches traced: 664 us -> 565 us
  Pallas kernels: 434 us -> 549 us
  waiting for transfers between devices: 104 us -> 0 us
  matrix products: 54.9 us -> 0 us
  starting transfers between devices: 30.1 us -> 0 us
  other arithmetic: 28.3 us -> 6.47 us
    pallas_call x0 -> x1, Pallas kernels: none -> 164 us  [middle(): pl.pallas_call(middle_kernel, in_specs=[vmem] * 6 + [hbm] * 3, out_specs=...]
    ppermute x21 -> x0, waiting for transfers between devices: 104 us -> none  [move(): return lax.ppermute(array, AXES, pairs)]
    dot_general x5 -> x0, matrix products: 54.9 us -> none  [the longest x1 22.7 us: on_small_mesh(): gate_and_up = jnp.dot(normed_two, weight_hidden, preferred_element_type=F32)]
    ppermute x21 -> x0, starting transfers between devices: 30.1 us -> none  [move(): return lax.ppermute(array, AXES, pairs)]
    pallas_call x1, Pallas kernels: 227 us -> 200 us  [backward(): pl.pallas_call(backward_kernel, in_specs=[vmem] * 12 + [hbm] * 4, out_spe...]
    pallas_call x1, Pallas kernels: 207 us -> 186 us  [forward(): pl.pallas_call(forward_kernel, in_specs=[vmem] * 3 + [smem] + [vmem] * 6...]
    concatenate x3 -> x0, other arithmetic: 17.2 us -> none  [the longest x1 15.1 us: spread_tokens(): return jnp.concatenate([rail, by_col(rail, 1)], 1)]
  transfers between devices with their start and end apart: 21 -> 0, of which waited for: 9 -> 0; matrix products, arithmetic and copies ran while one was open for 8% -> 0% of each run, Pallas kernels for 0% -> 0%
where the time goes in v4:
time: 565 us
  Pallas kernels  549 us (97%)
  local copies, waits for them, and re-layouts  8.26 us (1%)
  other arithmetic  6.47 us (1%)
    pallas_call x1, Pallas kernels, backward(): pl.pallas_call(backward_kernel, in_specs=[vmem] * 12 + [hbm] * 4, out_spe...  200 us
    pallas_call x1, Pallas kernels, forward(): pl.pallas_call(forward_kernel, in_specs=[vmem] * 3 + [smem] + [vmem] * 6...  186 us
    pallas_call x1, Pallas kernels, middle(): pl.pallas_call(middle_kernel, in_specs=[vmem] * 6 + [hbm] * 3, out_specs=...  164 us

profile of v4, /device:TPU:0, one launch (start us, length us, event | category | flops | bytes accessed | tf_op | source)
XLA Modules:
  0.0 564.7 jit_solution(1433228379403339760)
XLA Ops:
  0.6 185.5 %shard_map.195 = (bf16[1024,2048]{1,0:T(8,128)(2,1)}, bf16[2048,768]{1,0:T(8,128)(2,1)}, bf16[256,2048]{1,0:T(8,128)(2,1)}, bf16[1024,256]{1,0:T(8,128)(2,1)}, b...) custom-call(bf16[512,512]{1,0:T(8,128)(2,1)} %x_ref.3, ...), custom_call_target="tpu_custom_call" | custom-call | flops 3221225472 | bytes 67108864 | tf_op jit(solution)/shard_map/pallas_call | solution.py:902
  186.2 164.1 %shard_map.196 = (bf16[1024,2048]{1,0:T(8,128)(2,1)}, bf16[1024,1024]{1,0:T(8,128)(2,1)}, bf16[1024,1024]{1,0:T(8,128)(2,1)}, f32[512,512]{1,0:T(8,128)}, f32[1,...) custom-call(bf16[512,512]{1,0:T(8,128)(2,1)} %get-tuple-element.37.n2_ref, ...), custom_call_target="tpu_custom_call" | custom-call | flops 30064771072 | bytes 50331648 | tf_op jit(solution)/shard_map/pallas_call | solution.py:1460
  350.3 199.6 %shard_map.197 = (f32[512,512]{1,0:T(8,128)}, f32[512,768]{1,0:T(8,128)}, f32[256,512]{1,0:T(8,128)}, f32[8,512]{1,0:T(8,128)}, bf16[2,3,512,1024]{3,2,1,0:T(8,128)(2,1)}, /*index=5*/bf16[2,2,512,1024]{3,2,1,0:T(8,128)(2,1)}) custom-call(bf16[512,512]{1,0:T(8,128)(2,1)} %x_ref.3, f32[1,512]{1,0:T(1,128)} %bitcast.17, f32[512,1]{1,0:T(8,128)} %get-tuple-element.36.scale_ref, ...), custom_call_target="tpu_custom_call" | custom-call | flops 15032385536 | bytes 67108864 | tf_op jit(solution)/shard_map/pallas_call | solution.py:1857
  549.9 0.0 copy-start
  549.9 1.5 fusion.2
  551.4 0.0 slice-start
  551.4 2.7 fusion.1
  554.1 0.0 copy-done
  554.1 0.0 slice-start.1
  554.1 0.9 convert_element_type.8
  555.0 2.1 fusion
  557.1 0.0 slice-done
  557.1 0.0 slice-done.1
  557.1 1.5 convert_element_type.7
  558.6 1.9 slice_add_fusion
  560.6 0.0 copy-start.1
  560.6 0.0 copy-start.2
  560.6 2.3 slice_bitcast_fusion
  562.9 0.0 copy-done.1
  562.9 1.0 copy.24
  563.9 0.0 copy-done.2
  563.9 0.8 copy.25
  (1 shorter events, 0.0 us)
Async XLA Ops:
  549.9 4.2 copy-start
  551.4 5.7 %slice-start = ((s8[6291456]{0:T(1024)(128)(4,1)}), s8[4194304]{0:T(1024)(128)(4,1)S(1)}, s32[]{:S(2)}) async-start(s8[6291456]{0:T(1024)(128)(4,1)} %bitcast.10), calls=%async_computation | async-start | bytes 8388608
  554.1 3.0 slice-start.1
  560.6 2.3 copy-start.1
  560.6 3.3 copy-start.2

commit v5 on v4

--- a/solution.py
+++ b/solution.py
@@ -1013,18 +1013,45 @@
             for n, (z, got_z) in enumerate(self.arrays):
                 self.raw(z.at[p], got_z.at[slot], self.sem(n, p, 1), self.sem(n, p, 1), (d - 1, r, c)).start()
 
-    def step(self, s):
+    def begin(self):
         d = self.me[0]
 
-        @pl.when(d < DP // 2)
-        def _():
-            self.up(DP - 1 - s)
-            self.down(s)
-
-        @pl.when(d >= DP // 2)
-        def _():
-            self.down(s)
-            self.up(DP - 1 - s)
+        @pl.when(d == 0)
+        def _():
+            for p in (3, 2, 1):
+                self.up(p)
+
+        @pl.when(d == DP - 1)
+        def _():
+            for p in (0, 1, 2):
+                self.down(p)
+
+    def rest(self):
+        d = self.me[0]
+
+        @pl.when(d == 0)
+        def _():
+            self.down(0)
+
+        @pl.when(d == 1)
+        def _():
+            self.up(3)
+            self.up(2)
+            self.down(0)
+            self.down(1)
+            self.up(1)
+
+        @pl.when(d == 2)
+        def _():
+            self.down(0)
+            self.down(1)
+            self.up(3)
+            self.up(2)
+            self.down(2)
+
+        @pl.when(d == DP - 1)
+        def _():
+            self.up(3)
 
     def settle(self):
         d = self.me[0]
@@ -1183,26 +1210,37 @@
         own_down[at(t, 64), :] = down_ref[at(t, 64), :].astype(BF)
 
     loop(units // 64, cast_down)
-    first_sent = post.take(5)
+    first_sent = post.take(10)
 
     def place_of(i):
         return lax.rem(i, 2) * 2 + i // 2
 
-    def ship(way, i, target, src=None):
+    def piece(ref, n):
+        return ref.at[pl.ds(n * (units // 2), units // 2), :]
+
+    def ship(n, way, i, target, src=None):
         return raw(
-            own_down if src is None else src, wd.at[place_of(i)], first_sent + way, first_sent + i, target
+            piece(own_down if src is None else src, n), piece(wd.at[place_of(i)], n),
+            first_sent + 5 * n + way, first_sent + 5 * n + i, target,
         )
 
     keep_down = pltpu.make_async_copy(own_down, wd.at[0], local_sem.at[3])
-    to_core = ship(0, 1, sibling)
-    over_y = ship(1, 2 + core, (d, r, 2 * (1 - y)))
-    over_x = ship(2, 1 - core, (d, r ^ 1, 2 * y + 1))
-
-    def relay(i):
-        return ship(i + 1, 5 - i, (d, r ^ 1, 2 * y + 1), wd.at[PLACE[i]])
-
-    over_y.start()
-    over_x.start()
+
+    def to_core(n):
+        return ship(n, 0, 1, sibling)
+
+    def over_y(n):
+        return ship(n, 1, 2 + core, (d, r, 2 * (1 - y)))
+
+    def over_x(n):
+        return ship(n, 2, 1 - core, (d, r ^ 1, 2 * y + 1))
+
+    def relay(n, i):
+        return ship(n, i + 1, 5 - i, (d, r ^ 1, 2 * y + 1), wd.at[PLACE[i]])
+
+    for n in (0, 1):
+        over_y(n).start()
+        over_x(n).start()
 
     @pl.when(core == 0)
     def _():
@@ -1210,7 +1248,15 @@
 
     @pl.when(core == 1)
     def _():
-        to_core.start()
+        for n in (0, 1):
+            to_core(n).start()
+
+    def pass_down(n):
+        @pl.when(core == 0)
+        def _():
+            for i in (2, 3):
+                ship(n, 0, i, me).wait_recv()
+                relay(n, i).start()
 
     n2[0:block, 0:fc] = n2_ref[pl.ds(pl.multiple_of(y * block, block), block), :]
     cross.wait_recv()
@@ -1283,30 +1329,30 @@
     def _():
         arrival(2)
 
+    pass_down(0)
     project(turns[0])
+    pass_down(1)
+    project(turns[1])
+
+    @pl.when(jnp.logical_not(inner))
+    def _():
+        arrival(2)
+
+    @pl.when(inner)
+    def _():
+        arrival(3)
 
     @pl.when(core == 0)
     def _():
         keep_down.wait()
-        ship(0, 1, me).wait_recv()
-        for i in (2, 3):
-            ship(0, i, me).wait_recv()
-            relay(i).start()
-
-    project(turns[1])
-
-    @pl.when(jnp.logical_not(inner))
-    def _():
-        arrival(2)
-
-    @pl.when(inner)
-    def _():
-        arrival(3)
+        for n in (0, 1):
+            ship(n, 0, 1, me).wait_recv()
 
     @pl.when(core == 1)
     def _():
-        for i in (0, 1):
-            ship(0, i, me).wait_recv()
+        for n in (0, 1):
+            for i in (0, 1):
+                ship(n, 0, i, me).wait_recv()
 
     hidden_grads(0, True)
     project(turns[2])
@@ -1319,8 +1365,9 @@
 
     @pl.when(core == 1)
     def _():
-        for i in (2, 3):
-            ship(0, i, me).wait_recv()
+        for n in (0, 1):
+            for i in (2, 3):
+                ship(n, 0, i, me).wait_recv()
 
     hidden_grads(2, False)
 
@@ -1350,30 +1397,54 @@
         loop(units // TILE, down_grad)
 
     owners = PlaneSum(raw, stage, got, comb, post.take(10), local_sem, 4, me)
+
+    line = LineSum(raw, ((z, got_z),), post.take(8), me)
+
+    def plane_of(t):
+        return jnp.where(d < DP // 2, DP - 1 - t, t)
+
+    def to_sibling(t):
+        part = at(plane_of(t) ^ d, block)
+        return raw(given.at[part, :], arrived.at[part, :], first_given + t, first_given + t, sibling)
+
+    def give(t):
+        part = at(plane_of(t) ^ d, block)
+        given[part, :] = back(part, slice(half, None)).astype(BF)
+        to_sibling(t).start()
+
+    def keep(t):
+        p = plane_of(t)
+        part = at(p ^ d, block)
+        value = back(part, slice(0, half))
+        to_sibling(t).wait_recv()
+        z[p] = (value + arrived[part, :].astype(F32)).astype(BF)
+
+        if t < DP - 1:
+            @pl.when(d == 0)
+            def _():
+                line.up(DP - 1 - t)
+
+            @pl.when(d == DP - 1)
+            def _():
+                line.down(t)
+
+    first_given = post.take(DP)
+    give(0)
+    give(1)
     down_part(2)
     down_part(3)
     owners.start_far()
-
-    def given_part(t):
-        given[at(t, block), :] = back(at(t, block), slice(half, None)).astype(BF)
-
-    loop(DP, given_part)
-    to_sibling = post.send(given, arrived, sibling)
+    keep(0)
+    give(2)
+    keep(1)
+    give(3)
+    keep(2)
     down_part(0)
     down_part(1)
     owners.start_near()
-    to_sibling.wait_recv()
-
-    def kept_part(t):
-        part = at(t, block)
-        z[t ^ d] = (back(part, slice(0, half)) + arrived[part, :].astype(F32)).astype(BF)
-
-    loop(DP, kept_part)
-    line = LineSum(raw, ((z, got_z),), post.take(8), me)
-    line.step(0)
-    line.step(1)
+    keep(3)
     owners.combine(lambda kind, j: wg.at[pl.ds(0, units), pl.ds(j * fc, fc)], 5)
-    line.step(2)
+    line.rest()
 
     def settle_rows(t):
         part = at(t, 64)
@@ -1420,19 +1491,22 @@
 
     owners.settle()
     line.settle()
-    for copy in [cross, to_sibling, other] + small:
+    for copy in [cross, other] + small:
         copy.wait_send()
-    over_y.wait_send()
-    over_x.wait_send()
-
-    @pl.when(core == 0)
-    def _():
-        for i in (2, 3):
-            relay(i).wait_send()
-
-    @pl.when(core == 1)
-    def _():
-        to_core.wait_send()
+    for t in range(DP):
+        to_sibling(t).wait_send()
+    for n in (0, 1):
+        over_y(n).wait_send()
+        over_x(n).wait_send()
+
+        @pl.when(core == 0)
+        def _(n=n):
+            for i in (2, 3):
+                relay(n, i).wait_send()
+
+        @pl.when(core == 1)
+        def _(n=n):
+            to_core(n).wait_send()
 
     for p in range(DP):
         share(p).wait_send()
@@ -1508,7 +1582,7 @@
 def backward_kernel(
     x_ref, gain_ref, scale_ref, mid_ref, gain_two_ref, weight_in, weight_out, q_ref, kv_ref, att_ref, lse_ref,
     begin_ref, normed_hbm, n2_hbm, dgate_hbm, dup_hbm,
-    tokens_out, in_out, out_out, gains_out, got, comb,
+    tokens_out, query_out, key_out, value_out, out_out, gains_out, got, comb,
     n1, n2, dgu, dball, dotted, dproj, acc, spill, spilled, stage, own_f, arrived, landed,
     zq, zo, zkv, rq, ro, rkv, sums, gsum,
     send_sem, recv_sem, local_sem,
@@ -1595,6 +1669,22 @@
         ).astype(BF)
 
     loop(tiles, head_grad)
+
+    sent_out = [None] + [post.take(1) for _ in (1, 2, 3)]
+    outs = []
+    for place, m in enumerate((0, 2, 1, 3)):
+        value = lax.dot_general(
+            att_ref[...], dball[:, place * fc : (place + 1) * fc], over, preferred_element_type=F32
+        ).astype(BF)
+        if m == 0:
+            zo[c] = value
+        else:
+            n2[(m - 1) * width : m * width, half : half + fc] = value
+            staged = n2.at[pl.ds((m - 1) * width, width), pl.ds(half, fc)]
+            copy = raw(staged, zo.at[c], sent_out[m], sent_out[m], (d, r, c ^ m))
+            copy.start()
+            outs.append(copy)
+
     span = TILE + REACH
     scale = HEAD_DIM ** (-0.5)
     spills = []
@@ -1645,21 +1735,6 @@
         def _(copy=copy):
             copy.start()
 
-    sent_out = [None] + [post.take(1) for _ in (1, 2, 3)]
-    outs = []
-    for place, m in enumerate((0, 2, 1, 3)):
-        value = lax.dot_general(
-            att_ref[...], dball[:, place * fc : (place + 1) * fc], over, preferred_element_type=F32
-        ).astype(BF)
-        if m == 0:
-            zo[c] = value
-        else:
-            n2[(m - 1) * width : m * width, half : half + fc] = value
-            staged = n2.at[pl.ds((m - 1) * width, width), pl.ds(half, fc)]
-            copy = raw(staged, zo.at[c], sent_out[m], sent_out[m], (d, r, c ^ m))
-            copy.start()
-            outs.append(copy)
-
     def attention_grads(first_lane, lane_count, dest):
         lanes = slice(first_lane, first_lane + lane_count)
         slots = [None] + [post.take(1) for _ in (1, 2, 3)]
@@ -1710,6 +1785,12 @@
             loop(tiles, whole)
 
     kvs = attention_grads(width, 2 * width, zkv)
+    for copy in outs + qs:
+        copy.wait_recv()
+    first_line = post.take(24)
+    line_a = LineSum(raw, ((zq, rq), (zo, ro)), first_line, me)
+    line_b = LineSum(raw, ((zkv, rkv),), first_line + 16, me)
+    line_a.begin()
 
     def given_part(t):
         n2[at(t, TILE), 0:half] = lax.dot_general(
@@ -1745,27 +1826,16 @@
         post.send(low(own_rows, 1), landed.at[1], (d, r, c ^ 2)),
     ]
 
-    owners.start_near()
-    owners.combine(lambda kind, j: n1.at[pl.ds(j * fc, fc), pl.ds(kind * units, units)], 0)
-
-    def finish(line, z, got_z, dest, lanes):
+    def finish(line, z, got_z, dests):
         def one(t):
-            dest[at(t, 64), lanes] = line.total(z, got_z, at(t, 64))
+            value = line.total(z, got_z, at(t, 64))
+            for dest, lanes in dests:
+                dest[at(t, 64), :] = value[:, lanes]
 
         loop(z.shape[1] // 64, one)
 
-    for copy in outs + qs:
-        copy.wait_recv()
-    first_line = post.take(24)
-    line_a = LineSum(raw, ((zq, rq), (zo, ro)), first_line, me)
-    for s in range(DP - 1):
-        line_a.step(s)
-
-    for copy in kvs:
-        copy.wait_recv()
-    line_b = LineSum(raw, ((zkv, rkv),), first_line + 16, me)
-    for s in range(DP - 1):
-        line_b.step(s)
+    line_a.rest()
+
     for copy in pieces:
         copy.wait_recv()
 
@@ -1801,9 +1871,17 @@
     far = [(j, a) for j in range(DP) for a in (0, 1) if (j, a) != (0, 0)]
     for n, (j, a) in enumerate(far):
         gain_copy(n, j, a).start()
-    finish(line_a, zq, rq, in_out, slice(0, width))
-    finish(line_a, zo, ro, out_out, slice(0, fc))
-    finish(line_b, zkv, rkv, in_out, slice(width, 3 * width))
+    owners.start_near()
+    owners.combine(lambda kind, j: n1.at[pl.ds(j * fc, fc), pl.ds(kind * units, units)], 0)
+
+
+    for copy in kvs:
+        copy.wait_recv()
+    line_b.begin()
+    line_b.rest()
+    finish(line_a, zq, rq, ((query_out, slice(None)),))
+    finish(line_a, zo, ro, ((out_out, slice(None)),))
+    finish(line_b, zkv, rkv, ((key_out, slice(0, width)), (value_out, slice(width, None))))
     for copy in small:
         copy.wait_recv()
 
@@ -1857,10 +1935,12 @@
     return pl.pallas_call(
         backward_kernel,
         in_specs=[vmem] * 12 + [hbm] * 4,
-        out_specs=[vmem] * 4 + [hbm] * 2,
+        out_specs=[vmem] * 6 + [hbm] * 2,
         out_shape=[
             like((rows, fc), F32),
-            like((fc, 3 * width), F32),
+            like((fc, width), F32),
+            like((fc, width), F32),
+            like((fc, width), F32),
             like((width, fc), F32),
             like((8, fc), F32),
             like((2, 3, fc, units)),
@@ -1917,8 +1997,6 @@
     permutation,
 ):
     del permutation
-    units = gate_master.shape[1]
-    width = query_master.shape[1]
     (
         normed_one, weight_in, weight_out, q, key_value, own_attended, lse, mid, scale_two,
         n2, begin, scale_one, weight_gate, weight_up, grad_all,
@@ -1929,22 +2007,23 @@
     normed_two, grad_gate, grad_up, grad_mid, gain_two_part, got_down, _ = middle(
         n2, mid, scale_two, ffn_gain[None, :], cotangent, down_master, weight_gate, weight_up, grad_all
     )
-    grad_tokens, grad_in, grad_out, gains, got, _ = backward(
+    grad_tokens, grad_query, grad_key, grad_value, grad_out, gains, got, _ = backward(
         tokens, attn_gain[None, :], scale_one, grad_mid, gain_two_part, weight_in, weight_out, q,
         key_value, own_attended, lse, begin, normed_one, normed_two, grad_gate, grad_up,
     )
-    got = got.astype(F32)
-    grad_hidden_own = got[:, 0] + got[:, 1] + got[:, 2]
-    got_down = got_down[0].astype(F32)
+
+    def whole(pieces):
+        return pieces[0].astype(F32) + pieces[1].astype(F32) + pieces[2].astype(F32)
+
     return (
         grad_tokens,
-        grad_in[:, :width],
-        grad_in[:, width : 2 * width],
-        grad_in[:, 2 * width :],
+        grad_query,
+        grad_key,
+        grad_value,
         grad_out,
-        grad_hidden_own[0],
-        grad_hidden_own[1],
-        got_down[0] + got_down[1] + got_down[2],
+        whole(got[0]),
+        whole(got[1]),
+        whole(got_down[0]),
         gains[0],
         gains[1],
     )

time: 565 us -> 507 us (0.90); the launches traced: 565 us -> 499 us
  Pallas kernels: 549 us -> 482 us
    pallas_call x1, Pallas kernels: 200 us -> 163 us  [backward(): pl.pallas_call(backward_kernel, in_specs=[vmem] * 12 + [hbm] * 4, out_spe...]
    pallas_call x1, Pallas kernels: 164 us -> 133 us  [middle(): pl.pallas_call(middle_kernel, in_specs=[vmem] * 6 + [hbm] * 3, out_specs=...]
    add x2, other arithmetic: 4.03 us -> 9.87 us  [whole(): return pieces[0].astype(F32) + pieces[1].astype(F32) + pieces[2].astype(F32)]
where the time goes in v5:
time: 507 us; the launch traced here: 499 us
  Pallas kernels  482 us (95%)
  other arithmetic  9.87 us (2%)
  local copies, waits for them, and re-layouts  5.87 us (1%)
    pallas_call x1, Pallas kernels, forward(): pl.pallas_call(forward_kernel, in_specs=[vmem] * 3 + [smem] + [vmem] * 6...  186 us
    pallas_call x1, Pallas kernels, backward(): pl.pallas_call(backward_kernel, in_specs=[vmem] * 12 + [hbm] * 4, out_spe...  163 us
    pallas_call x1, Pallas kernels, middle(): pl.pallas_call(middle_kernel, in_specs=[vmem] * 6 + [hbm] * 3, out_specs=...  133 us

profile of v5, /device:TPU:0, one launch (start us, length us, event | category | flops | bytes accessed | tf_op | source)
XLA Modules:
  0.0 498.9 jit_solution(1230478796054447846)
XLA Ops:
  0.6 185.5 %shard_map.195 = (bf16[1024,2048]{1,0:T(8,128)(2,1)}, bf16[2048,768]{1,0:T(8,128)(2,1)}, bf16[256,2048]{1,0:T(8,128)(2,1)}, bf16[1024,256]{1,0:T(8,128)(2,1)}, b...) custom-call(bf16[512,512]{1,0:T(8,128)(2,1)} %x_ref.3, ...), custom_call_target="tpu_custom_call" | custom-call | flops 3221225472 | bytes 67108864 | tf_op jit(solution)/shard_map/pallas_call | solution.py:902
  186.2 133.3 %shard_map.196 = (bf16[1024,2048]{1,0:T(8,128)(2,1)}, bf16[1024,1024]{1,0:T(8,128)(2,1)}, bf16[1024,1024]{1,0:T(8,128)(2,1)}, f32[512,512]{1,0:T(8,128)}, f32[1,...) custom-call(bf16[512,512]{1,0:T(8,128)(2,1)} %get-tuple-element.39.n2_ref, ...), custom_call_target="tpu_custom_call" | custom-call | flops 30064771072 | bytes 50331648 | tf_op jit(solution)/shard_map/pallas_call | solution.py:1534
  319.5 163.2 %shard_map.197 = (f32[512,512]{1,0:T(8,128)}, f32[512,256]{1,0:T(8,128)}, f32[512,256]{1,0:T(8,128)}, f32[512,256]{1,0:T(8,128)}, f32[256,512]{1,0:T(8,128)}, /*...) custom-call(bf16[512,512]{1,0:T(8,128)(2,1)} %x_ref.3, f32[1,512]{1,0:T(1,128)} %bitcast.15, ...), custom_call_target="tpu_custom_call" | custom-call | flops 15032385536 | bytes 67108864 | tf_op jit(solution)/shard_map/pallas_call | solution.py:1935
  482.7 1.4 fusion
  484.1 3.6 add_bitcast_fusion
  487.7 0.0 copy-start
  487.7 6.3 %add_bitcast_fusion.1 = (f32[512,1024]{1,0:T(8,128)}, f32[512,1024]{1,0:T(8,128)}) fusion(bf16[2,3,512,1024]{3,2,1,0:T(8,128)(2,1)} %get-tuple-element.63), kind=kLoop, calls=%fused_computation.1 | loop fusion | flops 5242880 | bytes 10485760 | tf_op jit(solution)/shard_map/add | solution.py:2016
  494.0 0.0 copy-start.4
  494.0 0.0 copy-start.3
  494.0 0.0 copy-done
  494.0 0.0 copy-start.2
  494.0 1.0 copy.27
  495.0 0.3 copy-done.4
  495.3 0.0 copy-start.1
  495.3 0.8 copy.28
  496.1 0.0 copy-done.3
  496.1 0.8 copy.29
  496.9 0.0 copy-done.2
  496.9 0.8 copy.30
  497.7 0.0 copy-done.1
  497.7 0.8 copy.31
Async XLA Ops:
  487.7 6.3 %copy-start = (f32[512,512]{1,0:T(8,128)S(1)}, f32[512,512]{1,0:T(8,128)}, u32[]{:S(2)}) copy-start(f32[512,512]{1,0:T(8,128)} %get-tuple-element.80) | copy-start | bytes 3145732
  494.0 1.3 copy-start.4
  494.0 2.1 copy-start.3
  494.0 2.9 copy-start.2
  495.3 2.4 copy-start.1

commit v6 on v5

--- a/solution.py
+++ b/solution.py
@@ -429,10 +429,11 @@
 
 
 def forward_kernel(
-    x_ref, gain_one_ref, gain_two_ref, lengths_ref, query_ref, key_ref, value_ref, out_ref, gate_ref, up_ref,
+    x_ref, gain_one_ref, gain_two_ref, lengths_ref, query_ref, key_ref, value_ref, out_ref, gate_hbm, up_hbm,
     own_grad,
-    normed_ref, weight_in, weight_out, q_ref, kv_ref, att_ref, lse_ref, mid_ref, scale_ref, n2_ref, begin_ref, first_scale,
-    gate_all, up_all, grad_all,
+    mid_ref, scale_ref, n2_ref, begin_ref, first_scale,
+    normed_out, weight_in_out, weight_out_out, q_out, kv_out, att_out, lse_out, own_up, gate_all, up_all, grad_all,
+    normed_ref, weight_in, weight_out, q_ref, kv_ref, att_ref, lse_ref, masters,
     zin, zout, sums, wide, given, arrived, low, landed, x32, hidden_own,
     send_sem, recv_sem, local_sem,
 ):
@@ -444,6 +445,18 @@
     width = q_ref.shape[1]
     half = 2 * fc
     post = Post(send_sem, recv_sem)
+    fetches = [
+        pltpu.make_async_copy(src, masters.at[n], local_sem.at[8 + n]) for n, src in enumerate((gate_hbm, up_hbm))
+    ]
+    for copy in fetches:
+        copy.start()
+    copies = []
+
+    def copy_out(src, dst):
+        copy = pltpu.make_async_copy(src, dst, local_sem.at[10 + len(copies)])
+        copy.start()
+        copies.append(copy)
+
     in_plane = [(d, r ^ a, c ^ b) for a in (0, 1) for b in range(COL) if (a, b) != (0, 0)]
     greet([(d ^ j, r, c) for j in (1, 2, 3)] + in_plane)
 
@@ -458,14 +471,17 @@
     small = [post.send(sums.at[0], sums.at[m], (d, r, c ^ m)) for m in (1, 2, 3)]
 
     parts = (pl.ds(width, 2 * width), pl.ds(0, width))
-    first, first_down = post.take(2 * DP), post.take(2 * DP)
+    first, first_down = post.take(3 * DP), post.take(3 * DP)
+
+    def block_of(n, p):
+        return zin.at[p, :, parts[n]] if n < 2 else zout.at[p]
 
     def line(n, p, target_plane):
-        block = zin.at[p, :, parts[n]]
+        block = block_of(n, p)
         return post.ready(block, block, (target_plane, r, c), first + DP * n + p)
 
     def line_down(n, p, target_plane):
-        block = zin.at[p, :, parts[n]]
+        block = block_of(n, p)
         return pltpu.make_async_remote_copy(
             src_ref=block, dst_ref=block,
             send_sem=send_sem.at[first_down + DP * n + p], recv_sem=recv_sem.at[first + DP * n + p],
@@ -485,34 +501,38 @@
             zin[d, part, place * width : (place + 1) * width] = value
 
         cast_rows(master, put, fc)
-    for n in (0, 1):
+    def leave(n):
         @pl.when(d < DP - 1)
-        def _(n=n):
+        def _():
             line(n, d, d + 1).start()
 
         @pl.when(d > 0)
-        def _(n=n):
+        def _():
             line_down(n, d, d - 1).start()
 
-    first_cols = post.take(2 * DP)
+    leave(0)
+    leave(1)
+
+    first_cols = post.take(3 * DP)
 
     def place_of(m):
         return lax.rem(m, 2) * 2 + m // 2
 
+    def seat_of(n, place):
+        there = pl.ds(pl.multiple_of(place * fc, fc), fc)
+        return weight_in.at[there, parts[n]] if n < 2 else weight_out.at[:, there]
+
     def to_column(n, p):
-        there = pl.ds(pl.multiple_of(place_of(p ^ c) * fc, fc), fc)
         return pltpu.make_async_remote_copy(
-            src_ref=zin.at[p, :, parts[n]],
-            dst_ref=weight_in.at[there, parts[n]],
+            src_ref=block_of(n, p),
+            dst_ref=seat_of(n, place_of(p ^ c)),
             send_sem=send_sem.at[first_cols + DP * n + p],
             recv_sem=recv_sem.at[first_cols + DP * n + (p ^ c)],
             device_id=(d, r, p), device_id_type=MESH,
         )
 
     def keep(n):
-        return pltpu.make_async_copy(
-            zin.at[c, :, parts[n]], weight_in.at[pl.ds(0, fc), parts[n]], local_sem.at[n]
-        )
+        return pltpu.make_async_copy(block_of(n, c), seat_of(n, 0), local_sem.at[(0, 1, 5)[n]])
 
     def pass_on(n, p):
         @pl.when(p == c)
@@ -574,7 +594,8 @@
         def put(part, value):
             hidden_own[kind, part, :] = value
 
-        cast_rows((gate_ref, up_ref)[kind], put, fc)
+        fetches[kind].wait()
+        cast_rows(masters.at[kind], put, fc)
 
     cast_hidden(0)
     over_x(0).start()
@@ -607,6 +628,7 @@
     cast_hidden(1)
     start_home(0)
     start_home(1)
+    copy_out(hidden_own.at[1], own_up)
     over_x(1).start()
     half_rows = rows // 2
     grad_cross = post.send(
@@ -622,7 +644,7 @@
     grad_keep.start()
 
     def put_out(part, value):
-        zout[0, part, :] = value
+        zout[d, part, :] = value
 
     cast_rows(out_ref, put_out, width)
 
@@ -639,8 +661,8 @@
 
     lax.fori_loop(0, group // 128, find_begins, 0)
 
-    def line_step(s):
-        for n in (0, 1):
+    def line_step(s, which=(0, 1)):
+        for n in which:
             for p, valid, onward, forward in (
                 (d - s, d - s >= 0, d < DP - 1, lambda n, p: line(n, p, d + 1)),
                 (d + s, d + s < DP, d > 0, lambda n, p: line_down(n, p, d - 1)),
@@ -656,22 +678,24 @@
                     pass_on(n, p)
 
     line_step(1)
+    leave(2)
     line_step(2)
-    outs = [post.send(zout.at[0], zout.at[j], (d ^ j, r, c)) for j in (1, 2, 3)]
-    over_y(1).start()
+    pass_on(2, d)
+    line_step(1, (2,))
     for copy, where, place in ((beside, other_rows, 0), (beyond, own_rows, 1), (corner, other_rows, 1)):
         copy.wait_recv()
         shared.append(
             post.send(normed_ref.at[where, columns(place)], normed_ref.at[where, columns(place + 2)], sibling)
         )
     line_step(3)
+    line_step(2, (2,))
     start_relay(0)
 
     def arrived_blocks(n):
         keep(n).wait()
         for m in (1, 2, 3):
             pltpu.make_async_remote_copy(
-                src_ref=zin.at[0, :, parts[n]], dst_ref=weight_in.at[pl.ds(0, fc), parts[n]],
+                src_ref=block_of(n, 0), dst_ref=seat_of(n, 0),
                 send_sem=send_sem.at[first_cols], recv_sem=recv_sem.at[first_cols + DP * n + m],
                 device_id=(d, r, c), device_id_type=MESH,
             ).wait_recv()
@@ -679,6 +703,7 @@
     for copy in shared:
         copy.wait_recv()
     arrived_blocks(0)
+    copy_out(normed_ref, normed_out)
 
     def turned(t):
         return lax.rem(t + 2 * r, group // TILE)
@@ -710,13 +735,9 @@
 
     lax.fori_loop(0, group // TILE, project_q, 0)
 
-    for copy in outs:
-        copy.wait_recv()
-    out_cols = [
-        post.send(zout.at[d ^ c ^ m], weight_out.at[:, columns(PLACE[m])], (d, r, c ^ m)) for m in (1, 2, 3)
-    ]
-    out_keep = pltpu.make_async_copy(zout.at[d ^ c], weight_out.at[:, columns(0)], local_sem.at[6])
-    out_keep.start()
+    copy_out(weight_in, weight_in_out)
+    copy_out(q_ref, q_out)
+    line_step(3, (2,))
     grad_cross.wait_recv()
     grad_keep.wait()
     grads = [
@@ -742,6 +763,8 @@
     @pl.when(d > 0)
     def _():
         halo.wait_recv()
+
+    copy_out(kv_ref, kv_out)
 
     span = TILE + REACH
     for h in range(width // HEAD_DIM):
@@ -770,9 +793,10 @@
 
         lax.fori_loop(0, group // TILE, one, 0)
 
-    for copy in out_cols:
-        copy.wait_recv()
-    out_keep.wait()
+    copy_out(att_ref, att_out)
+    copy_out(lse_ref, lse_out)
+    arrived_blocks(2)
+    copy_out(weight_out, weight_out_out)
 
     def out_given(t, total):
         part = pl.ds(pl.multiple_of(t * TILE, TILE), TILE)
@@ -805,7 +829,6 @@
         post.send(low.at[other_rows, columns(0)], landed.at[0], (d, r ^ 1, c)),
         post.send(low.at[own_rows, columns(1)], landed.at[1], (d, r, c ^ 2)),
     ]
-    start_relay(1)
     for copy in pieces:
         copy.wait_recv()
 
@@ -842,25 +865,26 @@
         )
     for copy in grads_shared:
         copy.wait_recv()
+    over_y(0).wait_send()
     for kind in (0, 1):
-        over_y(kind).wait_send()
         over_x(kind).wait_send()
 
         @pl.when(core == 0)
         def _(kind=kind):
             keep_hidden(kind).wait()
             ship(kind, 0, 1, (d, r, c)).wait_recv()
-            for i in (2, 3):
-                relay(kind, i).wait_send()
+            if kind == 0:
+                for i in (2, 3):
+                    relay(kind, i).wait_send()
 
         @pl.when(core == 1)
         def _(kind=kind):
             to_core(kind).wait_send()
-            for i in range(COL):
+            for i in range(COL if kind == 0 else 2):
                 ship(kind, 0, i, (d, r, c)).wait_recv()
 
     for copy in (
-        small + [grad_cross, beside, beyond, corner] + shared + outs + out_cols + grads + grads_shared
+        small + [grad_cross, beside, beyond, corner] + shared + grads + grads_shared
         + [to_sibling] + pieces + again
     ):
         copy.wait_send()
@@ -869,7 +893,9 @@
     def _():
         halo.wait_send()
 
-    for n in (0, 1):
+    for copy in copies:
+        copy.wait()
+    for n in (0, 1, 2):
         for p in range(DP):
             @pl.when((d < DP - 1) & (p <= d))
             def _(n=n, p=p):
@@ -884,7 +910,7 @@
                 to_column(n, p).wait_send()
 
 
-SENDS = 80
+SENDS = 96
 
 
 def forward(x, gain_one, gain_two, lengths, query, key, value, out, gate, up, own_grad):
@@ -901,9 +927,14 @@
 
     return pl.pallas_call(
         forward_kernel,
-        in_specs=[vmem] * 3 + [smem] + [vmem] * 6 + [hbm],
-        out_specs=[vmem] * 12 + [hbm] * 3,
+        in_specs=[vmem] * 3 + [smem] + [vmem] * 4 + [hbm] * 3,
+        out_specs=[vmem] * 5 + [hbm] * 11,
         out_shape=[
+            like((rows, fc), F32),
+            like((rows, 1), F32),
+            like((rows, fc)),
+            like((group, 1), jnp.int32),
+            like((rows, 1), F32),
             like((group, D)),
             like((D, 3 * width)),
             like((width, D)),
@@ -911,16 +942,20 @@
             like((REACH + group, 2 * width)),
             like((group, width)),
             like((group, width), F32),
-            like((rows, fc), F32),
-            like((rows, 1), F32),
-            like((rows, fc)),
-            like((group, 1), jnp.int32),
-            like((rows, 1), F32),
+            like((fc, units)),
             like((D, units)),
             like((D, units)),
             like((group, D)),
         ],
         scratch_shapes=[
+            pltpu.VMEM((group, D), BF),
+            pltpu.VMEM((D, 3 * width), BF),
+            pltpu.VMEM((width, D), BF),
+            pltpu.VMEM((group, width), BF),
+            pltpu.VMEM((REACH + group, 2 * width), BF),
+            pltpu.VMEM((group, width), BF),
+            pltpu.VMEM((group, width), F32),
+            pltpu.VMEM((2, fc, units), F32),
             pltpu.VMEM((DP, fc, 3 * width), BF),
             pltpu.VMEM((DP, width, fc), BF),
             pltpu.VMEM((8, 8, rows), F32),
@@ -933,7 +968,7 @@
             pltpu.VMEM((2, fc, units), BF),
             pltpu.SemaphoreType.DMA((SENDS,)),
             pltpu.SemaphoreType.DMA((SENDS,)),
-            pltpu.SemaphoreType.DMA((8,)),
+            pltpu.SemaphoreType.DMA((20,)),
         ],
         compiler_params=pltpu.CompilerParams(
             collective_id=1, has_side_effects=True, vmem_limit_bytes=60 << 20
@@ -1128,21 +1163,18 @@
 
         @pl.when(core == 0)
         def _():
-            fetches = {}
             for i in (2, 3):
                 for kind in self.kinds:
                     self.raw(
                         self.stage.at[kind, i], self.comb.at[kind, i - 2], self.base,
                         self.base + 10 * kind + 3 + (i - 2), self.me,
                     ).wait_recv()
-                    fetches[i, kind] = pltpu.make_async_copy(
+                    fetch = pltpu.make_async_copy(
                         self.comb.at[kind, i - 2], room(kind, i - 2),
                         self.local_sem.at[local_base + 2 * kind + i - 2],
                     )
-                    fetches[i, kind].start()
-            for i in (2, 3):
-                for kind in self.kinds:
-                    fetches[i, kind].wait()
+                    fetch.start()
+                    fetch.wait()
 
                     def add(t, kind=kind, i=i):
                         self.stage[kind, i, at(t, 64), :] = (
@@ -1174,9 +1206,9 @@
 
 
 def middle_kernel(
-    n2_ref, mid_ref, scale_ref, gain_ref, own_grad, down_ref, gate_hbm, up_hbm, grad_hbm,
-    n2, dgate, dup, grad_out, gain_out, got, comb,
-    wg, wu, wd, gb, own_down, gate, up, du, hidden, given, arrived, z, got_z, crossing, crossed, gn, sums, stage,
+    n2_ref, mid_ref, scale_ref, gain_ref, own_grad, down_ref, own_up, gate_hbm, up_hbm, grad_hbm,
+    grad_out, gain_out, got, comb, n2_out, dgate_out, dup_out,
+    n2, dgate, dup, wg, wu, wd, gb, own_down, gate, up, du, hidden, given, arrived, z, got_z, crossing, crossed, gn, sums, stage,
     send_sem, recv_sem, local_sem,
 ):
     d, r, c = (lax.axis_index(name) for name in AXES)
@@ -1199,9 +1231,39 @@
         n2.at[pl.ds(0, block), pl.ds(fc, fc)],
         (d, r, c ^ 2),
     )
+    def half_of(ref, i, n):
+        return ref.at[pl.ds(pl.multiple_of(place_of(i) * fc + n * (fc // 2), fc // 2), fc // 2), :]
+
+    def place_of(i):
+        return lax.rem(i, 2) * 2 + i // 2
+
+    first_wide = post.take(8)
+
+    def up_over_y(n):
+        return raw(
+            own_up.at[pl.ds(n * (fc // 2), fc // 2), :], half_of(wu, 2 + core, n),
+            first_wide + 4 * n, first_wide + 4 * n + core, (d, r, 2 * (1 - y)),
+        )
+
+    def up_relay(n, i):
+        return raw(
+            half_of(wu, i, n), half_of(wu, 5 - i, n), first_wide + 4 * n + i - 1,
+            first_wide + 4 * n + 3 - i, (d, r ^ 1, 2 * y + 1),
+        )
+
+    def up_came(n, i):
+        return raw(half_of(wu, i, n), half_of(wu, i, n), first_wide, first_wide + 4 * n + i - 2, me)
+
+    for n in (0, 1):
+        up_over_y(n).start()
     loads = [
         pltpu.make_async_copy(src, dst, local_sem.at[n])
-        for n, (src, dst) in enumerate(((gate_hbm, wg), (up_hbm, wu), (grad_hbm, gb)))
+        for n, (src, dst) in zip((0, 1, 2, 9), (
+            (gate_hbm, wg),
+            (up_hbm.at[pl.ds(0, fc), :], wu.at[pl.ds(0, fc), :]),
+            (grad_hbm, gb),
+            (up_hbm.at[pl.ds(2 * fc, fc), :], wu.at[pl.ds(2 * fc, fc), :]),
+        ))
     ]
     for load in loads:
         load.start()
@@ -1211,9 +1273,6 @@
 
     loop(units // 64, cast_down)
     first_sent = post.take(10)
-
-    def place_of(i):
-        return lax.rem(i, 2) * 2 + i // 2
 
     def piece(ref, n):
         return ref.at[pl.ds(n * (units // 2), units // 2), :]
@@ -1239,8 +1298,8 @@
         return ship(n, i + 1, 5 - i, (d, r ^ 1, 2 * y + 1), wd.at[PLACE[i]])
 
     for n in (0, 1):
+        over_x(n).start()
         over_y(n).start()
-        over_x(n).start()
 
     @pl.when(core == 0)
     def _():
@@ -1293,7 +1352,17 @@
         share(p).wait_recv()
         part = at(p ^ d, block)
         gate[part, :] = jnp.dot(n2[part, :], wg[...], preferred_element_type=F32)
+
+    def project_up(t):
+        part = at(t, block)
         up[part, :] = jnp.dot(n2[part, :], wu[...], preferred_element_type=F32)
+
+    def pass_up(n):
+        @pl.when(core == 0)
+        def _():
+            for i in (2, 3):
+                up_came(n, i).wait_recv()
+                up_relay(n, i).start()
 
     def hidden_grads(first, fresh):
         def one(t):
@@ -1329,9 +1398,9 @@
     def _():
         arrival(2)
 
-    pass_down(0)
+    pass_up(0)
     project(turns[0])
-    pass_down(1)
+    pass_up(1)
     project(turns[1])
 
     @pl.when(jnp.logical_not(inner))
@@ -1341,6 +1410,9 @@
     @pl.when(inner)
     def _():
         arrival(3)
+
+    pass_down(0)
+    project(turns[2])
 
     @pl.when(core == 0)
     def _():
@@ -1354,14 +1426,23 @@
             for i in (0, 1):
                 ship(n, 0, i, me).wait_recv()
 
-    hidden_grads(0, True)
-    project(turns[2])
-
     @pl.when(jnp.logical_not(inner))
     def _():
         arrival(3)
 
+    hidden_grads(0, True)
+    pass_down(1)
     project(turns[3])
+    outs = [pltpu.make_async_copy(n2, n2_out, local_sem.at[0])]
+    outs[0].start()
+
+    @pl.when(core == 1)
+    def _():
+        for n in (0, 1):
+            for i in (2, 3):
+                up_came(n, i).wait_recv()
+
+    loop(DP, project_up)
 
     @pl.when(core == 1)
     def _():
@@ -1381,6 +1462,9 @@
         dup[part, :] = (grad * silu).astype(BF)
 
     loop(2 * rows // 64, units_of)
+    for n, (src, dst) in enumerate(((dgate, dgate_out), (dup, dup_out))):
+        outs.append(pltpu.make_async_copy(src, dst, local_sem.at[1 + n]))
+        outs[-1].start()
 
     def back(part, cols):
         return lax.dot_general(
@@ -1491,6 +1575,8 @@
 
     owners.settle()
     line.settle()
+    for copy in outs:
+        copy.wait()
     for copy in [cross, other] + small:
         copy.wait_send()
     for t in range(DP):
@@ -1498,11 +1584,13 @@
     for n in (0, 1):
         over_y(n).wait_send()
         over_x(n).wait_send()
+        up_over_y(n).wait_send()
 
         @pl.when(core == 0)
         def _(n=n):
             for i in (2, 3):
                 relay(n, i).wait_send()
+                up_relay(n, i).wait_send()
 
         @pl.when(core == 1)
         def _(n=n):
@@ -1520,7 +1608,7 @@
             go_down(p).wait_send()
 
 
-def middle(n2, mid, scale, gain, own_grad, down, gate, up, grad_all):
+def middle(n2, mid, scale, gain, own_grad, down, own_up, gate, up, grad_all):
     rows, fc = n2.shape
     group = 2 * rows
     block = rows // 2
@@ -1533,18 +1621,21 @@
 
     return pl.pallas_call(
         middle_kernel,
-        in_specs=[vmem] * 6 + [hbm] * 3,
-        out_specs=[vmem] * 5 + [hbm] * 2,
+        in_specs=[vmem] * 6 + [hbm] * 4,
+        out_specs=[vmem] * 2 + [hbm] * 5,
         out_shape=[
-            like((group, D)),
-            like((group, units)),
-            like((group, units)),
             like((rows, fc), F32),
             like((1, fc), F32),
             like((1, 3, units, fc)),
             like((1, 2, units, fc)),
+            like((group, D)),
+            like((group, units)),
+            like((group, units)),
         ],
         scratch_shapes=[
+            pltpu.VMEM((group, D), BF),
+            pltpu.VMEM((group, units), BF),
+            pltpu.VMEM((group, units), BF),
             pltpu.VMEM((D, units), BF),
             pltpu.VMEM((D, units), BF),
             pltpu.VMEM((COL, units, fc), BF),
@@ -1565,7 +1656,7 @@
             pltpu.VMEM((1, COL, units, fc), BF),
             pltpu.SemaphoreType.DMA((SENDS,)),
             pltpu.SemaphoreType.DMA((SENDS,)),
-            pltpu.SemaphoreType.DMA((8,)),
+            pltpu.SemaphoreType.DMA((12,)),
         ],
         compiler_params=pltpu.CompilerParams(
             collective_id=3, has_side_effects=True, vmem_limit_bytes=62 << 20
@@ -1573,17 +1664,17 @@
         cost_estimate=pl.CostEstimate(
             flops=14 * group * D * units, bytes_accessed=48 << 20, transcendentals=group * units
         ),
-    )(n2, mid, scale, gain, own_grad, down, gate, up, grad_all)
+    )(n2, mid, scale, gain, own_grad, down, own_up, gate, up, grad_all)
 
 
 POSTS = 112
 
 
 def backward_kernel(
-    x_ref, gain_ref, scale_ref, mid_ref, gain_two_ref, weight_in, weight_out, q_ref, kv_ref, att_ref, lse_ref,
-    begin_ref, normed_hbm, n2_hbm, dgate_hbm, dup_hbm,
+    x_ref, gain_ref, scale_ref, mid_ref, gain_two_ref, begin_ref, weight_in_hbm, weight_out_hbm, q_hbm, kv_hbm,
+    att_hbm, lse_hbm, normed_hbm, n2_hbm, dgate_hbm, dup_hbm,
     tokens_out, query_out, key_out, value_out, out_out, gains_out, got, comb,
-    n1, n2, dgu, dball, dotted, dproj, acc, spill, spilled, stage, own_f, arrived, landed,
+    weight_in, weight_out, q_ref, kv_ref, att_ref, lse_ref, n1, n2, dgu, dball, dotted, dproj, acc, spill, spilled, stage, own_f, arrived, landed,
     zq, zo, zkv, rq, ro, rkv, sums, gsum,
     send_sem, recv_sem, local_sem,
 ):
@@ -1591,7 +1682,7 @@
     y, core = c // 2, lax.rem(c, 2)
     rows, fc = x_ref.shape
     group = 2 * rows
-    width = q_ref.shape[1]
+    width = q_hbm.shape[1]
     units = dgate_hbm.shape[1]
     half = 2 * fc
     tiles = group // TILE
@@ -1599,12 +1690,18 @@
     across = (((1,), (1,)), ((), ()))
     post = Post(send_sem, recv_sem)
     loads = [
-        pltpu.make_async_copy(src, dst, local_sem.at[n])
+        pltpu.make_async_copy(src, dst, local_sem.at[8 + n])
         for n, (src, dst) in enumerate((
             (n2_hbm, n2),
             (dgate_hbm, dgu.at[pl.ds(0, group), :]),
             (dup_hbm, dgu.at[pl.ds(group, group), :]),
             (normed_hbm, n1),
+            (weight_out_hbm, weight_out),
+            (att_hbm, att_ref),
+            (q_hbm, q_ref),
+            (kv_hbm, kv_ref),
+            (lse_hbm, lse_ref),
+            (weight_in_hbm, weight_in),
         ))
     ]
     for load in loads:
@@ -1633,7 +1730,6 @@
     own_block = dball.at[own_rows, columns(0)]
     beside = post.send(own_block, dball.at[other_rows, columns(0)], (d, r ^ 1, c))
     beyond = post.send(own_block, dball.at[own_rows, columns(1)], (d, r, c ^ 2))
-    corner = post.send(own_block, dball.at[other_rows, columns(1)], (d, r ^ 1, c ^ 2))
     shared = [post.send(own_block, dball.at[own_rows, columns(2)], sibling)]
 
     for load in loads[:3]:
@@ -1652,14 +1748,25 @@
 
     hidden_part(2)
     hidden_part(3)
+    for load in loads[3:]:
+        load.wait()
+
+    upper = pl.ds(rows, rows // 2)
+    beside.wait_recv()
+    corner = [post.send(dball.at[upper, columns(0)], dball.at[upper, columns(1)], (d, r, c ^ 2))]
+    shared.append(post.send(dball.at[other_rows, columns(0)], dball.at[other_rows, columns(2)], sibling))
+    beyond.wait_recv()
+    corner.append(post.send(
+        dball.at[pl.ds(rows // 2, rows // 2), columns(1)],
+        dball.at[pl.ds(rows + rows // 2, rows // 2), columns(1)], (d, r ^ 1, c),
+    ))
+    shared.append(post.send(dball.at[own_rows, columns(1)], dball.at[own_rows, columns(3)], sibling))
     owners.start_far()
     hidden_part(0)
     hidden_part(1)
-    loads[3].wait()
-
-    for copy, where, place in ((beside, other_rows, 0), (beyond, own_rows, 1), (corner, other_rows, 1)):
+    for copy in corner:
         copy.wait_recv()
-        shared.append(post.send(dball.at[where, columns(place)], dball.at[where, columns(place + 2)], sibling))
+    shared.append(post.send(dball.at[other_rows, columns(1)], dball.at[other_rows, columns(3)], sibling))
     for copy in shared:
         copy.wait_recv()
 
@@ -1834,7 +1941,11 @@
 
         loop(z.shape[1] // 64, one)
 
+    owners.start_near()
     line_a.rest()
+    for copy in kvs:
+        copy.wait_recv()
+    line_b.begin()
 
     for copy in pieces:
         copy.wait_recv()
@@ -1871,13 +1982,9 @@
     far = [(j, a) for j in range(DP) for a in (0, 1) if (j, a) != (0, 0)]
     for n, (j, a) in enumerate(far):
         gain_copy(n, j, a).start()
-    owners.start_near()
     owners.combine(lambda kind, j: n1.at[pl.ds(j * fc, fc), pl.ds(kind * units, units)], 0)
 
 
-    for copy in kvs:
-        copy.wait_recv()
-    line_b.begin()
     line_b.rest()
     finish(line_a, zq, rq, ((query_out, slice(None)),))
     finish(line_a, zo, ro, ((out_out, slice(None)),))
@@ -1910,7 +2017,7 @@
     owners.settle()
     line_a.settle()
     line_b.settle()
-    for copy in [beside, beyond, corner] + shared + qs + kvs + [to_sibling] + pieces + small:
+    for copy in [beside, beyond] + corner + shared + qs + kvs + [to_sibling] + pieces + small:
         copy.wait_send()
     for n, (j, a) in enumerate(far):
         gain_copy(n, j, a).wait_send()
@@ -1934,7 +2041,7 @@
 
     return pl.pallas_call(
         backward_kernel,
-        in_specs=[vmem] * 12 + [hbm] * 4,
+        in_specs=[vmem] * 6 + [hbm] * 10,
         out_specs=[vmem] * 6 + [hbm] * 2,
         out_shape=[
             like((rows, fc), F32),
@@ -1947,6 +2054,12 @@
             like((2, 2, fc, units)),
         ],
         scratch_shapes=[
+            pltpu.VMEM((D, 3 * width), BF),
+            pltpu.VMEM((width, D), BF),
+            pltpu.VMEM((group, width), BF),
+            pltpu.VMEM((REACH + group, 2 * width), BF),
+            pltpu.VMEM((group, width), BF),
+            pltpu.VMEM((group, width), F32),
             pltpu.VMEM((group, D), BF),
             pltpu.VMEM((group, D), BF),
             pltpu.VMEM((2 * group, units), BF),
@@ -1970,7 +2083,7 @@
             pltpu.VMEM((2 * DP, 8, fc), F32),
             pltpu.SemaphoreType.DMA((POSTS,)),
             pltpu.SemaphoreType.DMA((POSTS,)),
-            pltpu.SemaphoreType.DMA((8,)),
+            pltpu.SemaphoreType.DMA((20,)),
         ],
         compiler_params=pltpu.CompilerParams(
             collective_id=2, has_side_effects=True, vmem_limit_bytes=62 << 20
@@ -1978,7 +2091,7 @@
         cost_estimate=pl.CostEstimate(
             flops=12 * group * D * width + 4 * group * D * units, bytes_accessed=64 << 20, transcendentals=0
         ),
-    )(x, gain, scale, mid, gain_two, weight_in, weight_out, q, kv, att, lse, begin, normed, n2, dgate, dup)
+    )(x, gain, scale, mid, gain_two, begin, weight_in, weight_out, q, kv, att, lse, normed, n2, dgate, dup)
 
 
 def on_small_mesh(
@@ -1998,14 +2111,15 @@
 ):
     del permutation
     (
-        normed_one, weight_in, weight_out, q, key_value, own_attended, lse, mid, scale_two,
-        n2, begin, scale_one, weight_gate, weight_up, grad_all,
+        mid, scale_two, n2, begin, scale_one, normed_one, weight_in, weight_out, q, key_value,
+        own_attended, lse, own_up, weight_gate, weight_up, grad_all,
     ) = forward(
         tokens, attn_gain[None, :], ffn_gain[None, :], lengths, query_master, key_master,
         value_master, out_master, gate_master, up_master, cotangent,
     )
-    normed_two, grad_gate, grad_up, grad_mid, gain_two_part, got_down, _ = middle(
-        n2, mid, scale_two, ffn_gain[None, :], cotangent, down_master, weight_gate, weight_up, grad_all
+    grad_mid, gain_two_part, got_down, _, normed_two, grad_gate, grad_up = middle(
+        n2, mid, scale_two, ffn_gain[None, :], cotangent, down_master, own_up, weight_gate,
+        weight_up, grad_all,
     )
     grad_tokens, grad_query, grad_key, grad_value, grad_out, gains, got, _ = backward(
         tokens, attn_gain[None, :], scale_one, grad_mid, gain_two_part, weight_in, weight_out, q,

time: 507 us -> 488 us (0.963)
  Pallas kernels: 482 us -> 464 us
    pallas_call x3, Pallas kernels: 482 us -> 464 us  [the longest x1 167 us: middle(): pl.pallas_call(middle_kernel, in_specs=[vmem] * 6 + [hbm] * 4, out_specs=...]
where the time goes in v6:
time: 488 us; the launch traced here: 481 us
  Pallas kernels  464 us (95%)
  other arithmetic  9.87 us (2%)
  local copies, waits for them, and re-layouts  5.87 us (1%)
    pallas_call x1, Pallas kernels, middle(): pl.pallas_call(middle_kernel, in_specs=[vmem] * 6 + [hbm] * 4, out_specs=...  167 us
    pallas_call x1, Pallas kernels, backward(): pl.pallas_call(backward_kernel, in_specs=[vmem] * 6 + [hbm] * 10, out_spe...  153 us
    pallas_call x1, Pallas kernels, forward(): pl.pallas_call(forward_kernel, in_specs=[vmem] * 3 + [smem] + [vmem] * 4...  144 us
    add x2, other arithmetic, whole(): return pieces[0].astype(F32) + pieces[1].astype(F32) + pieces[2].astype(F32)  9.87 us

profile of v6, /device:TPU:0, one launch (start us, length us, event | category | flops | bytes accessed | tf_op | source)
XLA Modules:
  0.0 481.3 jit_solution(9843057630741176401)
XLA Ops:
  0.6 144.3 %shard_map.195 = (f32[512,512]{1,0:T(8,128)}, f32[512,1]{1,0:T(8,128)}, bf16[512,512]{1,0:T(8,128)(2,1)}, s32[1024,1]{1,0:T(8,128)}, f32[512,1]{1,0:T(8,128)}, /...) custom-call(bf16[512,512]{1,0:T(8,128)(2,1)} %x_ref.3, ...), custom_call_target="tpu_custom_call" | custom-call | flops 3221225472 | bytes 67108864 | tf_op jit(solution)/shard_map/pallas_call | solution.py:928
  144.9 167.3 %shard_map.196 = (f32[512,512]{1,0:T(8,128)}, f32[1,512]{1,0:T(1,128)}, bf16[1,3,1024,512]{3,2,1,0:T(8,128)(2,1)}, bf16[1,2,1024,512]{3,2,1,0:T(8,128)(2,1)}, bf...) custom-call(bf16[512,512]{1,0:T(8,128)(2,1)} %get-tuple-element.40.n2_ref, ...), custom_call_target="tpu_custom_call" | custom-call | flops 30064771072 | bytes 50331648 | tf_op jit(solution)/shard_map/pallas_call | solution.py:1622
  312.2 152.8 %shard_map.197 = (f32[512,512]{1,0:T(8,128)}, f32[512,256]{1,0:T(8,128)}, f32[512,256]{1,0:T(8,128)}, f32[512,256]{1,0:T(8,128)}, f32[256,512]{1,0:T(8,128)}, /*...) custom-call(bf16[512,512]{1,0:T(8,128)(2,1)} %x_ref.3, f32[1,512]{1,0:T(1,128)} %bitcast.15, ...), custom_call_target="tpu_custom_call" | custom-call | flops 15032385536 | bytes 67108864 | tf_op jit(solution)/shard_map/pallas_call | solution.py:2042
  465.1 1.4 fusion
  466.4 3.6 add_bitcast_fusion
  470.0 0.0 copy-start
  470.0 6.3 %add_bitcast_fusion.1 = (f32[512,1024]{1,0:T(8,128)}, f32[512,1024]{1,0:T(8,128)}) fusion(bf16[2,3,512,1024]{3,2,1,0:T(8,128)(2,1)} %get-tuple-element.65), kind=kLoop, calls=%fused_computation.1 | loop fusion | flops 5242880 | bytes 10485760 | tf_op jit(solution)/shard_map/add | solution.py:2130
  476.3 0.0 copy-start.4
  476.3 0.0 copy-start.3
  476.3 0.0 copy-done
  476.3 0.0 copy-start.2
  476.3 1.0 copy.27
  477.3 0.3 copy-done.4
  477.6 0.0 copy-start.1
  477.6 0.8 copy.28
  478.4 0.0 copy-done.3
  478.4 0.8 copy.29
  479.2 0.0 copy-done.2
  479.2 0.8 copy.30
  480.0 0.0 copy-done.1
  480.0 0.8 copy.31
Async XLA Ops:
  470.0 6.3 %copy-start = (f32[512,512]{1,0:T(8,128)S(1)}, f32[512,512]{1,0:T(8,128)}, u32[]{:S(2)}) copy-start(f32[512,512]{1,0:T(8,128)} %get-tuple-element.82) | copy-start | bytes 3145732
  476.3 1.3 copy-start.4
  476.3 2.1 copy-start.3
  476.3 2.9 copy-start.2
  477.6 2.4 copy-start.1

commit v7 on v6

--- a/solution.py
+++ b/solution.py
@@ -428,6 +428,36 @@
     return jnp.transpose(row)[:, 0:1]
 
 
+def scatter_plane(post, low, landed, rows, me):
+    d, r, c = me
+    half = rows // 2
+    x_at, y_at = (d, r ^ 1, c), (d, r, c ^ 2)
+    upper, lower = pl.ds(0, half), pl.ds(half, half)
+    corner_x = post.send(low(rows, half, 1), landed.at[2, upper], x_at)
+    corner_y = post.send(low(rows + half, half, 1), landed.at[2, lower], y_at)
+    sent = [
+        post.send(low(rows, half, 0), landed.at[0, upper], x_at),
+        post.send(low(half, half, 1), landed.at[1, lower], y_at),
+    ]
+
+    def add(ref, first):
+        def one(t, total):
+            part = pl.ds(pl.multiple_of(t * 64, 64), 64)
+            there = pl.ds(pl.multiple_of(first + t * 64, 64), 64)
+            ref[part, :] = (ref[part, :].astype(F32) + landed[2, there, :].astype(F32)).astype(BF)
+            return total
+
+        lax.fori_loop(0, half // 64, one, 0)
+
+    corner_x.wait_recv()
+    add(low(0, half, 1), 0)
+    sent.append(post.send(low(0, half, 1), landed.at[1, upper], y_at))
+    corner_y.wait_recv()
+    add(low(rows + half, half, 0), half)
+    sent.append(post.send(low(rows + half, half, 0), landed.at[0, lower], x_at))
+    return sent, [corner_x, corner_y]
+
+
 def forward_kernel(
     x_ref, gain_one_ref, gain_two_ref, lengths_ref, query_ref, key_ref, value_ref, out_ref, gate_hbm, up_hbm,
     own_grad,
@@ -824,11 +854,9 @@
         return total
 
     lax.fori_loop(0, group // 128, add_low, 0)
-    pieces = [
-        post.send(low.at[other_rows, columns(1)], landed.at[2], (d, r ^ 1, c ^ 2)),
-        post.send(low.at[other_rows, columns(0)], landed.at[0], (d, r ^ 1, c)),
-        post.send(low.at[own_rows, columns(1)], landed.at[1], (d, r, c ^ 2)),
-    ]
+    pieces, corners = scatter_plane(
+        post, lambda first, count, place: low.at[pl.ds(first, count), columns(place)], landed, rows, (d, r, c)
+    )
     for copy in pieces:
         copy.wait_recv()
 
@@ -836,7 +864,7 @@
         part = pl.ds(pl.multiple_of(t * 128, 128), 128)
         value = (
             x32[part, :] + wide[part, 0:fc] + landed[0, part, :].astype(F32)
-            + landed[1, part, :].astype(F32) + landed[2, part, :].astype(F32)
+            + landed[1, part, :].astype(F32)
         )
         mid_ref[part, :] = value
         sums[4, :, part] = as_row(jnp.sum(value * value, axis=1, keepdims=True))
@@ -885,7 +913,7 @@
 
     for copy in (
         small + [grad_cross, beside, beyond, corner] + shared + grads + grads_shared
-        + [to_sibling] + pieces + again
+        + [to_sibling] + pieces + corners + again
     ):
         copy.wait_send()
 
@@ -2094,6 +2122,40 @@
     )(x, gain, scale, mid, gain_two, begin, weight_in, weight_out, q, kv, att, lse, normed, n2, dgate, dup)
 
 
+def closing_kernel(
+    tokens, query, key, value, out, hidden, down,
+    tokens_out, query_out, key_out, value_out, out_out, gate_out, up_out, down_out,
+):
+    for src, dst in (
+        (tokens, tokens_out), (query, query_out), (key, key_out), (value, value_out), (out, out_out)
+    ):
+        dst[...] = src[...]
+    for dst, kind in ((gate_out, 0), (up_out, 1)):
+        dst[...] = hidden[kind, 0].astype(F32) + hidden[kind, 1].astype(F32) + hidden[kind, 2].astype(F32)
+    down_out[...] = down[0, 0].astype(F32) + down[0, 1].astype(F32) + down[0, 2].astype(F32)
+
+
+def closing(tokens, query, key, value, out, hidden, down):
+    steps = 8
+
+    def rows_of(array):
+        rows, width = array.shape[-2:]
+        lead = array.shape[:-2]
+        return pl.BlockSpec(lead + (rows // steps, width), lambda t: (0,) * len(lead) + (t, 0))
+
+    finals = [tokens, query, key, value, out] + [
+        jax.ShapeDtypeStruct(a.shape[-2:], F32) for a in (hidden, hidden, down)
+    ]
+    return pl.pallas_call(
+        closing_kernel,
+        grid=(steps,),
+        in_specs=[rows_of(a) for a in (tokens, query, key, value, out, hidden, down)],
+        out_specs=[rows_of(a) for a in finals],
+        out_shape=[jax.ShapeDtypeStruct(a.shape, F32) for a in finals],
+        compiler_params=pltpu.CompilerParams(vmem_limit_bytes=62 << 20),
+    )(tokens, query, key, value, out, hidden, down)
+
+
 def on_small_mesh(
     tokens,
     cotangent,
@@ -2125,22 +2187,8 @@
         tokens, attn_gain[None, :], scale_one, grad_mid, gain_two_part, weight_in, weight_out, q,
         key_value, own_attended, lse, begin, normed_one, normed_two, grad_gate, grad_up,
     )
-
-    def whole(pieces):
-        return pieces[0].astype(F32) + pieces[1].astype(F32) + pieces[2].astype(F32)
-
-    return (
-        grad_tokens,
-        grad_query,
-        grad_key,
-        grad_value,
-        grad_out,
-        whole(got[0]),
-        whole(got[1]),
-        whole(got_down[0]),
-        gains[0],
-        gains[1],
-    )
+    finals = closing(grad_tokens, grad_query, grad_key, grad_value, grad_out, got, got_down)
+    return (*finals, gains[0], gains[1])
 
 
 def solution(mesh):

time: 488 us -> 479 us (0.982)
  other arithmetic: 9.87 us -> 0 us
  Pallas kernels: 464 us -> 469 us
    pallas_call x0 -> x1, Pallas kernels: none -> 10 us  [closing(): pl.pallas_call(closing_kernel, grid=(steps,), in_specs=[rows_of(a) for a...]
    add x2 -> x0, other arithmetic: 9.87 us -> none  [whole(): return pieces[0].astype(F32) + pieces[1].astype(F32) + pieces[2].astype(F32)]
    pallas_call x1, Pallas kernels: 144 us -> 139 us  [forward(): pl.pallas_call(forward_kernel, in_specs=[vmem] * 3 + [smem] + [vmem] * 4...]
where the time goes in v7:
time: 479 us; the launch traced here: 472 us
  Pallas kernels  469 us (98%)
    pallas_call x1, Pallas kernels, middle(): pl.pallas_call(middle_kernel, in_specs=[vmem] * 6 + [hbm] * 4, out_specs=...  167 us
    pallas_call x1, Pallas kernels, backward(): pl.pallas_call(backward_kernel, in_specs=[vmem] * 6 + [hbm] * 10, out_spe...  153 us
    pallas_call x1, Pallas kernels, forward(): pl.pallas_call(forward_kernel, in_specs=[vmem] * 3 + [smem] + [vmem] * 4...  139 us
    pallas_call x1, Pallas kernels, closing(): pl.pallas_call(closing_kernel, grid=(steps,), in_specs=[rows_of(a) for a...  10 us

profile of v7, /device:TPU:0, one launch (start us, length us, event | category | flops | bytes accessed | tf_op | source)
XLA Modules:
  0.0 471.6 jit_solution(3356370551604552449)
XLA Ops:
  0.6 138.6 %shard_map.195 = (f32[512,512]{1,0:T(8,128)}, f32[512,1]{1,0:T(8,128)}, bf16[512,512]{1,0:T(8,128)(2,1)}, s32[1024,1]{1,0:T(8,128)}, f32[512,1]{1,0:T(8,128)}, /...) custom-call(bf16[512,512]{1,0:T(8,128)(2,1)} %x_ref.3, ...), custom_call_target="tpu_custom_call" | custom-call | flops 3221225472 | bytes 67108864 | tf_op jit(solution)/shard_map/pallas_call | solution.py:956
  139.2 167.2 %shard_map.196 = (f32[512,512]{1,0:T(8,128)}, f32[1,512]{1,0:T(1,128)}, bf16[1,3,1024,512]{3,2,1,0:T(8,128)(2,1)}, bf16[1,2,1024,512]{3,2,1,0:T(8,128)(2,1)}, bf...) custom-call(bf16[512,512]{1,0:T(8,128)(2,1)} %get-tuple-element.48.n2_ref, ...), custom_call_target="tpu_custom_call" | custom-call | flops 30064771072 | bytes 50331648 | tf_op jit(solution)/shard_map/pallas_call | solution.py:1650
  306.4 153.3 %shard_map.197 = (f32[512,512]{1,0:T(8,128)}, f32[512,256]{1,0:T(8,128)}, f32[512,256]{1,0:T(8,128)}, f32[512,256]{1,0:T(8,128)}, f32[256,512]{1,0:T(8,128)}, /*...) custom-call(bf16[512,512]{1,0:T(8,128)(2,1)} %x_ref.3, f32[1,512]{1,0:T(1,128)} %bitcast.9, ...), custom_call_target="tpu_custom_call" | custom-call | flops 15032385536 | bytes 67108864 | tf_op jit(solution)/shard_map/pallas_call | solution.py:2070
  459.7 10.0 %shard_map.198 = (f32[512,512]{1,0:T(8,128)}, f32[512,256]{1,0:T(8,128)}, f32[512,256]{1,0:T(8,128)}, f32[512,256]{1,0:T(8,128)}, f32[256,512]{1,0:T(8,128)}, /*...) custom-call(f32[512,512]{1,0:T(8,128)} %get-tuple-element.68.tokens, ...), custom_call_target="tpu_custom_call" | custom-call | tf_op jit(solution)/shard_map/pallas_call | solution.py:2149
  469.8 1.4 fusion

commit v8 on v7

--- a/solution.py
+++ b/solution.py
@@ -449,13 +449,16 @@
 
         lax.fori_loop(0, half // 64, one, 0)
 
-    corner_x.wait_recv()
-    add(low(0, half, 1), 0)
-    sent.append(post.send(low(0, half, 1), landed.at[1, upper], y_at))
-    corner_y.wait_recv()
-    add(low(rows + half, half, 0), half)
-    sent.append(post.send(low(rows + half, half, 0), landed.at[0, lower], x_at))
-    return sent, [corner_x, corner_y]
+    def pass_pieces():
+        corner_x.wait_recv()
+        add(low(0, half, 1), 0)
+        later = [post.send(low(0, half, 1), landed.at[1, upper], y_at)]
+        corner_y.wait_recv()
+        add(low(rows + half, half, 0), half)
+        later.append(post.send(low(rows + half, half, 0), landed.at[0, lower], x_at))
+        return later
+
+    return sent, [corner_x, corner_y], pass_pieces
 
 
 def forward_kernel(
@@ -595,14 +598,36 @@
     def to_core(kind):
         return ship(kind, 0, 1, (d, r, c ^ 1))
 
-    def over_y(kind):
-        return ship(kind, 1, 2 + core, (d, r, 2 * (1 - y)))
+    first_half = post.take(8)
+
+    def gate_half(i, n):
+        step = fc // 2
+        return gate_all.at[pl.ds(pl.multiple_of(place_of(i) * fc + n * step, step), step), :]
+
+    def over_y(n):
+        return pltpu.make_async_remote_copy(
+            src_ref=hidden_own.at[0, pl.ds(n * (fc // 2), fc // 2), :], dst_ref=gate_half(2 + core, n),
+            send_sem=send_sem.at[first_half + 4 * n], recv_sem=recv_sem.at[first_half + 4 * n + core],
+            device_id=(d, r, 2 * (1 - y)), device_id_type=MESH,
+        )
 
     def over_x(kind):
         return ship(kind, 2, 1 - core, (d, r ^ 1, 2 * y + 1))
 
-    def relay(kind, i):
-        return ship(kind, i + 1, 5 - i, (d, r ^ 1, 2 * y + 1), slab(kind, i))
+    def relay(n, i):
+        return pltpu.make_async_remote_copy(
+            src_ref=gate_half(i, n), dst_ref=gate_half(5 - i, n),
+            send_sem=send_sem.at[first_half + 4 * n + i - 1],
+            recv_sem=recv_sem.at[first_half + 4 * n + 3 - i],
+            device_id=(d, r ^ 1, 2 * y + 1), device_id_type=MESH,
+        )
+
+    def gate_came(n, i):
+        return pltpu.make_async_remote_copy(
+            src_ref=gate_half(i, n), dst_ref=gate_half(i, n),
+            send_sem=send_sem.at[first_half], recv_sem=recv_sem.at[first_half + 4 * n + i - 2],
+            device_id=(d, r, c), device_id_type=MESH,
+        )
 
     def start_home(kind):
         @pl.when(core == 0)
@@ -613,12 +638,12 @@
         def _():
             to_core(kind).start()
 
-    def start_relay(kind):
+    def start_relay(n):
         @pl.when(core == 0)
         def _():
             for i in (2, 3):
-                ship(kind, 0, i, (d, r, c)).wait_recv()
-                relay(kind, i).start()
+                gate_came(n, i).wait_recv()
+                relay(n, i).start()
 
     def cast_hidden(kind):
         def put(part, value):
@@ -733,6 +758,7 @@
     for copy in shared:
         copy.wait_recv()
     arrived_blocks(0)
+    over_y(1).start()
     copy_out(normed_ref, normed_out)
 
     def turned(t):
@@ -768,10 +794,18 @@
     copy_out(weight_in, weight_in_out)
     copy_out(q_ref, q_out)
     line_step(3, (2,))
-    grad_cross.wait_recv()
-    grad_keep.wait()
+    @pl.when(d == 0)
+    def _():
+        kv_ref[pl.ds(0, REACH), :] = jnp.zeros((REACH, 2 * width), BF)
+
+    @pl.when(d > 0)
+    def _():
+        halo.wait_recv()
+
+    copy_out(kv_ref, kv_out)
+
     grads = [
-        post.send(
+        post.ready(
             grad_all.at[pl.ds(0, half_rows), pl.ds(0, half)],
             grad_all.at[pl.ds(j * half_rows, half_rows), pl.ds(0, half)],
             (d ^ j, r, c),
@@ -779,22 +813,20 @@
         for j in (1, 2, 3)
     ]
     grads_shared = [
-        post.send(
+        post.ready(
             grad_all.at[pl.ds(0, half_rows), pl.ds(0, half)],
             grad_all.at[pl.ds(0, half_rows), pl.ds(half, half)],
             sibling,
         )
     ]
 
-    @pl.when(d == 0)
-    def _():
-        kv_ref[pl.ds(0, REACH), :] = jnp.zeros((REACH, 2 * width), BF)
-
-    @pl.when(d > 0)
-    def _():
-        halo.wait_recv()
-
-    copy_out(kv_ref, kv_out)
+    def spread_grads():
+        grad_cross.wait_recv()
+        grad_keep.wait()
+        for copy in grads + grads_shared[:1]:
+            copy.start()
+
+    pl.when(d > 0)(spread_grads)
 
     span = TILE + REACH
     for h in range(width // HEAD_DIM):
@@ -823,6 +855,8 @@
 
         lax.fori_loop(0, group // TILE, one, 0)
 
+    pl.when(d == 0)(spread_grads)
+
     copy_out(att_ref, att_out)
     copy_out(lse_ref, lse_out)
     arrived_blocks(2)
@@ -854,9 +888,11 @@
         return total
 
     lax.fori_loop(0, group // 128, add_low, 0)
-    pieces, corners = scatter_plane(
+    pieces, corners, pass_pieces = scatter_plane(
         post, lambda first, count, place: low.at[pl.ds(first, count), columns(place)], landed, rows, (d, r, c)
     )
+    pieces = pieces + pass_pieces()
+    start_relay(1)
     for copy in pieces:
         copy.wait_recv()
 
@@ -893,7 +929,19 @@
         )
     for copy in grads_shared:
         copy.wait_recv()
-    over_y(0).wait_send()
+    for n in (0, 1):
+        over_y(n).wait_send()
+
+        @pl.when(core == 0)
+        def _(n=n):
+            for i in (2, 3):
+                relay(n, i).wait_send()
+
+        @pl.when(core == 1)
+        def _(n=n):
+            for i in (2, 3):
+                gate_came(n, i).wait_recv()
+
     for kind in (0, 1):
         over_x(kind).wait_send()
 
@@ -901,14 +949,11 @@
         def _(kind=kind):
             keep_hidden(kind).wait()
             ship(kind, 0, 1, (d, r, c)).wait_recv()
-            if kind == 0:
-                for i in (2, 3):
-                    relay(kind, i).wait_send()
 
         @pl.when(core == 1)
         def _(kind=kind):
             to_core(kind).wait_send()
-            for i in range(COL if kind == 0 else 2):
+            for i in (0, 1):
                 ship(kind, 0, i, (d, r, c)).wait_recv()
 
     for copy in (
@@ -938,7 +983,7 @@
                 to_column(n, p).wait_send()
 
 
-SENDS = 96
+SENDS = 104
 
 
 def forward(x, gain_one, gain_two, lengths, query, key, value, out, gate, up, own_grad):
@@ -1089,25 +1134,34 @@
             for p in (0, 1, 2):
                 self.down(p)
 
-    def rest(self):
+    def first(self):
         d = self.me[0]
-
-        @pl.when(d == 0)
-        def _():
-            self.down(0)
 
         @pl.when(d == 1)
         def _():
             self.up(3)
             self.up(2)
+
+        @pl.when(d == 2)
+        def _():
+            self.down(0)
+            self.down(1)
+
+    def last(self):
+        d = self.me[0]
+
+        @pl.when(d == 0)
+        def _():
+            self.down(0)
+
+        @pl.when(d == 1)
+        def _():
             self.down(0)
             self.down(1)
             self.up(1)
 
         @pl.when(d == 2)
         def _():
-            self.down(0)
-            self.down(1)
             self.up(3)
             self.up(2)
             self.down(2)
@@ -1115,6 +1169,10 @@
         @pl.when(d == DP - 1)
         def _():
             self.up(3)
+
+    def rest(self):
+        self.first()
+        self.last()
 
     def settle(self):
         d = self.me[0]
@@ -1952,14 +2010,9 @@
 
     loop(tiles, kept_part)
 
-    def low(where, place):
-        return n2.at[where, pl.ds(half + place * fc, fc)]
-
-    pieces = [
-        post.send(low(other_rows, 1), landed.at[2], (d, r ^ 1, c ^ 2)),
-        post.send(low(other_rows, 0), landed.at[0], (d, r ^ 1, c)),
-        post.send(low(own_rows, 1), landed.at[1], (d, r, c ^ 2)),
-    ]
+    pieces, corners, pass_pieces = scatter_plane(
+        post, lambda first, count, place: n2.at[pl.ds(first, count), pl.ds(half + place * fc, fc)], landed, rows, me
+    )
 
     def finish(line, z, got_z, dests):
         def one(t):
@@ -1969,11 +2022,13 @@
 
         loop(z.shape[1] // 64, one)
 
+    line_a.first()
+    pieces = pieces + pass_pieces()
     owners.start_near()
-    line_a.rest()
     for copy in kvs:
         copy.wait_recv()
     line_b.begin()
+    line_a.last()
 
     for copy in pieces:
         copy.wait_recv()
@@ -1981,7 +2036,7 @@
     def inner_sum(t):
         part = at(t, 128)
         value = own_f[part, :]
-        for n in range(3):
+        for n in range(2):
             value = value + landed[n, part, :].astype(F32)
         own_f[part, :] = value
         inner = value * gain_ref[...] * x_ref[part, :].astype(F32)
@@ -2045,7 +2100,7 @@
     owners.settle()
     line_a.settle()
     line_b.settle()
-    for copy in [beside, beyond] + corner + shared + qs + kvs + [to_sibling] + pieces + small:
+    for copy in [beside, beyond] + corner + shared + qs + kvs + [to_sibling] + pieces + corners + small:
         copy.wait_send()
     for n, (j, a) in enumerate(far):
         gain_copy(n, j, a).wait_send()
@@ -2123,8 +2178,8 @@
 
 
 def closing_kernel(
-    tokens, query, key, value, out, hidden, down,
-    tokens_out, query_out, key_out, value_out, out_out, gate_out, up_out, down_out,
+    tokens, query, key, value, out, hidden, down, gains,
+    tokens_out, query_out, key_out, value_out, out_out, gate_out, up_out, down_out, one_out, two_out,
 ):
     for src, dst in (
         (tokens, tokens_out), (query, query_out), (key, key_out), (value, value_out), (out, out_out)
@@ -2132,11 +2187,13 @@
         dst[...] = src[...]
     for dst, kind in ((gate_out, 0), (up_out, 1)):
         dst[...] = hidden[kind, 0].astype(F32) + hidden[kind, 1].astype(F32) + hidden[kind, 2].astype(F32)
+    one_out[...] = gains[0]
+    two_out[...] = gains[1]
     down_out[...] = down[0, 0].astype(F32) + down[0, 1].astype(F32) + down[0, 2].astype(F32)
 
 
-def closing(tokens, query, key, value, out, hidden, down):
-    steps = 8
+def closing(tokens, query, key, value, out, hidden, down, gains):
+    steps = 4
 
     def rows_of(array):
         rows, width = array.shape[-2:]
@@ -2149,11 +2206,13 @@
     return pl.pallas_call(
         closing_kernel,
         grid=(steps,),
-        in_specs=[rows_of(a) for a in (tokens, query, key, value, out, hidden, down)],
-        out_specs=[rows_of(a) for a in finals],
-        out_shape=[jax.ShapeDtypeStruct(a.shape, F32) for a in finals],
+        in_specs=[rows_of(a) for a in (tokens, query, key, value, out, hidden, down)]
+        + [pl.BlockSpec(gains.shape, lambda t: (0, 0))],
+        out_specs=[rows_of(a) for a in finals] + [pl.BlockSpec(gains.shape[1:], lambda t: (0,))] * 2,
+        out_shape=[jax.ShapeDtypeStruct(a.shape, F32) for a in finals]
+        + [jax.ShapeDtypeStruct(gains.shape[1:], F32)] * 2,
         compiler_params=pltpu.CompilerParams(vmem_limit_bytes=62 << 20),
-    )(tokens, query, key, value, out, hidden, down)
+    )(tokens, query, key, value, out, hidden, down, gains)
 
 
 def on_small_mesh(
@@ -2187,8 +2246,7 @@
         tokens, attn_gain[None, :], scale_one, grad_mid, gain_two_part, weight_in, weight_out, q,
         key_value, own_attended, lse, begin, normed_one, normed_two, grad_gate, grad_up,
     )
-    finals = closing(grad_tokens, grad_query, grad_key, grad_value, grad_out, got, got_down)
-    return (*finals, gains[0], gains[1])
+    return closing(grad_tokens, grad_query, grad_key, grad_value, grad_out, got, got_down, gains)
 
 
 def solution(mesh):

time: 479 us -> 468 us (0.977)
  Pallas kernels: 469 us -> 459 us
    pallas_call x1, Pallas kernels: 167 us -> 160 us  [middle(): pl.pallas_call(middle_kernel, in_specs=[vmem] * 6 + [hbm] * 4, out_specs=...]
where the time goes in v8:
time: 468 us; the launch traced here: 460 us
  Pallas kernels  459 us (98%)
    pallas_call x1, Pallas kernels, middle(): pl.pallas_call(middle_kernel, in_specs=[vmem] * 6 + [hbm] * 4, out_specs=...  160 us
    pallas_call x1, Pallas kernels, backward(): pl.pallas_call(backward_kernel, in_specs=[vmem] * 6 + [hbm] * 10, out_spe...  150 us
    pallas_call x1, Pallas kernels, forward(): pl.pallas_call(forward_kernel, in_specs=[vmem] * 3 + [smem] + [vmem] * 4...  141 us

profile of v8, /device:TPU:0, one launch (start us, length us, event | category | flops | bytes accessed | tf_op | source)
XLA Modules:
  0.0 460.3 jit_solution(10114186145297670032)
XLA Ops:
  0.6 141.4 %shard_map.195 = (f32[512,512]{1,0:T(8,128)}, f32[512,1]{1,0:T(8,128)}, bf16[512,512]{1,0:T(8,128)(2,1)}, s32[1024,1]{1,0:T(8,128)}, f32[512,1]{1,0:T(8,128)}, /...) custom-call(bf16[512,512]{1,0:T(8,128)(2,1)} %x_ref.3, ...), custom_call_target="tpu_custom_call" | custom-call | flops 3221225472 | bytes 67108864 | tf_op jit(solution)/shard_map/pallas_call | solution.py:1001
  142.1 159.9 %shard_map.196 = (f32[512,512]{1,0:T(8,128)}, f32[1,512]{1,0:T(1,128)}, bf16[1,3,1024,512]{3,2,1,0:T(8,128)(2,1)}, bf16[1,2,1024,512]{3,2,1,0:T(8,128)(2,1)}, bf...) custom-call(bf16[512,512]{1,0:T(8,128)(2,1)} %get-tuple-element.40.n2_ref, ...), custom_call_target="tpu_custom_call" | custom-call | flops 30064771072 | bytes 50331648 | tf_op jit(solution)/shard_map/pallas_call | solution.py:1708
  302.0 149.6 %shard_map.197 = (f32[512,512]{1,0:T(8,128)}, f32[512,256]{1,0:T(8,128)}, f32[512,256]{1,0:T(8,128)}, f32[512,256]{1,0:T(8,128)}, f32[256,512]{1,0:T(8,128)}, /*...) custom-call(bf16[512,512]{1,0:T(8,128)(2,1)} %x_ref.3, f32[1,512]{1,0:T(1,128)} %bitcast.5, ...), custom_call_target="tpu_custom_call" | custom-call | flops 15032385536 | bytes 67108864 | tf_op jit(solution)/shard_map/pallas_call | solution.py:2125
  451.6 8.3 %shard_map.198 = (f32[512,512]{1,0:T(8,128)}, f32[512,256]{1,0:T(8,128)}, f32[512,256]{1,0:T(8,128)}, f32[512,256]{1,0:T(8,128)}, f32[256,512]{1,0:T(8,128)}, /*...) custom-call(f32[512,512]{1,0:T(8,128)} %get-tuple-element.60.tokens, ...), custom_call_target="tpu_custom_call" | custom-call | tf_op jit(solution)/shard_map/pallas_call | solution.py:2206

commit v9 on v8

--- a/solution.py
+++ b/solution.py
@@ -1134,18 +1134,20 @@
             for p in (0, 1, 2):
                 self.down(p)
 
+    def hop(self, n):
+        d = self.me[0]
+
+        @pl.when(d == 1)
+        def _():
+            self.up(DP - 1 - n)
+
+        @pl.when(d == 2)
+        def _():
+            self.down(n)
+
     def first(self):
-        d = self.me[0]
-
-        @pl.when(d == 1)
-        def _():
-            self.up(3)
-            self.up(2)
-
-        @pl.when(d == 2)
-        def _():
-            self.down(0)
-            self.down(1)
+        self.hop(0)
+        self.hop(1)
 
     def last(self):
         d = self.me[0]
@@ -1530,32 +1532,12 @@
 
     loop(DP, project_up)
 
-    @pl.when(core == 1)
-    def _():
-        for n in (0, 1):
-            for i in (2, 3):
-                ship(n, 0, i, me).wait_recv()
-
-    hidden_grads(2, False)
-
-    def units_of(t):
+    def hidden_of(t):
         part = at(t, 64)
-        g, u, grad = gate[part, :], up[part, :], du[part, :]
-        sigmoid = 1.0 / (1.0 + jnp.exp(-g))
-        silu = g * sigmoid
-        hidden[part, :] = (silu * u).astype(BF)
-        dgate[part, :] = (grad * u * sigmoid * (1.0 + g * (1.0 - sigmoid))).astype(BF)
-        dup[part, :] = (grad * silu).astype(BF)
-
-    loop(2 * rows // 64, units_of)
-    for n, (src, dst) in enumerate(((dgate, dgate_out), (dup, dup_out))):
-        outs.append(pltpu.make_async_copy(src, dst, local_sem.at[1 + n]))
-        outs[-1].start()
-
-    def back(part, cols):
-        return lax.dot_general(
-            dgate[part, :], wg[cols, :], across, preferred_element_type=F32
-        ) + lax.dot_general(dup[part, :], wu[cols, :], across, preferred_element_type=F32)
+        g = gate[part, :]
+        hidden[part, :] = (g * (1.0 / (1.0 + jnp.exp(-g))) * up[part, :]).astype(BF)
+
+    loop(2 * rows // 64, hidden_of)
 
     def down_part(i):
         def down_grad(t):
@@ -1567,6 +1549,36 @@
         loop(units // TILE, down_grad)
 
     owners = PlaneSum(raw, stage, got, comb, post.take(10), local_sem, 4, me)
+    down_part(2)
+    down_part(3)
+
+    @pl.when(core == 1)
+    def _():
+        for n in (0, 1):
+            for i in (2, 3):
+                ship(n, 0, i, me).wait_recv()
+
+    hidden_grads(2, False)
+
+    owners.start_far()
+
+    def units_of(t):
+        part = at(t, 64)
+        g, u, grad = gate[part, :], up[part, :], du[part, :]
+        sigmoid = 1.0 / (1.0 + jnp.exp(-g))
+        silu = g * sigmoid
+        dgate[part, :] = (grad * u * sigmoid * (1.0 + g * (1.0 - sigmoid))).astype(BF)
+        dup[part, :] = (grad * silu).astype(BF)
+
+    loop(2 * rows // 64, units_of)
+    for n, (src, dst) in enumerate(((dgate, dgate_out), (dup, dup_out))):
+        outs.append(pltpu.make_async_copy(src, dst, local_sem.at[1 + n]))
+        outs[-1].start()
+
+    def back(part, cols):
+        return lax.dot_general(
+            dgate[part, :], wg[cols, :], across, preferred_element_type=F32
+        ) + lax.dot_general(dup[part, :], wu[cols, :], across, preferred_element_type=F32)
 
     line = LineSum(raw, ((z, got_z),), post.take(8), me)
 
@@ -1601,9 +1613,6 @@
     first_given = post.take(DP)
     give(0)
     give(1)
-    down_part(2)
-    down_part(3)
-    owners.start_far()
     keep(0)
     give(2)
     keep(1)
@@ -1613,8 +1622,15 @@
     down_part(1)
     owners.start_near()
     keep(3)
-    owners.combine(lambda kind, j: wg.at[pl.ds(0, units), pl.ds(j * fc, fc)], 5)
-    line.rest()
+
+    def combine():
+        owners.combine(lambda kind, j: wg.at[pl.ds(0, units), pl.ds(j * fc, fc)], 5)
+
+    pl.when(jnp.logical_not(inner))(combine)
+    line.hop(0)
+    pl.when(inner)(combine)
+    line.hop(1)
+    line.last()
 
     def settle_rows(t):
         part = at(t, 64)

time: 468 us -> 459 us (0.981)
  Pallas kernels: 459 us -> 450 us
    pallas_call x1, Pallas kernels: 160 us -> 151 us  [middle(): pl.pallas_call(middle_kernel, in_specs=[vmem] * 6 + [hbm] * 4, out_specs=...]
where the time goes in v9:
time: 459 us; the launch traced here: 451 us
  Pallas kernels  450 us (98%)
    pallas_call x1, Pallas kernels, middle(): pl.pallas_call(middle_kernel, in_specs=[vmem] * 6 + [hbm] * 4, out_specs=...  151 us
    pallas_call x1, Pallas kernels, backward(): pl.pallas_call(backward_kernel, in_specs=[vmem] * 6 + [hbm] * 10, out_spe...  150 us
    pallas_call x1, Pallas kernels, forward(): pl.pallas_call(forward_kernel, in_specs=[vmem] * 3 + [smem] + [vmem] * 4...  141 us

profile of v9, /device:TPU:0, one launch (start us, length us, event | category | flops | bytes accessed | tf_op | source)
XLA Modules:
  0.0 451.3 jit_solution(6415721356241412387)
XLA Ops:
  0.6 141.4 %shard_map.195 = (f32[512,512]{1,0:T(8,128)}, f32[512,1]{1,0:T(8,128)}, bf16[512,512]{1,0:T(8,128)(2,1)}, s32[1024,1]{1,0:T(8,128)}, f32[512,1]{1,0:T(8,128)}, /...) custom-call(bf16[512,512]{1,0:T(8,128)(2,1)} %x_ref.3, ...), custom_call_target="tpu_custom_call" | custom-call | flops 3221225472 | bytes 67108864 | tf_op jit(solution)/shard_map/pallas_call | solution.py:1001
  142.1 150.9 %shard_map.196 = (f32[512,512]{1,0:T(8,128)}, f32[1,512]{1,0:T(1,128)}, bf16[1,3,1024,512]{3,2,1,0:T(8,128)(2,1)}, bf16[1,2,1024,512]{3,2,1,0:T(8,128)(2,1)}, bf...) custom-call(bf16[512,512]{1,0:T(8,128)(2,1)} %get-tuple-element.40.n2_ref, ...), custom_call_target="tpu_custom_call" | custom-call | flops 30064771072 | bytes 50331648 | tf_op jit(solution)/shard_map/pallas_call | solution.py:1724
  293.0 149.6 %shard_map.197 = (f32[512,512]{1,0:T(8,128)}, f32[512,256]{1,0:T(8,128)}, f32[512,256]{1,0:T(8,128)}, f32[512,256]{1,0:T(8,128)}, f32[256,512]{1,0:T(8,128)}, /*...) custom-call(bf16[512,512]{1,0:T(8,128)(2,1)} %x_ref.3, f32[1,512]{1,0:T(1,128)} %bitcast.5, ...), custom_call_target="tpu_custom_call" | custom-call | flops 15032385536 | bytes 67108864 | tf_op jit(solution)/shard_map/pallas_call | solution.py:2141
  442.6 8.3 %shard_map.198 = (f32[512,512]{1,0:T(8,128)}, f32[512,256]{1,0:T(8,128)}, f32[512,256]{1,0:T(8,128)}, f32[512,256]{1,0:T(8,128)}, f32[256,512]{1,0:T(8,128)}, /*...) custom-call(f32[512,512]{1,0:T(8,128)} %get-tuple-element.60.tokens, ...), custom_call_target="tpu_custom_call" | custom-call | tf_op jit(solution)/shard_map/pallas_call | solution.py:2222

commit v10 on v9

--- a/solution.py
+++ b/solution.py
@@ -1231,28 +1231,30 @@
                 for kind in self.kinds:
                     self.from_one(kind, i).start()
 
-    def start_near(self):
+    def start_near(self, kinds=None):
+        kinds = self.kinds if kinds is None else kinds
         core = lax.rem(self.me[2], 2)
 
         @pl.when(core == 1)
         def _():
             for i in (0, 1):
-                for kind in self.kinds:
+                for kind in kinds:
                     self.from_one(kind, i).start()
 
         @pl.when(core == 0)
         def _():
-            for kind in self.kinds:
+            for kind in kinds:
                 self.home(kind).start()
                 self.from_zero(kind, 1).start()
 
-    def combine(self, room, local_base):
+    def combine(self, room, local_base, kinds=None):
+        kinds = self.kinds if kinds is None else kinds
         core = lax.rem(self.me[2], 2)
 
         @pl.when(core == 0)
         def _():
             for i in (2, 3):
-                for kind in self.kinds:
+                for kind in kinds:
                     self.raw(
                         self.stage.at[kind, i], self.comb.at[kind, i - 2], self.base,
                         self.base + 10 * kind + 3 + (i - 2), self.me,
@@ -2040,10 +2042,15 @@
 
     line_a.first()
     pieces = pieces + pass_pieces()
-    owners.start_near()
     for copy in kvs:
         copy.wait_recv()
     line_b.begin()
+
+    def combine(kind):
+        owners.combine(lambda kind, j: n1.at[pl.ds(j * fc, fc), pl.ds(kind * units, units)], 0, (kind,))
+
+    owners.start_near((0,))
+    combine(0)
     line_a.last()
 
     for copy in pieces:
@@ -2081,9 +2088,8 @@
     far = [(j, a) for j in range(DP) for a in (0, 1) if (j, a) != (0, 0)]
     for n, (j, a) in enumerate(far):
         gain_copy(n, j, a).start()
-    owners.combine(lambda kind, j: n1.at[pl.ds(j * fc, fc), pl.ds(kind * units, units)], 0)
-
-
+    owners.start_near((1,))
+    combine(1)
     line_b.rest()
     finish(line_a, zq, rq, ((query_out, slice(None)),))
     finish(line_a, zo, ro, ((out_out, slice(None)),))

time: 459 us -> 453 us (0.987)
  Pallas kernels: 450 us -> 445 us
    pallas_call x1, Pallas kernels: 150 us -> 145 us  [backward(): pl.pallas_call(backward_kernel, in_specs=[vmem] * 6 + [hbm] * 10, out_spe...]
where the time goes in v10:
time: 453 us; the launch traced here: 446 us
  Pallas kernels  445 us (98%)
    pallas_call x1, Pallas kernels, middle(): pl.pallas_call(middle_kernel, in_specs=[vmem] * 6 + [hbm] * 4, out_specs=...  151 us
    pallas_call x1, Pallas kernels, backward(): pl.pallas_call(backward_kernel, in_specs=[vmem] * 6 + [hbm] * 10, out_spe...  145 us
    pallas_call x1, Pallas kernels, forward(): pl.pallas_call(forward_kernel, in_specs=[vmem] * 3 + [smem] + [vmem] * 4...  141 us

profile of v10, /device:TPU:0, one launch (start us, length us, event | category | flops | bytes accessed | tf_op | source)
XLA Modules:
  0.0 446.3 jit_solution(4099929668076883158)
XLA Ops:
  0.6 141.4 %shard_map.195 = (f32[512,512]{1,0:T(8,128)}, f32[512,1]{1,0:T(8,128)}, bf16[512,512]{1,0:T(8,128)(2,1)}, s32[1024,1]{1,0:T(8,128)}, f32[512,1]{1,0:T(8,128)}, /...) custom-call(bf16[512,512]{1,0:T(8,128)(2,1)} %x_ref.3, ...), custom_call_target="tpu_custom_call" | custom-call | flops 3221225472 | bytes 67108864 | tf_op jit(solution)/shard_map/pallas_call | solution.py:1001
  142.1 150.9 %shard_map.196 = (f32[512,512]{1,0:T(8,128)}, f32[1,512]{1,0:T(1,128)}, bf16[1,3,1024,512]{3,2,1,0:T(8,128)(2,1)}, bf16[1,2,1024,512]{3,2,1,0:T(8,128)(2,1)}, bf...) custom-call(bf16[512,512]{1,0:T(8,128)(2,1)} %get-tuple-element.40.n2_ref, ...), custom_call_target="tpu_custom_call" | custom-call | flops 30064771072 | bytes 50331648 | tf_op jit(solution)/shard_map/pallas_call | solution.py:1726
  293.0 144.6 %shard_map.197 = (f32[512,512]{1,0:T(8,128)}, f32[512,256]{1,0:T(8,128)}, f32[512,256]{1,0:T(8,128)}, f32[512,256]{1,0:T(8,128)}, f32[256,512]{1,0:T(8,128)}, /*...) custom-call(bf16[512,512]{1,0:T(8,128)(2,1)} %x_ref.3, f32[1,512]{1,0:T(1,128)} %bitcast.5, ...), custom_call_target="tpu_custom_call" | custom-call | flops 15032385536 | bytes 67108864 | tf_op jit(solution)/shard_map/pallas_call | solution.py:2147
  437.6 8.3 %shard_map.198 = (f32[512,512]{1,0:T(8,128)}, f32[512,256]{1,0:T(8,128)}, f32[512,256]{1,0:T(8,128)}, f32[512,256]{1,0:T(8,128)}, f32[256,512]{1,0:T(8,128)}, /*...) custom-call(f32[512,512]{1,0:T(8,128)} %get-tuple-element.60.tokens, ...), custom_call_target="tpu_custom_call" | custom-call | tf_op jit(solution)/shard_map/pallas_call | solution.py:2228

commit v11 on v10

--- a/solution.py
+++ b/solution.py
@@ -826,7 +826,7 @@
         for copy in grads + grads_shared[:1]:
             copy.start()
 
-    pl.when(d > 0)(spread_grads)
+    pl.when(lax.rem(d, 2) == 1)(spread_grads)
 
     span = TILE + REACH
     for h in range(width // HEAD_DIM):
@@ -855,7 +855,7 @@
 
         lax.fori_loop(0, group // TILE, one, 0)
 
-    pl.when(d == 0)(spread_grads)
+    pl.when(lax.rem(d, 2) == 0)(spread_grads)
 
     copy_out(att_ref, att_out)
     copy_out(lse_ref, lse_out)

time: 453 us -> 450 us (level)
  no operation moved by 1% of the time
where the time goes in v11:
time: 450 us; the launch traced here: 443 us
  Pallas kernels  442 us (98%)
    pallas_call x1, Pallas kernels, middle(): pl.pallas_call(middle_kernel, in_specs=[vmem] * 6 + [hbm] * 4, out_specs=...  148 us
    pallas_call x1, Pallas kernels, backward(): pl.pallas_call(backward_kernel, in_specs=[vmem] * 6 + [hbm] * 10, out_spe...  144 us
    pallas_call x1, Pallas kernels, forward(): pl.pallas_call(forward_kernel, in_specs=[vmem] * 3 + [smem] + [vmem] * 4...  141 us

profile of v11, /device:TPU:0, one launch (start us, length us, event | category | flops | bytes accessed | tf_op | source)
XLA Modules:
  0.0 443.2 jit_solution(17004196042459610344)
XLA Ops:
  0.6 141.4 %shard_map.195 = (f32[512,512]{1,0:T(8,128)}, f32[512,1]{1,0:T(8,128)}, bf16[512,512]{1,0:T(8,128)(2,1)}, s32[1024,1]{1,0:T(8,128)}, f32[512,1]{1,0:T(8,128)}, /...) custom-call(bf16[512,512]{1,0:T(8,128)(2,1)} %x_ref.3, ...), custom_call_target="tpu_custom_call" | custom-call | flops 3221225472 | bytes 67108864 | tf_op jit(solution)/shard_map/pallas_call | solution.py:1001
  142.1 148.1 %shard_map.196 = (f32[512,512]{1,0:T(8,128)}, f32[1,512]{1,0:T(1,128)}, bf16[1,3,1024,512]{3,2,1,0:T(8,128)(2,1)}, bf16[1,2,1024,512]{3,2,1,0:T(8,128)(2,1)}, bf...) custom-call(bf16[512,512]{1,0:T(8,128)(2,1)} %get-tuple-element.40.n2_ref, ...), custom_call_target="tpu_custom_call" | custom-call | flops 30064771072 | bytes 50331648 | tf_op jit(solution)/shard_map/pallas_call | solution.py:1726
  290.2 144.2 %shard_map.197 = (f32[512,512]{1,0:T(8,128)}, f32[512,256]{1,0:T(8,128)}, f32[512,256]{1,0:T(8,128)}, f32[512,256]{1,0:T(8,128)}, f32[256,512]{1,0:T(8,128)}, /*...) custom-call(bf16[512,512]{1,0:T(8,128)(2,1)} %x_ref.3, f32[1,512]{1,0:T(1,128)} %bitcast.5, ...), custom_call_target="tpu_custom_call" | custom-call | flops 15032385536 | bytes 67108864 | tf_op jit(solution)/shard_map/pallas_call | solution.py:2147
  434.5 8.3 %shard_map.198 = (f32[512,512]{1,0:T(8,128)}, f32[512,256]{1,0:T(8,128)}, f32[512,256]{1,0:T(8,128)}, f32[512,256]{1,0:T(8,128)}, f32[256,512]{1,0:T(8,128)}, /*...) custom-call(f32[512,512]{1,0:T(8,128)} %get-tuple-element.60.tokens, ...), custom_call_target="tpu_custom_call" | custom-call | tf_op jit(solution)/shard_map/pallas_call | solution.py:2228

commit v12 on v11

--- a/solution.py
+++ b/solution.py
@@ -1314,38 +1314,6 @@
     raw = maker(send_sem, recv_sem)
     sibling = (d, r, c ^ 1)
     others = [(a, b) for a in (0, 1) for b in range(COL) if (a, b) != (0, 0)]
-    greet([(d, r ^ a, c ^ b) for a, b in others] + [(d ^ j, r, c) for j in (1, 2, 3)])
-
-    cross = post.send(
-        n2_ref.at[pl.ds(pl.multiple_of((1 - y) * block, block), block), :],
-        n2.at[pl.ds(0, block), pl.ds(fc, fc)],
-        (d, r, c ^ 2),
-    )
-    def half_of(ref, i, n):
-        return ref.at[pl.ds(pl.multiple_of(place_of(i) * fc + n * (fc // 2), fc // 2), fc // 2), :]
-
-    def place_of(i):
-        return lax.rem(i, 2) * 2 + i // 2
-
-    first_wide = post.take(8)
-
-    def up_over_y(n):
-        return raw(
-            own_up.at[pl.ds(n * (fc // 2), fc // 2), :], half_of(wu, 2 + core, n),
-            first_wide + 4 * n, first_wide + 4 * n + core, (d, r, 2 * (1 - y)),
-        )
-
-    def up_relay(n, i):
-        return raw(
-            half_of(wu, i, n), half_of(wu, 5 - i, n), first_wide + 4 * n + i - 1,
-            first_wide + 4 * n + 3 - i, (d, r ^ 1, 2 * y + 1),
-        )
-
-    def up_came(n, i):
-        return raw(half_of(wu, i, n), half_of(wu, i, n), first_wide, first_wide + 4 * n + i - 2, me)
-
-    for n in (0, 1):
-        up_over_y(n).start()
     loads = [
         pltpu.make_async_copy(src, dst, local_sem.at[n])
         for n, (src, dst) in zip((0, 1, 2, 9), (
@@ -1362,6 +1330,38 @@
         own_down[at(t, 64), :] = down_ref[at(t, 64), :].astype(BF)
 
     loop(units // 64, cast_down)
+    greet([(d, r ^ a, c ^ b) for a, b in others] + [(d ^ j, r, c) for j in (1, 2, 3)])
+
+    cross = post.send(
+        n2_ref.at[pl.ds(pl.multiple_of((1 - y) * block, block), block), :],
+        n2.at[pl.ds(0, block), pl.ds(fc, fc)],
+        (d, r, c ^ 2),
+    )
+    def half_of(ref, i, n):
+        return ref.at[pl.ds(pl.multiple_of(place_of(i) * fc + n * (fc // 2), fc // 2), fc // 2), :]
+
+    def place_of(i):
+        return lax.rem(i, 2) * 2 + i // 2
+
+    first_wide = post.take(8)
+
+    def up_over_y(n):
+        return raw(
+            own_up.at[pl.ds(n * (fc // 2), fc // 2), :], half_of(wu, 2 + core, n),
+            first_wide + 4 * n, first_wide + 4 * n + core, (d, r, 2 * (1 - y)),
+        )
+
+    def up_relay(n, i):
+        return raw(
+            half_of(wu, i, n), half_of(wu, 5 - i, n), first_wide + 4 * n + i - 1,
+            first_wide + 4 * n + 3 - i, (d, r ^ 1, 2 * y + 1),
+        )
+
+    def up_came(n, i):
+        return raw(half_of(wu, i, n), half_of(wu, i, n), first_wide, first_wide + 4 * n + i - 2, me)
+
+    for n in (0, 1):
+        up_over_y(n).start()
     first_sent = post.take(10)
 
     def piece(ref, n):

time: 450 us -> 450 us (level)
  no operation moved by 1% of the time
where the time goes in v12:
time: 450 us; the launch traced here: 443 us
  Pallas kernels  442 us (98%)
    pallas_call x1, Pallas kernels, middle(): pl.pallas_call(middle_kernel, in_specs=[vmem] * 6 + [hbm] * 4, out_specs=...  148 us
    pallas_call x1, Pallas kernels, backward(): pl.pallas_call(backward_kernel, in_specs=[vmem] * 6 + [hbm] * 10, out_spe...  144 us
    pallas_call x1, Pallas kernels, forward(): pl.pallas_call(forward_kernel, in_specs=[vmem] * 3 + [smem] + [vmem] * 4...  141 us

profile of v12, /device:TPU:0, one launch (start us, length us, event | category | flops | bytes accessed | tf_op | source)
XLA Modules:
  0.0 443.2 jit_solution(14910799062337659516)
XLA Ops:
  0.6 141.4 %shard_map.195 = (f32[512,512]{1,0:T(8,128)}, f32[512,1]{1,0:T(8,128)}, bf16[512,512]{1,0:T(8,128)(2,1)}, s32[1024,1]{1,0:T(8,128)}, f32[512,1]{1,0:T(8,128)}, /...) custom-call(bf16[512,512]{1,0:T(8,128)(2,1)} %x_ref.3, ...), custom_call_target="tpu_custom_call" | custom-call | flops 3221225472 | bytes 67108864 | tf_op jit(solution)/shard_map/pallas_call | solution.py:1001
  142.1 148.2 %shard_map.196 = (f32[512,512]{1,0:T(8,128)}, f32[1,512]{1,0:T(1,128)}, bf16[1,3,1024,512]{3,2,1,0:T(8,128)(2,1)}, bf16[1,2,1024,512]{3,2,1,0:T(8,128)(2,1)}, bf...) custom-call(bf16[512,512]{1,0:T(8,128)(2,1)} %get-tuple-element.40.n2_ref, ...), custom_call_target="tpu_custom_call" | custom-call | flops 30064771072 | bytes 50331648 | tf_op jit(solution)/shard_map/pallas_call | solution.py:1726
  290.3 144.2 %shard_map.197 = (f32[512,512]{1,0:T(8,128)}, f32[512,256]{1,0:T(8,128)}, f32[512,256]{1,0:T(8,128)}, f32[512,256]{1,0:T(8,128)}, f32[256,512]{1,0:T(8,128)}, /*...) custom-call(bf16[512,512]{1,0:T(8,128)(2,1)} %x_ref.3, f32[1,512]{1,0:T(1,128)} %bitcast.5, ...), custom_call_target="tpu_custom_call" | custom-call | flops 15032385536 | bytes 67108864 | tf_op jit(solution)/shard_map/pallas_call | solution.py:2147
  434.5 8.3 %shard_map.198 = (f32[512,512]{1,0:T(8,128)}, f32[512,256]{1,0:T(8,128)}, f32[512,256]{1,0:T(8,128)}, f32[512,256]{1,0:T(8,128)}, f32[256,512]{1,0:T(8,128)}, /*...) custom-call(f32[512,512]{1,0:T(8,128)} %get-tuple-element.60.tokens, ...), custom_call_target="tpu_custom_call" | custom-call | tf_op jit(solution)/shard_map/pallas_call | solution.py:2228
